TPU v7x, 32 devices: a whole 2x2x4 slice. The times are simulated.
32 devices in a mesh: groups: 2 (over y), seq: 4 (over z), strand: 2 (over core), chan: 2 (over x).
Axes of the slice: x: 2, y: 2, z: 4, core: 2. Of those that a mesh axis runs over, the one named last changes fastest.
Arguments:
- seq_in: bfloat16 [2, 6144, 512], P('strand', ('groups', 'seq', 'chan')), parts along dimension 1, may hold values from -6 to 6
- conv_norm: float32 [2, 512], replicated, may hold values from 0.1 to 1.9
- conv_weight: bfloat16 [2, 3, 512, 512], P(None, None, None, ('seq', 'chan')), may hold values from -0.15625 to 0.15625
- ff_norm: float32 [2, 512], replicated, may hold values from 0.1 to 1.9
- up_weight: bfloat16 [2, 512, 2048], P(None, None, ('seq', 'chan')), may hold values from -0.25 to 0.25
- down_weight: bfloat16 [2, 2048, 512], P(None, ('seq', 'chan')), may hold values from -0.125 to 0.125
- head_norm: float32 [512], replicated, may hold values from 0.1 to 1.9
- value_weight: bfloat16 [512, 512], replicated, may hold values from -0.25 to 0.25
- gate_weight: bfloat16 [512, 512], replicated, may hold values from -0.25 to 0.25
- out_weight: bfloat16 [512, 512], replicated, may hold values from -0.25 to 0.25
Outputs:
- strand_out: bfloat16 [2, 6144, 512], P('strand', ('groups', 'seq', 'chan')), parts along dimension 1
There are 2 independent parts, one for each index of `groups`. A program takes and returns all parts, laid end to end along the dimension named above; an argument that names none is the same for every part. Nothing has to cross between parts.
All inputs are finite; a program needn't handle non-finite values.
Results may differ from a plain program's by a relative error of at most 0.015.
Values may be sent and summed in bfloat16 or wider, within the bound.
No kernel may reach another device: no remote copies, remote signals or barrier semaphores. Data moves between devices by JAX's collectives and lax.ppermute only.
A program may use at most 64 MiB of HBM per device.

v0:
```python
import jax
import jax.numpy as jnp
from jax import lax
from jax.sharding import PartitionSpec as P


def passed_along(value, axis, steps):
    count = lax.axis_size(axis)
    initial, last = (max(0, -steps), min(count, count - steps))
    return lax.ppermute(value, axis, [(source, source + steps) for source in range(initial, last)])


def swapped(x, axis, stride):
    return lax.ppermute(x, axis, [(i, i ^ 1 << stride) for i in range(lax.axis_size(axis))])


def normalize(values, gain):
    return values * lax.rsqrt(jnp.mean(values * values, axis=-1, keepdims=True) + 1e-06) * gain


def matmul(left, right):
    return jnp.dot(left, right, preferred_element_type=jnp.float32)


def local(
    seq_in,
    conv_norm,
    conv_weight,
    ff_norm,
    up_weight,
    down_weight,
    head_norm,
    value_weight,
    gate_weight,
    out_weight,
):
    state = seq_in[0].astype(jnp.float32)
    seq_count = lax.axis_size("seq")
    for block in range(conv_weight.shape[0]):
        reach = min(2**block, seq_count // 2)
        normed = normalize(state, conv_norm[block]).astype(jnp.bfloat16)
        before = passed_along(normed, "seq", reach)
        after = passed_along(normed, "seq", -reach)
        piece = lax.all_gather(conv_weight[block], ("seq", "chan"), axis=2, tiled=True)
        total = matmul(before, piece[0]) + matmul(normed, piece[1]) + matmul(after, piece[2])
        conv = total.astype(jnp.bfloat16)
        state = state + conv.astype(jnp.float32)
        mixed = normalize(state, ff_norm[block]).astype(jnp.bfloat16)
        hidden = jax.nn.gelu(
            matmul(mixed, lax.all_gather(up_weight[block], ("seq", "chan"), axis=1, tiled=True))
        ).astype(jnp.bfloat16)
        state = state + matmul(
            hidden, lax.all_gather(down_weight[block], ("seq", "chan"), axis=0, tiled=True)
        )
    final = normalize(state, head_norm).astype(jnp.bfloat16)
    value = matmul(final, value_weight)
    bit_count = (seq_count * lax.axis_size("chan")).bit_length() - 1
    opposite = swapped(final, "strand", 0)
    for digit in range(bit_count):
        opposite = swapped(opposite, ("seq", "chan"), digit)
    opposite = jnp.flip(opposite, 0)
    mirrored = matmul(opposite, gate_weight).astype(jnp.bfloat16)
    gated = (value * jax.nn.sigmoid(mirrored.astype(jnp.float32))).astype(jnp.bfloat16)
    result = matmul(gated, out_weight)
    return result.astype(jnp.bfloat16)[None]


def solution(mesh):
    in_specs = (
        P("strand", ("groups", "seq", "chan"), None),
        P(),
        P(None, None, None, ("seq", "chan")),
        P(),
        P(None, None, ("seq", "chan")),
        P(None, ("seq", "chan"), None),
        P(),
        P(),
        P(),
        P(),
    )
    out_specs = P("strand", ("groups", "seq", "chan"), None)
    return jax.shard_map(local, mesh=mesh, in_specs=in_specs, out_specs=out_specs, check_vma=False)
```

profile of v0, /device:TPU:1, one launch (start us, length us, event | category | flops | bytes accessed | tf_op | source)
XLA Modules:
  0.0 374.9 jit_solution(10085259237027235437)
XLA Ops:
  6.5 0.0 all-gather.13.cloned.1.call-start
  6.6 1.9 fusion.86
  8.5 0.0 all-gather.15.cloned.1.call-start
  8.6 1.9 fusion.84
  10.5 0.0 all-gather.17.cloned.1.call-start
  10.5 0.8 fusion.85
  11.4 0.0 all-gather.19.cloned.1.call-start
  11.4 0.5 all-gather.19.cloned.1.call-update
  12.0 0.0 all-gather.21.cloned.1.call-start
  12.0 0.5 all-gather.21.cloned.1.call-update
  12.6 0.0 all-gather.23.cloned.1.call-start
  12.6 0.2 fusion.55
  12.8 0.2 fusion.57
  13.0 1.3 collective-permute-start.1
  14.3 0.0 all-gather.23.cloned.1.call-update
  14.3 4.7 %collective-permute-start = (bf16[384,512]{1,0:T(8,128)(2,1)S(1)}, bf16[384,512]{1,0:T(8,128)(2,1)S(1)}, u32[]{:S(2)}, u32[]{:S(2)}) collective-permute-start(bf16[384,512]{1,0:T(8,128)(2,1)S(1)} %fusion.57), channel_id=1, source_target_pairs={{0,4},{4,8},{8,12},{1,5},{5,9},{9,13},{2,6},{6,10},{10,14},{3,7},{... | collective-permute-start | bytes 1179656 | tf_op jit(solution)/shard_map/ppermute | solution.py:10
  19.0 9.7 %collective-permute-done.1 = bf16[384,512]{1,0:T(8,128)(2,1)S(1)} collective-permute-done((bf16[384,512]{1,0:T(8,128)(2,1)S(1)}, bf16[384,512]{1,0:T(8,128)(2,1)S(1)}, u32[]{:S(2)}, u32[]{:S(2)}) %collective-permute-start.1) | collective-permute-done | bytes 393248 | tf_op jit(solution)/shard_map/ppermute | solution.py:10
  28.7 29.1 %all-gather.13.cloned.1.call-done = bf16[1,3,512,512]{2,3,1,0:T(8,128)(2,1)} async-done(((bf16[1,3,512,64]{2,3,1,0:T(8,128)(2,1)}), bf16[1,3,512,512]{2,3,1,0:T(8,128)(2,1)}) %all-gather.13.cloned.1.call-update) | async-done | bytes 1572880 | tf_op jit(solution)/shard_map/all_gather | solution.py:44
  57.8 1.4 fusion.62
  59.3 1.5 fusion.63
  60.7 1.6 multiply_reduce_fusion.3
  62.3 47.5 %all-gather.15.cloned.1.call-done = bf16[1,512,2048]{2,1,0:T(8,128)(2,1)} async-done(((bf16[1,512,256]{2,1,0:T(8,128)(2,1)}), bf16[1,512,2048]{2,1,0:T(8,128)(2,1)}) %all-gather.15.cloned.1.call-update) | async-done | bytes 2097168 | tf_op jit(solution)/shard_map/all_gather | solution.py:50
  109.8 49.1 %all-gather.17.cloned.1.call-done = bf16[1,2048,512]{2,1,0:T(8,128)(2,1)} async-done(((bf16[1,256,512]{2,1,0:T(8,128)(2,1)}), bf16[1,2048,512]{2,1,0:T(8,128)(2,1)}) %all-gather.17.cloned.1.call-update) | async-done | bytes 2097168 | tf_op jit(solution)/shard_map/all_gather | solution.py:53
  158.9 4.3 %multiply_reduce_fusion.2 = (f32[384]{0:T(512)S(1)}, f32[384,512]{1,0:T(8,128)S(1)}) fusion(f32[384,512]{1,0:T(8,128)S(1)} %get-tuple-element.16, bf16[1,2048,512]{2,1,0:T(8,128)(2,1)} %all-gather.17.cloned.1.call-done, bf16[1,512,2048]{2,1,0:T(8,128)(2,1)} %all-gather.15.cloned.1.call-done, f32[512]{0:T(512)S(1)} %bitcast.91, f32[384]{0:T(512)S(1)} %add_rsqrt_fusion.3), kind=kOutput, calls=%fused_computation.62 | convolution fusion | flops 1618869888 | bytes 5772288 | tf_op jit(solution)/shard_map/dot_general | solution.py:22
  163.3 0.1 multiply_convert_fusion.4
  163.4 1.3 collective-permute-start.3
  164.7 4.9 %collective-permute-start.2 = (bf16[384,512]{1,0:T(8,128)(2,1)S(1)}, bf16[384,512]{1,0:T(8,128)(2,1)S(1)}, u32[]{:S(2)}, u32[]{:S(2)}) collective-permute-start(bf16[384,512]{1,0:T(8,128)(2,1)S(1)} %multiply_convert_fusion.4), channel_id=1, source_target_pairs={{0,8},{4,12},{1,9},{5,13},{2,10},{6,14},{3,11},{7,15},{16,24},{20,... | collective-permute-start | bytes 1179656 | tf_op jit(solution)/shard_map/ppermute | solution.py:10
  169.7 47.7 %all-gather.19.cloned.1.call-done = bf16[1,3,512,512]{2,3,1,0:T(8,128)(2,1)} async-done(((bf16[1,3,512,64]{2,3,1,0:T(8,128)(2,1)}), bf16[1,3,512,512]{2,3,1,0:T(8,128)(2,1)}) %all-gather.19.cloned.1.call-update) | async-done | bytes 1572880 | tf_op jit(solution)/shard_map/all_gather | solution.py:44
  217.4 1.4 fusion.61
  218.8 1.4 fusion.60
  220.3 1.6 multiply_reduce_fusion.1
  221.9 47.3 %all-gather.21.cloned.1.call-done = bf16[1,512,2048]{2,1,0:T(8,128)(2,1)} async-done(((bf16[1,512,256]{2,1,0:T(8,128)(2,1)}), bf16[1,512,2048]{2,1,0:T(8,128)(2,1)}) %all-gather.21.cloned.1.call-update) | async-done | bytes 2097168 | tf_op jit(solution)/shard_map/all_gather | solution.py:50
  269.2 49.0 %all-gather.23.cloned.1.call-done = bf16[1,2048,512]{2,1,0:T(8,128)(2,1)} async-done(((bf16[1,256,512]{2,1,0:T(8,128)(2,1)}), bf16[1,2048,512]{2,1,0:T(8,128)(2,1)}) %all-gather.23.cloned.1.call-update) | async-done | bytes 2097168 | tf_op jit(solution)/shard_map/all_gather | solution.py:53
  318.2 4.4 %multiply_reduce_fusion = (f32[384]{0:T(512)S(1)}, f32[384,512]{1,0:T(8,128)S(1)}) fusion(f32[384,512]{1,0:T(8,128)S(1)} %get-tuple-element.20, bf16[1,2048,512]{2,1,0:T(8,128)(2,1)} %all-gather.23.cloned.1.call-done, bf16[1,512,2048]{2,1,0:T(8,128)(2,1)} %all-gather.21.cloned.1.call-done, f32[512]{0:T(512)S(1)} %bitcast.90, f32[384]{0:T(512)S(1)} %add_rsqrt_fusion.1), kind=kOutput, calls=%fused_computation.58 | convolution fusion | flops 1618869888 | bytes 5772288 | tf_op jit(solution)/shard_map/dot_general | solution.py:22
  322.6 0.1 multiply_convert_fusion
  322.7 1.8 collective-permute-start.4
  324.5 1.3 collective-permute-done.4
  325.9 0.3 collective-permute-start.5
  326.2 10.0 %collective-permute-done.5 = bf16[384,512]{1,0:T(8,128)(2,1)S(1)} collective-permute-done((bf16[384,512]{1,0:T(8,128)(2,1)S(1)}, bf16[384,512]{1,0:T(8,128)(2,1)S(1)}, u32[]{:S(2)}, u32[]{:S(2)}) %collective-permute-start.5) | collective-permute-done | bytes 393248 | tf_op jit(solution)/shard_map/ppermute | solution.py:14
  336.2 1.2 collective-permute-start.6
  337.4 8.2 %collective-permute-done.6 = bf16[384,512]{1,0:T(8,128)(2,1)S(1)} collective-permute-done((bf16[384,512]{1,0:T(8,128)(2,1)S(1)}, bf16[384,512]{1,0:T(8,128)(2,1)S(1)}, u32[]{:S(2)}, u32[]{:S(2)}) %collective-permute-start.6) | collective-permute-done | bytes 393248 | tf_op jit(solution)/shard_map/ppermute | solution.py:14
  345.6 1.5 collective-permute-start.7
  347.2 17.8 %collective-permute-done.7 = bf16[384,512]{1,0:T(8,128)(2,1)S(1)} collective-permute-done((bf16[384,512]{1,0:T(8,128)(2,1)S(1)}, bf16[384,512]{1,0:T(8,128)(2,1)S(1)}, u32[]{:S(2)}, u32[]{:S(2)}) %collective-permute-start.7) | collective-permute-done | bytes 393248 | tf_op jit(solution)/shard_map/ppermute | solution.py:14
  365.0 0.5 rev.4
  365.5 0.5 fusion.47
  366.0 0.5 copy-done.2
  366.5 0.2 copy-done.3
  366.7 1.4 fusion.48
  (27 shorter events, 0.1 us)
Async XLA Ops:
  6.5 358.9 %copy-start = (bf16[512,512]{1,0:T(8,128)(2,1)S(1)}, bf16[512,512]{1,0:T(8,128)(2,1)}, u32[]{:S(2)}) copy-start(bf16[512,512]{1,0:T(8,128)(2,1)} %param.18) | copy-start | bytes 1572868
  6.5 4.0 %copy-start.4 = (bf16[2,256,512]{2,1,0:T(8,128)(2,1)S(1)}, bf16[2,256,512]{2,1,0:T(8,128)(2,1)}, u32[]{:S(2)}) copy-start(bf16[2,256,512]{2,1,0:T(8,128)(2,1)} %param.15) | copy-start | bytes 1572868
  6.5 6.1 %copy-start.1 = (bf16[1,384,512]{2,1,0:T(8,128)(2,1)S(1)}, bf16[1,384,512]{2,1,0:T(8,128)(2,1)}, u32[]{:S(2)}) copy-start(bf16[1,384,512]{2,1,0:T(8,128)(2,1)} %param.10) | copy-start | bytes 1179652
  6.5 6.2 %copy-start.5 = (f32[2,512]{1,0:T(2,128)S(1)}, f32[2,512]{1,0:T(2,128)}, u32[]{:S(2)}) copy-start(f32[2,512]{1,0:T(2,128)} %param.11) | copy-start | bytes 12292
  6.5 51.3 %all-gather.13.cloned.1.call-start = ((), (), s32[]{:S(2)}) async-start(), calls=%async_computation | async-start | bytes 1769472 | tf_op jit(solution)/shard_map/all_gather | solution.py:44
  8.5 10.5 %copy-start.6 = (f32[2,512]{1,0:T(2,128)S(1)}, f32[2,512]{1,0:T(2,128)}, u32[]{:S(2)}) copy-start(f32[2,512]{1,0:T(2,128)} %param.13) | copy-start | bytes 12292
  8.5 101.2 %all-gather.15.cloned.1.call-start = ((), (), s32[]{:S(2)}) async-start(), calls=%async_computation.1 | async-start | bytes 2359296 | tf_op jit(solution)/shard_map/all_gather | solution.py:50
  10.5 148.4 %all-gather.17.cloned.1.call-start = ((), (), s32[]{:S(2)}) async-start(), calls=%async_computation.2 | async-start | bytes 2359296 | tf_op jit(solution)/shard_map/all_gather | solution.py:53
  11.4 206.0 %all-gather.19.cloned.1.call-start = ((), (), s32[]{:S(2)}) async-start(), calls=%async_computation.3 | async-start | bytes 1769472 | tf_op jit(solution)/shard_map/all_gather | solution.py:44
  12.0 257.2 %all-gather.21.cloned.1.call-start = ((), (), s32[]{:S(2)}) async-start(), calls=%async_computation.4 | async-start | bytes 2359296 | tf_op jit(solution)/shard_map/all_gather | solution.py:50
  12.6 305.6 %all-gather.23.cloned.1.call-start = ((), (), s32[]{:S(2)}) async-start(), calls=%async_computation.5 | async-start | bytes 2359296 | tf_op jit(solution)/shard_map/all_gather | solution.py:53
  13.0 15.7 %collective-permute-start.1 = (bf16[384,512]{1,0:T(8,128)(2,1)S(1)}, bf16[384,512]{1,0:T(8,128)(2,1)S(1)}, u32[]{:S(2)}, u32[]{:S(2)}) collective-permute-start(bf16[384,512]{1,0:T(8,128)(2,1)S(1)} %fusion.57), channel_id=1, source_target_pairs={{4,0},{8,4},{12,8},{5,1},{9,5},{13,9},{6,2},{10,6},{14,10},{7,3},{... | collective-permute-start | bytes 1179656 | tf_op jit(solution)/shard_map/ppermute | solution.py:10
  14.3 46.4 %collective-permute-start = (bf16[384,512]{1,0:T(8,128)(2,1)S(1)}, bf16[384,512]{1,0:T(8,128)(2,1)S(1)}, u32[]{:S(2)}, u32[]{:S(2)}) collective-permute-start(bf16[384,512]{1,0:T(8,128)(2,1)S(1)} %fusion.57), channel_id=1, source_target_pairs={{0,4},{4,8},{8,12},{1,5},{5,9},{9,13},{2,6},{6,10},{10,14},{3,7},{... | collective-permute-start | bytes 1179656 | tf_op jit(solution)/shard_map/ppermute | solution.py:10
  163.4 55.4 %collective-permute-start.3 = (bf16[384,512]{1,0:T(8,128)(2,1)S(1)}, bf16[384,512]{1,0:T(8,128)(2,1)S(1)}, u32[]{:S(2)}, u32[]{:S(2)}) collective-permute-start(bf16[384,512]{1,0:T(8,128)(2,1)S(1)} %multiply_convert_fusion.4), channel_id=1, source_target_pairs={{8,0},{12,4},{9,1},{13,5},{10,2},{14,6},{11,3},{15,7},{24,16},{28,... | collective-permute-start | bytes 1179656 | tf_op jit(solution)/shard_map/ppermute | solution.py:10
  164.7 55.5 %collective-permute-start.2 = (bf16[384,512]{1,0:T(8,128)(2,1)S(1)}, bf16[384,512]{1,0:T(8,128)(2,1)S(1)}, u32[]{:S(2)}, u32[]{:S(2)}) collective-permute-start(bf16[384,512]{1,0:T(8,128)(2,1)S(1)} %multiply_convert_fusion.4), channel_id=1, source_target_pairs={{0,8},{4,12},{1,9},{5,13},{2,10},{6,14},{3,11},{7,15},{16,24},{20,... | collective-permute-start | bytes 1179656 | tf_op jit(solution)/shard_map/ppermute | solution.py:10
  318.2 4.4 %copy-start.7 = (f32[512]{0:T(512)S(1)}, f32[512]{0:T(512)}, u32[]{:S(2)}) copy-start(f32[512]{0:T(512)} %param.16) | copy-start | bytes 6148
  322.7 3.2 collective-permute-start.4
  325.9 10.3 %collective-permute-start.5 = (bf16[384,512]{1,0:T(8,128)(2,1)S(1)}, bf16[384,512]{1,0:T(8,128)(2,1)S(1)}, u32[]{:S(2)}, u32[]{:S(2)}) collective-permute-start(bf16[384,512]{1,0:T(8,128)(2,1)S(1)} %collective-permute-done.4), channel_id=1, source_target_pairs={{0,1},{1,0},{4,5},{5,4},{8,9},{9,8},{12,13},{13,12},{2,3},{3,2},{6... | collective-permute-start | bytes 1179656 | tf_op jit(solution)/shard_map/ppermute | solution.py:14
  336.2 9.4 %collective-permute-start.6 = (bf16[384,512]{1,0:T(8,128)(2,1)S(1)}, bf16[384,512]{1,0:T(8,128)(2,1)S(1)}, u32[]{:S(2)}, u32[]{:S(2)}) collective-permute-start(bf16[384,512]{1,0:T(8,128)(2,1)S(1)} %collective-permute-done.5), channel_id=1, source_target_pairs={{0,4},{1,5},{4,0},{5,1},{8,12},{9,13},{12,8},{13,9},{2,6},{3,7},{6... | collective-permute-start | bytes 1179656 | tf_op jit(solution)/shard_map/ppermute | solution.py:14
  345.6 19.4 %collective-permute-start.7 = (bf16[384,512]{1,0:T(8,128)(2,1)S(1)}, bf16[384,512]{1,0:T(8,128)(2,1)S(1)}, u32[]{:S(2)}, u32[]{:S(2)}) collective-permute-start(bf16[384,512]{1,0:T(8,128)(2,1)S(1)} %collective-permute-done.6), channel_id=1, source_target_pairs={{0,8},{1,9},{4,12},{5,13},{8,0},{9,1},{12,4},{13,5},{2,10},{3,11},... | collective-permute-start | bytes 1179656 | tf_op jit(solution)/shard_map/ppermute | solution.py:14
  365.5 1.0 copy-start.2
  365.5 1.2 copy-start.3
Sparse Core Ops, SparseCore 0:
  9.6 48.2 all-gather.12
  59.9 49.8 all-gather.14
  111.9 46.9 all-gather.16
  161.0 56.3 all-gather.18
  219.3 49.8 all-gather.20
  271.2 46.9 all-gather.22
where the time goes:
time: 377 us; the launch traced here: 375 us
  waiting for transfers between devices  318 us (84%)
  matrix products  19.5 us (5%)
  starting transfers between devices  17.3 us (5%)
  between operations  13.7 us (4%)
  local copies, waits for them, and re-layouts  5.8 us (2%)
    all_gather x2, waiting for transfers between devices, local(): lax.all_gather(down_weight[block], ('seq', 'chan'), axis=0, tiled=True)  98.1 us
    all_gather x2, waiting for transfers between devices, local(): lax.all_gather(up_weight[block], ('seq', 'chan'), axis=1, tiled=True)  94.8 us
    all_gather x2, waiting for transfers between devices, local(): lax.all_gather(conv_weight[block], ('seq', 'chan'), axis=2, tiled=True)  76.8 us
    ppermute x4, waiting for transfers between devices, swapped(): lax.ppermute(x, axis, [(i, i ^ 1 << stride) for i in range(lax.axis_size(...  37.4 us
    dot_general x10, matrix products, matmul(): return jnp.dot(left, right, preferred_element_type=jnp.float32)  19.5 us
    ppermute x4, starting transfers between devices, passed_along(): lax.ppermute(value, axis, [(source, source + steps) for source in range(i...  12.2 us
    ppermute x4, waiting for transfers between devices, passed_along(): lax.ppermute(value, axis, [(source, source + steps) for source in range(i...  9.7 us
  transfers between devices with their start and end apart: 14, of which 11 were waited for; matrix products, arithmetic and copies ran while one was open for 4% of the time, Pallas kernels for 0%

commit v1 on v0

v1 whole, which is shorter than its diff:
```python
import functools
import itertools

import jax
import jax.numpy as jnp
from jax import lax
from jax.experimental import pallas as pl
from jax.experimental.pallas import tpu as pltpu
from jax.sharding import PartitionSpec as P

AXES = ("groups", "seq", "strand", "chan")
BF16, F32 = jnp.bfloat16, jnp.float32
PARAMS = pltpu.CompilerParams(vmem_limit_bytes=40 * 2**20)
VMEM_SPEC = pl.BlockSpec(memory_space=pltpu.VMEM)
ANY_SPEC = pl.BlockSpec(memory_space=pl.ANY)


def normalize(values, gain):
    return values * lax.rsqrt(jnp.mean(values * values, axis=-1, keepdims=True) + 1e-06) * gain


def matmul(left, right):
    return jnp.dot(left, right, preferred_element_type=F32)


def matmul_nt(left, right):
    return lax.dot_general(left, right, (((1,), (1,)), ((), ())), preferred_element_type=F32)


def passed_along(value, axis, steps):
    count = lax.axis_size(axis)
    initial, last = (max(0, -steps), min(count, count - steps))
    return lax.ppermute(value, axis, [(source, source + steps) for source in range(initial, last)])


def swapped(x, axis, stride):
    return lax.ppermute(x, axis, [(i, i ^ 1 << stride) for i in range(lax.axis_size(axis))])


def local_plain(
    seq_in, conv_norm, conv_weight, ff_norm, up_weight, down_weight,
    head_norm, value_weight, gate_weight, out_weight,
):
    state = seq_in[0].astype(F32)
    seq_count = lax.axis_size("seq")
    for block in range(conv_weight.shape[0]):
        reach = min(2**block, seq_count // 2)
        normed = normalize(state, conv_norm[block]).astype(BF16)
        before = passed_along(normed, "seq", reach)
        after = passed_along(normed, "seq", -reach)
        piece = lax.all_gather(conv_weight[block], ("seq", "chan"), axis=2, tiled=True)
        total = matmul(before, piece[0]) + matmul(normed, piece[1]) + matmul(after, piece[2])
        state = state + total.astype(BF16).astype(F32)
        mixed = normalize(state, ff_norm[block]).astype(BF16)
        up = lax.all_gather(up_weight[block], ("seq", "chan"), axis=1, tiled=True)
        hidden = jax.nn.gelu(matmul(mixed, up)).astype(BF16)
        down = lax.all_gather(down_weight[block], ("seq", "chan"), axis=0, tiled=True)
        state = state + matmul(hidden, down)
    final = normalize(state, head_norm).astype(BF16)
    value = matmul(final, value_weight)
    bit_count = (seq_count * lax.axis_size("chan")).bit_length() - 1
    opposite = swapped(final, "strand", 0)
    for digit in range(bit_count):
        opposite = swapped(opposite, ("seq", "chan"), digit)
    opposite = jnp.flip(opposite, 0)
    mirrored = matmul(opposite, gate_weight).astype(BF16)
    gated = (value * jax.nn.sigmoid(mirrored.astype(F32))).astype(BF16)
    return matmul(gated, out_weight).astype(BF16)[None]


def moved(value, go):
    sizes = [lax.axis_size(a) for a in AXES]

    def flat(at):
        number = 0
        for n, k in zip(sizes, at):
            number = number * n + k
        return number

    pairs = [(flat(at), flat(go(*at))) for at in itertools.product(*map(range, sizes))]
    return lax.ppermute(value, AXES, pairs)


def plan(count, block):
    def first(g):
        flip = (g + block) % 2
        return 1 + flip

    return first, count - 1


def origins(block, half_of_mine):
    g, i, c = (lax.axis_index(a) for a in ("groups", "seq", "chan"))
    n, m = lax.axis_size("seq"), lax.axis_size("chan")
    mine = 1 + lax.rem(g + block, 2)
    other = 1 + lax.rem(g + block + 1, 2)
    last = n - 1
    back = lambda k: lax.rem(i + n - k, n)
    x = 1 - c
    at = [
        (i, c), (back(mine), c), (back(last), c), (i, x),
        (back(mine), x), (back(last), x), (back(other), c), (back(other), x),
    ]
    return [a * m + b for a, b in at]


def gathered(mine, block):
    n = lax.axis_size("seq")
    first, last = plan(n, block)
    along = lambda v, k: moved(v, lambda g, i, s, c: (g, (i + k(g)) % n, s, c))
    across = lambda v: moved(v, lambda g, i, s, c: (g, i, s, 1 - c))
    planes = lambda v: moved(v, lambda g, i, s, c: (1 - g, i, s, c))
    a1 = along(mine, first)
    a2 = along(mine, lambda g: last)
    a3 = across(mine)
    a4 = across(a1)
    a5 = across(a2)
    a6 = planes(a1)
    a7 = planes(a4)
    return [a1, a2, a3, a4, a5, a6, a7]


def other_core(value):
    return moved(value, lambda g, i, s, c: (g, i, 1 - s, c))


def pack_kernel(conv_ref, up_ref, down_ref, mine_ref, other_ref):
    first = lax.axis_index("strand") == 0
    at = 0

    def put(whole):
        nonlocal at
        half = whole.shape[0] // 2
        top, low = whole[:half], whole[half:]
        mine_ref[at : at + half] = jnp.where(first, top, low)
        other_ref[at : at + half] = jnp.where(first, low, top)
        at += half

    put(up_ref[0].T)
    put(down_ref[0])
    for tap in range(conv_ref.shape[1]):
        put(conv_ref[0, tap].T)


def pack(conv_weight, up_weight, down_weight, block):
    taps, width, chans = conv_weight.shape[1:]
    hidden = up_weight.shape[2]
    rows = hidden + taps * chans // 2
    shape = jax.ShapeDtypeStruct((rows, width), BF16)
    index = lambda rank: (lambda i: (block,) + (0,) * (rank - 1))
    spec = lambda a: pl.BlockSpec((1,) + a.shape[1:], index(a.ndim))
    return pl.pallas_call(
        pack_kernel,
        out_shape=[shape, shape],
        grid=(1,),
        in_specs=[spec(conv_weight), spec(up_weight), spec(down_weight)],
        out_specs=[pl.BlockSpec((rows, width), lambda i: (0, 0))] * 2,
        compiler_params=PARAMS,
        name=f"pack{block}",
    )(conv_weight, up_weight, down_weight)


def split_kernel(rows_ref, *out_refs):
    n = lax.axis_size("seq")
    i, s = lax.axis_index("seq"), lax.axis_index("strand")
    size = out_refs[0].shape[0]
    for k, out in enumerate(out_refs):
        j = lax.rem(i + k, n)
        sub = jnp.where(s == 0, j, n - 1 - j)
        out[...] = rows_ref[pl.ds(pl.multiple_of(sub * size, size), size)]


def join_kernel(*refs):
    *parts, out = refs
    n = lax.axis_size("seq")
    i, s = lax.axis_index("seq"), lax.axis_index("strand")
    size = parts[0].shape[0]
    for k, part in enumerate(parts):
        j = lax.rem(i + n - k, n)
        sub = jnp.where(s == 0, j, n - 1 - j)
        out[pl.ds(pl.multiple_of(sub * size, size), size)] = part[...]


def conv_kernel(block, parts, hidden, gain_ref, *refs):
    n = lax.axis_size("seq")
    states, refs = refs[:parts], refs[parts:]
    count = (len(refs) - 4) // 2
    mine, other = refs[:count], refs[count : 2 * count]
    out, weight, acc, sems = refs[2 * count :]
    width = acc.shape[1]
    taps = weight.shape[0] // width
    half = (mine[0].shape[0] - hidden) // taps
    s, j = lax.axis_index("strand"), lax.axis_index("seq")
    copies = []
    for r, shard in enumerate(origins(block, s)):
        for q, (ref, part) in enumerate(((mine[r], s), (other[r], 1 - s))):
            start = pl.multiple_of((shard * 2 + part) * half, half)
            for tap in range(taps):
                copy = pltpu.make_async_copy(
                    ref.at[pl.ds(hidden + tap * half, half)],
                    weight.at[pl.ds(tap * width + start, half)],
                    sems.at[(r * 2 + q) * taps + tap],
                )
                copy.start()
                copies.append(copy)
    if parts > 1:
        size = states[0].shape[0]
        for k, state in enumerate(states):
            at = lax.rem(j + n - k, n)
            out[pl.ds(pl.multiple_of(at * size, size), size)] = state[...].astype(F32)
        state = out[...]
    else:
        state = states[0][...]
    normed = normalize(state, gain_ref[block : block + 1]).astype(BF16)
    shift = state.shape[0] // n * min(2**block, n // 2)
    for copy in copies:
        copy.wait()
    acc[...] = matmul_nt(normed, weight[width : 2 * width])
    acc[shift:] += matmul_nt(normed[:-shift], weight[:width])
    acc[:-shift] += matmul_nt(normed[shift:], weight[2 * width :])
    out[...] = state + acc[...].astype(BF16).astype(F32)


def conv(states, gain, mine, other, block, hidden, taps):
    width = gain.shape[1]
    rows = sum(v.shape[0] for v in states)
    arrays = len(mine) + len(other)
    return pl.pallas_call(
        functools.partial(conv_kernel, block, len(states), hidden),
        out_shape=jax.ShapeDtypeStruct((rows, width), F32),
        in_specs=[VMEM_SPEC] * (1 + len(states)) + [ANY_SPEC] * arrays,
        out_specs=VMEM_SPEC,
        scratch_shapes=[
            pltpu.VMEM((taps * width, width), BF16),
            pltpu.VMEM((rows, width), F32),
            pltpu.SemaphoreType.DMA((arrays * taps,)),
        ],
        compiler_params=PARAMS,
        name=f"conv{block}",
    )(gain, *states, *mine, *other)


def ff_kernel(block, first, ends, half, gain_ref, head_ref, state_ref, *refs):
    if not first:
        mixed_ref, refs = refs[0], refs[1:]
    outs = 1 if ends else 2
    count = (len(refs) - outs - 4) // 2
    mine, other = refs[:count], refs[count : 2 * count]
    out = refs[2 * count]
    up, down, hid, sems = refs[-4:]
    copies = []
    for r in range(count):
        for q, ref in enumerate((mine[r], other[r])):
            at = (2 * r + q) * half
            for w, to in enumerate((up, down)):
                copy = pltpu.make_async_copy(
                    ref.at[pl.ds(w * half, half)], to.at[pl.ds(at, half)], sems.at[(2 * r + q) * 2 + w]
                )
                copy.start()
                copies.append(copy)
    state = state_ref[...]
    if first:
        mixed = normalize(state, gain_ref[block : block + 1]).astype(BF16)
    else:
        mixed = mixed_ref[...]
    for r in range(count):
        for copy in copies[4 * r : 4 * r + 4]:
            copy.wait()
        part = slice(2 * r * half, 2 * (r + 1) * half)
        hid[:, part] = jax.nn.gelu(matmul_nt(mixed, up[part])).astype(BF16)
    state = state + matmul(hid[...], down[...])
    if ends == "head":
        state = normalize(state, head_ref[...]).astype(BF16)
    out[...] = state
    if not ends:
        refs[2 * count + 1][...] = mixed


def feed_forward(state, mixed, gain, head, mine, other, block, half, ends):
    rows, width = state.shape
    arrays = len(mine) + len(other)
    out = [jax.ShapeDtypeStruct((rows, width), BF16 if ends == "head" else F32)]
    if not ends:
        out.append(jax.ShapeDtypeStruct((rows, width), BF16))
    given = [state] if mixed is None else [state, mixed]
    return pl.pallas_call(
        functools.partial(ff_kernel, block, mixed is None, ends, half),
        out_shape=out,
        in_specs=[VMEM_SPEC] * (2 + len(given)) + [ANY_SPEC] * arrays,
        out_specs=[VMEM_SPEC] * len(out),
        scratch_shapes=[
            pltpu.VMEM((arrays * half, width), BF16),
            pltpu.VMEM((arrays * half, width), BF16),
            pltpu.VMEM((rows, arrays * half), BF16),
            pltpu.SemaphoreType.DMA((arrays * 2,)),
        ],
        compiler_params=PARAMS,
        name=f"ff{block}",
    )(gain, head, *given, *mine, *other)


def head_kernel(final_ref, opposite_ref, value_ref, gate_ref, out_ref, *refs):
    *outs, result = refs
    n = len(outs)
    size = outs[0].shape[0]
    j = lax.axis_index("seq")
    value = matmul(final_ref[...], value_ref[...])
    row = lax.broadcasted_iota(jnp.int32, (size, size), 0)
    col = lax.broadcasted_iota(jnp.int32, (size, size), 1)
    reverse = jnp.where(row + col == size - 1, 1.0, 0.0).astype(BF16)
    flipped = [
        matmul(reverse, opposite_ref[(n - 1 - i) * size : (n - i) * size]).astype(BF16) for i in range(n)
    ]
    mirrored = matmul(jnp.concatenate(flipped, 0), gate_ref[...]).astype(BF16)
    gated = (value * jax.nn.sigmoid(mirrored.astype(F32))).astype(BF16)
    result[...] = matmul(gated, out_ref[...]).astype(BF16)
    for k, out in enumerate(outs):
        at = lax.rem(j + k, n)
        out[...] = result[pl.ds(pl.multiple_of(at * size, size), size)]


def local_spread(
    seq_in, conv_norm, conv_weight, ff_norm, up_weight, down_weight,
    head_norm, value_weight, gate_weight, out_weight,
):
    n = lax.axis_size("seq")
    blocks, taps, width, _ = conv_weight.shape
    hidden = up_weight.shape[2]
    rows = seq_in.shape[1]
    part = jax.ShapeDtypeStruct((rows // n, width), BF16)
    halves = [pack(conv_weight, up_weight, down_weight, b) for b in range(blocks)]
    to = lambda k: (lambda g, i, s, c: (g, (i + k) % n, s, c if s == 0 else 1 - c))
    parts = pl.pallas_call(
        split_kernel, out_shape=[part] * n, in_specs=[VMEM_SPEC], out_specs=[VMEM_SPEC] * n,
        compiler_params=PARAMS, name="split",
    )(seq_in[0])
    states = [moved(p, to(k)) for k, p in enumerate(parts)]
    head = head_norm[None]
    for b, (mine, other) in enumerate(halves):
        a = gathered(mine, b)
        mine = [mine] + a
        other = [other] + [other_core(v) for v in a]
        state = conv(states, conv_norm, mine, other, b, hidden, taps)
        if b < blocks - 1:
            (state,) = feed_forward(state, None, ff_norm, head, mine, other, b, hidden // 2, "state")
        else:
            early = len(mine) // 2
            state, mixed = feed_forward(
                state, None, ff_norm, head, mine[:early], other[:early], b, hidden // 2, ""
            )
            (state,) = feed_forward(
                state, mixed, ff_norm, head, mine[early:], other[early:], b, hidden // 2, "head"
            )
        states = [state]
    opposite = other_core(state)
    results = pl.pallas_call(
        head_kernel, out_shape=[part] * n, in_specs=[VMEM_SPEC] * 5, out_specs=[VMEM_SPEC] * n,
        scratch_shapes=[pltpu.VMEM((rows, width), BF16)], compiler_params=PARAMS, name="head",
    )(state, opposite, value_weight, gate_weight, out_weight)
    home = [moved(r, to(k)) for k, r in enumerate(results)]
    joined = pl.pallas_call(
        join_kernel, out_shape=jax.ShapeDtypeStruct((rows, width), BF16), in_specs=[VMEM_SPEC] * n,
        out_specs=VMEM_SPEC, compiler_params=PARAMS, name="join",
    )(*home)
    return joined[None]


def solution(mesh):
    in_specs = (
        P("strand", ("groups", "seq", "chan"), None),
        P(),
        P(None, None, None, ("seq", "chan")),
        P(),
        P(None, None, ("seq", "chan")),
        P(None, ("seq", "chan"), None),
        P(),
        P(),
        P(),
        P(),
    )
    out_specs = P("strand", ("groups", "seq", "chan"), None)

    def step(seq_in, conv_norm, conv_weight, *rest):
        size = mesh.shape
        shards = size["seq"] * size["chan"]
        tiled = conv_weight.shape[3] % (32 * shards) == 0
        spread = tiled and (size["groups"], size["seq"], size["strand"], size["chan"]) == (2, 4, 2, 2)
        local = local_spread if spread else local_plain
        run = jax.shard_map(local, mesh=mesh, in_specs=in_specs, out_specs=out_specs, check_vma=False)
        return run(seq_in, conv_norm, conv_weight, *rest)

    return step
```

time: 377 us -> 140 us (0.37)
  waiting for transfers between devices: 318 us -> 40.1 us
  starting transfers between devices: 17.3 us -> 67.3 us
  Pallas kernels: 0 us -> 30.3 us
  matrix products: 19.5 us -> 0 us
  between operations: 13.7 us -> 0.26 us
  local copies, waits for them, and re-layouts: 5.8 us -> 1.5 us
    all_gather x6 -> x0, waiting for transfers between devices: 270 us -> none  [the longest x2 98.1 us: local(): lax.all_gather(down_weight[block], ('seq', 'chan'), axis=0, tiled=True)]
    ppermute x8 -> x37, starting transfers between devices: 17.1 us -> 67.3 us  [moved(): return lax.ppermute(value, AXES, pairs)]
    pallas_call x0 -> x10, Pallas kernels: none -> 30.3 us  [the longest x3 20.4 us: feed_forward(): pl.pallas_call(functools.partial(ff_kernel, block, mixed is None, ends, h...]
    dot_general x10 -> x0, matrix products: 19.5 us -> none  [matmul(): return jnp.dot(left, right, preferred_element_type=jnp.float32)]
    ppermute x8 -> x37, waiting for transfers between devices: 47.1 us -> 40.1 us  [moved(): return lax.ppermute(value, AXES, pairs)]
    slice x5 -> x0, local copies, waits for them, and re-layouts: 4.62 us -> none  [the longest x1 1.92 us: local(): conv_weight[block]]
  transfers between devices with their start and end apart: 14 -> 37, of which waited for: 11 -> 12; matrix products, arithmetic and copies ran while one was open for 4% -> 0% of each run, Pallas kernels for 0% -> 10%
where the time goes in v1:
time: 140 us; the launch traced here: 139 us
  starting transfers between devices  67.3 us (48%)
  waiting for transfers between devices  40.1 us (29%)
  Pallas kernels  30.3 us (22%)
  local copies, waits for them, and re-layouts  1.5 us (1%)
    ppermute x37, starting transfers between devices, moved(): return lax.ppermute(value, AXES, pairs)  67.3 us
    ppermute x37, waiting for transfers between devices, moved(): return lax.ppermute(value, AXES, pairs)  40.1 us
    pallas_call x3, Pallas kernels, feed_forward(): pl.pallas_call(functools.partial(ff_kernel, block, mixed is None, ends, h...  20.4 us
    pallas_call x2, Pallas kernels, conv(): pl.pallas_call(functools.partial(conv_kernel, block, len(states), hidden)...  7.67 us
  transfers between devices with their start and end apart: 37, of which 12 were waited for; matrix products, arithmetic and copies ran while one was open for 0% of the time, Pallas kernels for 10%

profile of v1, /device:TPU:1, one launch (start us, length us, event | category | flops | bytes accessed | tf_op | source)
XLA Modules:
  0.0 139.5 jit_solution(170176576163899087)
XLA Ops:
  0.0 1.5 %copy.11.conv_ref = bf16[2,3,512,64]{3,2,1,0:T(8,128)(2,1)S(1)} copy(bf16[2,3,512,64]{2,3,1,0:T(8,128)(2,1)} %param.12) | data formatting | bytes 786432 | tf_op args[2]
  1.7 2.2 %collective-permute-start.4 = (bf16[352,512]{1,0:T(8,128)(2,1)S(1)}, bf16[352,512]{1,0:T(8,128)(2,1)S(1)}, u32[]{:S(2)}, u32[]{:S(2)}) collective-permute-start(bf16[352,512]{1,0:T(8,128)(2,1)S(1)} %get-tuple-element.23.refs_4_.refs_0_), channel_id=1, source_target_pairs={{0,4},{1,5},{2,6},{3,7},{4,8},{5,9},{6,10},{7,11},{8,12},{9,13},{1... | collective-permute-start | bytes 1081352 | tf_op jit(solution)/shard_map/ppermute | solution.py:81
  3.9 2.1 %collective-permute-start.5 = (bf16[352,512]{1,0:T(8,128)(2,1)S(1)}, bf16[352,512]{1,0:T(8,128)(2,1)S(1)}, u32[]{:S(2)}, u32[]{:S(2)}) collective-permute-start(bf16[352,512]{1,0:T(8,128)(2,1)S(1)} %get-tuple-element.23.refs_4_.refs_0_), channel_id=1, source_target_pairs={{0,12},{1,13},{2,14},{3,15},{4,0},{5,1},{6,2},{7,3},{8,4},{9,5},{1... | collective-permute-start | bytes 1081352 | tf_op jit(solution)/shard_map/ppermute | solution.py:81
  6.0 1.2 collective-permute-start.6
  7.2 2.2 %collective-permute-start = (bf16[96,512]{1,0:T(8,128)(2,1)S(1)}, bf16[96,512]{1,0:T(8,128)(2,1)S(1)}, u32[]{:S(2)}, u32[]{:S(2)}) collective-permute-start(bf16[96,512]{1,0:T(8,128)(2,1)S(1)} %get-tuple-element.19), channel_id=1, source_target_pairs={{0,0},{1,1},{2,3},{3,2},{4,4},{5,5},{6,7},{7,6},{8,8},{9,9},{10,11... | collective-permute-start | bytes 294920 | tf_op jit(solution)/shard_map/ppermute | solution.py:81
  9.4 0.4 collective-permute-start.1
  9.7 7.3 %collective-permute-done.refs_0_ = bf16[96,512]{1,0:T(8,128)(2,1)S(1)} collective-permute-done((bf16[96,512]{1,0:T(8,128)(2,1)S(1)}, bf16[96,512]{1,0:T(8,128)(2,1)S(1)}, u32[]{:S(2)}, u32[]{:S(2)}) %collective-permute-start) | collective-permute-done | bytes 98336 | tf_op jit(solution)/shard_map/ppermute | solution.py:81
  17.0 1.6 %collective-permute-start.2 = (bf16[96,512]{1,0:T(8,128)(2,1)S(1)}, bf16[96,512]{1,0:T(8,128)(2,1)S(1)}, u32[]{:S(2)}, u32[]{:S(2)}) collective-permute-start(bf16[96,512]{1,0:T(8,128)(2,1)S(1)} %get-tuple-element.21), channel_id=1, source_target_pairs={{0,8},{1,9},{2,11},{3,10},{4,12},{5,13},{6,15},{7,14},{8,0},{9,1},... | collective-permute-start | bytes 294920 | tf_op jit(solution)/shard_map/ppermute | solution.py:81
  18.6 5.7 %collective-permute-done.1.refs_1_ = bf16[96,512]{1,0:T(8,128)(2,1)S(1)} collective-permute-done((bf16[96,512]{1,0:T(8,128)(2,1)S(1)}, bf16[96,512]{1,0:T(8,128)(2,1)S(1)}, u32[]{:S(2)}, u32[]{:S(2)}) %collective-permute-start.1) | collective-permute-done | bytes 98336 | tf_op jit(solution)/shard_map/ppermute | solution.py:81
  24.3 1.6 %collective-permute-start.3 = (bf16[96,512]{1,0:T(8,128)(2,1)S(1)}, bf16[96,512]{1,0:T(8,128)(2,1)S(1)}, u32[]{:S(2)}, u32[]{:S(2)}) collective-permute-start(bf16[96,512]{1,0:T(8,128)(2,1)S(1)} %get-tuple-element.22), channel_id=1, source_target_pairs={{0,12},{1,13},{2,15},{3,14},{4,0},{5,1},{6,3},{7,2},{8,4},{9,5},{1... | collective-permute-start | bytes 294920 | tf_op jit(solution)/shard_map/ppermute | solution.py:81
  26.1 3.4 %collective-permute-done.2.refs_2_ = bf16[96,512]{1,0:T(8,128)(2,1)S(1)} collective-permute-done((bf16[96,512]{1,0:T(8,128)(2,1)S(1)}, bf16[96,512]{1,0:T(8,128)(2,1)S(1)}, u32[]{:S(2)}, u32[]{:S(2)}) %collective-permute-start.2) | collective-permute-done | bytes 98336 | tf_op jit(solution)/shard_map/ppermute | solution.py:81
  29.6 1.5 %collective-permute-done.3.refs_3_ = bf16[96,512]{1,0:T(8,128)(2,1)S(1)} collective-permute-done((bf16[96,512]{1,0:T(8,128)(2,1)S(1)}, bf16[96,512]{1,0:T(8,128)(2,1)S(1)}, u32[]{:S(2)}, u32[]{:S(2)}) %collective-permute-start.3) | collective-permute-done | bytes 98336 | tf_op jit(solution)/shard_map/ppermute | solution.py:81
  31.1 0.9 collective-permute-start.19
  31.9 0.4 collective-permute-start.20
  32.4 1.0 collective-permute-start.7
  33.4 11.2 %collective-permute-start.9 = (bf16[352,512]{1,0:T(8,128)(2,1)S(1)}, bf16[352,512]{1,0:T(8,128)(2,1)S(1)}, u32[]{:S(2)}, u32[]{:S(2)}) collective-permute-start(bf16[352,512]{1,0:T(8,128)(2,1)S(1)} %collective-permute-done.4.refs_5_.refs_1_), channel_id=1, source_target_pairs={{0,16},{1,17},{2,18},{3,19},{4,20},{5,21},{6,22},{7,23},{8,24},{9,... | collective-permute-start | bytes 1081352 | tf_op jit(solution)/shard_map/ppermute | solution.py:81
  44.7 2.5 %collective-permute-done.18.refs_2_.refs_1_ = bf16[352,512]{1,0:T(8,128)(2,1)S(1)} collective-permute-done((bf16[352,512]{1,0:T(8,128)(2,1)S(1)}, bf16[352,512]{1,0:T(8,128)(2,1)S(1)}, u32[]{:S(2)}, u32[]{:S(2)}) %collective-permute-start.18) | collective-permute-done | bytes 360480 | tf_op jit(solution)/shard_map/ppermute | solution.py:81
  47.1 1.0 collective-permute-done.19.refs_3_.refs_2_
  48.2 1.2 collective-permute-start.11
  49.4 1.3 collective-permute-start.13
  50.7 0.9 collective-permute-done.9.refs_10_.refs_6_
  51.6 1.0 collective-permute-start.21
  52.6 4.2 %collective-permute-done.8.refs_9_.refs_5_ = bf16[352,512]{1,0:T(8,128)(2,1)S(1)} collective-permute-done((bf16[352,512]{1,0:T(8,128)(2,1)S(1)}, bf16[352,512]{1,0:T(8,128)(2,1)S(1)}, u32[]{:S(2)}, u32[]{:S(2)}) %collective-permute-start.8) | collective-permute-done | bytes 360480 | tf_op jit(solution)/shard_map/ppermute | solution.py:81
  56.9 10.5 %collective-permute-start.23 = (bf16[352,512]{1,0:T(8,128)(2,1)S(1)}, bf16[352,512]{1,0:T(8,128)(2,1)S(1)}, u32[]{:S(2)}, u32[]{:S(2)}) collective-permute-start(bf16[352,512]{1,0:T(8,128)(2,1)S(1)} %collective-permute-done.18.refs_2_.refs_1_), channel_id=1, source_target_pairs={{0,16},{1,17},{2,18},{3,19},{4,20},{5,21},{6,22},{7,23},{8,24},{9,... | collective-permute-start | bytes 1081352 | tf_op jit(solution)/shard_map/ppermute | solution.py:81
  67.3 1.0 collective-permute-start.22
  68.4 4.8 %collective-permute-start.25 = (bf16[352,512]{1,0:T(8,128)(2,1)S(1)}, bf16[352,512]{1,0:T(8,128)(2,1)S(1)}, u32[]{:S(2)}, u32[]{:S(2)}) collective-permute-start(bf16[352,512]{1,0:T(8,128)(2,1)S(1)} %collective-permute-done.18.refs_2_.refs_1_), channel_id=1, source_target_pairs={{0,2},{1,3},{2,0},{3,1},{4,6},{5,7},{6,4},{7,5},{8,10},{9,11},{10,... | collective-permute-start | bytes 1081352 | tf_op jit(solution)/shard_map/ppermute | solution.py:81
  73.2 1.8 %collective-permute-start.10 = (bf16[352,512]{1,0:T(8,128)(2,1)S(1)}, bf16[352,512]{1,0:T(8,128)(2,1)S(1)}, u32[]{:S(2)}, u32[]{:S(2)}) collective-permute-start(bf16[352,512]{1,0:T(8,128)(2,1)S(1)} %collective-permute-done.7.refs_8_.refs_4_), channel_id=1, source_target_pairs={{0,16},{1,17},{2,18},{3,19},{4,20},{5,21},{6,22},{7,23},{8,24},{9,... | collective-permute-start | bytes 1081352 | tf_op jit(solution)/shard_map/ppermute | solution.py:81
  75.0 4.2 %collective-permute-start.14 = (bf16[352,512]{1,0:T(8,128)(2,1)S(1)}, bf16[352,512]{1,0:T(8,128)(2,1)S(1)}, u32[]{:S(2)}, u32[]{:S(2)}) collective-permute-start(bf16[352,512]{1,0:T(8,128)(2,1)S(1)} %collective-permute-done.7.refs_8_.refs_4_), channel_id=1, source_target_pairs={{0,2},{1,3},{2,0},{3,1},{4,6},{5,7},{6,4},{7,5},{8,10},{9,11},{10,... | collective-permute-start | bytes 1081352 | tf_op jit(solution)/shard_map/ppermute | solution.py:81
  79.3 0.4 collective-permute-start.15
  79.7 5.2 %collective-permute-start.24 = (bf16[352,512]{1,0:T(8,128)(2,1)S(1)}, bf16[352,512]{1,0:T(8,128)(2,1)S(1)}, u32[]{:S(2)}, u32[]{:S(2)}) collective-permute-start(bf16[352,512]{1,0:T(8,128)(2,1)S(1)} %collective-permute-done.21.refs_5_.refs_1_), channel_id=1, source_target_pairs={{0,16},{1,17},{2,18},{3,19},{4,20},{5,21},{6,22},{7,23},{8,24},{9,... | collective-permute-start | bytes 1081352 | tf_op jit(solution)/shard_map/ppermute | solution.py:81
  85.0 0.7 collective-permute-start.17
  85.8 0.4 collective-permute-start.28
  86.3 7.1 %collective-permute-done.24.refs_8_.refs_4_ = bf16[352,512]{1,0:T(8,128)(2,1)S(1)} collective-permute-done((bf16[352,512]{1,0:T(8,128)(2,1)S(1)}, bf16[352,512]{1,0:T(8,128)(2,1)S(1)}, u32[]{:S(2)}, u32[]{:S(2)}) %collective-permute-start.24) | collective-permute-done | bytes 360480 | tf_op jit(solution)/shard_map/ppermute | solution.py:81
  93.4 1.0 collective-permute-start.29
  94.4 3.9 %conv0.1.state_ref = f32[384,512]{1,0:T(8,128)S(1)} custom-call(f32[2,512]{1,0:T(2,128)S(1)} %copy-done.8, bf16[96,512]{1,0:T(8,128)(2,1)S(1)} %collective-permute-done.refs_0_, bf16[96,512]{1,0:T(8,128)(2,1)S(1)} %collective-permute-done.1.refs_1_, bf16[96,512]{1,0:T(8,128)(2,1)S(1)} %collective-permute-done.2.refs_2_, ...), custom_call_target="tpu_custom_call" | custom-call | tf_op jit(solution)/shard_map/conv0/pallas_call | solution.py:228
  98.3 10.2 %ff0.1.refs_0_ = f32[384,512]{1,0:T(8,128)S(1)} custom-call(f32[2,512]{1,0:T(2,128)S(1)} %copy-done.6, f32[1,512]{1,0:T(1,128)S(1)} %bitcast.4, f32[384,512]{1,0:T(8,128)S(1)} %conv0.1.state_ref, bf16[352,512]{1,0:T(8,128)(2,1)S(1)} %get-tuple-element.23.refs_4_.refs_0_, bf16[352,512]{1,0:T(8,128)(2,1)S(1)} %collective-permute-done.4.refs_5_.refs_1_, ...), custom_call_target="tpu_custom_call" | custom-call | tf_op jit(solution)/shard_map/ff0/pallas_call | solution.py:286
  108.6 3.8 %conv1.1.state_ref = f32[384,512]{1,0:T(8,128)S(1)} custom-call(f32[2,512]{1,0:T(2,128)S(1)} %copy-done.8, f32[384,512]{1,0:T(8,128)S(1)} %ff0.1.refs_0_, bf16[352,512]{1,0:T(8,128)(2,1)S(1)} %get-tuple-element.25.refs_1_.refs_0_, bf16[352,512]{1,0:T(8,128)(2,1)S(1)} %collective-permute-done.18.refs_2_.refs_1_, ...), custom_call_target="tpu_custom_call" | custom-call | tf_op jit(solution)/shard_map/conv1/pallas_call | solution.py:228
  112.4 5.1 %ff1.2 = (f32[384,512]{1,0:T(8,128)S(1)}, bf16[384,512]{1,0:T(8,128)(2,1)S(1)}) custom-call(f32[2,512]{1,0:T(2,128)S(1)} %copy-done.6, f32[1,512]{1,0:T(1,128)S(1)} %bitcast.5, f32[384,512]{1,0:T(8,128)S(1)} %conv1.1.state_ref, bf16[352,512]{1,0:T(8,128)(2,1)S(1)} %get-tuple-element.25.refs_1_.refs_0_, ...), custom_call_target="tpu_custom_call" | custom-call | tf_op jit(solution)/shard_map/ff1/pallas_call | solution.py:286
  117.5 5.1 %ff1.3.final_ref = bf16[384,512]{1,0:T(8,128)(2,1)S(1)} custom-call(f32[2,512]{1,0:T(2,128)S(1)} %copy-done.6, f32[1,512]{1,0:T(1,128)S(1)} %bitcast.6, f32[384,512]{1,0:T(8,128)S(1)} %get-tuple-element.27.state_ref, bf16[384,512]{1,0:T(8,128)(2,1)S(1)} %get-tuple-element.28.refs_0_, bf16[352,512]{1,0:T(8,128)(2,1)S(1)} %collective-permute-done.21.refs_5_.refs_1_, ...), custom_call_target="tpu_custom_call" | custom-call | tf_op jit(solution)/shard_map/ff1/pallas_call | solution.py:286
  122.6 0.5 collective-permute-start.32
  123.1 1.3 collective-permute-done.32.opposite_ref
  124.5 1.0 head.1
  125.5 3.1 %collective-permute-start.33 = (bf16[96,512]{1,0:T(8,128)(2,1)S(1)}, bf16[96,512]{1,0:T(8,128)(2,1)S(1)}, u32[]{:S(2)}, u32[]{:S(2)}) collective-permute-start(bf16[96,512]{1,0:T(8,128)(2,1)S(1)} %get-tuple-element.29), channel_id=1, source_target_pairs={{0,0},{1,1},{2,3},{3,2},{4,4},{5,5},{6,7},{7,6},{8,8},{9,9},{10,11... | collective-permute-start | bytes 294920 | tf_op jit(solution)/shard_map/ppermute | solution.py:81
  128.7 3.0 %collective-permute-start.35 = (bf16[96,512]{1,0:T(8,128)(2,1)S(1)}, bf16[96,512]{1,0:T(8,128)(2,1)S(1)}, u32[]{:S(2)}, u32[]{:S(2)}) collective-permute-start(bf16[96,512]{1,0:T(8,128)(2,1)S(1)} %get-tuple-element.31), channel_id=1, source_target_pairs={{0,8},{1,9},{2,11},{3,10},{4,12},{5,13},{6,15},{7,14},{8,0},{9,1},... | collective-permute-start | bytes 294920 | tf_op jit(solution)/shard_map/ppermute | solution.py:81
  131.8 1.8 %collective-permute-start.36 = (bf16[96,512]{1,0:T(8,128)(2,1)S(1)}, bf16[96,512]{1,0:T(8,128)(2,1)S(1)}, u32[]{:S(2)}, u32[]{:S(2)}) collective-permute-start(bf16[96,512]{1,0:T(8,128)(2,1)S(1)} %get-tuple-element.32), channel_id=1, source_target_pairs={{0,12},{1,13},{2,15},{3,14},{4,0},{5,1},{6,3},{7,2},{8,4},{9,5},{1... | collective-permute-start | bytes 294920 | tf_op jit(solution)/shard_map/ppermute | solution.py:81
  133.6 2.4 %collective-permute-done.34.refs_1_ = bf16[96,512]{1,0:T(8,128)(2,1)S(1)} collective-permute-done((bf16[96,512]{1,0:T(8,128)(2,1)S(1)}, bf16[96,512]{1,0:T(8,128)(2,1)S(1)}, u32[]{:S(2)}, u32[]{:S(2)}) %collective-permute-start.34) | collective-permute-done | bytes 98336 | tf_op jit(solution)/shard_map/ppermute | solution.py:81
  136.0 2.7 %collective-permute-done.35.refs_2_ = bf16[96,512]{1,0:T(8,128)(2,1)S(1)} collective-permute-done((bf16[96,512]{1,0:T(8,128)(2,1)S(1)}, bf16[96,512]{1,0:T(8,128)(2,1)S(1)}, u32[]{:S(2)}, u32[]{:S(2)}) %collective-permute-start.35) | collective-permute-done | bytes 98336 | tf_op jit(solution)/shard_map/ppermute | solution.py:81
  138.7 0.8 join.1
  (55 shorter events, 0.9 us)
Async XLA Ops:
  0.0 1.5 %copy-start = (bf16[2,512,256]{2,1,0:T(8,128)(2,1)S(1)}, bf16[2,512,256]{2,1,0:T(8,128)(2,1)}, u32[]{:S(2)}) copy-start(bf16[2,512,256]{2,1,0:T(8,128)(2,1)} %up_ref.3) | copy-start | bytes 1572868
  0.0 1.5 %copy-start.1 = (bf16[2,256,512]{2,1,0:T(8,128)(2,1)S(1)}, bf16[2,256,512]{2,1,0:T(8,128)(2,1)}, u32[]{:S(2)}) copy-start(bf16[2,256,512]{2,1,0:T(8,128)(2,1)} %down_ref.3) | copy-start | bytes 1572868
  1.5 5.7 %copy-start.5 = (bf16[1,384,512]{2,1,0:T(8,128)(2,1)S(1)}, bf16[1,384,512]{2,1,0:T(8,128)(2,1)}, u32[]{:S(2)}) copy-start(bf16[1,384,512]{2,1,0:T(8,128)(2,1)} %param.10) | copy-start | bytes 1179652
  1.7 30.2 %collective-permute-start.4 = (bf16[352,512]{1,0:T(8,128)(2,1)S(1)}, bf16[352,512]{1,0:T(8,128)(2,1)S(1)}, u32[]{:S(2)}, u32[]{:S(2)}) collective-permute-start(bf16[352,512]{1,0:T(8,128)(2,1)S(1)} %get-tuple-element.23.refs_4_.refs_0_), channel_id=1, source_target_pairs={{0,4},{1,5},{2,6},{3,7},{4,8},{5,9},{6,10},{7,11},{8,12},{9,13},{1... | collective-permute-start | bytes 1081352 | tf_op jit(solution)/shard_map/ppermute | solution.py:81
  3.9 28.5 %collective-permute-start.5 = (bf16[352,512]{1,0:T(8,128)(2,1)S(1)}, bf16[352,512]{1,0:T(8,128)(2,1)S(1)}, u32[]{:S(2)}, u32[]{:S(2)}) collective-permute-start(bf16[352,512]{1,0:T(8,128)(2,1)S(1)} %get-tuple-element.23.refs_4_.refs_0_), channel_id=1, source_target_pairs={{0,12},{1,13},{2,14},{3,15},{4,0},{5,1},{6,2},{7,3},{8,4},{9,5},{1... | collective-permute-start | bytes 1081352 | tf_op jit(solution)/shard_map/ppermute | solution.py:81
  6.0 27.4 %collective-permute-start.6 = (bf16[352,512]{1,0:T(8,128)(2,1)S(1)}, bf16[352,512]{1,0:T(8,128)(2,1)S(1)}, u32[]{:S(2)}, u32[]{:S(2)}) collective-permute-start(bf16[352,512]{1,0:T(8,128)(2,1)S(1)} %get-tuple-element.23.refs_4_.refs_0_), channel_id=1, source_target_pairs={{0,1},{1,0},{2,3},{3,2},{4,5},{5,4},{6,7},{7,6},{8,9},{9,8},{10,11... | collective-permute-start | bytes 1081352 | tf_op jit(solution)/shard_map/ppermute | solution.py:81
  7.2 9.8 %collective-permute-start = (bf16[96,512]{1,0:T(8,128)(2,1)S(1)}, bf16[96,512]{1,0:T(8,128)(2,1)S(1)}, u32[]{:S(2)}, u32[]{:S(2)}) collective-permute-start(bf16[96,512]{1,0:T(8,128)(2,1)S(1)} %get-tuple-element.19), channel_id=1, source_target_pairs={{0,0},{1,1},{2,3},{3,2},{4,4},{5,5},{6,7},{7,6},{8,8},{9,9},{10,11... | collective-permute-start | bytes 294920 | tf_op jit(solution)/shard_map/ppermute | solution.py:81
  9.4 14.9 %collective-permute-start.1 = (bf16[96,512]{1,0:T(8,128)(2,1)S(1)}, bf16[96,512]{1,0:T(8,128)(2,1)S(1)}, u32[]{:S(2)}, u32[]{:S(2)}) collective-permute-start(bf16[96,512]{1,0:T(8,128)(2,1)S(1)} %get-tuple-element.20), channel_id=1, source_target_pairs={{0,4},{1,5},{2,7},{3,6},{4,8},{5,9},{6,11},{7,10},{8,12},{9,13},{1... | collective-permute-start | bytes 294920 | tf_op jit(solution)/shard_map/ppermute | solution.py:81
  17.0 12.5 %collective-permute-start.2 = (bf16[96,512]{1,0:T(8,128)(2,1)S(1)}, bf16[96,512]{1,0:T(8,128)(2,1)S(1)}, u32[]{:S(2)}, u32[]{:S(2)}) collective-permute-start(bf16[96,512]{1,0:T(8,128)(2,1)S(1)} %get-tuple-element.21), channel_id=1, source_target_pairs={{0,8},{1,9},{2,11},{3,10},{4,12},{5,13},{6,15},{7,14},{8,0},{9,1},... | collective-permute-start | bytes 294920 | tf_op jit(solution)/shard_map/ppermute | solution.py:81
  24.3 6.7 %collective-permute-start.3 = (bf16[96,512]{1,0:T(8,128)(2,1)S(1)}, bf16[96,512]{1,0:T(8,128)(2,1)S(1)}, u32[]{:S(2)}, u32[]{:S(2)}) collective-permute-start(bf16[96,512]{1,0:T(8,128)(2,1)S(1)} %get-tuple-element.22), channel_id=1, source_target_pairs={{0,12},{1,13},{2,15},{3,14},{4,0},{5,1},{6,3},{7,2},{8,4},{9,5},{1... | collective-permute-start | bytes 294920 | tf_op jit(solution)/shard_map/ppermute | solution.py:81
  25.9 68.4 %copy-start.8 = (f32[2,512]{1,0:T(2,128)S(1)}, f32[2,512]{1,0:T(2,128)}, u32[]{:S(2)}) copy-start(f32[2,512]{1,0:T(2,128)} %gain_ref.7) | copy-start | bytes 12292
  29.6 17.6 %collective-permute-start.18 = (bf16[352,512]{1,0:T(8,128)(2,1)S(1)}, bf16[352,512]{1,0:T(8,128)(2,1)S(1)}, u32[]{:S(2)}, u32[]{:S(2)}) collective-permute-start(bf16[352,512]{1,0:T(8,128)(2,1)S(1)} %get-tuple-element.25.refs_1_.refs_0_), channel_id=1, source_target_pairs={{0,8},{1,9},{2,10},{3,11},{4,12},{5,13},{6,14},{7,15},{8,0},{9,1},... | collective-permute-start | bytes 1081352 | tf_op jit(solution)/shard_map/ppermute | solution.py:81
  31.1 17.1 %collective-permute-start.19 = (bf16[352,512]{1,0:T(8,128)(2,1)S(1)}, bf16[352,512]{1,0:T(8,128)(2,1)S(1)}, u32[]{:S(2)}, u32[]{:S(2)}) collective-permute-start(bf16[352,512]{1,0:T(8,128)(2,1)S(1)} %get-tuple-element.25.refs_1_.refs_0_), channel_id=1, source_target_pairs={{0,12},{1,13},{2,14},{3,15},{4,0},{5,1},{6,2},{7,3},{8,4},{9,5},{1... | collective-permute-start | bytes 1081352 | tf_op jit(solution)/shard_map/ppermute | solution.py:81
  31.9 17.4 %collective-permute-start.20 = (bf16[352,512]{1,0:T(8,128)(2,1)S(1)}, bf16[352,512]{1,0:T(8,128)(2,1)S(1)}, u32[]{:S(2)}, u32[]{:S(2)}) collective-permute-start(bf16[352,512]{1,0:T(8,128)(2,1)S(1)} %get-tuple-element.25.refs_1_.refs_0_), channel_id=1, source_target_pairs={{0,1},{1,0},{2,3},{3,2},{4,5},{5,4},{6,7},{7,6},{8,9},{9,8},{10,11... | collective-permute-start | bytes 1081352 | tf_op jit(solution)/shard_map/ppermute | solution.py:81
  32.4 17.0 %collective-permute-start.7 = (bf16[352,512]{1,0:T(8,128)(2,1)S(1)}, bf16[352,512]{1,0:T(8,128)(2,1)S(1)}, u32[]{:S(2)}, u32[]{:S(2)}) collective-permute-start(bf16[352,512]{1,0:T(8,128)(2,1)S(1)} %collective-permute-done.4.refs_5_.refs_1_), channel_id=1, source_target_pairs={{0,1},{1,0},{2,3},{3,2},{4,5},{5,4},{6,7},{7,6},{8,9},{9,8},{10,11... | collective-permute-start | bytes 1081352 | tf_op jit(solution)/shard_map/ppermute | solution.py:81
  33.4 18.2 %collective-permute-start.9 = (bf16[352,512]{1,0:T(8,128)(2,1)S(1)}, bf16[352,512]{1,0:T(8,128)(2,1)S(1)}, u32[]{:S(2)}, u32[]{:S(2)}) collective-permute-start(bf16[352,512]{1,0:T(8,128)(2,1)S(1)} %collective-permute-done.4.refs_5_.refs_1_), channel_id=1, source_target_pairs={{0,16},{1,17},{2,18},{3,19},{4,20},{5,21},{6,22},{7,23},{8,24},{9,... | collective-permute-start | bytes 1081352 | tf_op jit(solution)/shard_map/ppermute | solution.py:81
  47.1 9.7 %collective-permute-start.8 = (bf16[352,512]{1,0:T(8,128)(2,1)S(1)}, bf16[352,512]{1,0:T(8,128)(2,1)S(1)}, u32[]{:S(2)}, u32[]{:S(2)}) collective-permute-start(bf16[352,512]{1,0:T(8,128)(2,1)S(1)} %collective-permute-done.5.refs_6_.refs_2_), channel_id=1, source_target_pairs={{0,1},{1,0},{2,3},{3,2},{4,5},{5,4},{6,7},{7,6},{8,9},{9,8},{10,11... | collective-permute-start | bytes 1081352 | tf_op jit(solution)/shard_map/ppermute | solution.py:81
  48.2 19.2 %collective-permute-start.11 = (bf16[352,512]{1,0:T(8,128)(2,1)S(1)}, bf16[352,512]{1,0:T(8,128)(2,1)S(1)}, u32[]{:S(2)}, u32[]{:S(2)}) collective-permute-start(bf16[352,512]{1,0:T(8,128)(2,1)S(1)} %collective-permute-done.4.refs_5_.refs_1_), channel_id=1, source_target_pairs={{0,2},{1,3},{2,0},{3,1},{4,6},{5,7},{6,4},{7,5},{8,10},{9,11},{10,... | collective-permute-start | bytes 1081352 | tf_op jit(solution)/shard_map/ppermute | solution.py:81
  49.4 19.0 %collective-permute-start.12 = (bf16[352,512]{1,0:T(8,128)(2,1)S(1)}, bf16[352,512]{1,0:T(8,128)(2,1)S(1)}, u32[]{:S(2)}, u32[]{:S(2)}) collective-permute-start(bf16[352,512]{1,0:T(8,128)(2,1)S(1)} %collective-permute-done.5.refs_6_.refs_2_), channel_id=1, source_target_pairs={{0,2},{1,3},{2,0},{3,1},{4,6},{5,7},{6,4},{7,5},{8,10},{9,11},{10,... | collective-permute-start | bytes 1081352 | tf_op jit(solution)/shard_map/ppermute | solution.py:81
  49.4 23.8 %collective-permute-start.13 = (bf16[352,512]{1,0:T(8,128)(2,1)S(1)}, bf16[352,512]{1,0:T(8,128)(2,1)S(1)}, u32[]{:S(2)}, u32[]{:S(2)}) collective-permute-start(bf16[352,512]{1,0:T(8,128)(2,1)S(1)} %collective-permute-done.6.refs_7_.refs_3_), channel_id=1, source_target_pairs={{0,2},{1,3},{2,0},{3,1},{4,6},{5,7},{6,4},{7,5},{8,10},{9,11},{10,... | collective-permute-start | bytes 1081352 | tf_op jit(solution)/shard_map/ppermute | solution.py:81
  51.6 21.6 %collective-permute-start.21 = (bf16[352,512]{1,0:T(8,128)(2,1)S(1)}, bf16[352,512]{1,0:T(8,128)(2,1)S(1)}, u32[]{:S(2)}, u32[]{:S(2)}) collective-permute-start(bf16[352,512]{1,0:T(8,128)(2,1)S(1)} %collective-permute-done.18.refs_2_.refs_1_), channel_id=1, source_target_pairs={{0,1},{1,0},{2,3},{3,2},{4,5},{5,4},{6,7},{7,6},{8,9},{9,8},{10,11... | collective-permute-start | bytes 1081352 | tf_op jit(solution)/shard_map/ppermute | solution.py:81
  56.9 18.2 %collective-permute-start.23 = (bf16[352,512]{1,0:T(8,128)(2,1)S(1)}, bf16[352,512]{1,0:T(8,128)(2,1)S(1)}, u32[]{:S(2)}, u32[]{:S(2)}) collective-permute-start(bf16[352,512]{1,0:T(8,128)(2,1)S(1)} %collective-permute-done.18.refs_2_.refs_1_), channel_id=1, source_target_pairs={{0,16},{1,17},{2,18},{3,19},{4,20},{5,21},{6,22},{7,23},{8,24},{9,... | collective-permute-start | bytes 1081352 | tf_op jit(solution)/shard_map/ppermute | solution.py:81
  67.3 11.9 %collective-permute-start.22 = (bf16[352,512]{1,0:T(8,128)(2,1)S(1)}, bf16[352,512]{1,0:T(8,128)(2,1)S(1)}, u32[]{:S(2)}, u32[]{:S(2)}) collective-permute-start(bf16[352,512]{1,0:T(8,128)(2,1)S(1)} %collective-permute-done.19.refs_3_.refs_2_), channel_id=1, source_target_pairs={{0,1},{1,0},{2,3},{3,2},{4,5},{5,4},{6,7},{7,6},{8,9},{9,8},{10,11... | collective-permute-start | bytes 1081352 | tf_op jit(solution)/shard_map/ppermute | solution.py:81
  68.4 10.9 %collective-permute-start.25 = (bf16[352,512]{1,0:T(8,128)(2,1)S(1)}, bf16[352,512]{1,0:T(8,128)(2,1)S(1)}, u32[]{:S(2)}, u32[]{:S(2)}) collective-permute-start(bf16[352,512]{1,0:T(8,128)(2,1)S(1)} %collective-permute-done.18.refs_2_.refs_1_), channel_id=1, source_target_pairs={{0,2},{1,3},{2,0},{3,1},{4,6},{5,7},{6,4},{7,5},{8,10},{9,11},{10,... | collective-permute-start | bytes 1081352 | tf_op jit(solution)/shard_map/ppermute | solution.py:81
  73.2 6.6 %collective-permute-start.26 = (bf16[352,512]{1,0:T(8,128)(2,1)S(1)}, bf16[352,512]{1,0:T(8,128)(2,1)S(1)}, u32[]{:S(2)}, u32[]{:S(2)}) collective-permute-start(bf16[352,512]{1,0:T(8,128)(2,1)S(1)} %collective-permute-done.19.refs_3_.refs_2_), channel_id=1, source_target_pairs={{0,2},{1,3},{2,0},{3,1},{4,6},{5,7},{6,4},{7,5},{8,10},{9,11},{10,... | collective-permute-start | bytes 1081352 | tf_op jit(solution)/shard_map/ppermute | solution.py:81
  73.2 11.8 %collective-permute-start.10 = (bf16[352,512]{1,0:T(8,128)(2,1)S(1)}, bf16[352,512]{1,0:T(8,128)(2,1)S(1)}, u32[]{:S(2)}, u32[]{:S(2)}) collective-permute-start(bf16[352,512]{1,0:T(8,128)(2,1)S(1)} %collective-permute-done.7.refs_8_.refs_4_), channel_id=1, source_target_pairs={{0,16},{1,17},{2,18},{3,19},{4,20},{5,21},{6,22},{7,23},{8,24},{9,... | collective-permute-start | bytes 1081352 | tf_op jit(solution)/shard_map/ppermute | solution.py:81
  75.0 10.7 %collective-permute-start.14 = (bf16[352,512]{1,0:T(8,128)(2,1)S(1)}, bf16[352,512]{1,0:T(8,128)(2,1)S(1)}, u32[]{:S(2)}, u32[]{:S(2)}) collective-permute-start(bf16[352,512]{1,0:T(8,128)(2,1)S(1)} %collective-permute-done.7.refs_8_.refs_4_), channel_id=1, source_target_pairs={{0,2},{1,3},{2,0},{3,1},{4,6},{5,7},{6,4},{7,5},{8,10},{9,11},{10,... | collective-permute-start | bytes 1081352 | tf_op jit(solution)/shard_map/ppermute | solution.py:81
  79.2 6.6 %collective-permute-start.16 = (bf16[352,512]{1,0:T(8,128)(2,1)S(1)}, bf16[352,512]{1,0:T(8,128)(2,1)S(1)}, u32[]{:S(2)}, u32[]{:S(2)}) collective-permute-start(bf16[352,512]{1,0:T(8,128)(2,1)S(1)} %collective-permute-done.9.refs_10_.refs_6_), channel_id=1, source_target_pairs={{0,2},{1,3},{2,0},{3,1},{4,6},{5,7},{6,4},{7,5},{8,10},{9,11},{10,... | collective-permute-start | bytes 1081352 | tf_op jit(solution)/shard_map/ppermute | solution.py:81
  79.3 6.9 %collective-permute-start.15 = (bf16[352,512]{1,0:T(8,128)(2,1)S(1)}, bf16[352,512]{1,0:T(8,128)(2,1)S(1)}, u32[]{:S(2)}, u32[]{:S(2)}) collective-permute-start(bf16[352,512]{1,0:T(8,128)(2,1)S(1)} %collective-permute-done.8.refs_9_.refs_5_), channel_id=1, source_target_pairs={{0,2},{1,3},{2,0},{3,1},{4,6},{5,7},{6,4},{7,5},{8,10},{9,11},{10,... | collective-permute-start | bytes 1081352 | tf_op jit(solution)/shard_map/ppermute | solution.py:81
  79.7 13.7 %collective-permute-start.24 = (bf16[352,512]{1,0:T(8,128)(2,1)S(1)}, bf16[352,512]{1,0:T(8,128)(2,1)S(1)}, u32[]{:S(2)}, u32[]{:S(2)}) collective-permute-start(bf16[352,512]{1,0:T(8,128)(2,1)S(1)} %collective-permute-done.21.refs_5_.refs_1_), channel_id=1, source_target_pairs={{0,16},{1,17},{2,18},{3,19},{4,20},{5,21},{6,22},{7,23},{8,24},{9,... | collective-permute-start | bytes 1081352 | tf_op jit(solution)/shard_map/ppermute | solution.py:81
  85.0 9.4 %collective-permute-start.17 = (bf16[352,512]{1,0:T(8,128)(2,1)S(1)}, bf16[352,512]{1,0:T(8,128)(2,1)S(1)}, u32[]{:S(2)}, u32[]{:S(2)}) collective-permute-start(bf16[352,512]{1,0:T(8,128)(2,1)S(1)} %collective-permute-done.10.refs_11_.refs_7_), channel_id=1, source_target_pairs={{0,2},{1,3},{2,0},{3,1},{4,6},{5,7},{6,4},{7,5},{8,10},{9,11},{10,... | collective-permute-start | bytes 1081352 | tf_op jit(solution)/shard_map/ppermute | solution.py:81
  85.7 22.8 %collective-permute-start.27 = (bf16[352,512]{1,0:T(8,128)(2,1)S(1)}, bf16[352,512]{1,0:T(8,128)(2,1)S(1)}, u32[]{:S(2)}, u32[]{:S(2)}) collective-permute-start(bf16[352,512]{1,0:T(8,128)(2,1)S(1)} %collective-permute-done.20.refs_4_.refs_3_), channel_id=1, source_target_pairs={{0,2},{1,3},{2,0},{3,1},{4,6},{5,7},{6,4},{7,5},{8,10},{9,11},{10,... | collective-permute-start | bytes 1081352 | tf_op jit(solution)/shard_map/ppermute | solution.py:81
  85.8 22.8 %collective-permute-start.28 = (bf16[352,512]{1,0:T(8,128)(2,1)S(1)}, bf16[352,512]{1,0:T(8,128)(2,1)S(1)}, u32[]{:S(2)}, u32[]{:S(2)}) collective-permute-start(bf16[352,512]{1,0:T(8,128)(2,1)S(1)} %collective-permute-done.21.refs_5_.refs_1_), channel_id=1, source_target_pairs={{0,2},{1,3},{2,0},{3,1},{4,6},{5,7},{6,4},{7,5},{8,10},{9,11},{10,... | collective-permute-start | bytes 1081352 | tf_op jit(solution)/shard_map/ppermute | solution.py:81
  86.2 22.3 %collective-permute-start.30 = (bf16[352,512]{1,0:T(8,128)(2,1)S(1)}, bf16[352,512]{1,0:T(8,128)(2,1)S(1)}, u32[]{:S(2)}, u32[]{:S(2)}) collective-permute-start(bf16[352,512]{1,0:T(8,128)(2,1)S(1)} %collective-permute-done.23.refs_7_.refs_3_), channel_id=1, source_target_pairs={{0,2},{1,3},{2,0},{3,1},{4,6},{5,7},{6,4},{7,5},{8,10},{9,11},{10,... | collective-permute-start | bytes 1081352 | tf_op jit(solution)/shard_map/ppermute | solution.py:81
  93.4 15.2 %collective-permute-start.29 = (bf16[352,512]{1,0:T(8,128)(2,1)S(1)}, bf16[352,512]{1,0:T(8,128)(2,1)S(1)}, u32[]{:S(2)}, u32[]{:S(2)}) collective-permute-start(bf16[352,512]{1,0:T(8,128)(2,1)S(1)} %collective-permute-done.22.refs_6_.refs_2_), channel_id=1, source_target_pairs={{0,2},{1,3},{2,0},{3,1},{4,6},{5,7},{6,4},{7,5},{8,10},{9,11},{10,... | collective-permute-start | bytes 1081352 | tf_op jit(solution)/shard_map/ppermute | solution.py:81
  94.4 14.2 %collective-permute-start.31 = (bf16[352,512]{1,0:T(8,128)(2,1)S(1)}, bf16[352,512]{1,0:T(8,128)(2,1)S(1)}, u32[]{:S(2)}, u32[]{:S(2)}) collective-permute-start(bf16[352,512]{1,0:T(8,128)(2,1)S(1)} %collective-permute-done.24.refs_8_.refs_4_), channel_id=1, source_target_pairs={{0,2},{1,3},{2,0},{3,1},{4,6},{5,7},{6,4},{7,5},{8,10},{9,11},{10,... | collective-permute-start | bytes 1081352 | tf_op jit(solution)/shard_map/ppermute | solution.py:81
  94.4 3.9 %copy-start.6 = (f32[2,512]{1,0:T(2,128)S(1)}, f32[2,512]{1,0:T(2,128)}, u32[]{:S(2)}) copy-start(f32[2,512]{1,0:T(2,128)} %gain_ref.9) | copy-start | bytes 12292
  94.4 3.9 %copy-start.7 = (f32[512]{0:T(512)S(1)}, f32[512]{0:T(512)}, u32[]{:S(2)}) copy-start(f32[512]{0:T(512)} %param.16) | copy-start | bytes 6148
  117.5 7.0 %copy-start.2 = (bf16[512,512]{1,0:T(8,128)(2,1)S(1)}, bf16[512,512]{1,0:T(8,128)(2,1)}, u32[]{:S(2)}) copy-start(bf16[512,512]{1,0:T(8,128)(2,1)} %value_ref.1) | copy-start | bytes 1572868
  117.5 7.0 %copy-start.3 = (bf16[512,512]{1,0:T(8,128)(2,1)S(1)}, bf16[512,512]{1,0:T(8,128)(2,1)}, u32[]{:S(2)}) copy-start(bf16[512,512]{1,0:T(8,128)(2,1)} %gate_ref.1) | copy-start | bytes 1572868
  117.5 7.0 %copy-start.4 = (bf16[512,512]{1,0:T(8,128)(2,1)S(1)}, bf16[512,512]{1,0:T(8,128)(2,1)}, u32[]{:S(2)}) copy-start(bf16[512,512]{1,0:T(8,128)(2,1)} %out_ref.1) | copy-start | bytes 1572868
  122.6 1.9 %collective-permute-start.32 = (bf16[384,512]{1,0:T(8,128)(2,1)S(1)}, bf16[384,512]{1,0:T(8,128)(2,1)S(1)}, u32[]{:S(2)}, u32[]{:S(2)}) collective-permute-start(bf16[384,512]{1,0:T(8,128)(2,1)S(1)} %ff1.3.final_ref), channel_id=1, source_target_pairs={{0,2},{1,3},{2,0},{3,1},{4,6},{5,7},{6,4},{7,5},{8,10},{9,11},{10,... | collective-permute-start | bytes 1179656 | tf_op jit(solution)/shard_map/ppermute | solution.py:81
  125.5 8.1 %collective-permute-start.33 = (bf16[96,512]{1,0:T(8,128)(2,1)S(1)}, bf16[96,512]{1,0:T(8,128)(2,1)S(1)}, u32[]{:S(2)}, u32[]{:S(2)}) collective-permute-start(bf16[96,512]{1,0:T(8,128)(2,1)S(1)} %get-tuple-element.29), channel_id=1, source_target_pairs={{0,0},{1,1},{2,3},{3,2},{4,4},{5,5},{6,7},{7,6},{8,8},{9,9},{10,11... | collective-permute-start | bytes 294920 | tf_op jit(solution)/shard_map/ppermute | solution.py:81
  128.7 7.3 %collective-permute-start.34 = (bf16[96,512]{1,0:T(8,128)(2,1)S(1)}, bf16[96,512]{1,0:T(8,128)(2,1)S(1)}, u32[]{:S(2)}, u32[]{:S(2)}) collective-permute-start(bf16[96,512]{1,0:T(8,128)(2,1)S(1)} %get-tuple-element.30), channel_id=1, source_target_pairs={{0,4},{1,5},{2,7},{3,6},{4,8},{5,9},{6,11},{7,10},{8,12},{9,13},{1... | collective-permute-start | bytes 294920 | tf_op jit(solution)/shard_map/ppermute | solution.py:81
  128.7 10.0 %collective-permute-start.35 = (bf16[96,512]{1,0:T(8,128)(2,1)S(1)}, bf16[96,512]{1,0:T(8,128)(2,1)S(1)}, u32[]{:S(2)}, u32[]{:S(2)}) collective-permute-start(bf16[96,512]{1,0:T(8,128)(2,1)S(1)} %get-tuple-element.31), channel_id=1, source_target_pairs={{0,8},{1,9},{2,11},{3,10},{4,12},{5,13},{6,15},{7,14},{8,0},{9,1},... | collective-permute-start | bytes 294920 | tf_op jit(solution)/shard_map/ppermute | solution.py:81
  131.8 6.9 %collective-permute-start.36 = (bf16[96,512]{1,0:T(8,128)(2,1)S(1)}, bf16[96,512]{1,0:T(8,128)(2,1)S(1)}, u32[]{:S(2)}, u32[]{:S(2)}) collective-permute-start(bf16[96,512]{1,0:T(8,128)(2,1)S(1)} %get-tuple-element.32), channel_id=1, source_target_pairs={{0,12},{1,13},{2,15},{3,14},{4,0},{5,1},{6,3},{7,2},{8,4},{9,5},{1... | collective-permute-start | bytes 294920 | tf_op jit(solution)/shard_map/ppermute | solution.py:81

commit v2 on v1

v2 whole, which is shorter than its diff:
```python
import functools
import itertools

import jax
import jax.numpy as jnp
from jax import lax
from jax.experimental import pallas as pl
from jax.experimental.pallas import tpu as pltpu
from jax.sharding import PartitionSpec as P

AXES = ("groups", "seq", "strand", "chan")
BF16, F32 = jnp.bfloat16, jnp.float32
PARAMS = pltpu.CompilerParams(vmem_limit_bytes=40 * 2**20)
VMEM_SPEC = pl.BlockSpec(memory_space=pltpu.VMEM)


def normalize(values, gain):
    return values * lax.rsqrt(jnp.mean(values * values, axis=-1, keepdims=True) + 1e-06) * gain


def matmul(left, right):
    return jnp.dot(left, right, preferred_element_type=F32)


def matmul_nt(left, right):
    return lax.dot_general(left, right, (((1,), (1,)), ((), ())), preferred_element_type=F32)


def passed_along(value, axis, steps):
    count = lax.axis_size(axis)
    initial, last = (max(0, -steps), min(count, count - steps))
    return lax.ppermute(value, axis, [(source, source + steps) for source in range(initial, last)])


def swapped(x, axis, stride):
    return lax.ppermute(x, axis, [(i, i ^ 1 << stride) for i in range(lax.axis_size(axis))])


def local_plain(
    seq_in, conv_norm, conv_weight, ff_norm, up_weight, down_weight,
    head_norm, value_weight, gate_weight, out_weight,
):
    state = seq_in[0].astype(F32)
    seq_count = lax.axis_size("seq")
    for block in range(conv_weight.shape[0]):
        reach = min(2**block, seq_count // 2)
        normed = normalize(state, conv_norm[block]).astype(BF16)
        before = passed_along(normed, "seq", reach)
        after = passed_along(normed, "seq", -reach)
        piece = lax.all_gather(conv_weight[block], ("seq", "chan"), axis=2, tiled=True)
        total = matmul(before, piece[0]) + matmul(normed, piece[1]) + matmul(after, piece[2])
        state = state + total.astype(BF16).astype(F32)
        mixed = normalize(state, ff_norm[block]).astype(BF16)
        up = lax.all_gather(up_weight[block], ("seq", "chan"), axis=1, tiled=True)
        hidden = jax.nn.gelu(matmul(mixed, up)).astype(BF16)
        down = lax.all_gather(down_weight[block], ("seq", "chan"), axis=0, tiled=True)
        state = state + matmul(hidden, down)
    final = normalize(state, head_norm).astype(BF16)
    value = matmul(final, value_weight)
    bit_count = (seq_count * lax.axis_size("chan")).bit_length() - 1
    opposite = swapped(final, "strand", 0)
    for digit in range(bit_count):
        opposite = swapped(opposite, ("seq", "chan"), digit)
    opposite = jnp.flip(opposite, 0)
    mirrored = matmul(opposite, gate_weight).astype(BF16)
    gated = (value * jax.nn.sigmoid(mirrored.astype(F32))).astype(BF16)
    return matmul(gated, out_weight).astype(BF16)[None]


def moved(value, go):
    sizes = [lax.axis_size(a) for a in AXES]

    def flat(at):
        number = 0
        for n, k in zip(sizes, at):
            number = number * n + k
        return number

    pairs = [(flat(at), flat(go(*at))) for at in itertools.product(*map(range, sizes))]
    return lax.ppermute(value, AXES, pairs)


def across(value):
    return moved(value, lambda g, i, s, c: (g, i, s, 1 - c))


def planes(value):
    return moved(value, lambda g, i, s, c: (1 - g, i, s, c))


def other_core(value):
    return moved(value, lambda g, i, s, c: (g, i, 1 - s, c))


def along(value):
    n = lax.axis_size("seq")
    return moved(value, lambda g, i, s, c: (g, (i + 1 - 2 * g) % n, s, c))


def after(values, events):
    values, _ = lax.optimization_barrier((tuple(values), tuple(events)))
    return values


def origins():
    g, i, c = (lax.axis_index(a) for a in ("groups", "seq", "chan"))
    n, m = lax.axis_size("seq"), lax.axis_size("chan")
    a = lax.rem(i + n - 1 + 2 * g, n)
    b = lax.rem(i + 2, n)
    ya = lax.rem(i + n + 1 - 2 * g, n)
    x = 1 - c
    at = [(i, c), (a, c), (b, c), (i, x), (a, x), (b, x), (ya, c), (ya, x)]
    return [k * m + h for k, h in at]


def pack_kernel(plan, *refs):
    first = lax.axis_index("strand") == 0
    refs, mine_ref, other_ref = refs[:-2], refs[-2], refs[-1]
    at = 0
    for ref, block, turn in zip(refs, *plan):
        whole = ref[block].T if turn else ref[block]
        taps = whole[None] if whole.ndim == 2 else whole
        for tap in range(taps.shape[0]):
            half = taps.shape[1] // 2
            top, low = taps[tap, :half], taps[tap, half:]
            mine_ref[at : at + half] = jnp.where(first, top, low)
            other_ref[at : at + half] = jnp.where(first, low, top)
            at += half


def pack(arrays, blocks, turned, rows, name):
    shape = jax.ShapeDtypeStruct((rows, arrays[-1].shape[-1]), BF16)
    return pl.pallas_call(
        functools.partial(pack_kernel, (blocks, turned)),
        out_shape=[shape, shape],
        in_specs=[VMEM_SPEC] * len(arrays),
        out_specs=[VMEM_SPEC] * 2,
        compiler_params=PARAMS,
        name=name,
    )(*arrays)


def split_kernel(rows_ref, *out_refs):
    n = lax.axis_size("seq")
    i, s = lax.axis_index("seq"), lax.axis_index("strand")
    size = out_refs[0].shape[0]
    for k, out in enumerate(out_refs):
        j = lax.rem(i + k, n)
        sub = jnp.where(s == 0, j, n - 1 - j)
        out[...] = rows_ref[pl.ds(pl.multiple_of(sub * size, size), size)]


def join_kernel(*refs):
    *parts, out = refs
    n = lax.axis_size("seq")
    i, s = lax.axis_index("seq"), lax.axis_index("strand")
    size = parts[0].shape[0]
    for k, part in enumerate(parts):
        j = lax.rem(i + n - k, n)
        sub = jnp.where(s == 0, j, n - 1 - j)
        out[pl.ds(pl.multiple_of(sub * size, size), size)] = part[...]


def conv_kernel(block, parts, start, gain_ref, *refs):
    n = lax.axis_size("seq")
    states, refs = refs[:parts], refs[parts:]
    count = (len(refs) - 3) // 2
    mine, other = refs[:count], refs[count : 2 * count]
    out, weight, acc = refs[2 * count :]
    width = acc.shape[1]
    taps = weight.shape[0] // width
    half = width // count // 2
    s, j = lax.axis_index("strand"), lax.axis_index("seq")
    for r, shard in enumerate(origins()):
        for ref, part in ((mine[r], s), (other[r], 1 - s)):
            at = pl.multiple_of((shard * 2 + part) * half, half)
            for tap in range(taps):
                weight[pl.ds(tap * width + at, half)] = ref[start + tap * half : start + (tap + 1) * half]
    if parts > 1:
        size = states[0].shape[0]
        for k, state in enumerate(states):
            at = lax.rem(j + n - k, n)
            out[pl.ds(pl.multiple_of(at * size, size), size)] = state[...].astype(F32)
        state = out[...]
    else:
        state = states[0][...]
    normed = normalize(state, gain_ref[block : block + 1]).astype(BF16)
    shift = state.shape[0] // n * min(2**block, n // 2)
    acc[...] = matmul_nt(normed, weight[width : 2 * width])
    acc[shift:] += matmul_nt(normed[:-shift], weight[:width])
    acc[:-shift] += matmul_nt(normed[shift:], weight[2 * width :])
    out[...] = state + acc[...].astype(BF16).astype(F32)


def conv(states, gain, mine, other, block, start, taps):
    width = gain.shape[1]
    rows = sum(v.shape[0] for v in states)
    arrays = len(mine) + len(other)
    return pl.pallas_call(
        functools.partial(conv_kernel, block, len(states), start),
        out_shape=jax.ShapeDtypeStruct((rows, width), F32),
        in_specs=[VMEM_SPEC] * (1 + len(states) + arrays),
        out_specs=VMEM_SPEC,
        scratch_shapes=[pltpu.VMEM((taps * width, width), BF16), pltpu.VMEM((rows, width), F32)],
        compiler_params=PARAMS,
        name=f"conv{block}",
    )(gain, *states, *mine, *other)


def ff_kernel(block, first, ends, half, gain_ref, head_ref, state_ref, *refs):
    if not first:
        mixed_ref, refs = refs[0], refs[1:]
    outs = 1 if ends else 2
    count = (len(refs) - outs - 1) // 2
    mine, other = refs[:count], refs[count : 2 * count]
    out, hid = refs[2 * count], refs[-1]
    state = state_ref[...]
    if first:
        mixed = normalize(state, gain_ref[block : block + 1]).astype(BF16)
    else:
        mixed = mixed_ref[...]
    down = []
    for r in range(count):
        up = jnp.concatenate([mine[r][:half], other[r][:half]], 0)
        hid[:, 2 * r * half : 2 * (r + 1) * half] = jax.nn.gelu(matmul_nt(mixed, up)).astype(BF16)
        down += [mine[r][half : 2 * half], other[r][half : 2 * half]]
    state = state + matmul(hid[...], jnp.concatenate(down, 0))
    if ends == "head":
        state = normalize(state, head_ref[...]).astype(BF16)
    out[...] = state
    if not ends:
        refs[2 * count + 1][...] = mixed


def feed_forward(state, mixed, gain, head, mine, other, block, half, ends):
    rows, width = state.shape
    arrays = len(mine) + len(other)
    out = [jax.ShapeDtypeStruct((rows, width), BF16 if ends == "head" else F32)]
    if not ends:
        out.append(jax.ShapeDtypeStruct((rows, width), BF16))
    given = [state] if mixed is None else [state, mixed]
    return pl.pallas_call(
        functools.partial(ff_kernel, block, mixed is None, ends, half),
        out_shape=out,
        in_specs=[VMEM_SPEC] * (2 + len(given) + arrays),
        out_specs=[VMEM_SPEC] * len(out),
        scratch_shapes=[pltpu.VMEM((rows, arrays * half), BF16)],
        compiler_params=PARAMS,
        name=f"ff{block}",
    )(gain, head, *given, *mine, *other)


def head_kernel(final_ref, opposite_ref, value_ref, gate_ref, out_ref, *refs):
    *outs, result = refs
    n = len(outs)
    size = outs[0].shape[0]
    j = lax.axis_index("seq")
    value = matmul(final_ref[...], value_ref[...])
    row = lax.broadcasted_iota(jnp.int32, (size, size), 0)
    col = lax.broadcasted_iota(jnp.int32, (size, size), 1)
    reverse = jnp.where(row + col == size - 1, 1.0, 0.0).astype(BF16)
    flipped = [
        matmul(reverse, opposite_ref[(n - 1 - i) * size : (n - i) * size]).astype(BF16) for i in range(n)
    ]
    mirrored = matmul(jnp.concatenate(flipped, 0), gate_ref[...]).astype(BF16)
    gated = (value * jax.nn.sigmoid(mirrored.astype(F32))).astype(BF16)
    result[...] = matmul(gated, out_ref[...]).astype(BF16)
    for k, out in enumerate(outs):
        at = lax.rem(j + k, n)
        out[...] = result[pl.ds(pl.multiple_of(at * size, size), size)]


def local_spread(
    seq_in, conv_norm, conv_weight, ff_norm, up_weight, down_weight,
    head_norm, value_weight, gate_weight, out_weight,
):
    n = lax.axis_size("seq")
    blocks, taps, width, chans = conv_weight.shape
    hidden = up_weight.shape[2]
    half = hidden // 2
    rows = seq_in.shape[1]
    part = jax.ShapeDtypeStruct((rows // n, width), BF16)
    turned = jnp.swapaxes(conv_weight, 2, 3)
    mine0, other0 = pack(
        (up_weight, down_weight, turned, turned), (0, 0, 0, 1), (True, False, False, False),
        hidden + taps * chans, "pack0",
    )
    mine1, other1 = pack((up_weight, down_weight), (1, 1), (True, False), hidden, "pack1")
    to = lambda k: (lambda g, i, s, c: (g, (i + k) % n, s, c if s == 0 else 1 - c))
    parts = pl.pallas_call(
        split_kernel, out_shape=[part] * n, in_specs=[VMEM_SPEC], out_specs=[VMEM_SPEC] * n,
        compiler_params=PARAMS, name="split",
    )(seq_in[0])

    a0 = along(mine0)
    x0 = across(mine0)
    b0 = along(a0)
    xa0 = across(a0)
    ya0 = planes(a0)
    parts = after(parts, [b0])
    states = [moved(p, to(k)) for k, p in enumerate(parts)]
    xb0 = across(b0)
    yxa0 = planes(xa0)
    (own1,) = after([mine1], [b0])
    a1 = along(own1)
    (own1x,) = after([mine1], [xb0])
    x1 = across(own1x)
    b1 = along(a1)
    xa1 = across(a1)
    ya1 = planes(a1)
    xb1 = across(b1)
    yxa1 = planes(xa1)

    got0 = [a0, b0, x0, xa0, xb0, ya0, yxa0]
    got1 = [a1, b1, x1, xa1, xb1, ya1, yxa1]
    mine_0, other_0 = [mine0] + got0, [other0] + [other_core(v) for v in got0]
    mine_1, other_1 = [mine1] + got1, [other1] + [other_core(v) for v in got1]
    head = head_norm[None]
    state = conv(states, conv_norm, mine_0, other_0, 0, hidden, taps)
    (state,) = feed_forward(state, None, ff_norm, head, mine_0, other_0, 0, half, "state")
    state = conv([state], conv_norm, mine_0, other_0, 1, hidden + taps * chans // 2, taps)
    early, late = (0, 1, 2, 3, 6), (4, 5, 7)
    pick = lambda values, which: [values[k] for k in which]
    state, mixed = feed_forward(
        state, None, ff_norm, head, pick(mine_1, early), pick(other_1, early), 1, half, ""
    )
    (final,) = feed_forward(
        state, mixed, ff_norm, head, pick(mine_1, late), pick(other_1, late), 1, half, "head"
    )
    opposite = other_core(final)
    results = pl.pallas_call(
        head_kernel, out_shape=[part] * n, in_specs=[VMEM_SPEC] * 5, out_specs=[VMEM_SPEC] * n,
        scratch_shapes=[pltpu.VMEM((rows, width), BF16)], compiler_params=PARAMS, name="head",
    )(final, opposite, value_weight, gate_weight, out_weight)
    home = [moved(r, to(k)) for k, r in enumerate(results)]
    joined = pl.pallas_call(
        join_kernel, out_shape=jax.ShapeDtypeStruct((rows, width), BF16), in_specs=[VMEM_SPEC] * n,
        out_specs=VMEM_SPEC, compiler_params=PARAMS, name="join",
    )(*home)
    return joined[None]


def solution(mesh):
    in_specs = (
        P("strand", ("groups", "seq", "chan"), None),
        P(),
        P(None, None, None, ("seq", "chan")),
        P(),
        P(None, None, ("seq", "chan")),
        P(None, ("seq", "chan"), None),
        P(),
        P(),
        P(),
        P(),
    )
    out_specs = P("strand", ("groups", "seq", "chan"), None)

    def step(seq_in, conv_norm, conv_weight, *rest):
        size = mesh.shape
        shards = size["seq"] * size["chan"]
        tiled = conv_weight.shape[3] % (32 * shards) == 0
        blocks = conv_weight.shape[0]
        spread = tiled and blocks == 2 and [size[a] for a in AXES] == [2, 4, 2, 2]
        local = local_spread if spread else local_plain
        run = jax.shard_map(local, mesh=mesh, in_specs=in_specs, out_specs=out_specs, check_vma=False)
        return run(seq_in, conv_norm, conv_weight, *rest)

    return step
```

time: 140 us -> 103 us (0.74)
  Pallas kernels: 30.3 us -> 8.29 us
  starting transfers between devices: 67.3 us -> 49.1 us
  local copies, waits for them, and re-layouts: 1.5 us -> 3.12 us
  waiting for transfers between devices: 40.1 us -> 41.7 us
    ppermute x37, starting transfers between devices: 67.3 us -> 49.1 us  [moved(): return lax.ppermute(value, AXES, pairs)]
    pallas_call x3, Pallas kernels: 20.4 us -> 4.45 us  [feed_forward(): pl.pallas_call(functools.partial(ff_kernel, block, mixed is None, ends, h...]
    pallas_call x4, Pallas kernels: 8.07 us -> 2 us  [the longest x2 1.76 us: conv(): pl.pallas_call(functools.partial(conv_kernel, block, len(states), start),...]
    unnamed x19 -> x20, local copies, waits for them, and re-layouts: 1.5 us -> 3.12 us
    ppermute x37, waiting for transfers between devices: 40.1 us -> 41.7 us  [moved(): return lax.ppermute(value, AXES, pairs)]
  transfers between devices with their start and end apart: 37 -> 37, of which waited for: 12 -> 11; matrix products, arithmetic and copies ran while one was open for 0% -> 0% of each run, Pallas kernels for 10% -> 5%
where the time goes in v2:
time: 103 us; the launch traced here: 102 us
  starting transfers between devices  49.1 us (48%)
  waiting for transfers between devices  41.7 us (40%)
  Pallas kernels  8.29 us (8%)
  local copies, waits for them, and re-layouts  3.12 us (3%)
    ppermute x37, starting transfers between devices, moved(): return lax.ppermute(value, AXES, pairs)  49.1 us
    ppermute x37, waiting for transfers between devices, moved(): return lax.ppermute(value, AXES, pairs)  41.7 us
    pallas_call x3, Pallas kernels, feed_forward(): pl.pallas_call(functools.partial(ff_kernel, block, mixed is None, ends, h...  4.45 us
    unnamed x20, local copies, waits for them, and re-layouts  3.12 us
  transfers between devices with their start and end apart: 37, of which 11 were waited for; matrix products, arithmetic and copies ran while one was open for 0% of the time, Pallas kernels for 5%

profile of v2, /device:TPU:1, one launch (start us, length us, event | category | flops | bytes accessed | tf_op | source)
XLA Modules:
  0.0 102.5 jit_solution(11748387808003122177)
XLA Ops:
  0.0 1.0 %copy-done = bf16[2,512,256]{2,1,0:T(8,128)(2,1)S(1)} copy-done((bf16[2,512,256]{2,1,0:T(8,128)(2,1)S(1)}, bf16[2,512,256]{2,1,0:T(8,128)(2,1)}, u32[]{:S(2)}) %copy-start) | copy-done | bytes 524312
  1.0 1.0 %copy-done.1 = bf16[2,256,512]{2,1,0:T(8,128)(2,1)S(1)} copy-done((bf16[2,256,512]{2,1,0:T(8,128)(2,1)S(1)}, bf16[2,256,512]{2,1,0:T(8,128)(2,1)}, u32[]{:S(2)}) %copy-start.1) | copy-done | bytes 524312
  2.1 1.0 copy-done.2
  3.2 2.2 %collective-permute-start = (bf16[448,512]{1,0:T(8,128)(2,1)S(1)}, bf16[448,512]{1,0:T(8,128)(2,1)S(1)}, u32[]{:S(2)}, u32[]{:S(2)}) collective-permute-start(bf16[448,512]{1,0:T(8,128)(2,1)S(1)} %get-tuple-element.29.refs_4_.refs_0_.refs_1_), channel_id=1, source_target_pairs={{0,4},{1,5},{2,6},{3,7},{4,8},{5,9},{6,10},{7,11},{8,12},{9,13},{1... | collective-permute-start | bytes 1376264 | tf_op jit(solution)/shard_map/ppermute | solution.py:80
  5.4 1.2 %collective-permute-start.6 = (bf16[448,512]{1,0:T(8,128)(2,1)S(1)}, bf16[448,512]{1,0:T(8,128)(2,1)S(1)}, u32[]{:S(2)}, u32[]{:S(2)}) collective-permute-start(bf16[448,512]{1,0:T(8,128)(2,1)S(1)} %get-tuple-element.29.refs_4_.refs_0_.refs_1_), channel_id=1, source_target_pairs={{0,1},{1,0},{2,3},{3,2},{4,5},{5,4},{6,7},{7,6},{8,9},{9,8},{10,11... | collective-permute-start | bytes 1376264 | tf_op jit(solution)/shard_map/ppermute | solution.py:80
  6.6 11.1 %collective-permute-done.refs_5_.refs_1_.refs_2_ = bf16[448,512]{1,0:T(8,128)(2,1)S(1)} collective-permute-done((bf16[448,512]{1,0:T(8,128)(2,1)S(1)}, bf16[448,512]{1,0:T(8,128)(2,1)S(1)}, u32[]{:S(2)}, u32[]{:S(2)}) %collective-permute-start) | collective-permute-done | bytes 458784 | tf_op jit(solution)/shard_map/ppermute | solution.py:80
  17.7 1.0 collective-permute-start.7
  18.6 4.4 %collective-permute-start.9 = (bf16[448,512]{1,0:T(8,128)(2,1)S(1)}, bf16[448,512]{1,0:T(8,128)(2,1)S(1)}, u32[]{:S(2)}, u32[]{:S(2)}) collective-permute-start(bf16[448,512]{1,0:T(8,128)(2,1)S(1)} %collective-permute-done.refs_5_.refs_1_.refs_2_), channel_id=1, source_target_pairs={{0,16},{1,17},{2,18},{3,19},{4,20},{5,21},{6,22},{7,23},{8,24},{9,... | collective-permute-start | bytes 1376264 | tf_op jit(solution)/shard_map/ppermute | solution.py:80
  23.1 2.4 %collective-permute-start.11 = (bf16[448,512]{1,0:T(8,128)(2,1)S(1)}, bf16[448,512]{1,0:T(8,128)(2,1)S(1)}, u32[]{:S(2)}, u32[]{:S(2)}) collective-permute-start(bf16[448,512]{1,0:T(8,128)(2,1)S(1)} %collective-permute-done.refs_5_.refs_1_.refs_2_), channel_id=1, source_target_pairs={{0,2},{1,3},{2,0},{3,1},{4,6},{5,7},{6,4},{7,5},{8,10},{9,11},{10,... | collective-permute-start | bytes 1376264 | tf_op jit(solution)/shard_map/ppermute | solution.py:80
  25.6 4.7 %collective-permute-done.1.refs_6_.refs_2_.refs_3_ = bf16[448,512]{1,0:T(8,128)(2,1)S(1)} collective-permute-done((bf16[448,512]{1,0:T(8,128)(2,1)S(1)}, bf16[448,512]{1,0:T(8,128)(2,1)S(1)}, u32[]{:S(2)}, u32[]{:S(2)}) %collective-permute-start.1) | collective-permute-done | bytes 458784 | tf_op jit(solution)/shard_map/ppermute | solution.py:80
  30.3 2.6 %collective-permute-start.2 = (bf16[96,512]{1,0:T(8,128)(2,1)S(1)}, bf16[96,512]{1,0:T(8,128)(2,1)S(1)}, u32[]{:S(2)}, u32[]{:S(2)}) collective-permute-start(bf16[96,512]{1,0:T(8,128)(2,1)S(1)} %get-tuple-element.30), channel_id=1, source_target_pairs={{0,0},{1,1},{2,3},{3,2},{4,4},{5,5},{6,7},{7,6},{8,8},{9,9},{10,11... | collective-permute-start | bytes 294920 | tf_op jit(solution)/shard_map/ppermute | solution.py:80
  33.0 0.8 collective-permute-start.8
  33.9 3.9 %collective-permute-start.10 = (bf16[448,512]{1,0:T(8,128)(2,1)S(1)}, bf16[448,512]{1,0:T(8,128)(2,1)S(1)}, u32[]{:S(2)}, u32[]{:S(2)}) collective-permute-start(bf16[448,512]{1,0:T(8,128)(2,1)S(1)} %collective-permute-done.7.refs_8_.refs_4_.refs_5_), channel_id=1, source_target_pairs={{0,16},{1,17},{2,18},{3,19},{4,20},{5,21},{6,22},{7,23},{8,24},{9,... | collective-permute-start | bytes 1376264 | tf_op jit(solution)/shard_map/ppermute | solution.py:80
  37.7 1.1 %collective-permute-start.4 = (bf16[96,512]{1,0:T(8,128)(2,1)S(1)}, bf16[96,512]{1,0:T(8,128)(2,1)S(1)}, u32[]{:S(2)}, u32[]{:S(2)}) collective-permute-start(bf16[96,512]{1,0:T(8,128)(2,1)S(1)} %get-tuple-element.32), channel_id=1, source_target_pairs={{0,8},{1,9},{2,11},{3,10},{4,12},{5,13},{6,15},{7,14},{8,0},{9,1},... | collective-permute-start | bytes 294920 | tf_op jit(solution)/shard_map/ppermute | solution.py:80
  38.8 1.3 %collective-permute-done.3.refs_1_ = bf16[96,512]{1,0:T(8,128)(2,1)S(1)} collective-permute-done((bf16[96,512]{1,0:T(8,128)(2,1)S(1)}, bf16[96,512]{1,0:T(8,128)(2,1)S(1)}, u32[]{:S(2)}, u32[]{:S(2)}) %collective-permute-start.3) | collective-permute-done | bytes 98336 | tf_op jit(solution)/shard_map/ppermute | solution.py:80
  40.1 1.7 %collective-permute-start.5 = (bf16[96,512]{1,0:T(8,128)(2,1)S(1)}, bf16[96,512]{1,0:T(8,128)(2,1)S(1)}, u32[]{:S(2)}, u32[]{:S(2)}) collective-permute-start(bf16[96,512]{1,0:T(8,128)(2,1)S(1)} %get-tuple-element.33), channel_id=1, source_target_pairs={{0,12},{1,13},{2,15},{3,14},{4,0},{5,1},{6,3},{7,2},{8,4},{9,5},{1... | collective-permute-start | bytes 294920 | tf_op jit(solution)/shard_map/ppermute | solution.py:80
  41.9 5.0 %collective-permute-done.4.refs_2_ = bf16[96,512]{1,0:T(8,128)(2,1)S(1)} collective-permute-done((bf16[96,512]{1,0:T(8,128)(2,1)S(1)}, bf16[96,512]{1,0:T(8,128)(2,1)S(1)}, u32[]{:S(2)}, u32[]{:S(2)}) %collective-permute-start.4) | collective-permute-done | bytes 98336 | tf_op jit(solution)/shard_map/ppermute | solution.py:80
  46.8 0.9 collective-permute-start.12
  47.7 0.3 collective-permute-start.14
  48.3 1.4 %collective-permute-start.19 = (bf16[256,512]{1,0:T(8,128)(2,1)S(1)}, bf16[256,512]{1,0:T(8,128)(2,1)S(1)}, u32[]{:S(2)}, u32[]{:S(2)}) collective-permute-start(bf16[256,512]{1,0:T(8,128)(2,1)S(1)} %collective-permute-done.18.refs_1_), channel_id=1, source_target_pairs={{0,4},{1,5},{2,6},{3,7},{4,8},{5,9},{6,10},{7,11},{8,12},{9,13},{1... | collective-permute-start | bytes 786440 | tf_op jit(solution)/shard_map/ppermute | solution.py:80
  49.7 5.5 %collective-permute-start.21 = (bf16[256,512]{1,0:T(8,128)(2,1)S(1)}, bf16[256,512]{1,0:T(8,128)(2,1)S(1)}, u32[]{:S(2)}, u32[]{:S(2)}) collective-permute-start(bf16[256,512]{1,0:T(8,128)(2,1)S(1)} %collective-permute-done.18.refs_1_), channel_id=1, source_target_pairs={{0,16},{1,17},{2,18},{3,19},{4,20},{5,21},{6,22},{7,23},{8,24},{9,... | collective-permute-start | bytes 786440 | tf_op jit(solution)/shard_map/ppermute | solution.py:80
  55.2 1.8 %collective-permute-start.22 = (bf16[256,512]{1,0:T(8,128)(2,1)S(1)}, bf16[256,512]{1,0:T(8,128)(2,1)S(1)}, u32[]{:S(2)}, u32[]{:S(2)}) collective-permute-start(bf16[256,512]{1,0:T(8,128)(2,1)S(1)} %collective-permute-done.18.refs_1_), channel_id=1, source_target_pairs={{0,2},{1,3},{2,0},{3,1},{4,6},{5,7},{6,4},{7,5},{8,10},{9,11},{10,... | collective-permute-start | bytes 786440 | tf_op jit(solution)/shard_map/ppermute | solution.py:80
  57.0 1.1 %collective-permute-start.26 = (bf16[256,512]{1,0:T(8,128)(2,1)S(1)}, bf16[256,512]{1,0:T(8,128)(2,1)S(1)}, u32[]{:S(2)}, u32[]{:S(2)}) collective-permute-start(bf16[256,512]{1,0:T(8,128)(2,1)S(1)} %collective-permute-done.18.refs_1_), channel_id=1, source_target_pairs={{0,1},{1,0},{2,3},{3,2},{4,5},{5,4},{6,7},{7,6},{8,9},{9,8},{10,11... | collective-permute-start | bytes 786440 | tf_op jit(solution)/shard_map/ppermute | solution.py:80
  58.1 0.4 collective-permute-start.20
  58.5 0.6 collective-permute-start.15
  59.1 1.3 %collective-permute-done.21.refs_4_ = bf16[256,512]{1,0:T(8,128)(2,1)S(1)} collective-permute-done((bf16[256,512]{1,0:T(8,128)(2,1)S(1)}, bf16[256,512]{1,0:T(8,128)(2,1)S(1)}, u32[]{:S(2)}, u32[]{:S(2)}) %collective-permute-start.21) | collective-permute-done | bytes 262176 | tf_op jit(solution)/shard_map/ppermute | solution.py:80
  60.4 2.1 %collective-permute-start.17 = (bf16[448,512]{1,0:T(8,128)(2,1)S(1)}, bf16[448,512]{1,0:T(8,128)(2,1)S(1)}, u32[]{:S(2)}, u32[]{:S(2)}) collective-permute-start(bf16[448,512]{1,0:T(8,128)(2,1)S(1)} %collective-permute-done.10.refs_11_.refs_7_.refs_8_), channel_id=1, source_target_pairs={{0,2},{1,3},{2,0},{3,1},{4,6},{5,7},{6,4},{7,5},{8,10},{9,11},{10,... | collective-permute-start | bytes 1376264 | tf_op jit(solution)/shard_map/ppermute | solution.py:80
  62.5 2.4 %collective-permute-done.26.refs_1_ = bf16[256,512]{1,0:T(8,128)(2,1)S(1)} collective-permute-done((bf16[256,512]{1,0:T(8,128)(2,1)S(1)}, bf16[256,512]{1,0:T(8,128)(2,1)S(1)}, u32[]{:S(2)}, u32[]{:S(2)}) %collective-permute-start.26) | collective-permute-done | bytes 262176 | tf_op jit(solution)/shard_map/ppermute | solution.py:80
  64.9 1.1 %collective-permute-start.27 = (bf16[256,512]{1,0:T(8,128)(2,1)S(1)}, bf16[256,512]{1,0:T(8,128)(2,1)S(1)}, u32[]{:S(2)}, u32[]{:S(2)}) collective-permute-start(bf16[256,512]{1,0:T(8,128)(2,1)S(1)} %collective-permute-done.19.refs_2_), channel_id=1, source_target_pairs={{0,1},{1,0},{2,3},{3,2},{4,5},{5,4},{6,7},{7,6},{8,9},{9,8},{10,11... | collective-permute-start | bytes 786440 | tf_op jit(solution)/shard_map/ppermute | solution.py:80
  65.9 4.5 %collective-permute-done.20.refs_3_ = bf16[256,512]{1,0:T(8,128)(2,1)S(1)} collective-permute-done((bf16[256,512]{1,0:T(8,128)(2,1)S(1)}, bf16[256,512]{1,0:T(8,128)(2,1)S(1)}, u32[]{:S(2)}, u32[]{:S(2)}) %collective-permute-start.20) | collective-permute-done | bytes 262176 | tf_op jit(solution)/shard_map/ppermute | solution.py:80
  70.5 1.4 %collective-permute-start.25 = (bf16[256,512]{1,0:T(8,128)(2,1)S(1)}, bf16[256,512]{1,0:T(8,128)(2,1)S(1)}, u32[]{:S(2)}, u32[]{:S(2)}) collective-permute-start(bf16[256,512]{1,0:T(8,128)(2,1)S(1)} %collective-permute-done.21.refs_4_), channel_id=1, source_target_pairs={{0,2},{1,3},{2,0},{3,1},{4,6},{5,7},{6,4},{7,5},{8,10},{9,11},{10,... | collective-permute-start | bytes 786440 | tf_op jit(solution)/shard_map/ppermute | solution.py:80
  71.9 4.2 %collective-permute-done.27.refs_2_ = bf16[256,512]{1,0:T(8,128)(2,1)S(1)} collective-permute-done((bf16[256,512]{1,0:T(8,128)(2,1)S(1)}, bf16[256,512]{1,0:T(8,128)(2,1)S(1)}, u32[]{:S(2)}, u32[]{:S(2)}) %collective-permute-start.27) | collective-permute-done | bytes 262176 | tf_op jit(solution)/shard_map/ppermute | solution.py:80
  76.1 0.9 collective-permute-start.24
  77.0 2.2 %collective-permute-start.29 = (bf16[256,512]{1,0:T(8,128)(2,1)S(1)}, bf16[256,512]{1,0:T(8,128)(2,1)S(1)}, u32[]{:S(2)}, u32[]{:S(2)}) collective-permute-start(bf16[256,512]{1,0:T(8,128)(2,1)S(1)} %collective-permute-done.26.refs_1_), channel_id=1, source_target_pairs={{0,2},{1,3},{2,0},{3,1},{4,6},{5,7},{6,4},{7,5},{8,10},{9,11},{10,... | collective-permute-start | bytes 786440 | tf_op jit(solution)/shard_map/ppermute | solution.py:80
  79.2 0.5 collective-permute-start.31
  79.7 0.9 conv0.1.state_ref
  80.7 2.0 %ff0.1.refs_0_ = f32[384,512]{1,0:T(8,128)S(1)} custom-call(f32[2,512]{1,0:T(2,128)S(1)} %copy-done.7, f32[1,512]{1,0:T(1,128)S(1)} %bitcast.7, f32[384,512]{1,0:T(8,128)S(1)} %conv0.1.state_ref, bf16[448,512]{1,0:T(8,128)(2,1)S(1)} %get-tuple-element.29.refs_4_.refs_0_.refs_1_, bf16[448,512]{1,0:T(8,128)(2,1)S(1)} %collective-permute-done.refs_5_.refs_1_.refs_2_, ...), custom_call_target="tpu_custom_call" | custom-call | tf_op jit(solution)/shard_map/ff0/pallas_call | solution.py:242
  82.6 0.9 conv1.1.state_ref
  83.5 1.4 %ff1.2 = (f32[384,512]{1,0:T(8,128)S(1)}, bf16[384,512]{1,0:T(8,128)(2,1)S(1)}) custom-call(f32[2,512]{1,0:T(2,128)S(1)} %copy-done.7, f32[1,512]{1,0:T(1,128)S(1)} %bitcast.8, f32[384,512]{1,0:T(8,128)S(1)} %conv1.1.state_ref, bf16[256,512]{1,0:T(8,128)(2,1)S(1)} %get-tuple-element.37.refs_0_, bf16[256,512]{1,0:T(8,128)(2,1)S(1)} %collective-permute-done.18.refs_1_, ...), custom_call_target="tpu_custom_call" | custom-call | tf_op jit(solution)/shard_map/ff1/pallas_call | solution.py:242
  85.0 1.1 %ff1.3.final_ref = bf16[384,512]{1,0:T(8,128)(2,1)S(1)} custom-call(f32[2,512]{1,0:T(2,128)S(1)} %copy-done.7, f32[1,512]{1,0:T(1,128)S(1)} %bitcast.9, f32[384,512]{1,0:T(8,128)S(1)} %get-tuple-element.39.state_ref, bf16[384,512]{1,0:T(8,128)(2,1)S(1)} %get-tuple-element.40.refs_0_, bf16[256,512]{1,0:T(8,128)(2,1)S(1)} %collective-permute-done.26.refs_1_, ...), custom_call_target="tpu_custom_call" | custom-call | tf_op jit(solution)/shard_map/ff1/pallas_call | solution.py:242
  86.2 1.6 %collective-permute-done.32.opposite_ref = bf16[384,512]{1,0:T(8,128)(2,1)S(1)} collective-permute-done((bf16[384,512]{1,0:T(8,128)(2,1)S(1)}, bf16[384,512]{1,0:T(8,128)(2,1)S(1)}, u32[]{:S(2)}, u32[]{:S(2)}) %collective-permute-start.32) | collective-permute-done | bytes 393248 | tf_op jit(solution)/shard_map/ppermute | solution.py:80
  87.9 1.0 %head.1 = (bf16[96,512]{1,0:T(8,128)(2,1)S(1)}, bf16[96,512]{1,0:T(8,128)(2,1)S(1)}, bf16[96,512]{1,0:T(8,128)(2,1)S(1)}, bf16[96,512]{1,0:T(8,128)(2,1)S(1)}) custom-call(bf16[384,512]{1,0:T(8,128)(2,1)S(1)} %ff1.3.final_ref, bf16[384,512]{1,0:T(8,128)(2,1)S(1)} %collective-permute-done.32.opposite_ref, bf16[512,512]{1,0:T(8,128)(2,1)S(1)} %copy-done.3, ...), custom_call_target="tpu_custom_call" | custom-call | tf_op jit(solution)/shard_map/head/pallas_call | solution.py:331
  88.9 3.0 %collective-permute-start.33 = (bf16[96,512]{1,0:T(8,128)(2,1)S(1)}, bf16[96,512]{1,0:T(8,128)(2,1)S(1)}, u32[]{:S(2)}, u32[]{:S(2)}) collective-permute-start(bf16[96,512]{1,0:T(8,128)(2,1)S(1)} %get-tuple-element.41), channel_id=1, source_target_pairs={{0,0},{1,1},{2,3},{3,2},{4,4},{5,5},{6,7},{7,6},{8,8},{9,9},{10,11... | collective-permute-start | bytes 294920 | tf_op jit(solution)/shard_map/ppermute | solution.py:80
  92.0 0.9 collective-permute-start.35
  92.9 3.3 %collective-permute-start.36 = (bf16[96,512]{1,0:T(8,128)(2,1)S(1)}, bf16[96,512]{1,0:T(8,128)(2,1)S(1)}, u32[]{:S(2)}, u32[]{:S(2)}) collective-permute-start(bf16[96,512]{1,0:T(8,128)(2,1)S(1)} %get-tuple-element.44), channel_id=1, source_target_pairs={{0,12},{1,13},{2,15},{3,14},{4,0},{5,1},{6,3},{7,2},{8,4},{9,5},{1... | collective-permute-start | bytes 294920 | tf_op jit(solution)/shard_map/ppermute | solution.py:80
  96.1 3.1 %collective-permute-done.34.refs_1_ = bf16[96,512]{1,0:T(8,128)(2,1)S(1)} collective-permute-done((bf16[96,512]{1,0:T(8,128)(2,1)S(1)}, bf16[96,512]{1,0:T(8,128)(2,1)S(1)}, u32[]{:S(2)}, u32[]{:S(2)}) %collective-permute-start.34) | collective-permute-done | bytes 98336 | tf_op jit(solution)/shard_map/ppermute | solution.py:80
  99.2 2.5 %collective-permute-done.35.refs_2_ = bf16[96,512]{1,0:T(8,128)(2,1)S(1)} collective-permute-done((bf16[96,512]{1,0:T(8,128)(2,1)S(1)}, bf16[96,512]{1,0:T(8,128)(2,1)S(1)}, u32[]{:S(2)}, u32[]{:S(2)}) %collective-permute-start.35) | collective-permute-done | bytes 98336 | tf_op jit(solution)/shard_map/ppermute | solution.py:80
  101.7 0.8 join.1
  (56 shorter events, 0.9 us)
Async XLA Ops:
  0.0 1.0 %copy-start = (bf16[2,512,256]{2,1,0:T(8,128)(2,1)S(1)}, bf16[2,512,256]{2,1,0:T(8,128)(2,1)}, u32[]{:S(2)}) copy-start(bf16[2,512,256]{2,1,0:T(8,128)(2,1)} %refs_0_.3) | copy-start | bytes 1572868
  1.0 1.0 %copy-start.1 = (bf16[2,256,512]{2,1,0:T(8,128)(2,1)S(1)}, bf16[2,256,512]{2,1,0:T(8,128)(2,1)}, u32[]{:S(2)}) copy-start(bf16[2,256,512]{2,1,0:T(8,128)(2,1)} %refs_1_.3) | copy-start | bytes 1572868
  2.1 1.0 copy-start.2
  3.2 27.1 %copy-start.6 = (bf16[1,384,512]{2,1,0:T(8,128)(2,1)S(1)}, bf16[1,384,512]{2,1,0:T(8,128)(2,1)}, u32[]{:S(2)}) copy-start(bf16[1,384,512]{2,1,0:T(8,128)(2,1)} %param.10) | copy-start | bytes 1179652
  3.2 14.4 %collective-permute-start = (bf16[448,512]{1,0:T(8,128)(2,1)S(1)}, bf16[448,512]{1,0:T(8,128)(2,1)S(1)}, u32[]{:S(2)}, u32[]{:S(2)}) collective-permute-start(bf16[448,512]{1,0:T(8,128)(2,1)S(1)} %get-tuple-element.29.refs_4_.refs_0_.refs_1_), channel_id=1, source_target_pairs={{0,4},{1,5},{2,6},{3,7},{4,8},{5,9},{6,10},{7,11},{8,12},{9,13},{1... | collective-permute-start | bytes 1376264 | tf_op jit(solution)/shard_map/ppermute | solution.py:80
  5.4 20.1 %collective-permute-start.6 = (bf16[448,512]{1,0:T(8,128)(2,1)S(1)}, bf16[448,512]{1,0:T(8,128)(2,1)S(1)}, u32[]{:S(2)}, u32[]{:S(2)}) collective-permute-start(bf16[448,512]{1,0:T(8,128)(2,1)S(1)} %get-tuple-element.29.refs_4_.refs_0_.refs_1_), channel_id=1, source_target_pairs={{0,1},{1,0},{2,3},{3,2},{4,5},{5,4},{6,7},{7,6},{8,9},{9,8},{10,11... | collective-permute-start | bytes 1376264 | tf_op jit(solution)/shard_map/ppermute | solution.py:80
  17.7 12.6 %collective-permute-start.1 = (bf16[448,512]{1,0:T(8,128)(2,1)S(1)}, bf16[448,512]{1,0:T(8,128)(2,1)S(1)}, u32[]{:S(2)}, u32[]{:S(2)}) collective-permute-start(bf16[448,512]{1,0:T(8,128)(2,1)S(1)} %collective-permute-done.refs_5_.refs_1_.refs_2_), channel_id=1, source_target_pairs={{0,4},{1,5},{2,6},{3,7},{4,8},{5,9},{6,10},{7,11},{8,12},{9,13},{1... | collective-permute-start | bytes 1376264 | tf_op jit(solution)/shard_map/ppermute | solution.py:80
  17.7 12.6 %collective-permute-start.7 = (bf16[448,512]{1,0:T(8,128)(2,1)S(1)}, bf16[448,512]{1,0:T(8,128)(2,1)S(1)}, u32[]{:S(2)}, u32[]{:S(2)}) collective-permute-start(bf16[448,512]{1,0:T(8,128)(2,1)S(1)} %collective-permute-done.refs_5_.refs_1_.refs_2_), channel_id=1, source_target_pairs={{0,1},{1,0},{2,3},{3,2},{4,5},{5,4},{6,7},{7,6},{8,9},{9,8},{10,11... | collective-permute-start | bytes 1376264 | tf_op jit(solution)/shard_map/ppermute | solution.py:80
  18.6 14.3 %collective-permute-start.9 = (bf16[448,512]{1,0:T(8,128)(2,1)S(1)}, bf16[448,512]{1,0:T(8,128)(2,1)S(1)}, u32[]{:S(2)}, u32[]{:S(2)}) collective-permute-start(bf16[448,512]{1,0:T(8,128)(2,1)S(1)} %collective-permute-done.refs_5_.refs_1_.refs_2_), channel_id=1, source_target_pairs={{0,16},{1,17},{2,18},{3,19},{4,20},{5,21},{6,22},{7,23},{8,24},{9,... | collective-permute-start | bytes 1376264 | tf_op jit(solution)/shard_map/ppermute | solution.py:80
  23.1 10.0 %collective-permute-start.11 = (bf16[448,512]{1,0:T(8,128)(2,1)S(1)}, bf16[448,512]{1,0:T(8,128)(2,1)S(1)}, u32[]{:S(2)}, u32[]{:S(2)}) collective-permute-start(bf16[448,512]{1,0:T(8,128)(2,1)S(1)} %collective-permute-done.refs_5_.refs_1_.refs_2_), channel_id=1, source_target_pairs={{0,2},{1,3},{2,0},{3,1},{4,6},{5,7},{6,4},{7,5},{8,10},{9,11},{10,... | collective-permute-start | bytes 1376264 | tf_op jit(solution)/shard_map/ppermute | solution.py:80
  25.5 8.4 %collective-permute-start.13 = (bf16[448,512]{1,0:T(8,128)(2,1)S(1)}, bf16[448,512]{1,0:T(8,128)(2,1)S(1)}, u32[]{:S(2)}, u32[]{:S(2)}) collective-permute-start(bf16[448,512]{1,0:T(8,128)(2,1)S(1)} %collective-permute-done.6.refs_7_.refs_3_.refs_4_), channel_id=1, source_target_pairs={{0,2},{1,3},{2,0},{3,1},{4,6},{5,7},{6,4},{7,5},{8,10},{9,11},{10,... | collective-permute-start | bytes 1376264 | tf_op jit(solution)/shard_map/ppermute | solution.py:80
  30.3 17.8 %collective-permute-start.18 = (bf16[256,512]{1,0:T(8,128)(2,1)S(1)}, bf16[256,512]{1,0:T(8,128)(2,1)S(1)}, u32[]{:S(2)}, u32[]{:S(2)}) collective-permute-start(bf16[256,512]{1,0:T(8,128)(2,1)S(1)} %get-tuple-element.37.refs_0_), channel_id=1, source_target_pairs={{0,4},{1,5},{2,6},{3,7},{4,8},{5,9},{6,10},{7,11},{8,12},{9,13},{1... | collective-permute-start | bytes 786440 | tf_op jit(solution)/shard_map/ppermute | solution.py:80
  30.3 49.4 %copy-start.9 = (f32[2,512]{1,0:T(2,128)S(1)}, f32[2,512]{1,0:T(2,128)}, u32[]{:S(2)}) copy-start(f32[2,512]{1,0:T(2,128)} %gain_ref.7) | copy-start | bytes 12292
  30.3 7.4 %collective-permute-start.2 = (bf16[96,512]{1,0:T(8,128)(2,1)S(1)}, bf16[96,512]{1,0:T(8,128)(2,1)S(1)}, u32[]{:S(2)}, u32[]{:S(2)}) collective-permute-start(bf16[96,512]{1,0:T(8,128)(2,1)S(1)} %get-tuple-element.30), channel_id=1, source_target_pairs={{0,0},{1,1},{2,3},{3,2},{4,4},{5,5},{6,7},{7,6},{8,8},{9,9},{10,11... | collective-permute-start | bytes 294920 | tf_op jit(solution)/shard_map/ppermute | solution.py:80
  33.0 7.2 %collective-permute-start.3 = (bf16[96,512]{1,0:T(8,128)(2,1)S(1)}, bf16[96,512]{1,0:T(8,128)(2,1)S(1)}, u32[]{:S(2)}, u32[]{:S(2)}) collective-permute-start(bf16[96,512]{1,0:T(8,128)(2,1)S(1)} %get-tuple-element.31), channel_id=1, source_target_pairs={{0,4},{1,5},{2,7},{3,6},{4,8},{5,9},{6,11},{7,10},{8,12},{9,13},{1... | collective-permute-start | bytes 294920 | tf_op jit(solution)/shard_map/ppermute | solution.py:80
  33.0 15.2 %collective-permute-start.8 = (bf16[448,512]{1,0:T(8,128)(2,1)S(1)}, bf16[448,512]{1,0:T(8,128)(2,1)S(1)}, u32[]{:S(2)}, u32[]{:S(2)}) collective-permute-start(bf16[448,512]{1,0:T(8,128)(2,1)S(1)} %collective-permute-done.1.refs_6_.refs_2_.refs_3_), channel_id=1, source_target_pairs={{0,1},{1,0},{2,3},{3,2},{4,5},{5,4},{6,7},{7,6},{8,9},{9,8},{10,11... | collective-permute-start | bytes 1376264 | tf_op jit(solution)/shard_map/ppermute | solution.py:80
  33.9 15.8 %collective-permute-start.10 = (bf16[448,512]{1,0:T(8,128)(2,1)S(1)}, bf16[448,512]{1,0:T(8,128)(2,1)S(1)}, u32[]{:S(2)}, u32[]{:S(2)}) collective-permute-start(bf16[448,512]{1,0:T(8,128)(2,1)S(1)} %collective-permute-done.7.refs_8_.refs_4_.refs_5_), channel_id=1, source_target_pairs={{0,16},{1,17},{2,18},{3,19},{4,20},{5,21},{6,22},{7,23},{8,24},{9,... | collective-permute-start | bytes 1376264 | tf_op jit(solution)/shard_map/ppermute | solution.py:80
  37.7 9.1 %collective-permute-start.4 = (bf16[96,512]{1,0:T(8,128)(2,1)S(1)}, bf16[96,512]{1,0:T(8,128)(2,1)S(1)}, u32[]{:S(2)}, u32[]{:S(2)}) collective-permute-start(bf16[96,512]{1,0:T(8,128)(2,1)S(1)} %get-tuple-element.32), channel_id=1, source_target_pairs={{0,8},{1,9},{2,11},{3,10},{4,12},{5,13},{6,15},{7,14},{8,0},{9,1},... | collective-permute-start | bytes 294920 | tf_op jit(solution)/shard_map/ppermute | solution.py:80
  40.1 7.6 %collective-permute-start.5 = (bf16[96,512]{1,0:T(8,128)(2,1)S(1)}, bf16[96,512]{1,0:T(8,128)(2,1)S(1)}, u32[]{:S(2)}, u32[]{:S(2)}) collective-permute-start(bf16[96,512]{1,0:T(8,128)(2,1)S(1)} %get-tuple-element.33), channel_id=1, source_target_pairs={{0,12},{1,13},{2,15},{3,14},{4,0},{5,1},{6,3},{7,2},{8,4},{9,5},{1... | collective-permute-start | bytes 294920 | tf_op jit(solution)/shard_map/ppermute | solution.py:80
  46.8 8.4 %collective-permute-start.12 = (bf16[448,512]{1,0:T(8,128)(2,1)S(1)}, bf16[448,512]{1,0:T(8,128)(2,1)S(1)}, u32[]{:S(2)}, u32[]{:S(2)}) collective-permute-start(bf16[448,512]{1,0:T(8,128)(2,1)S(1)} %collective-permute-done.1.refs_6_.refs_2_.refs_3_), channel_id=1, source_target_pairs={{0,2},{1,3},{2,0},{3,1},{4,6},{5,7},{6,4},{7,5},{8,10},{9,11},{10,... | collective-permute-start | bytes 1376264 | tf_op jit(solution)/shard_map/ppermute | solution.py:80
  47.7 9.3 %collective-permute-start.14 = (bf16[448,512]{1,0:T(8,128)(2,1)S(1)}, bf16[448,512]{1,0:T(8,128)(2,1)S(1)}, u32[]{:S(2)}, u32[]{:S(2)}) collective-permute-start(bf16[448,512]{1,0:T(8,128)(2,1)S(1)} %collective-permute-done.7.refs_8_.refs_4_.refs_5_), channel_id=1, source_target_pairs={{0,2},{1,3},{2,0},{3,1},{4,6},{5,7},{6,4},{7,5},{8,10},{9,11},{10,... | collective-permute-start | bytes 1376264 | tf_op jit(solution)/shard_map/ppermute | solution.py:80
  48.1 10.0 %collective-permute-start.16 = (bf16[448,512]{1,0:T(8,128)(2,1)S(1)}, bf16[448,512]{1,0:T(8,128)(2,1)S(1)}, u32[]{:S(2)}, u32[]{:S(2)}) collective-permute-start(bf16[448,512]{1,0:T(8,128)(2,1)S(1)} %collective-permute-done.9.refs_10_.refs_6_.refs_7_), channel_id=1, source_target_pairs={{0,2},{1,3},{2,0},{3,1},{4,6},{5,7},{6,4},{7,5},{8,10},{9,11},{10,... | collective-permute-start | bytes 1376264 | tf_op jit(solution)/shard_map/ppermute | solution.py:80
  48.3 10.2 %collective-permute-start.19 = (bf16[256,512]{1,0:T(8,128)(2,1)S(1)}, bf16[256,512]{1,0:T(8,128)(2,1)S(1)}, u32[]{:S(2)}, u32[]{:S(2)}) collective-permute-start(bf16[256,512]{1,0:T(8,128)(2,1)S(1)} %collective-permute-done.18.refs_1_), channel_id=1, source_target_pairs={{0,4},{1,5},{2,6},{3,7},{4,8},{5,9},{6,10},{7,11},{8,12},{9,13},{1... | collective-permute-start | bytes 786440 | tf_op jit(solution)/shard_map/ppermute | solution.py:80
  49.7 10.7 %collective-permute-start.21 = (bf16[256,512]{1,0:T(8,128)(2,1)S(1)}, bf16[256,512]{1,0:T(8,128)(2,1)S(1)}, u32[]{:S(2)}, u32[]{:S(2)}) collective-permute-start(bf16[256,512]{1,0:T(8,128)(2,1)S(1)} %collective-permute-done.18.refs_1_), channel_id=1, source_target_pairs={{0,16},{1,17},{2,18},{3,19},{4,20},{5,21},{6,22},{7,23},{8,24},{9,... | collective-permute-start | bytes 786440 | tf_op jit(solution)/shard_map/ppermute | solution.py:80
  55.2 7.3 %collective-permute-start.22 = (bf16[256,512]{1,0:T(8,128)(2,1)S(1)}, bf16[256,512]{1,0:T(8,128)(2,1)S(1)}, u32[]{:S(2)}, u32[]{:S(2)}) collective-permute-start(bf16[256,512]{1,0:T(8,128)(2,1)S(1)} %collective-permute-done.18.refs_1_), channel_id=1, source_target_pairs={{0,2},{1,3},{2,0},{3,1},{4,6},{5,7},{6,4},{7,5},{8,10},{9,11},{10,... | collective-permute-start | bytes 786440 | tf_op jit(solution)/shard_map/ppermute | solution.py:80
  57.0 7.9 %collective-permute-start.26 = (bf16[256,512]{1,0:T(8,128)(2,1)S(1)}, bf16[256,512]{1,0:T(8,128)(2,1)S(1)}, u32[]{:S(2)}, u32[]{:S(2)}) collective-permute-start(bf16[256,512]{1,0:T(8,128)(2,1)S(1)} %collective-permute-done.18.refs_1_), channel_id=1, source_target_pairs={{0,1},{1,0},{2,3},{3,2},{4,5},{5,4},{6,7},{7,6},{8,9},{9,8},{10,11... | collective-permute-start | bytes 786440 | tf_op jit(solution)/shard_map/ppermute | solution.py:80
  58.1 12.4 %collective-permute-start.20 = (bf16[256,512]{1,0:T(8,128)(2,1)S(1)}, bf16[256,512]{1,0:T(8,128)(2,1)S(1)}, u32[]{:S(2)}, u32[]{:S(2)}) collective-permute-start(bf16[256,512]{1,0:T(8,128)(2,1)S(1)} %get-tuple-element.37.refs_0_), channel_id=1, source_target_pairs={{0,1},{1,0},{2,3},{3,2},{4,5},{5,4},{6,7},{7,6},{8,9},{9,8},{10,11... | collective-permute-start | bytes 786440 | tf_op jit(solution)/shard_map/ppermute | solution.py:80
  58.5 20.7 %collective-permute-start.15 = (bf16[448,512]{1,0:T(8,128)(2,1)S(1)}, bf16[448,512]{1,0:T(8,128)(2,1)S(1)}, u32[]{:S(2)}, u32[]{:S(2)}) collective-permute-start(bf16[448,512]{1,0:T(8,128)(2,1)S(1)} %collective-permute-done.8.refs_9_.refs_5_.refs_6_), channel_id=1, source_target_pairs={{0,2},{1,3},{2,0},{3,1},{4,6},{5,7},{6,4},{7,5},{8,10},{9,11},{10,... | collective-permute-start | bytes 1376264 | tf_op jit(solution)/shard_map/ppermute | solution.py:80
  60.4 18.9 %collective-permute-start.17 = (bf16[448,512]{1,0:T(8,128)(2,1)S(1)}, bf16[448,512]{1,0:T(8,128)(2,1)S(1)}, u32[]{:S(2)}, u32[]{:S(2)}) collective-permute-start(bf16[448,512]{1,0:T(8,128)(2,1)S(1)} %collective-permute-done.10.refs_11_.refs_7_.refs_8_), channel_id=1, source_target_pairs={{0,2},{1,3},{2,0},{3,1},{4,6},{5,7},{6,4},{7,5},{8,10},{9,11},{10,... | collective-permute-start | bytes 1376264 | tf_op jit(solution)/shard_map/ppermute | solution.py:80
  62.5 8.0 %collective-permute-start.23 = (bf16[256,512]{1,0:T(8,128)(2,1)S(1)}, bf16[256,512]{1,0:T(8,128)(2,1)S(1)}, u32[]{:S(2)}, u32[]{:S(2)}) collective-permute-start(bf16[256,512]{1,0:T(8,128)(2,1)S(1)} %collective-permute-done.19.refs_2_), channel_id=1, source_target_pairs={{0,2},{1,3},{2,0},{3,1},{4,6},{5,7},{6,4},{7,5},{8,10},{9,11},{10,... | collective-permute-start | bytes 786440 | tf_op jit(solution)/shard_map/ppermute | solution.py:80
  64.9 11.2 %collective-permute-start.27 = (bf16[256,512]{1,0:T(8,128)(2,1)S(1)}, bf16[256,512]{1,0:T(8,128)(2,1)S(1)}, u32[]{:S(2)}, u32[]{:S(2)}) collective-permute-start(bf16[256,512]{1,0:T(8,128)(2,1)S(1)} %collective-permute-done.19.refs_2_), channel_id=1, source_target_pairs={{0,1},{1,0},{2,3},{3,2},{4,5},{5,4},{6,7},{7,6},{8,9},{9,8},{10,11... | collective-permute-start | bytes 786440 | tf_op jit(solution)/shard_map/ppermute | solution.py:80
  70.5 6.5 %collective-permute-start.28 = (bf16[256,512]{1,0:T(8,128)(2,1)S(1)}, bf16[256,512]{1,0:T(8,128)(2,1)S(1)}, u32[]{:S(2)}, u32[]{:S(2)}) collective-permute-start(bf16[256,512]{1,0:T(8,128)(2,1)S(1)} %collective-permute-done.26.refs_1_), channel_id=1, source_target_pairs={{0,16},{1,17},{2,18},{3,19},{4,20},{5,21},{6,22},{7,23},{8,24},{9,... | collective-permute-start | bytes 786440 | tf_op jit(solution)/shard_map/ppermute | solution.py:80
  70.5 13.0 %collective-permute-start.25 = (bf16[256,512]{1,0:T(8,128)(2,1)S(1)}, bf16[256,512]{1,0:T(8,128)(2,1)S(1)}, u32[]{:S(2)}, u32[]{:S(2)}) collective-permute-start(bf16[256,512]{1,0:T(8,128)(2,1)S(1)} %collective-permute-done.21.refs_4_), channel_id=1, source_target_pairs={{0,2},{1,3},{2,0},{3,1},{4,6},{5,7},{6,4},{7,5},{8,10},{9,11},{10,... | collective-permute-start | bytes 786440 | tf_op jit(solution)/shard_map/ppermute | solution.py:80
  76.1 7.4 %collective-permute-start.24 = (bf16[256,512]{1,0:T(8,128)(2,1)S(1)}, bf16[256,512]{1,0:T(8,128)(2,1)S(1)}, u32[]{:S(2)}, u32[]{:S(2)}) collective-permute-start(bf16[256,512]{1,0:T(8,128)(2,1)S(1)} %collective-permute-done.20.refs_3_), channel_id=1, source_target_pairs={{0,2},{1,3},{2,0},{3,1},{4,6},{5,7},{6,4},{7,5},{8,10},{9,11},{10,... | collective-permute-start | bytes 786440 | tf_op jit(solution)/shard_map/ppermute | solution.py:80
  77.0 8.0 %collective-permute-start.29 = (bf16[256,512]{1,0:T(8,128)(2,1)S(1)}, bf16[256,512]{1,0:T(8,128)(2,1)S(1)}, u32[]{:S(2)}, u32[]{:S(2)}) collective-permute-start(bf16[256,512]{1,0:T(8,128)(2,1)S(1)} %collective-permute-done.26.refs_1_), channel_id=1, source_target_pairs={{0,2},{1,3},{2,0},{3,1},{4,6},{5,7},{6,4},{7,5},{8,10},{9,11},{10,... | collective-permute-start | bytes 786440 | tf_op jit(solution)/shard_map/ppermute | solution.py:80
  79.2 5.7 %collective-permute-start.30 = (bf16[256,512]{1,0:T(8,128)(2,1)S(1)}, bf16[256,512]{1,0:T(8,128)(2,1)S(1)}, u32[]{:S(2)}, u32[]{:S(2)}) collective-permute-start(bf16[256,512]{1,0:T(8,128)(2,1)S(1)} %collective-permute-done.27.refs_2_), channel_id=1, source_target_pairs={{0,2},{1,3},{2,0},{3,1},{4,6},{5,7},{6,4},{7,5},{8,10},{9,11},{10,... | collective-permute-start | bytes 786440 | tf_op jit(solution)/shard_map/ppermute | solution.py:80
  79.2 5.7 %collective-permute-start.31 = (bf16[256,512]{1,0:T(8,128)(2,1)S(1)}, bf16[256,512]{1,0:T(8,128)(2,1)S(1)}, u32[]{:S(2)}, u32[]{:S(2)}) collective-permute-start(bf16[256,512]{1,0:T(8,128)(2,1)S(1)} %collective-permute-done.28.refs_3_), channel_id=1, source_target_pairs={{0,2},{1,3},{2,0},{3,1},{4,6},{5,7},{6,4},{7,5},{8,10},{9,11},{10,... | collective-permute-start | bytes 786440 | tf_op jit(solution)/shard_map/ppermute | solution.py:80
  79.7 0.9 copy-start.7
  79.7 0.9 copy-start.8
  85.0 2.9 %copy-start.3 = (bf16[512,512]{1,0:T(8,128)(2,1)S(1)}, bf16[512,512]{1,0:T(8,128)(2,1)}, u32[]{:S(2)}) copy-start(bf16[512,512]{1,0:T(8,128)(2,1)} %value_ref.1) | copy-start | bytes 1572868
  85.0 2.9 %copy-start.4 = (bf16[512,512]{1,0:T(8,128)(2,1)S(1)}, bf16[512,512]{1,0:T(8,128)(2,1)}, u32[]{:S(2)}) copy-start(bf16[512,512]{1,0:T(8,128)(2,1)} %gate_ref.1) | copy-start | bytes 1572868
  85.0 2.9 %copy-start.5 = (bf16[512,512]{1,0:T(8,128)(2,1)S(1)}, bf16[512,512]{1,0:T(8,128)(2,1)}, u32[]{:S(2)}) copy-start(bf16[512,512]{1,0:T(8,128)(2,1)} %out_ref.1) | copy-start | bytes 1572868
  86.1 1.8 %collective-permute-start.32 = (bf16[384,512]{1,0:T(8,128)(2,1)S(1)}, bf16[384,512]{1,0:T(8,128)(2,1)S(1)}, u32[]{:S(2)}, u32[]{:S(2)}) collective-permute-start(bf16[384,512]{1,0:T(8,128)(2,1)S(1)} %ff1.3.final_ref), channel_id=1, source_target_pairs={{0,2},{1,3},{2,0},{3,1},{4,6},{5,7},{6,4},{7,5},{8,10},{9,11},{10,... | collective-permute-start | bytes 1179656 | tf_op jit(solution)/shard_map/ppermute | solution.py:80
  88.9 7.2 %collective-permute-start.33 = (bf16[96,512]{1,0:T(8,128)(2,1)S(1)}, bf16[96,512]{1,0:T(8,128)(2,1)S(1)}, u32[]{:S(2)}, u32[]{:S(2)}) collective-permute-start(bf16[96,512]{1,0:T(8,128)(2,1)S(1)} %get-tuple-element.41), channel_id=1, source_target_pairs={{0,0},{1,1},{2,3},{3,2},{4,4},{5,5},{6,7},{7,6},{8,8},{9,9},{10,11... | collective-permute-start | bytes 294920 | tf_op jit(solution)/shard_map/ppermute | solution.py:80
  91.9 7.3 %collective-permute-start.34 = (bf16[96,512]{1,0:T(8,128)(2,1)S(1)}, bf16[96,512]{1,0:T(8,128)(2,1)S(1)}, u32[]{:S(2)}, u32[]{:S(2)}) collective-permute-start(bf16[96,512]{1,0:T(8,128)(2,1)S(1)} %get-tuple-element.42), channel_id=1, source_target_pairs={{0,4},{1,5},{2,7},{3,6},{4,8},{5,9},{6,11},{7,10},{8,12},{9,13},{1... | collective-permute-start | bytes 294920 | tf_op jit(solution)/shard_map/ppermute | solution.py:80
  92.0 9.7 %collective-permute-start.35 = (bf16[96,512]{1,0:T(8,128)(2,1)S(1)}, bf16[96,512]{1,0:T(8,128)(2,1)S(1)}, u32[]{:S(2)}, u32[]{:S(2)}) collective-permute-start(bf16[96,512]{1,0:T(8,128)(2,1)S(1)} %get-tuple-element.43), channel_id=1, source_target_pairs={{0,8},{1,9},{2,11},{3,10},{4,12},{5,13},{6,15},{7,14},{8,0},{9,1},... | collective-permute-start | bytes 294920 | tf_op jit(solution)/shard_map/ppermute | solution.py:80
  92.9 8.9 %collective-permute-start.36 = (bf16[96,512]{1,0:T(8,128)(2,1)S(1)}, bf16[96,512]{1,0:T(8,128)(2,1)S(1)}, u32[]{:S(2)}, u32[]{:S(2)}) collective-permute-start(bf16[96,512]{1,0:T(8,128)(2,1)S(1)} %get-tuple-element.44), channel_id=1, source_target_pairs={{0,12},{1,13},{2,15},{3,14},{4,0},{5,1},{6,3},{7,2},{8,4},{9,5},{1... | collective-permute-start | bytes 294920 | tf_op jit(solution)/shard_map/ppermute | solution.py:80

commit v3 on v2

--- a/solution.py
+++ b/solution.py
@@ -207,7 +207,7 @@
     )(gain, *states, *mine, *other)
 
 
-def ff_kernel(block, first, ends, half, gain_ref, head_ref, state_ref, *refs):
+def ff_kernel(block, first, ends, start, half, gain_ref, head_ref, state_ref, *refs):
     if not first:
         mixed_ref, refs = refs[0], refs[1:]
     outs = 1 if ends else 2
@@ -221,9 +221,9 @@
         mixed = mixed_ref[...]
     down = []
     for r in range(count):
-        up = jnp.concatenate([mine[r][:half], other[r][:half]], 0)
+        up = jnp.concatenate([v[r][start : start + half] for v in (mine, other)], 0)
         hid[:, 2 * r * half : 2 * (r + 1) * half] = jax.nn.gelu(matmul_nt(mixed, up)).astype(BF16)
-        down += [mine[r][half : 2 * half], other[r][half : 2 * half]]
+        down += [v[r][start + half : start + 2 * half] for v in (mine, other)]
     state = state + matmul(hid[...], jnp.concatenate(down, 0))
     if ends == "head":
         state = normalize(state, head_ref[...]).astype(BF16)
@@ -232,7 +232,7 @@
         refs[2 * count + 1][...] = mixed
 
 
-def feed_forward(state, mixed, gain, head, mine, other, block, half, ends):
+def feed_forward(state, mixed, gain, head, mine, other, block, start, half, ends):
     rows, width = state.shape
     arrays = len(mine) + len(other)
     out = [jax.ShapeDtypeStruct((rows, width), BF16 if ends == "head" else F32)]
@@ -240,7 +240,7 @@
         out.append(jax.ShapeDtypeStruct((rows, width), BF16))
     given = [state] if mixed is None else [state, mixed]
     return pl.pallas_call(
-        functools.partial(ff_kernel, block, mixed is None, ends, half),
+        functools.partial(ff_kernel, block, mixed is None, ends, start, half),
         out_shape=out,
         in_specs=[VMEM_SPEC] * (2 + len(given) + arrays),
         out_specs=[VMEM_SPEC] * len(out),
@@ -281,52 +281,33 @@
     rows = seq_in.shape[1]
     part = jax.ShapeDtypeStruct((rows // n, width), BF16)
     turned = jnp.swapaxes(conv_weight, 2, 3)
-    mine0, other0 = pack(
-        (up_weight, down_weight, turned, turned), (0, 0, 0, 1), (True, False, False, False),
-        hidden + taps * chans, "pack0",
+    cut = hidden + taps * chans
+    own, own_other = pack(
+        (up_weight, down_weight, turned, turned, up_weight, down_weight),
+        (0, 0, 0, 1, 1, 1), (True, False, False, False, True, False), cut + hidden, "pack",
     )
-    mine1, other1 = pack((up_weight, down_weight), (1, 1), (True, False), hidden, "pack1")
     to = lambda k: (lambda g, i, s, c: (g, (i + k) % n, s, c if s == 0 else 1 - c))
     parts = pl.pallas_call(
         split_kernel, out_shape=[part] * n, in_specs=[VMEM_SPEC], out_specs=[VMEM_SPEC] * n,
         compiler_params=PARAMS, name="split",
     )(seq_in[0])
 
-    a0 = along(mine0)
-    x0 = across(mine0)
-    b0 = along(a0)
-    xa0 = across(a0)
-    ya0 = planes(a0)
-    parts = after(parts, [b0])
+    a = along(own)
+    x = across(own)
+    b = along(a)
+    xa = across(a)
+    ya = planes(a)
+    xb = across(b)
+    yxa = planes(xa)
+    parts = after(parts, [b])
     states = [moved(p, to(k)) for k, p in enumerate(parts)]
-    xb0 = across(b0)
-    yxa0 = planes(xa0)
-    (own1,) = after([mine1], [b0])
-    a1 = along(own1)
-    (own1x,) = after([mine1], [xb0])
-    x1 = across(own1x)
-    b1 = along(a1)
-    xa1 = across(a1)
-    ya1 = planes(a1)
-    xb1 = across(b1)
-    yxa1 = planes(xa1)
-
-    got0 = [a0, b0, x0, xa0, xb0, ya0, yxa0]
-    got1 = [a1, b1, x1, xa1, xb1, ya1, yxa1]
-    mine_0, other_0 = [mine0] + got0, [other0] + [other_core(v) for v in got0]
-    mine_1, other_1 = [mine1] + got1, [other1] + [other_core(v) for v in got1]
+    mine = [own, a, b, x, xa, xb, ya, yxa]
+    other = [own_other] + [other_core(v) for v in mine[1:]]
     head = head_norm[None]
-    state = conv(states, conv_norm, mine_0, other_0, 0, hidden, taps)
-    (state,) = feed_forward(state, None, ff_norm, head, mine_0, other_0, 0, half, "state")
-    state = conv([state], conv_norm, mine_0, other_0, 1, hidden + taps * chans // 2, taps)
-    early, late = (0, 1, 2, 3, 6), (4, 5, 7)
-    pick = lambda values, which: [values[k] for k in which]
-    state, mixed = feed_forward(
-        state, None, ff_norm, head, pick(mine_1, early), pick(other_1, early), 1, half, ""
-    )
-    (final,) = feed_forward(
-        state, mixed, ff_norm, head, pick(mine_1, late), pick(other_1, late), 1, half, "head"
-    )
+    state = conv(states, conv_norm, mine, other, 0, hidden, taps)
+    (state,) = feed_forward(state, None, ff_norm, head, mine, other, 0, 0, half, "state")
+    state = conv([state], conv_norm, mine, other, 1, hidden + taps * chans // 2, taps)
+    (final,) = feed_forward(state, None, ff_norm, head, mine, other, 1, cut, half, "head")
     opposite = other_core(final)
     results = pl.pallas_call(
         head_kernel, out_shape=[part] * n, in_specs=[VMEM_SPEC] * 5, out_specs=[VMEM_SPEC] * n,

time: 103 us -> 93.6 us (0.909)
  starting transfers between devices: 49.1 us -> 28.2 us
  waiting for transfers between devices: 41.7 us -> 53.6 us
    ppermute x37 -> x23, starting transfers between devices: 49.1 us -> 28.2 us  [moved(): return lax.ppermute(value, AXES, pairs)]
    ppermute x37 -> x23, waiting for transfers between devices: 41.7 us -> 53.6 us  [moved(): return lax.ppermute(value, AXES, pairs)]
    pallas_call x3 -> x2, Pallas kernels: 4.45 us -> 4.13 us  [feed_forward(): pl.pallas_call(functools.partial(ff_kernel, block, mixed is None, ends, s...]
  transfers between devices with their start and end apart: 37 -> 23, of which waited for: 11 -> 13; matrix products, arithmetic and copies ran while one was open for 0% -> 0% of each run, Pallas kernels for 5% -> 0%
where the time goes in v3:
time: 93.6 us; the launch traced here: 93.1 us
  waiting for transfers between devices  53.6 us (57%)
  starting transfers between devices  28.2 us (30%)
  Pallas kernels  7.97 us (9%)
  local copies, waits for them, and re-layouts  3.11 us (3%)
    ppermute x23, waiting for transfers between devices, moved(): return lax.ppermute(value, AXES, pairs)  53.6 us
    ppermute x23, starting transfers between devices, moved(): return lax.ppermute(value, AXES, pairs)  28.2 us
    pallas_call x2, Pallas kernels, feed_forward(): pl.pallas_call(functools.partial(ff_kernel, block, mixed is None, ends, s...  4.13 us
    unnamed x20, local copies, waits for them, and re-layouts  3.11 us
  transfers between devices with their start and end apart: 23, of which 13 were waited for; matrix products, arithmetic and copies ran while one was open for 0% of the time, Pallas kernels for 0%

profile of v3, /device:TPU:1, one launch (start us, length us, event | category | flops | bytes accessed | tf_op | source)
XLA Modules:
  0.0 93.1 jit_solution(7943483279418033017)
XLA Ops:
  0.0 1.0 %copy-done = bf16[2,512,256]{2,1,0:T(8,128)(2,1)S(1)} copy-done((bf16[2,512,256]{2,1,0:T(8,128)(2,1)S(1)}, bf16[2,512,256]{2,1,0:T(8,128)(2,1)}, u32[]{:S(2)}) %copy-start) | copy-done | bytes 524312
  1.0 1.0 %copy-done.1 = bf16[2,256,512]{2,1,0:T(8,128)(2,1)S(1)} copy-done((bf16[2,256,512]{2,1,0:T(8,128)(2,1)S(1)}, bf16[2,256,512]{2,1,0:T(8,128)(2,1)}, u32[]{:S(2)}) %copy-start.1) | copy-done | bytes 524312
  2.1 1.0 %copy-done.2 = bf16[2,3,512,64]{2,3,1,0:T(8,128)(2,1)S(1)} copy-done((bf16[2,3,512,64]{2,3,1,0:T(8,128)(2,1)S(1)}, bf16[2,3,512,64]{2,3,1,0:T(8,128)(2,1)}, u32[]{:S(2)}) %copy-start.2) | copy-done | bytes 393240
  3.1 0.2 pack.1
  3.3 2.2 %collective-permute-start = (bf16[704,512]{1,0:T(8,128)(2,1)S(1)}, bf16[704,512]{1,0:T(8,128)(2,1)S(1)}, u32[]{:S(2)}, u32[]{:S(2)}) collective-permute-start(bf16[704,512]{1,0:T(8,128)(2,1)S(1)} %get-tuple-element.23.refs_4_.refs_0_.refs_1_), channel_id=1, source_target_pairs={{0,4},{1,5},{2,6},{3,7},{4,8},{5,9},{6,10},{7,11},{8,12},{9,13},{1... | collective-permute-start | bytes 2162696 | tf_op jit(solution)/shard_map/ppermute | solution.py:80
  5.5 1.2 %collective-permute-start.6 = (bf16[704,512]{1,0:T(8,128)(2,1)S(1)}, bf16[704,512]{1,0:T(8,128)(2,1)S(1)}, u32[]{:S(2)}, u32[]{:S(2)}) collective-permute-start(bf16[704,512]{1,0:T(8,128)(2,1)S(1)} %get-tuple-element.23.refs_4_.refs_0_.refs_1_), channel_id=1, source_target_pairs={{0,1},{1,0},{2,3},{3,2},{4,5},{5,4},{6,7},{7,6},{8,9},{9,8},{10,11... | collective-permute-start | bytes 2162696 | tf_op jit(solution)/shard_map/ppermute | solution.py:80
  6.7 16.7 %collective-permute-done.refs_5_.refs_1_.refs_2_ = bf16[704,512]{1,0:T(8,128)(2,1)S(1)} collective-permute-done((bf16[704,512]{1,0:T(8,128)(2,1)S(1)}, bf16[704,512]{1,0:T(8,128)(2,1)S(1)}, u32[]{:S(2)}, u32[]{:S(2)}) %collective-permute-start) | collective-permute-done | bytes 720928 | tf_op jit(solution)/shard_map/ppermute | solution.py:80
  23.4 1.0 %collective-permute-start.7 = (bf16[704,512]{1,0:T(8,128)(2,1)S(1)}, bf16[704,512]{1,0:T(8,128)(2,1)S(1)}, u32[]{:S(2)}, u32[]{:S(2)}) collective-permute-start(bf16[704,512]{1,0:T(8,128)(2,1)S(1)} %collective-permute-done.refs_5_.refs_1_.refs_2_), channel_id=1, source_target_pairs={{0,1},{1,0},{2,3},{3,2},{4,5},{5,4},{6,7},{7,6},{8,9},{9,8},{10,11... | collective-permute-start | bytes 2162696 | tf_op jit(solution)/shard_map/ppermute | solution.py:80
  24.3 0.0 collective-permute-start.1
  24.3 0.0 collective-permute-done.6.refs_7_.refs_3_.refs_4_
  24.3 1.8 %collective-permute-start.13 = (bf16[704,512]{1,0:T(8,128)(2,1)S(1)}, bf16[704,512]{1,0:T(8,128)(2,1)S(1)}, u32[]{:S(2)}, u32[]{:S(2)}) collective-permute-start(bf16[704,512]{1,0:T(8,128)(2,1)S(1)} %collective-permute-done.6.refs_7_.refs_3_.refs_4_), channel_id=1, source_target_pairs={{0,2},{1,3},{2,0},{3,1},{4,6},{5,7},{6,4},{7,5},{8,10},{9,11},{10,... | collective-permute-start | bytes 2162696 | tf_op jit(solution)/shard_map/ppermute | solution.py:80
  26.1 0.1 collective-permute-start.11
  26.2 4.7 %collective-permute-start.9 = (bf16[704,512]{1,0:T(8,128)(2,1)S(1)}, bf16[704,512]{1,0:T(8,128)(2,1)S(1)}, u32[]{:S(2)}, u32[]{:S(2)}) collective-permute-start(bf16[704,512]{1,0:T(8,128)(2,1)S(1)} %collective-permute-done.refs_5_.refs_1_.refs_2_), channel_id=1, source_target_pairs={{0,16},{1,17},{2,18},{3,19},{4,20},{5,21},{6,22},{7,23},{8,24},{9,... | collective-permute-start | bytes 2162696 | tf_op jit(solution)/shard_map/ppermute | solution.py:80
  30.9 8.9 %collective-permute-done.7.refs_8_.refs_4_.refs_5_ = bf16[704,512]{1,0:T(8,128)(2,1)S(1)} collective-permute-done((bf16[704,512]{1,0:T(8,128)(2,1)S(1)}, bf16[704,512]{1,0:T(8,128)(2,1)S(1)}, u32[]{:S(2)}, u32[]{:S(2)}) %collective-permute-start.7) | collective-permute-done | bytes 720928 | tf_op jit(solution)/shard_map/ppermute | solution.py:80
  39.8 1.1 %collective-permute-start.10 = (bf16[704,512]{1,0:T(8,128)(2,1)S(1)}, bf16[704,512]{1,0:T(8,128)(2,1)S(1)}, u32[]{:S(2)}, u32[]{:S(2)}) collective-permute-start(bf16[704,512]{1,0:T(8,128)(2,1)S(1)} %collective-permute-done.7.refs_8_.refs_4_.refs_5_), channel_id=1, source_target_pairs={{0,16},{1,17},{2,18},{3,19},{4,20},{5,21},{6,22},{7,23},{8,24},{9,... | collective-permute-start | bytes 2162696 | tf_op jit(solution)/shard_map/ppermute | solution.py:80
  40.9 1.1 %collective-permute-done.1.refs_6_.refs_2_.refs_3_ = bf16[704,512]{1,0:T(8,128)(2,1)S(1)} collective-permute-done((bf16[704,512]{1,0:T(8,128)(2,1)S(1)}, bf16[704,512]{1,0:T(8,128)(2,1)S(1)}, u32[]{:S(2)}, u32[]{:S(2)}) %collective-permute-start.1) | collective-permute-done | bytes 720928 | tf_op jit(solution)/shard_map/ppermute | solution.py:80
  42.0 0.7 collective-permute-start.8
  42.8 0.0 copy-start.8
  42.8 2.6 %collective-permute-start.2 = (bf16[96,512]{1,0:T(8,128)(2,1)S(1)}, bf16[96,512]{1,0:T(8,128)(2,1)S(1)}, u32[]{:S(2)}, u32[]{:S(2)}) collective-permute-start(bf16[96,512]{1,0:T(8,128)(2,1)S(1)} %get-tuple-element.24), channel_id=1, source_target_pairs={{0,0},{1,1},{2,3},{3,2},{4,4},{5,5},{6,7},{7,6},{8,8},{9,9},{10,11... | collective-permute-start | bytes 294920 | tf_op jit(solution)/shard_map/ppermute | solution.py:80
  45.5 0.1 collective-permute-start.3
  45.5 1.4 %collective-permute-done.9.refs_10_.refs_6_.refs_7_ = bf16[704,512]{1,0:T(8,128)(2,1)S(1)} collective-permute-done((bf16[704,512]{1,0:T(8,128)(2,1)S(1)}, bf16[704,512]{1,0:T(8,128)(2,1)S(1)}, u32[]{:S(2)}, u32[]{:S(2)}) %collective-permute-start.9) | collective-permute-done | bytes 720928 | tf_op jit(solution)/shard_map/ppermute | solution.py:80
  46.9 1.4 %collective-permute-start.4 = (bf16[96,512]{1,0:T(8,128)(2,1)S(1)}, bf16[96,512]{1,0:T(8,128)(2,1)S(1)}, u32[]{:S(2)}, u32[]{:S(2)}) collective-permute-start(bf16[96,512]{1,0:T(8,128)(2,1)S(1)} %get-tuple-element.26), channel_id=1, source_target_pairs={{0,8},{1,9},{2,11},{3,10},{4,12},{5,13},{6,15},{7,14},{8,0},{9,1},... | collective-permute-start | bytes 294920 | tf_op jit(solution)/shard_map/ppermute | solution.py:80
  48.3 12.9 %collective-permute-done.2.refs_0_ = bf16[96,512]{1,0:T(8,128)(2,1)S(1)} collective-permute-done((bf16[96,512]{1,0:T(8,128)(2,1)S(1)}, bf16[96,512]{1,0:T(8,128)(2,1)S(1)}, u32[]{:S(2)}, u32[]{:S(2)}) %collective-permute-start.2) | collective-permute-done | bytes 98336 | tf_op jit(solution)/shard_map/ppermute | solution.py:80
  61.2 2.5 %collective-permute-start.5 = (bf16[96,512]{1,0:T(8,128)(2,1)S(1)}, bf16[96,512]{1,0:T(8,128)(2,1)S(1)}, u32[]{:S(2)}, u32[]{:S(2)}) collective-permute-start(bf16[96,512]{1,0:T(8,128)(2,1)S(1)} %get-tuple-element.27), channel_id=1, source_target_pairs={{0,12},{1,13},{2,15},{3,14},{4,0},{5,1},{6,3},{7,2},{8,4},{9,5},{1... | collective-permute-start | bytes 294920 | tf_op jit(solution)/shard_map/ppermute | solution.py:80
  63.7 0.5 collective-permute-start.12
  64.2 1.4 %collective-permute-done.5.refs_3_ = bf16[96,512]{1,0:T(8,128)(2,1)S(1)} collective-permute-done((bf16[96,512]{1,0:T(8,128)(2,1)S(1)}, bf16[96,512]{1,0:T(8,128)(2,1)S(1)}, u32[]{:S(2)}, u32[]{:S(2)}) %collective-permute-start.5) | collective-permute-done | bytes 98336 | tf_op jit(solution)/shard_map/ppermute | solution.py:80
  65.6 0.5 collective-permute-start.17
  66.1 0.1 collective-permute-start.15
  66.1 1.8 %collective-permute-done.16.refs_18_.refs_14_.refs_15_ = bf16[704,512]{1,0:T(8,128)(2,1)S(1)} collective-permute-done((bf16[704,512]{1,0:T(8,128)(2,1)S(1)}, bf16[704,512]{1,0:T(8,128)(2,1)S(1)}, u32[]{:S(2)}, u32[]{:S(2)}) %collective-permute-start.16) | collective-permute-done | bytes 720928 | tf_op jit(solution)/shard_map/ppermute | solution.py:80
  67.9 1.0 %collective-permute-done.17.refs_19_.refs_15_.refs_16_ = bf16[704,512]{1,0:T(8,128)(2,1)S(1)} collective-permute-done((bf16[704,512]{1,0:T(8,128)(2,1)S(1)}, bf16[704,512]{1,0:T(8,128)(2,1)S(1)}, u32[]{:S(2)}, u32[]{:S(2)}) %collective-permute-start.17) | collective-permute-done | bytes 720928 | tf_op jit(solution)/shard_map/ppermute | solution.py:80
  69.0 1.0 %collective-permute-done.15.refs_17_.refs_13_.refs_14_ = bf16[704,512]{1,0:T(8,128)(2,1)S(1)} collective-permute-done((bf16[704,512]{1,0:T(8,128)(2,1)S(1)}, bf16[704,512]{1,0:T(8,128)(2,1)S(1)}, u32[]{:S(2)}, u32[]{:S(2)}) %collective-permute-start.15) | collective-permute-done | bytes 720928 | tf_op jit(solution)/shard_map/ppermute | solution.py:80
  70.0 0.9 conv0.1.state_ref
  70.9 2.0 %ff0.1.refs_0_ = f32[384,512]{1,0:T(8,128)S(1)} custom-call(f32[2,512]{1,0:T(2,128)S(1)} %copy-done.7, f32[1,512]{1,0:T(1,128)S(1)} %bitcast.7, f32[384,512]{1,0:T(8,128)S(1)} %conv0.1.state_ref, bf16[704,512]{1,0:T(8,128)(2,1)S(1)} %get-tuple-element.23.refs_4_.refs_0_.refs_1_, bf16[704,512]{1,0:T(8,128)(2,1)S(1)} %collective-permute-done.refs_5_.refs_1_.refs_2_, ...), custom_call_target="tpu_custom_call" | custom-call | tf_op jit(solution)/shard_map/ff0/pallas_call | solution.py:242
  73.0 0.9 conv1.1.state_ref
  73.8 0.0 copy-start.3
  73.9 0.0 copy-start.4
  73.9 0.0 copy-start.5
  73.9 2.1 %ff1.1.final_ref = bf16[384,512]{1,0:T(8,128)(2,1)S(1)} custom-call(f32[2,512]{1,0:T(2,128)S(1)} %copy-done.7, f32[1,512]{1,0:T(1,128)S(1)} %bitcast.8, f32[384,512]{1,0:T(8,128)S(1)} %conv1.1.state_ref, bf16[704,512]{1,0:T(8,128)(2,1)S(1)} %get-tuple-element.23.refs_4_.refs_0_.refs_1_, bf16[704,512]{1,0:T(8,128)(2,1)S(1)} %collective-permute-done.refs_5_.refs_1_.refs_2_, ...), custom_call_target="tpu_custom_call" | custom-call | tf_op jit(solution)/shard_map/ff1/pallas_call | solution.py:242
  76.0 0.2 collective-permute-start.18
  76.2 1.6 %collective-permute-done.18.opposite_ref = bf16[384,512]{1,0:T(8,128)(2,1)S(1)} collective-permute-done((bf16[384,512]{1,0:T(8,128)(2,1)S(1)}, bf16[384,512]{1,0:T(8,128)(2,1)S(1)}, u32[]{:S(2)}, u32[]{:S(2)}) %collective-permute-start.18) | collective-permute-done | bytes 393248 | tf_op jit(solution)/shard_map/ppermute | solution.py:80
  77.8 1.0 %head.1 = (bf16[96,512]{1,0:T(8,128)(2,1)S(1)}, bf16[96,512]{1,0:T(8,128)(2,1)S(1)}, bf16[96,512]{1,0:T(8,128)(2,1)S(1)}, bf16[96,512]{1,0:T(8,128)(2,1)S(1)}) custom-call(bf16[384,512]{1,0:T(8,128)(2,1)S(1)} %ff1.1.final_ref, bf16[384,512]{1,0:T(8,128)(2,1)S(1)} %collective-permute-done.18.opposite_ref, bf16[512,512]{1,0:T(8,128)(2,1)S(1)} %copy-done.3, ...), custom_call_target="tpu_custom_call" | custom-call | tf_op jit(solution)/shard_map/head/pallas_call | solution.py:312
  78.8 2.7 %collective-permute-start.19 = (bf16[96,512]{1,0:T(8,128)(2,1)S(1)}, bf16[96,512]{1,0:T(8,128)(2,1)S(1)}, u32[]{:S(2)}, u32[]{:S(2)}) collective-permute-start(bf16[96,512]{1,0:T(8,128)(2,1)S(1)} %get-tuple-element.29), channel_id=1, source_target_pairs={{0,0},{1,1},{2,3},{3,2},{4,4},{5,5},{6,7},{7,6},{8,8},{9,9},{10,11... | collective-permute-start | bytes 294920 | tf_op jit(solution)/shard_map/ppermute | solution.py:80
  81.6 0.1 collective-permute-start.20
  81.7 4.7 %collective-permute-start.21 = (bf16[96,512]{1,0:T(8,128)(2,1)S(1)}, bf16[96,512]{1,0:T(8,128)(2,1)S(1)}, u32[]{:S(2)}, u32[]{:S(2)}) collective-permute-start(bf16[96,512]{1,0:T(8,128)(2,1)S(1)} %get-tuple-element.31), channel_id=1, source_target_pairs={{0,8},{1,9},{2,11},{3,10},{4,12},{5,13},{6,15},{7,14},{8,0},{9,1},... | collective-permute-start | bytes 294920 | tf_op jit(solution)/shard_map/ppermute | solution.py:80
  86.4 2.6 %collective-permute-done.20.refs_1_ = bf16[96,512]{1,0:T(8,128)(2,1)S(1)} collective-permute-done((bf16[96,512]{1,0:T(8,128)(2,1)S(1)}, bf16[96,512]{1,0:T(8,128)(2,1)S(1)}, u32[]{:S(2)}, u32[]{:S(2)}) %collective-permute-start.20) | collective-permute-done | bytes 98336 | tf_op jit(solution)/shard_map/ppermute | solution.py:80
  89.0 2.3 %collective-permute-done.21.refs_2_ = bf16[96,512]{1,0:T(8,128)(2,1)S(1)} collective-permute-done((bf16[96,512]{1,0:T(8,128)(2,1)S(1)}, bf16[96,512]{1,0:T(8,128)(2,1)S(1)}, u32[]{:S(2)}, u32[]{:S(2)}) %collective-permute-start.21) | collective-permute-done | bytes 98336 | tf_op jit(solution)/shard_map/ppermute | solution.py:80
  91.4 1.0 %collective-permute-done.22.refs_3_ = bf16[96,512]{1,0:T(8,128)(2,1)S(1)} collective-permute-done((bf16[96,512]{1,0:T(8,128)(2,1)S(1)}, bf16[96,512]{1,0:T(8,128)(2,1)S(1)}, u32[]{:S(2)}, u32[]{:S(2)}) %collective-permute-start.22) | collective-permute-done | bytes 98336 | tf_op jit(solution)/shard_map/ppermute | solution.py:80
  92.3 0.8 join.1
  (26 shorter events, 0.1 us)
Async XLA Ops:
  0.0 1.0 %copy-start = (bf16[2,512,256]{2,1,0:T(8,128)(2,1)S(1)}, bf16[2,512,256]{2,1,0:T(8,128)(2,1)}, u32[]{:S(2)}) copy-start(bf16[2,512,256]{2,1,0:T(8,128)(2,1)} %refs_4_.1) | copy-start | bytes 1572868
  1.0 1.0 %copy-start.1 = (bf16[2,256,512]{2,1,0:T(8,128)(2,1)S(1)}, bf16[2,256,512]{2,1,0:T(8,128)(2,1)}, u32[]{:S(2)}) copy-start(bf16[2,256,512]{2,1,0:T(8,128)(2,1)} %refs_5_.1) | copy-start | bytes 1572868
  2.1 1.0 %copy-start.2 = (bf16[2,3,512,64]{2,3,1,0:T(8,128)(2,1)S(1)}, bf16[2,3,512,64]{2,3,1,0:T(8,128)(2,1)}, u32[]{:S(2)}) copy-start(bf16[2,3,512,64]{2,3,1,0:T(8,128)(2,1)} %param.12) | copy-start | bytes 1179652
  3.1 39.7 %copy-start.6 = (bf16[1,384,512]{2,1,0:T(8,128)(2,1)S(1)}, bf16[1,384,512]{2,1,0:T(8,128)(2,1)}, u32[]{:S(2)}) copy-start(bf16[1,384,512]{2,1,0:T(8,128)(2,1)} %param.10) | copy-start | bytes 1179652
  3.3 20.1 %collective-permute-start = (bf16[704,512]{1,0:T(8,128)(2,1)S(1)}, bf16[704,512]{1,0:T(8,128)(2,1)S(1)}, u32[]{:S(2)}, u32[]{:S(2)}) collective-permute-start(bf16[704,512]{1,0:T(8,128)(2,1)S(1)} %get-tuple-element.23.refs_4_.refs_0_.refs_1_), channel_id=1, source_target_pairs={{0,4},{1,5},{2,6},{3,7},{4,8},{5,9},{6,10},{7,11},{8,12},{9,13},{1... | collective-permute-start | bytes 2162696 | tf_op jit(solution)/shard_map/ppermute | solution.py:80
  5.5 18.9 %collective-permute-start.6 = (bf16[704,512]{1,0:T(8,128)(2,1)S(1)}, bf16[704,512]{1,0:T(8,128)(2,1)S(1)}, u32[]{:S(2)}, u32[]{:S(2)}) collective-permute-start(bf16[704,512]{1,0:T(8,128)(2,1)S(1)} %get-tuple-element.23.refs_4_.refs_0_.refs_1_), channel_id=1, source_target_pairs={{0,1},{1,0},{2,3},{3,2},{4,5},{5,4},{6,7},{7,6},{8,9},{9,8},{10,11... | collective-permute-start | bytes 2162696 | tf_op jit(solution)/shard_map/ppermute | solution.py:80
  23.4 16.4 %collective-permute-start.7 = (bf16[704,512]{1,0:T(8,128)(2,1)S(1)}, bf16[704,512]{1,0:T(8,128)(2,1)S(1)}, u32[]{:S(2)}, u32[]{:S(2)}) collective-permute-start(bf16[704,512]{1,0:T(8,128)(2,1)S(1)} %collective-permute-done.refs_5_.refs_1_.refs_2_), channel_id=1, source_target_pairs={{0,1},{1,0},{2,3},{3,2},{4,5},{5,4},{6,7},{7,6},{8,9},{9,8},{10,11... | collective-permute-start | bytes 2162696 | tf_op jit(solution)/shard_map/ppermute | solution.py:80
  24.3 17.7 %collective-permute-start.1 = (bf16[704,512]{1,0:T(8,128)(2,1)S(1)}, bf16[704,512]{1,0:T(8,128)(2,1)S(1)}, u32[]{:S(2)}, u32[]{:S(2)}) collective-permute-start(bf16[704,512]{1,0:T(8,128)(2,1)S(1)} %collective-permute-done.refs_5_.refs_1_.refs_2_), channel_id=1, source_target_pairs={{0,4},{1,5},{2,6},{3,7},{4,8},{5,9},{6,10},{7,11},{8,12},{9,13},{1... | collective-permute-start | bytes 2162696 | tf_op jit(solution)/shard_map/ppermute | solution.py:80
  24.3 18.5 %collective-permute-start.13 = (bf16[704,512]{1,0:T(8,128)(2,1)S(1)}, bf16[704,512]{1,0:T(8,128)(2,1)S(1)}, u32[]{:S(2)}, u32[]{:S(2)}) collective-permute-start(bf16[704,512]{1,0:T(8,128)(2,1)S(1)} %collective-permute-done.6.refs_7_.refs_3_.refs_4_), channel_id=1, source_target_pairs={{0,2},{1,3},{2,0},{3,1},{4,6},{5,7},{6,4},{7,5},{8,10},{9,11},{10,... | collective-permute-start | bytes 2162696 | tf_op jit(solution)/shard_map/ppermute | solution.py:80
  26.1 19.4 %collective-permute-start.11 = (bf16[704,512]{1,0:T(8,128)(2,1)S(1)}, bf16[704,512]{1,0:T(8,128)(2,1)S(1)}, u32[]{:S(2)}, u32[]{:S(2)}) collective-permute-start(bf16[704,512]{1,0:T(8,128)(2,1)S(1)} %collective-permute-done.refs_5_.refs_1_.refs_2_), channel_id=1, source_target_pairs={{0,2},{1,3},{2,0},{3,1},{4,6},{5,7},{6,4},{7,5},{8,10},{9,11},{10,... | collective-permute-start | bytes 2162696 | tf_op jit(solution)/shard_map/ppermute | solution.py:80
  26.2 20.8 %collective-permute-start.9 = (bf16[704,512]{1,0:T(8,128)(2,1)S(1)}, bf16[704,512]{1,0:T(8,128)(2,1)S(1)}, u32[]{:S(2)}, u32[]{:S(2)}) collective-permute-start(bf16[704,512]{1,0:T(8,128)(2,1)S(1)} %collective-permute-done.refs_5_.refs_1_.refs_2_), channel_id=1, source_target_pairs={{0,16},{1,17},{2,18},{3,19},{4,20},{5,21},{6,22},{7,23},{8,24},{9,... | collective-permute-start | bytes 2162696 | tf_op jit(solution)/shard_map/ppermute | solution.py:80
  39.8 25.8 %collective-permute-start.10 = (bf16[704,512]{1,0:T(8,128)(2,1)S(1)}, bf16[704,512]{1,0:T(8,128)(2,1)S(1)}, u32[]{:S(2)}, u32[]{:S(2)}) collective-permute-start(bf16[704,512]{1,0:T(8,128)(2,1)S(1)} %collective-permute-done.7.refs_8_.refs_4_.refs_5_), channel_id=1, source_target_pairs={{0,16},{1,17},{2,18},{3,19},{4,20},{5,21},{6,22},{7,23},{8,24},{9,... | collective-permute-start | bytes 2162696 | tf_op jit(solution)/shard_map/ppermute | solution.py:80
  42.0 24.1 %collective-permute-start.8 = (bf16[704,512]{1,0:T(8,128)(2,1)S(1)}, bf16[704,512]{1,0:T(8,128)(2,1)S(1)}, u32[]{:S(2)}, u32[]{:S(2)}) collective-permute-start(bf16[704,512]{1,0:T(8,128)(2,1)S(1)} %collective-permute-done.1.refs_6_.refs_2_.refs_3_), channel_id=1, source_target_pairs={{0,1},{1,0},{2,3},{3,2},{4,5},{5,4},{6,7},{7,6},{8,9},{9,8},{10,11... | collective-permute-start | bytes 2162696 | tf_op jit(solution)/shard_map/ppermute | solution.py:80
  42.8 27.2 %copy-start.8 = (f32[2,512]{1,0:T(2,128)S(1)}, f32[2,512]{1,0:T(2,128)}, u32[]{:S(2)}) copy-start(f32[2,512]{1,0:T(2,128)} %gain_ref.6) | copy-start | bytes 12292
  42.8 18.4 %collective-permute-start.2 = (bf16[96,512]{1,0:T(8,128)(2,1)S(1)}, bf16[96,512]{1,0:T(8,128)(2,1)S(1)}, u32[]{:S(2)}, u32[]{:S(2)}) collective-permute-start(bf16[96,512]{1,0:T(8,128)(2,1)S(1)} %get-tuple-element.24), channel_id=1, source_target_pairs={{0,0},{1,1},{2,3},{3,2},{4,4},{5,5},{6,7},{7,6},{8,8},{9,9},{10,11... | collective-permute-start | bytes 294920 | tf_op jit(solution)/shard_map/ppermute | solution.py:80
  45.5 18.2 %collective-permute-start.3 = (bf16[96,512]{1,0:T(8,128)(2,1)S(1)}, bf16[96,512]{1,0:T(8,128)(2,1)S(1)}, u32[]{:S(2)}, u32[]{:S(2)}) collective-permute-start(bf16[96,512]{1,0:T(8,128)(2,1)S(1)} %get-tuple-element.25), channel_id=1, source_target_pairs={{0,4},{1,5},{2,7},{3,6},{4,8},{5,9},{6,11},{7,10},{8,12},{9,13},{1... | collective-permute-start | bytes 294920 | tf_op jit(solution)/shard_map/ppermute | solution.py:80
  46.9 16.7 %collective-permute-start.4 = (bf16[96,512]{1,0:T(8,128)(2,1)S(1)}, bf16[96,512]{1,0:T(8,128)(2,1)S(1)}, u32[]{:S(2)}, u32[]{:S(2)}) collective-permute-start(bf16[96,512]{1,0:T(8,128)(2,1)S(1)} %get-tuple-element.26), channel_id=1, source_target_pairs={{0,8},{1,9},{2,11},{3,10},{4,12},{5,13},{6,15},{7,14},{8,0},{9,1},... | collective-permute-start | bytes 294920 | tf_op jit(solution)/shard_map/ppermute | solution.py:80
  61.2 4.4 %collective-permute-start.5 = (bf16[96,512]{1,0:T(8,128)(2,1)S(1)}, bf16[96,512]{1,0:T(8,128)(2,1)S(1)}, u32[]{:S(2)}, u32[]{:S(2)}) collective-permute-start(bf16[96,512]{1,0:T(8,128)(2,1)S(1)} %get-tuple-element.27), channel_id=1, source_target_pairs={{0,12},{1,13},{2,15},{3,14},{4,0},{5,1},{6,3},{7,2},{8,4},{9,5},{1... | collective-permute-start | bytes 294920 | tf_op jit(solution)/shard_map/ppermute | solution.py:80
  63.7 4.3 %collective-permute-start.14 = (bf16[704,512]{1,0:T(8,128)(2,1)S(1)}, bf16[704,512]{1,0:T(8,128)(2,1)S(1)}, u32[]{:S(2)}, u32[]{:S(2)}) collective-permute-start(bf16[704,512]{1,0:T(8,128)(2,1)S(1)} %collective-permute-done.7.refs_8_.refs_4_.refs_5_), channel_id=1, source_target_pairs={{0,2},{1,3},{2,0},{3,1},{4,6},{5,7},{6,4},{7,5},{8,10},{9,11},{10,... | collective-permute-start | bytes 2162696 | tf_op jit(solution)/shard_map/ppermute | solution.py:80
  63.7 4.3 %collective-permute-start.12 = (bf16[704,512]{1,0:T(8,128)(2,1)S(1)}, bf16[704,512]{1,0:T(8,128)(2,1)S(1)}, u32[]{:S(2)}, u32[]{:S(2)}) collective-permute-start(bf16[704,512]{1,0:T(8,128)(2,1)S(1)} %collective-permute-done.1.refs_6_.refs_2_.refs_3_), channel_id=1, source_target_pairs={{0,2},{1,3},{2,0},{3,1},{4,6},{5,7},{6,4},{7,5},{8,10},{9,11},{10,... | collective-permute-start | bytes 2162696 | tf_op jit(solution)/shard_map/ppermute | solution.py:80
  65.5 2.4 %collective-permute-start.16 = (bf16[704,512]{1,0:T(8,128)(2,1)S(1)}, bf16[704,512]{1,0:T(8,128)(2,1)S(1)}, u32[]{:S(2)}, u32[]{:S(2)}) collective-permute-start(bf16[704,512]{1,0:T(8,128)(2,1)S(1)} %collective-permute-done.9.refs_10_.refs_6_.refs_7_), channel_id=1, source_target_pairs={{0,2},{1,3},{2,0},{3,1},{4,6},{5,7},{6,4},{7,5},{8,10},{9,11},{10,... | collective-permute-start | bytes 2162696 | tf_op jit(solution)/shard_map/ppermute | solution.py:80
  65.6 3.4 %collective-permute-start.17 = (bf16[704,512]{1,0:T(8,128)(2,1)S(1)}, bf16[704,512]{1,0:T(8,128)(2,1)S(1)}, u32[]{:S(2)}, u32[]{:S(2)}) collective-permute-start(bf16[704,512]{1,0:T(8,128)(2,1)S(1)} %collective-permute-done.10.refs_11_.refs_7_.refs_8_), channel_id=1, source_target_pairs={{0,2},{1,3},{2,0},{3,1},{4,6},{5,7},{6,4},{7,5},{8,10},{9,11},{10,... | collective-permute-start | bytes 2162696 | tf_op jit(solution)/shard_map/ppermute | solution.py:80
  66.1 3.9 %collective-permute-start.15 = (bf16[704,512]{1,0:T(8,128)(2,1)S(1)}, bf16[704,512]{1,0:T(8,128)(2,1)S(1)}, u32[]{:S(2)}, u32[]{:S(2)}) collective-permute-start(bf16[704,512]{1,0:T(8,128)(2,1)S(1)} %collective-permute-done.8.refs_9_.refs_5_.refs_6_), channel_id=1, source_target_pairs={{0,2},{1,3},{2,0},{3,1},{4,6},{5,7},{6,4},{7,5},{8,10},{9,11},{10,... | collective-permute-start | bytes 2162696 | tf_op jit(solution)/shard_map/ppermute | solution.py:80
  70.0 0.9 %copy-start.7 = (f32[2,512]{1,0:T(2,128)S(1)}, f32[2,512]{1,0:T(2,128)}, u32[]{:S(2)}) copy-start(f32[2,512]{1,0:T(2,128)} %gain_ref.7) | copy-start | bytes 12292
  70.0 0.9 %copy-start.9 = (f32[512]{0:T(512)S(1)}, f32[512]{0:T(512)}, u32[]{:S(2)}) copy-start(f32[512]{0:T(512)} %param.16) | copy-start | bytes 6148
  73.8 3.9 %copy-start.3 = (bf16[512,512]{1,0:T(8,128)(2,1)S(1)}, bf16[512,512]{1,0:T(8,128)(2,1)}, u32[]{:S(2)}) copy-start(bf16[512,512]{1,0:T(8,128)(2,1)} %value_ref.1) | copy-start | bytes 1572868
  73.9 3.9 %copy-start.4 = (bf16[512,512]{1,0:T(8,128)(2,1)S(1)}, bf16[512,512]{1,0:T(8,128)(2,1)}, u32[]{:S(2)}) copy-start(bf16[512,512]{1,0:T(8,128)(2,1)} %gate_ref.1) | copy-start | bytes 1572868
  73.9 3.9 %copy-start.5 = (bf16[512,512]{1,0:T(8,128)(2,1)S(1)}, bf16[512,512]{1,0:T(8,128)(2,1)}, u32[]{:S(2)}) copy-start(bf16[512,512]{1,0:T(8,128)(2,1)} %out_ref.1) | copy-start | bytes 1572868
  76.0 1.8 %collective-permute-start.18 = (bf16[384,512]{1,0:T(8,128)(2,1)S(1)}, bf16[384,512]{1,0:T(8,128)(2,1)S(1)}, u32[]{:S(2)}, u32[]{:S(2)}) collective-permute-start(bf16[384,512]{1,0:T(8,128)(2,1)S(1)} %ff1.1.final_ref), channel_id=1, source_target_pairs={{0,2},{1,3},{2,0},{3,1},{4,6},{5,7},{6,4},{7,5},{8,10},{9,11},{10,... | collective-permute-start | bytes 1179656 | tf_op jit(solution)/shard_map/ppermute | solution.py:80
  78.8 7.6 %collective-permute-start.19 = (bf16[96,512]{1,0:T(8,128)(2,1)S(1)}, bf16[96,512]{1,0:T(8,128)(2,1)S(1)}, u32[]{:S(2)}, u32[]{:S(2)}) collective-permute-start(bf16[96,512]{1,0:T(8,128)(2,1)S(1)} %get-tuple-element.29), channel_id=1, source_target_pairs={{0,0},{1,1},{2,3},{3,2},{4,4},{5,5},{6,7},{7,6},{8,8},{9,9},{10,11... | collective-permute-start | bytes 294920 | tf_op jit(solution)/shard_map/ppermute | solution.py:80
  81.6 7.5 %collective-permute-start.20 = (bf16[96,512]{1,0:T(8,128)(2,1)S(1)}, bf16[96,512]{1,0:T(8,128)(2,1)S(1)}, u32[]{:S(2)}, u32[]{:S(2)}) collective-permute-start(bf16[96,512]{1,0:T(8,128)(2,1)S(1)} %get-tuple-element.30), channel_id=1, source_target_pairs={{0,4},{1,5},{2,7},{3,6},{4,8},{5,9},{6,11},{7,10},{8,12},{9,13},{1... | collective-permute-start | bytes 294920 | tf_op jit(solution)/shard_map/ppermute | solution.py:80
  81.7 9.7 %collective-permute-start.21 = (bf16[96,512]{1,0:T(8,128)(2,1)S(1)}, bf16[96,512]{1,0:T(8,128)(2,1)S(1)}, u32[]{:S(2)}, u32[]{:S(2)}) collective-permute-start(bf16[96,512]{1,0:T(8,128)(2,1)S(1)} %get-tuple-element.31), channel_id=1, source_target_pairs={{0,8},{1,9},{2,11},{3,10},{4,12},{5,13},{6,15},{7,14},{8,0},{9,1},... | collective-permute-start | bytes 294920 | tf_op jit(solution)/shard_map/ppermute | solution.py:80
  86.4 5.9 %collective-permute-start.22 = (bf16[96,512]{1,0:T(8,128)(2,1)S(1)}, bf16[96,512]{1,0:T(8,128)(2,1)S(1)}, u32[]{:S(2)}, u32[]{:S(2)}) collective-permute-start(bf16[96,512]{1,0:T(8,128)(2,1)S(1)} %get-tuple-element.32), channel_id=1, source_target_pairs={{0,12},{1,13},{2,15},{3,14},{4,0},{5,1},{6,3},{7,2},{8,4},{9,5},{1... | collective-permute-start | bytes 294920 | tf_op jit(solution)/shard_map/ppermute | solution.py:80

commit v4 on v3

--- a/solution.py
+++ b/solution.py
@@ -113,31 +113,54 @@
     return [k * m + h for k, h in at]
 
 
-def pack_kernel(plan, *refs):
-    first = lax.axis_index("strand") == 0
-    refs, mine_ref, other_ref = refs[:-2], refs[-2], refs[-1]
-    at = 0
-    for ref, block, turn in zip(refs, *plan):
-        whole = ref[block].T if turn else ref[block]
-        taps = whole[None] if whole.ndim == 2 else whole
-        for tap in range(taps.shape[0]):
-            half = taps.shape[1] // 2
-            top, low = taps[tap, :half], taps[tap, half:]
-            mine_ref[at : at + half] = jnp.where(first, top, low)
-            other_ref[at : at + half] = jnp.where(first, low, top)
+def pack_kernel(plan, mine, *refs):
+    blocks, turned = plan
+    refs, (out, wide, sems) = refs[:-3], refs[-3:]
+    s = lax.axis_index("strand")
+    part = s if mine else 1 - s
+    at, turns, copies = 0, [], []
+
+    def copy(source, target):
+        copies.append(pltpu.make_async_copy(source, target, sems.at[len(copies)]))
+        copies[-1].start()
+
+    for ref, block, turn in zip(refs, blocks, turned):
+        if turn:
+            half = ref.shape[2] // 2
+            columns = pl.ds(pl.multiple_of(part * half, half), half)
+            copy(ref.at[block, :, columns], wide.at[len(turns)])
+            turns.append((at, half, copies[-1]))
             at += half
-
-
-def pack(arrays, blocks, turned, rows, name):
-    shape = jax.ShapeDtypeStruct((rows, arrays[-1].shape[-1]), BF16)
+        else:
+            half = ref.shape[-2] // 2
+            rows = pl.ds(pl.multiple_of(part * half, half), half)
+            for tap in range(ref.shape[1]) if len(ref.shape) == 4 else (None,):
+                source = ref.at[block, rows] if tap is None else ref.at[block, tap, rows]
+                copy(source, out.at[at : at + half])
+                at += half
+    for k, (at, half, done) in enumerate(turns):
+        done.wait()
+        out[at : at + half] = wide[k].T
+    for done in copies:
+        if all(done is not turn[2] for turn in turns):
+            done.wait()
+
+
+def pack(arrays, blocks, turned, rows, mine):
+    width = arrays[0].shape[1]
+    half = arrays[0].shape[2] // 2
     return pl.pallas_call(
-        functools.partial(pack_kernel, (blocks, turned)),
-        out_shape=[shape, shape],
-        in_specs=[VMEM_SPEC] * len(arrays),
-        out_specs=[VMEM_SPEC] * 2,
+        functools.partial(pack_kernel, (blocks, turned), mine),
+        out_shape=jax.ShapeDtypeStruct((rows, width), BF16),
+        in_specs=[pl.BlockSpec(memory_space=pltpu.HBM)] * len(arrays),
+        out_specs=VMEM_SPEC,
+        scratch_shapes=[
+            pltpu.VMEM((sum(turned), width, half), BF16),
+            pltpu.SemaphoreType.DMA((2 * rows // 32,)),
+        ],
         compiler_params=PARAMS,
-        name=name,
-    )(*arrays)
+        name="pack_own" if mine else "pack_rest",
+    )(*[pltpu.with_memory_space_constraint(v, pltpu.HBM) for v in arrays])
 
 
 def split_kernel(rows_ref, *out_refs):
@@ -161,21 +184,20 @@
         out[pl.ds(pl.multiple_of(sub * size, size), size)] = part[...]
 
 
-def conv_kernel(block, parts, start, gain_ref, *refs):
-    n = lax.axis_size("seq")
-    states, refs = refs[:parts], refs[parts:]
-    count = (len(refs) - 3) // 2
-    mine, other = refs[:count], refs[count : 2 * count]
-    out, weight, acc = refs[2 * count :]
+def conv_kernel(block, parts, places, start, gain_ref, *refs):
+    n = lax.axis_size("seq")
+    states, arrays = refs[:parts], refs[parts:-3]
+    out, weight, acc = refs[-3:]
     width = acc.shape[1]
     taps = weight.shape[0] // width
-    half = width // count // 2
+    half = width // len(places[0]) // 2
     s, j = lax.axis_index("strand"), lax.axis_index("seq")
-    for r, shard in enumerate(origins()):
-        for ref, part in ((mine[r], s), (other[r], 1 - s)):
+    for side, part in zip(places, (s, 1 - s)):
+        for (k, row), shard in zip(side, origins()):
             at = pl.multiple_of((shard * 2 + part) * half, half)
             for tap in range(taps):
-                weight[pl.ds(tap * width + at, half)] = ref[start + tap * half : start + (tap + 1) * half]
+                first = row + start + tap * half
+                weight[pl.ds(tap * width + at, half)] = arrays[k][first : first + half]
     if parts > 1:
         size = states[0].shape[0]
         for k, state in enumerate(states):
@@ -192,62 +214,57 @@
     out[...] = state + acc[...].astype(BF16).astype(F32)
 
 
-def conv(states, gain, mine, other, block, start, taps):
+def conv(states, gain, arrays, places, block, start, taps):
     width = gain.shape[1]
     rows = sum(v.shape[0] for v in states)
-    arrays = len(mine) + len(other)
     return pl.pallas_call(
-        functools.partial(conv_kernel, block, len(states), start),
+        functools.partial(conv_kernel, block, len(states), places, start),
         out_shape=jax.ShapeDtypeStruct((rows, width), F32),
-        in_specs=[VMEM_SPEC] * (1 + len(states) + arrays),
+        in_specs=[VMEM_SPEC] * (1 + len(states) + len(arrays)),
         out_specs=VMEM_SPEC,
         scratch_shapes=[pltpu.VMEM((taps * width, width), BF16), pltpu.VMEM((rows, width), F32)],
         compiler_params=PARAMS,
         name=f"conv{block}",
-    )(gain, *states, *mine, *other)
-
-
-def ff_kernel(block, first, ends, start, half, gain_ref, head_ref, state_ref, *refs):
+    )(gain, *states, *arrays)
+
+
+def ff_kernel(block, first, ends, places, start, half, gain_ref, head_ref, state_ref, *refs):
     if not first:
         mixed_ref, refs = refs[0], refs[1:]
-    outs = 1 if ends else 2
-    count = (len(refs) - outs - 1) // 2
-    mine, other = refs[:count], refs[count : 2 * count]
-    out, hid = refs[2 * count], refs[-1]
+    arrays, out, hid = refs, refs[-2 if ends else -3], refs[-1]
     state = state_ref[...]
     if first:
         mixed = normalize(state, gain_ref[block : block + 1]).astype(BF16)
     else:
         mixed = mixed_ref[...]
     down = []
-    for r in range(count):
-        up = jnp.concatenate([v[r][start : start + half] for v in (mine, other)], 0)
+    for r, pair in enumerate(zip(*places)):
+        up = jnp.concatenate([arrays[k][row + start : row + start + half] for k, row in pair], 0)
         hid[:, 2 * r * half : 2 * (r + 1) * half] = jax.nn.gelu(matmul_nt(mixed, up)).astype(BF16)
-        down += [v[r][start + half : start + 2 * half] for v in (mine, other)]
+        down += [arrays[k][row + start + half : row + start + 2 * half] for k, row in pair]
     state = state + matmul(hid[...], jnp.concatenate(down, 0))
     if ends == "head":
         state = normalize(state, head_ref[...]).astype(BF16)
     out[...] = state
     if not ends:
-        refs[2 * count + 1][...] = mixed
-
-
-def feed_forward(state, mixed, gain, head, mine, other, block, start, half, ends):
+        refs[-2][...] = mixed
+
+
+def feed_forward(state, mixed, gain, head, arrays, places, block, start, half, ends):
     rows, width = state.shape
-    arrays = len(mine) + len(other)
     out = [jax.ShapeDtypeStruct((rows, width), BF16 if ends == "head" else F32)]
     if not ends:
         out.append(jax.ShapeDtypeStruct((rows, width), BF16))
     given = [state] if mixed is None else [state, mixed]
     return pl.pallas_call(
-        functools.partial(ff_kernel, block, mixed is None, ends, start, half),
+        functools.partial(ff_kernel, block, mixed is None, ends, places, start, half),
         out_shape=out,
-        in_specs=[VMEM_SPEC] * (2 + len(given) + arrays),
+        in_specs=[VMEM_SPEC] * (2 + len(given) + len(arrays)),
         out_specs=[VMEM_SPEC] * len(out),
-        scratch_shapes=[pltpu.VMEM((rows, arrays * half), BF16)],
+        scratch_shapes=[pltpu.VMEM((rows, 2 * len(places[0]) * half), BF16)],
         compiler_params=PARAMS,
         name=f"ff{block}",
-    )(gain, head, *given, *mine, *other)
+    )(gain, head, *given, *arrays)
 
 
 def head_kernel(final_ref, opposite_ref, value_ref, gate_ref, out_ref, *refs):
@@ -282,10 +299,9 @@
     part = jax.ShapeDtypeStruct((rows // n, width), BF16)
     turned = jnp.swapaxes(conv_weight, 2, 3)
     cut = hidden + taps * chans
-    own, own_other = pack(
-        (up_weight, down_weight, turned, turned, up_weight, down_weight),
-        (0, 0, 0, 1, 1, 1), (True, False, False, False, True, False), cut + hidden, "pack",
-    )
+    shard = (up_weight, down_weight, turned, turned, up_weight, down_weight)
+    which = (0, 0, 0, 1, 1, 1), (True, False, False, False, True, False)
+    own = pack(shard, *which, cut + hidden, True)
     to = lambda k: (lambda g, i, s, c: (g, (i + k) % n, s, c if s == 0 else 1 - c))
     parts = pl.pallas_call(
         split_kernel, out_shape=[part] * n, in_specs=[VMEM_SPEC], out_specs=[VMEM_SPEC] * n,
@@ -297,17 +313,29 @@
     b = along(a)
     xa = across(a)
     ya = planes(a)
-    xb = across(b)
+    swaps = [other_core(a), other_core(x)]
+    states = [moved(parts[0], to(0))]
+    events = [*swaps, states[0]]
+    parts = after(parts, [b, ya, *events])
+    size = cut + hidden
     yxa = planes(xa)
-    parts = after(parts, [b])
-    states = [moved(p, to(k)) for k, p in enumerate(parts)]
+    keep = size - 176
+    xb0 = across(b[:keep])
+    xb1 = along(xa[keep:])
+    states += [moved(p, to(k + 1)) for k, p in enumerate(parts[1:])]
+    xb = jnp.concatenate([xb0, xb1], 0)
+    rest = pack(shard, *which, cut + hidden, False)
     mine = [own, a, b, x, xa, xb, ya, yxa]
-    other = [own_other] + [other_core(v) for v in mine[1:]]
+    swap_a, swap_x = swaps
+    bs, xas, yas = after([b, xa, ya], [states[-1]])
+    others = [swap_a, other_core(bs), swap_x, other_core(xas), other_core(xb), other_core(yas), other_core(yxa)]
+    arrays = mine + [rest] + others
+    places = [[(k, 0) for k in range(8)], [(k + 8, 0) for k in range(8)]]
     head = head_norm[None]
-    state = conv(states, conv_norm, mine, other, 0, hidden, taps)
-    (state,) = feed_forward(state, None, ff_norm, head, mine, other, 0, 0, half, "state")
-    state = conv([state], conv_norm, mine, other, 1, hidden + taps * chans // 2, taps)
-    (final,) = feed_forward(state, None, ff_norm, head, mine, other, 1, cut, half, "head")
+    state = conv(states, conv_norm, arrays, places, 0, hidden, taps)
+    (state,) = feed_forward(state, None, ff_norm, head, arrays, places, 0, 0, half, "state")
+    state = conv([state], conv_norm, arrays, places, 1, hidden + taps * chans // 2, taps)
+    (final,) = feed_forward(state, None, ff_norm, head, arrays, places, 1, cut, half, "head")
     opposite = other_core(final)
     results = pl.pallas_call(
         head_kernel, out_shape=[part] * n, in_specs=[VMEM_SPEC] * 5, out_specs=[VMEM_SPEC] * n,

time: 93.6 us -> 90.1 us (0.963)
  waiting for transfers between devices: 53.6 us -> 49.6 us
  Pallas kernels: 7.97 us -> 11 us
  local copies, waits for them, and re-layouts: 3.11 us -> 0.13 us
    ppermute x23 -> x24, waiting for transfers between devices: 53.6 us -> 49.6 us  [moved(): return lax.ppermute(value, AXES, pairs)]
    pallas_call x5 -> x6, Pallas kernels: 6.13 us -> 9.2 us  [the longest x2 4.14 us: feed_forward(): pl.pallas_call(functools.partial(ff_kernel, block, mixed is None, ends, p...]
    unnamed x20 -> x15, local copies, waits for them, and re-layouts: 3.11 us -> 0.07 us
    ppermute x23 -> x24, starting transfers between devices: 28.2 us -> 28.9 us  [moved(): return lax.ppermute(value, AXES, pairs)]
  transfers between devices with their start and end apart: 23 -> 24, of which waited for: 13 -> 13; matrix products, arithmetic and copies ran while one was open for 0% -> 0% of each run, Pallas kernels for 0% -> 2%
where the time goes in v4:
time: 90.1 us; the launch traced here: 89.9 us
  waiting for transfers between devices  49.6 us (55%)
  starting transfers between devices  28.9 us (32%)
  Pallas kernels  11 us (12%)
    ppermute x24, waiting for transfers between devices, moved(): return lax.ppermute(value, AXES, pairs)  49.6 us
    ppermute x24, starting transfers between devices, moved(): return lax.ppermute(value, AXES, pairs)  28.9 us
    pallas_call x2, Pallas kernels, feed_forward(): pl.pallas_call(functools.partial(ff_kernel, block, mixed is None, ends, p...  4.14 us
    pallas_call x2, Pallas kernels, pack(): pl.pallas_call(functools.partial(pack_kernel, (blocks, turned), mine), ou...  3.28 us
  transfers between devices with their start and end apart: 24, of which 13 were waited for; matrix products, arithmetic and copies ran while one was open for 0% of the time, Pallas kernels for 2%

profile of v4, /device:TPU:1, one launch (start us, length us, event | category | flops | bytes accessed | tf_op | source)
XLA Modules:
  0.0 89.9 jit_solution(8444626436867794149)
XLA Ops:
  0.0 1.7 %pack_own.1.refs_4_.refs_0_.refs_1_ = bf16[704,512]{1,0:T(8,128)(2,1)S(1)} custom-call(bf16[2,512,256]{2,1,0:T(8,128)(2,1)} %refs_4_.3, bf16[2,256,512]{2,1,0:T(8,128)(2,1)} %refs_5_.3, bf16[2,3,64,512]{3,2,1,0:T(8,128)(2,1)} %bitcast.7, bf16[2,3,64,512]{3,2,1,0:T(8,128)(2,1)} %bitcast.8, bf16[2,512,256]{2,1,0:T(8,128)(2,1)} %refs_4_.3, ...), custom_call_target="tpu_custom_call" | custom-call | tf_op jit(solution)/shard_map/pack_own/pallas_call | solution.py:152
  1.7 2.2 %collective-permute-start.1 = (bf16[704,512]{1,0:T(8,128)(2,1)S(1)}, bf16[704,512]{1,0:T(8,128)(2,1)S(1)}, u32[]{:S(2)}, u32[]{:S(2)}) collective-permute-start(bf16[704,512]{1,0:T(8,128)(2,1)S(1)} %pack_own.1.refs_4_.refs_0_.refs_1_), channel_id=1, source_target_pairs={{0,4},{1,5},{2,6},{3,7},{4,8},{5,9},{6,10},{7,11},{8,12},{9,13},{1... | collective-permute-start | bytes 2162696 | tf_op jit(solution)/shard_map/ppermute | solution.py:80
  3.9 1.2 %collective-permute-start.5 = (bf16[704,512]{1,0:T(8,128)(2,1)S(1)}, bf16[704,512]{1,0:T(8,128)(2,1)S(1)}, u32[]{:S(2)}, u32[]{:S(2)}) collective-permute-start(bf16[704,512]{1,0:T(8,128)(2,1)S(1)} %pack_own.1.refs_4_.refs_0_.refs_1_), channel_id=1, source_target_pairs={{0,1},{1,0},{2,3},{3,2},{4,5},{5,4},{6,7},{7,6},{8,9},{9,8},{10,11... | collective-permute-start | bytes 2162696 | tf_op jit(solution)/shard_map/ppermute | solution.py:80
  5.1 16.7 %collective-permute-done.1.refs_5_.refs_1_.refs_2_ = bf16[704,512]{1,0:T(8,128)(2,1)S(1)} collective-permute-done((bf16[704,512]{1,0:T(8,128)(2,1)S(1)}, bf16[704,512]{1,0:T(8,128)(2,1)S(1)}, u32[]{:S(2)}, u32[]{:S(2)}) %collective-permute-start.1) | collective-permute-done | bytes 720928 | tf_op jit(solution)/shard_map/ppermute | solution.py:80
  21.7 0.0 collective-permute-start.2
  21.7 1.0 %collective-permute-start.10 = (bf16[704,512]{1,0:T(8,128)(2,1)S(1)}, bf16[704,512]{1,0:T(8,128)(2,1)S(1)}, u32[]{:S(2)}, u32[]{:S(2)}) collective-permute-start(bf16[704,512]{1,0:T(8,128)(2,1)S(1)} %collective-permute-done.1.refs_5_.refs_1_.refs_2_), channel_id=1, source_target_pairs={{0,1},{1,0},{2,3},{3,2},{4,5},{5,4},{6,7},{7,6},{8,9},{9,8},{10,11... | collective-permute-start | bytes 2162696 | tf_op jit(solution)/shard_map/ppermute | solution.py:80
  22.7 0.0 collective-permute-done.5.refs_7_.refs_3_.refs_4_
  22.7 1.8 %collective-permute-start.6 = (bf16[704,512]{1,0:T(8,128)(2,1)S(1)}, bf16[704,512]{1,0:T(8,128)(2,1)S(1)}, u32[]{:S(2)}, u32[]{:S(2)}) collective-permute-start(bf16[704,512]{1,0:T(8,128)(2,1)S(1)} %collective-permute-done.5.refs_7_.refs_3_.refs_4_), channel_id=1, source_target_pairs={{0,2},{1,3},{2,0},{3,1},{4,6},{5,7},{6,4},{7,5},{8,10},{9,11},{10,... | collective-permute-start | bytes 2162696 | tf_op jit(solution)/shard_map/ppermute | solution.py:80
  24.5 0.0 collective-permute-start.4
  24.5 4.8 %collective-permute-start.3 = (bf16[704,512]{1,0:T(8,128)(2,1)S(1)}, bf16[704,512]{1,0:T(8,128)(2,1)S(1)}, u32[]{:S(2)}, u32[]{:S(2)}) collective-permute-start(bf16[704,512]{1,0:T(8,128)(2,1)S(1)} %collective-permute-done.1.refs_5_.refs_1_.refs_2_), channel_id=1, source_target_pairs={{0,16},{1,17},{2,18},{3,19},{4,20},{5,21},{6,22},{7,23},{8,24},{9,... | collective-permute-start | bytes 2162696 | tf_op jit(solution)/shard_map/ppermute | solution.py:80
  29.3 10.7 %collective-permute-done.2.refs_6_.refs_2_.refs_3_ = bf16[704,512]{1,0:T(8,128)(2,1)S(1)} collective-permute-done((bf16[704,512]{1,0:T(8,128)(2,1)S(1)}, bf16[704,512]{1,0:T(8,128)(2,1)S(1)}, u32[]{:S(2)}, u32[]{:S(2)}) %collective-permute-start.2) | collective-permute-done | bytes 720928 | tf_op jit(solution)/shard_map/ppermute | solution.py:80
  39.9 2.6 %collective-permute-start = (bf16[96,512]{1,0:T(8,128)(2,1)S(1)}, bf16[96,512]{1,0:T(8,128)(2,1)S(1)}, u32[]{:S(2)}, u32[]{:S(2)}) collective-permute-start(bf16[96,512]{1,0:T(8,128)(2,1)S(1)} %get-tuple-element.19), channel_id=1, source_target_pairs={{0,0},{1,1},{2,3},{3,2},{4,4},{5,5},{6,7},{7,6},{8,8},{9,9},{10,11... | collective-permute-start | bytes 294920 | tf_op jit(solution)/shard_map/ppermute | solution.py:80
  42.6 3.0 %collective-permute-done.refs_0_ = bf16[96,512]{1,0:T(8,128)(2,1)S(1)} collective-permute-done((bf16[96,512]{1,0:T(8,128)(2,1)S(1)}, bf16[96,512]{1,0:T(8,128)(2,1)S(1)}, u32[]{:S(2)}, u32[]{:S(2)}) %collective-permute-start) | collective-permute-done | bytes 98336 | tf_op jit(solution)/shard_map/ppermute | solution.py:80
  45.6 0.6 collective-permute-start.11
  46.2 0.5 collective-permute-start.13
  46.7 3.7 %collective-permute-start.9 = (bf16[96,512]{1,0:T(8,128)(2,1)S(1)}, bf16[96,512]{1,0:T(8,128)(2,1)S(1)}, u32[]{:S(2)}, u32[]{:S(2)}) collective-permute-start(bf16[96,512]{1,0:T(8,128)(2,1)S(1)} %get-tuple-element.25), channel_id=1, source_target_pairs={{0,12},{1,13},{2,15},{3,14},{4,0},{5,1},{6,3},{7,2},{8,4},{9,5},{1... | collective-permute-start | bytes 294920 | tf_op jit(solution)/shard_map/ppermute | solution.py:80
  50.4 0.1 collective-permute-start.12
  50.5 0.1 collective-permute-start.7
  50.6 2.5 %collective-permute-done.9.refs_3_ = bf16[96,512]{1,0:T(8,128)(2,1)S(1)} collective-permute-done((bf16[96,512]{1,0:T(8,128)(2,1)S(1)}, bf16[96,512]{1,0:T(8,128)(2,1)S(1)}, u32[]{:S(2)}, u32[]{:S(2)}) %collective-permute-start.9) | collective-permute-done | bytes 98336 | tf_op jit(solution)/shard_map/ppermute | solution.py:80
  53.0 1.9 %collective-permute-start.8 = (bf16[96,512]{1,0:T(8,128)(2,1)S(1)}, bf16[96,512]{1,0:T(8,128)(2,1)S(1)}, u32[]{:S(2)}, u32[]{:S(2)}) collective-permute-start(bf16[96,512]{1,0:T(8,128)(2,1)S(1)} %get-tuple-element.24), channel_id=1, source_target_pairs={{0,8},{1,9},{2,11},{3,10},{4,12},{5,13},{6,15},{7,14},{8,0},{9,1},... | collective-permute-start | bytes 294920 | tf_op jit(solution)/shard_map/ppermute | solution.py:80
  54.9 3.8 %collective-permute-done.11 = bf16[528,512]{1,0:T(8,128)(2,1)S(1)} collective-permute-done((bf16[528,512]{1,0:T(8,128)(2,1)S(1)}, bf16[528,512]{1,0:T(8,128)(2,1)S(1)}, u32[]{:S(2)}, u32[]{:S(2)}) %collective-permute-start.11) | collective-permute-done | bytes 540704 | tf_op jit(solution)/shard_map/ppermute | solution.py:80
  58.7 0.1 collective-permute-done.12
  58.9 0.5 collective-permute-start.15
  59.3 0.0 copy-start.5
  59.3 1.7 %collective-permute-done.7.refs_1_ = bf16[96,512]{1,0:T(8,128)(2,1)S(1)} collective-permute-done((bf16[96,512]{1,0:T(8,128)(2,1)S(1)}, bf16[96,512]{1,0:T(8,128)(2,1)S(1)}, u32[]{:S(2)}, u32[]{:S(2)}) %collective-permute-start.7) | collective-permute-done | bytes 98336 | tf_op jit(solution)/shard_map/ppermute | solution.py:80
  61.0 3.1 %collective-permute-done.8.refs_2_ = bf16[96,512]{1,0:T(8,128)(2,1)S(1)} collective-permute-done((bf16[96,512]{1,0:T(8,128)(2,1)S(1)}, bf16[96,512]{1,0:T(8,128)(2,1)S(1)}, u32[]{:S(2)}, u32[]{:S(2)}) %collective-permute-start.8) | collective-permute-done | bytes 98336 | tf_op jit(solution)/shard_map/ppermute | solution.py:80
  64.1 0.6 collective-permute-start.16
  64.7 0.0 collective-permute-start.18
  64.7 1.6 %pack_rest.1.refs_12_.refs_8_.refs_9_ = bf16[704,512]{1,0:T(8,128)(2,1)S(1)} custom-call(bf16[2,512,256]{2,1,0:T(8,128)(2,1)} %refs_4_.3, bf16[2,256,512]{2,1,0:T(8,128)(2,1)} %refs_5_.3, bf16[2,3,64,512]{3,2,1,0:T(8,128)(2,1)} %bitcast.9, bf16[2,3,64,512]{3,2,1,0:T(8,128)(2,1)} %bitcast.10, bf16[2,512,256]{2,1,0:T(8,128)(2,1)} %refs_4_.3, ...), custom_call_target="tpu_custom_call" | custom-call | tf_op jit(solution)/shard_map/pack_rest/pallas_call | solution.py:152
  66.4 0.2 collective-permute-done.16.refs_17_.refs_13_.refs_14_
  66.5 1.0 %collective-permute-done.18.refs_19_.refs_15_.refs_16_ = bf16[704,512]{1,0:T(8,128)(2,1)S(1)} collective-permute-done((bf16[704,512]{1,0:T(8,128)(2,1)S(1)}, bf16[704,512]{1,0:T(8,128)(2,1)S(1)}, u32[]{:S(2)}, u32[]{:S(2)}) %collective-permute-start.18) | collective-permute-done | bytes 720928 | tf_op jit(solution)/shard_map/ppermute | solution.py:80
  67.5 0.9 %conv0.1.state_ref = f32[384,512]{1,0:T(8,128)S(1)} custom-call(f32[2,512]{1,0:T(2,128)S(1)} %copy-done.5, bf16[96,512]{1,0:T(8,128)(2,1)S(1)} %collective-permute-done.refs_0_, bf16[96,512]{1,0:T(8,128)(2,1)S(1)} %collective-permute-done.7.refs_1_, bf16[96,512]{1,0:T(8,128)(2,1)S(1)} %collective-permute-done.8.refs_2_, ...), custom_call_target="tpu_custom_call" | custom-call | tf_op jit(solution)/shard_map/conv0/pallas_call | solution.py:220
  68.5 2.0 %ff0.1.refs_0_ = f32[384,512]{1,0:T(8,128)S(1)} custom-call(f32[2,512]{1,0:T(2,128)S(1)} %copy-done.4, f32[1,512]{1,0:T(1,128)S(1)} %bitcast.5, f32[384,512]{1,0:T(8,128)S(1)} %conv0.1.state_ref, bf16[704,512]{1,0:T(8,128)(2,1)S(1)} %pack_own.1.refs_4_.refs_0_.refs_1_, bf16[704,512]{1,0:T(8,128)(2,1)S(1)} %collective-permute-done.1.refs_5_.refs_1_.refs_2_, ...), custom_call_target="tpu_custom_call" | custom-call | tf_op jit(solution)/shard_map/ff0/pallas_call | solution.py:259
  70.5 0.9 conv1.1.state_ref
  71.4 0.0 copy-start
  71.4 0.0 copy-start.1
  71.4 0.0 copy-start.2
  71.4 2.1 %ff1.1.final_ref = bf16[384,512]{1,0:T(8,128)(2,1)S(1)} custom-call(f32[2,512]{1,0:T(2,128)S(1)} %copy-done.4, f32[1,512]{1,0:T(1,128)S(1)} %bitcast.6, f32[384,512]{1,0:T(8,128)S(1)} %conv1.1.state_ref, bf16[704,512]{1,0:T(8,128)(2,1)S(1)} %pack_own.1.refs_4_.refs_0_.refs_1_, bf16[704,512]{1,0:T(8,128)(2,1)S(1)} %collective-permute-done.1.refs_5_.refs_1_.refs_2_, ...), custom_call_target="tpu_custom_call" | custom-call | tf_op jit(solution)/shard_map/ff1/pallas_call | solution.py:259
  73.6 0.5 collective-permute-start.19
  74.0 1.3 %collective-permute-done.19.opposite_ref = bf16[384,512]{1,0:T(8,128)(2,1)S(1)} collective-permute-done((bf16[384,512]{1,0:T(8,128)(2,1)S(1)}, bf16[384,512]{1,0:T(8,128)(2,1)S(1)}, u32[]{:S(2)}, u32[]{:S(2)}) %collective-permute-start.19) | collective-permute-done | bytes 393248 | tf_op jit(solution)/shard_map/ppermute | solution.py:80
  75.4 1.0 %head.1 = (bf16[96,512]{1,0:T(8,128)(2,1)S(1)}, bf16[96,512]{1,0:T(8,128)(2,1)S(1)}, bf16[96,512]{1,0:T(8,128)(2,1)S(1)}, bf16[96,512]{1,0:T(8,128)(2,1)S(1)}) custom-call(bf16[384,512]{1,0:T(8,128)(2,1)S(1)} %ff1.1.final_ref, bf16[384,512]{1,0:T(8,128)(2,1)S(1)} %collective-permute-done.19.opposite_ref, bf16[512,512]{1,0:T(8,128)(2,1)S(1)} %copy-done, ...), custom_call_target="tpu_custom_call" | custom-call | tf_op jit(solution)/shard_map/head/pallas_call | solution.py:340
  76.4 2.9 %collective-permute-start.20 = (bf16[96,512]{1,0:T(8,128)(2,1)S(1)}, bf16[96,512]{1,0:T(8,128)(2,1)S(1)}, u32[]{:S(2)}, u32[]{:S(2)}) collective-permute-start(bf16[96,512]{1,0:T(8,128)(2,1)S(1)} %get-tuple-element.29), channel_id=1, source_target_pairs={{0,0},{1,1},{2,3},{3,2},{4,4},{5,5},{6,7},{7,6},{8,8},{9,9},{10,11... | collective-permute-start | bytes 294920 | tf_op jit(solution)/shard_map/ppermute | solution.py:80
  79.3 0.1 collective-permute-start.21
  79.4 1.0 %collective-permute-start.22 = (bf16[96,512]{1,0:T(8,128)(2,1)S(1)}, bf16[96,512]{1,0:T(8,128)(2,1)S(1)}, u32[]{:S(2)}, u32[]{:S(2)}) collective-permute-start(bf16[96,512]{1,0:T(8,128)(2,1)S(1)} %get-tuple-element.31), channel_id=1, source_target_pairs={{0,8},{1,9},{2,11},{3,10},{4,12},{5,13},{6,15},{7,14},{8,0},{9,1},... | collective-permute-start | bytes 294920 | tf_op jit(solution)/shard_map/ppermute | solution.py:80
  80.4 3.1 %collective-permute-start.23 = (bf16[96,512]{1,0:T(8,128)(2,1)S(1)}, bf16[96,512]{1,0:T(8,128)(2,1)S(1)}, u32[]{:S(2)}, u32[]{:S(2)}) collective-permute-start(bf16[96,512]{1,0:T(8,128)(2,1)S(1)} %get-tuple-element.32), channel_id=1, source_target_pairs={{0,12},{1,13},{2,15},{3,14},{4,0},{5,1},{6,3},{7,2},{8,4},{9,5},{1... | collective-permute-start | bytes 294920 | tf_op jit(solution)/shard_map/ppermute | solution.py:80
  83.5 3.1 %collective-permute-done.21.refs_1_ = bf16[96,512]{1,0:T(8,128)(2,1)S(1)} collective-permute-done((bf16[96,512]{1,0:T(8,128)(2,1)S(1)}, bf16[96,512]{1,0:T(8,128)(2,1)S(1)}, u32[]{:S(2)}, u32[]{:S(2)}) %collective-permute-start.21) | collective-permute-done | bytes 98336 | tf_op jit(solution)/shard_map/ppermute | solution.py:80
  86.6 2.5 %collective-permute-done.22.refs_2_ = bf16[96,512]{1,0:T(8,128)(2,1)S(1)} collective-permute-done((bf16[96,512]{1,0:T(8,128)(2,1)S(1)}, bf16[96,512]{1,0:T(8,128)(2,1)S(1)}, u32[]{:S(2)}, u32[]{:S(2)}) %collective-permute-start.22) | collective-permute-done | bytes 98336 | tf_op jit(solution)/shard_map/ppermute | solution.py:80
  89.1 0.8 join.1
  (27 shorter events, 0.2 us)
Async XLA Ops:
  0.0 29.3 %copy-start.3 = (bf16[1,384,512]{2,1,0:T(8,128)(2,1)S(1)}, bf16[1,384,512]{2,1,0:T(8,128)(2,1)}, u32[]{:S(2)}) copy-start(bf16[1,384,512]{2,1,0:T(8,128)(2,1)} %param.10) | copy-start | bytes 1179652
  1.7 20.1 %collective-permute-start.1 = (bf16[704,512]{1,0:T(8,128)(2,1)S(1)}, bf16[704,512]{1,0:T(8,128)(2,1)S(1)}, u32[]{:S(2)}, u32[]{:S(2)}) collective-permute-start(bf16[704,512]{1,0:T(8,128)(2,1)S(1)} %pack_own.1.refs_4_.refs_0_.refs_1_), channel_id=1, source_target_pairs={{0,4},{1,5},{2,6},{3,7},{4,8},{5,9},{6,10},{7,11},{8,12},{9,13},{1... | collective-permute-start | bytes 2162696 | tf_op jit(solution)/shard_map/ppermute | solution.py:80
  3.9 18.9 %collective-permute-start.5 = (bf16[704,512]{1,0:T(8,128)(2,1)S(1)}, bf16[704,512]{1,0:T(8,128)(2,1)S(1)}, u32[]{:S(2)}, u32[]{:S(2)}) collective-permute-start(bf16[704,512]{1,0:T(8,128)(2,1)S(1)} %pack_own.1.refs_4_.refs_0_.refs_1_), channel_id=1, source_target_pairs={{0,1},{1,0},{2,3},{3,2},{4,5},{5,4},{6,7},{7,6},{8,9},{9,8},{10,11... | collective-permute-start | bytes 2162696 | tf_op jit(solution)/shard_map/ppermute | solution.py:80
  21.7 18.2 %collective-permute-start.2 = (bf16[704,512]{1,0:T(8,128)(2,1)S(1)}, bf16[704,512]{1,0:T(8,128)(2,1)S(1)}, u32[]{:S(2)}, u32[]{:S(2)}) collective-permute-start(bf16[704,512]{1,0:T(8,128)(2,1)S(1)} %collective-permute-done.1.refs_5_.refs_1_.refs_2_), channel_id=1, source_target_pairs={{0,4},{1,5},{2,6},{3,7},{4,8},{5,9},{6,10},{7,11},{8,12},{9,13},{1... | collective-permute-start | bytes 2162696 | tf_op jit(solution)/shard_map/ppermute | solution.py:80
  21.7 24.5 %collective-permute-start.10 = (bf16[704,512]{1,0:T(8,128)(2,1)S(1)}, bf16[704,512]{1,0:T(8,128)(2,1)S(1)}, u32[]{:S(2)}, u32[]{:S(2)}) collective-permute-start(bf16[704,512]{1,0:T(8,128)(2,1)S(1)} %collective-permute-done.1.refs_5_.refs_1_.refs_2_), channel_id=1, source_target_pairs={{0,1},{1,0},{2,3},{3,2},{4,5},{5,4},{6,7},{7,6},{8,9},{9,8},{10,11... | collective-permute-start | bytes 2162696 | tf_op jit(solution)/shard_map/ppermute | solution.py:80
  22.7 24.0 %collective-permute-start.6 = (bf16[704,512]{1,0:T(8,128)(2,1)S(1)}, bf16[704,512]{1,0:T(8,128)(2,1)S(1)}, u32[]{:S(2)}, u32[]{:S(2)}) collective-permute-start(bf16[704,512]{1,0:T(8,128)(2,1)S(1)} %collective-permute-done.5.refs_7_.refs_3_.refs_4_), channel_id=1, source_target_pairs={{0,2},{1,3},{2,0},{3,1},{4,6},{5,7},{6,4},{7,5},{8,10},{9,11},{10,... | collective-permute-start | bytes 2162696 | tf_op jit(solution)/shard_map/ppermute | solution.py:80
  24.5 22.2 %collective-permute-start.4 = (bf16[704,512]{1,0:T(8,128)(2,1)S(1)}, bf16[704,512]{1,0:T(8,128)(2,1)S(1)}, u32[]{:S(2)}, u32[]{:S(2)}) collective-permute-start(bf16[704,512]{1,0:T(8,128)(2,1)S(1)} %collective-permute-done.1.refs_5_.refs_1_.refs_2_), channel_id=1, source_target_pairs={{0,2},{1,3},{2,0},{3,1},{4,6},{5,7},{6,4},{7,5},{8,10},{9,11},{10,... | collective-permute-start | bytes 2162696 | tf_op jit(solution)/shard_map/ppermute | solution.py:80
  24.5 22.2 %collective-permute-start.3 = (bf16[704,512]{1,0:T(8,128)(2,1)S(1)}, bf16[704,512]{1,0:T(8,128)(2,1)S(1)}, u32[]{:S(2)}, u32[]{:S(2)}) collective-permute-start(bf16[704,512]{1,0:T(8,128)(2,1)S(1)} %collective-permute-done.1.refs_5_.refs_1_.refs_2_), channel_id=1, source_target_pairs={{0,16},{1,17},{2,18},{3,19},{4,20},{5,21},{6,22},{7,23},{8,24},{9,... | collective-permute-start | bytes 2162696 | tf_op jit(solution)/shard_map/ppermute | solution.py:80
  39.9 5.6 %collective-permute-start = (bf16[96,512]{1,0:T(8,128)(2,1)S(1)}, bf16[96,512]{1,0:T(8,128)(2,1)S(1)}, u32[]{:S(2)}, u32[]{:S(2)}) collective-permute-start(bf16[96,512]{1,0:T(8,128)(2,1)S(1)} %get-tuple-element.19), channel_id=1, source_target_pairs={{0,0},{1,1},{2,3},{3,2},{4,4},{5,5},{6,7},{7,6},{8,8},{9,9},{10,11... | collective-permute-start | bytes 294920 | tf_op jit(solution)/shard_map/ppermute | solution.py:80
  45.6 13.1 %collective-permute-start.11 = (bf16[528,512]{1,0:T(8,128)(2,1)S(1)}, bf16[528,512]{1,0:T(8,128)(2,1)S(1)}, u32[]{:S(2)}, u32[]{:S(2)}) collective-permute-start(bf16[528,512]{1,0:T(8,128)(2,1)S(1)} %slice.8), channel_id=1, source_target_pairs={{0,1},{1,0},{2,3},{3,2},{4,5},{5,4},{6,7},{7,6},{8,9},{9,8},{10,11... | collective-permute-start | bytes 1622024 | tf_op jit(solution)/shard_map/ppermute | solution.py:80
  46.2 18.5 %collective-permute-start.13 = (bf16[704,512]{1,0:T(8,128)(2,1)S(1)}, bf16[704,512]{1,0:T(8,128)(2,1)S(1)}, u32[]{:S(2)}, u32[]{:S(2)}) collective-permute-start(bf16[704,512]{1,0:T(8,128)(2,1)S(1)} %collective-permute-done.10.refs_8_.refs_4_.refs_5_), channel_id=1, source_target_pairs={{0,16},{1,17},{2,18},{3,19},{4,20},{5,21},{6,22},{7,23},{8,24},{9,... | collective-permute-start | bytes 2162696 | tf_op jit(solution)/shard_map/ppermute | solution.py:80
  46.7 6.3 %collective-permute-start.9 = (bf16[96,512]{1,0:T(8,128)(2,1)S(1)}, bf16[96,512]{1,0:T(8,128)(2,1)S(1)}, u32[]{:S(2)}, u32[]{:S(2)}) collective-permute-start(bf16[96,512]{1,0:T(8,128)(2,1)S(1)} %get-tuple-element.25), channel_id=1, source_target_pairs={{0,12},{1,13},{2,15},{3,14},{4,0},{5,1},{6,3},{7,2},{8,4},{9,5},{1... | collective-permute-start | bytes 294920 | tf_op jit(solution)/shard_map/ppermute | solution.py:80
  50.4 8.4 %collective-permute-start.12 = (bf16[176,512]{1,0:T(8,128)(2,1)S(1)}, bf16[176,512]{1,0:T(8,128)(2,1)S(1)}, u32[]{:S(2)}, u32[]{:S(2)}) collective-permute-start(bf16[176,512]{1,0:T(8,128)(2,1)S(1)} %slice.9), channel_id=1, source_target_pairs={{0,4},{1,5},{2,6},{3,7},{4,8},{5,9},{6,10},{7,11},{8,12},{9,13},{1... | collective-permute-start | bytes 540680 | tf_op jit(solution)/shard_map/ppermute | solution.py:80
  50.5 10.5 %collective-permute-start.7 = (bf16[96,512]{1,0:T(8,128)(2,1)S(1)}, bf16[96,512]{1,0:T(8,128)(2,1)S(1)}, u32[]{:S(2)}, u32[]{:S(2)}) collective-permute-start(bf16[96,512]{1,0:T(8,128)(2,1)S(1)} %get-tuple-element.23), channel_id=1, source_target_pairs={{0,4},{1,5},{2,7},{3,6},{4,8},{5,9},{6,11},{7,10},{8,12},{9,13},{1... | collective-permute-start | bytes 294920 | tf_op jit(solution)/shard_map/ppermute | solution.py:80
  53.0 11.0 %collective-permute-start.8 = (bf16[96,512]{1,0:T(8,128)(2,1)S(1)}, bf16[96,512]{1,0:T(8,128)(2,1)S(1)}, u32[]{:S(2)}, u32[]{:S(2)}) collective-permute-start(bf16[96,512]{1,0:T(8,128)(2,1)S(1)} %get-tuple-element.24), channel_id=1, source_target_pairs={{0,8},{1,9},{2,11},{3,10},{4,12},{5,13},{6,15},{7,14},{8,0},{9,1},... | collective-permute-start | bytes 294920 | tf_op jit(solution)/shard_map/ppermute | solution.py:80
  58.7 7.6 %collective-permute-start.14 = (bf16[704,512]{1,0:T(8,128)(2,1)S(1)}, bf16[704,512]{1,0:T(8,128)(2,1)S(1)}, u32[]{:S(2)}, u32[]{:S(2)}) collective-permute-start(bf16[704,512]{1,0:T(8,128)(2,1)S(1)} %collective-permute-done.2.refs_6_.refs_2_.refs_3_), channel_id=1, source_target_pairs={{0,2},{1,3},{2,0},{3,1},{4,6},{5,7},{6,4},{7,5},{8,10},{9,11},{10,... | collective-permute-start | bytes 2162696 | tf_op jit(solution)/shard_map/ppermute | solution.py:80
  58.9 7.5 %collective-permute-start.15 = (bf16[704,512]{1,0:T(8,128)(2,1)S(1)}, bf16[704,512]{1,0:T(8,128)(2,1)S(1)}, u32[]{:S(2)}, u32[]{:S(2)}) collective-permute-start(bf16[704,512]{1,0:T(8,128)(2,1)S(1)} %collective-permute-done.10.refs_8_.refs_4_.refs_5_), channel_id=1, source_target_pairs={{0,2},{1,3},{2,0},{3,1},{4,6},{5,7},{6,4},{7,5},{8,10},{9,11},{10,... | collective-permute-start | bytes 2162696 | tf_op jit(solution)/shard_map/ppermute | solution.py:80
  59.3 8.2 %copy-start.5 = (f32[2,512]{1,0:T(2,128)S(1)}, f32[2,512]{1,0:T(2,128)}, u32[]{:S(2)}) copy-start(f32[2,512]{1,0:T(2,128)} %gain_ref.6) | copy-start | bytes 12292
  61.0 5.3 %collective-permute-start.17 = (bf16[704,512]{1,0:T(8,128)(2,1)S(1)}, bf16[704,512]{1,0:T(8,128)(2,1)S(1)}, u32[]{:S(2)}, u32[]{:S(2)}) collective-permute-start(bf16[704,512]{1,0:T(8,128)(2,1)S(1)} %collective-permute-done.3.refs_10_.refs_6_.refs_7_), channel_id=1, source_target_pairs={{0,2},{1,3},{2,0},{3,1},{4,6},{5,7},{6,4},{7,5},{8,10},{9,11},{10,... | collective-permute-start | bytes 2162696 | tf_op jit(solution)/shard_map/ppermute | solution.py:80
  64.1 2.4 %collective-permute-start.16 = (bf16[704,512]{1,0:T(8,128)(2,1)S(1)}, bf16[704,512]{1,0:T(8,128)(2,1)S(1)}, u32[]{:S(2)}, u32[]{:S(2)}) collective-permute-start(bf16[704,512]{1,0:T(8,128)(2,1)S(1)} %constant_dynamic-update-slice_fusion.refs_9_.refs_5_.refs_6_), channel_id=1, source_target_pairs={{0,2},{1,3},{2,0},{3,1},{4,6},{5,7},{6,4},{7,5},{8,10},{9,11},{10,... | collective-permute-start | bytes 2162696 | tf_op jit(solution)/shard_map/ppermute | solution.py:80
  64.7 2.8 %collective-permute-start.18 = (bf16[704,512]{1,0:T(8,128)(2,1)S(1)}, bf16[704,512]{1,0:T(8,128)(2,1)S(1)}, u32[]{:S(2)}, u32[]{:S(2)}) collective-permute-start(bf16[704,512]{1,0:T(8,128)(2,1)S(1)} %collective-permute-done.13.refs_11_.refs_7_.refs_8_), channel_id=1, source_target_pairs={{0,2},{1,3},{2,0},{3,1},{4,6},{5,7},{6,4},{7,5},{8,10},{9,11},{10,... | collective-permute-start | bytes 2162696 | tf_op jit(solution)/shard_map/ppermute | solution.py:80
  67.5 0.9 %copy-start.4 = (f32[2,512]{1,0:T(2,128)S(1)}, f32[2,512]{1,0:T(2,128)}, u32[]{:S(2)}) copy-start(f32[2,512]{1,0:T(2,128)} %gain_ref.7) | copy-start | bytes 12292
  67.5 0.9 %copy-start.6 = (f32[512]{0:T(512)S(1)}, f32[512]{0:T(512)}, u32[]{:S(2)}) copy-start(f32[512]{0:T(512)} %param.16) | copy-start | bytes 6148
  71.4 4.0 %copy-start = (bf16[512,512]{1,0:T(8,128)(2,1)S(1)}, bf16[512,512]{1,0:T(8,128)(2,1)}, u32[]{:S(2)}) copy-start(bf16[512,512]{1,0:T(8,128)(2,1)} %value_ref.1) | copy-start | bytes 1572868
  71.4 4.0 %copy-start.1 = (bf16[512,512]{1,0:T(8,128)(2,1)S(1)}, bf16[512,512]{1,0:T(8,128)(2,1)}, u32[]{:S(2)}) copy-start(bf16[512,512]{1,0:T(8,128)(2,1)} %gate_ref.1) | copy-start | bytes 1572868
  71.4 3.9 %copy-start.2 = (bf16[512,512]{1,0:T(8,128)(2,1)S(1)}, bf16[512,512]{1,0:T(8,128)(2,1)}, u32[]{:S(2)}) copy-start(bf16[512,512]{1,0:T(8,128)(2,1)} %out_ref.1) | copy-start | bytes 1572868
  73.6 1.8 %collective-permute-start.19 = (bf16[384,512]{1,0:T(8,128)(2,1)S(1)}, bf16[384,512]{1,0:T(8,128)(2,1)S(1)}, u32[]{:S(2)}, u32[]{:S(2)}) collective-permute-start(bf16[384,512]{1,0:T(8,128)(2,1)S(1)} %ff1.1.final_ref), channel_id=1, source_target_pairs={{0,2},{1,3},{2,0},{3,1},{4,6},{5,7},{6,4},{7,5},{8,10},{9,11},{10,... | collective-permute-start | bytes 1179656 | tf_op jit(solution)/shard_map/ppermute | solution.py:80
  76.4 7.1 %collective-permute-start.20 = (bf16[96,512]{1,0:T(8,128)(2,1)S(1)}, bf16[96,512]{1,0:T(8,128)(2,1)S(1)}, u32[]{:S(2)}, u32[]{:S(2)}) collective-permute-start(bf16[96,512]{1,0:T(8,128)(2,1)S(1)} %get-tuple-element.29), channel_id=1, source_target_pairs={{0,0},{1,1},{2,3},{3,2},{4,4},{5,5},{6,7},{7,6},{8,8},{9,9},{10,11... | collective-permute-start | bytes 294920 | tf_op jit(solution)/shard_map/ppermute | solution.py:80
  79.3 7.3 %collective-permute-start.21 = (bf16[96,512]{1,0:T(8,128)(2,1)S(1)}, bf16[96,512]{1,0:T(8,128)(2,1)S(1)}, u32[]{:S(2)}, u32[]{:S(2)}) collective-permute-start(bf16[96,512]{1,0:T(8,128)(2,1)S(1)} %get-tuple-element.30), channel_id=1, source_target_pairs={{0,4},{1,5},{2,7},{3,6},{4,8},{5,9},{6,11},{7,10},{8,12},{9,13},{1... | collective-permute-start | bytes 294920 | tf_op jit(solution)/shard_map/ppermute | solution.py:80
  79.4 9.8 %collective-permute-start.22 = (bf16[96,512]{1,0:T(8,128)(2,1)S(1)}, bf16[96,512]{1,0:T(8,128)(2,1)S(1)}, u32[]{:S(2)}, u32[]{:S(2)}) collective-permute-start(bf16[96,512]{1,0:T(8,128)(2,1)S(1)} %get-tuple-element.31), channel_id=1, source_target_pairs={{0,8},{1,9},{2,11},{3,10},{4,12},{5,13},{6,15},{7,14},{8,0},{9,1},... | collective-permute-start | bytes 294920 | tf_op jit(solution)/shard_map/ppermute | solution.py:80
  80.4 8.7 %collective-permute-start.23 = (bf16[96,512]{1,0:T(8,128)(2,1)S(1)}, bf16[96,512]{1,0:T(8,128)(2,1)S(1)}, u32[]{:S(2)}, u32[]{:S(2)}) collective-permute-start(bf16[96,512]{1,0:T(8,128)(2,1)S(1)} %get-tuple-element.32), channel_id=1, source_target_pairs={{0,12},{1,13},{2,15},{3,14},{4,0},{5,1},{6,3},{7,2},{8,4},{9,5},{1... | collective-permute-start | bytes 294920 | tf_op jit(solution)/shard_map/ppermute | solution.py:80

commit v5 on v4

--- a/solution.py
+++ b/solution.py
@@ -168,7 +168,7 @@
     i, s = lax.axis_index("seq"), lax.axis_index("strand")
     size = out_refs[0].shape[0]
     for k, out in enumerate(out_refs):
-        j = lax.rem(i + k, n)
+        j = i ^ k
         sub = jnp.where(s == 0, j, n - 1 - j)
         out[...] = rows_ref[pl.ds(pl.multiple_of(sub * size, size), size)]
 
@@ -179,7 +179,7 @@
     i, s = lax.axis_index("seq"), lax.axis_index("strand")
     size = parts[0].shape[0]
     for k, part in enumerate(parts):
-        j = lax.rem(i + n - k, n)
+        j = i ^ k
         sub = jnp.where(s == 0, j, n - 1 - j)
         out[pl.ds(pl.multiple_of(sub * size, size), size)] = part[...]
 
@@ -201,7 +201,7 @@
     if parts > 1:
         size = states[0].shape[0]
         for k, state in enumerate(states):
-            at = lax.rem(j + n - k, n)
+            at = j ^ k
             out[pl.ds(pl.multiple_of(at * size, size), size)] = state[...].astype(F32)
         state = out[...]
     else:
@@ -283,7 +283,7 @@
     gated = (value * jax.nn.sigmoid(mirrored.astype(F32))).astype(BF16)
     result[...] = matmul(gated, out_ref[...]).astype(BF16)
     for k, out in enumerate(outs):
-        at = lax.rem(j + k, n)
+        at = j ^ k
         out[...] = result[pl.ds(pl.multiple_of(at * size, size), size)]
 
 
@@ -302,7 +302,7 @@
     shard = (up_weight, down_weight, turned, turned, up_weight, down_weight)
     which = (0, 0, 0, 1, 1, 1), (True, False, False, False, True, False)
     own = pack(shard, *which, cut + hidden, True)
-    to = lambda k: (lambda g, i, s, c: (g, (i + k) % n, s, c if s == 0 else 1 - c))
+    to = lambda k: (lambda g, i, s, c: (g, i ^ k, s, c if s == 0 else 1 - c))
     parts = pl.pallas_call(
         split_kernel, out_shape=[part] * n, in_specs=[VMEM_SPEC], out_specs=[VMEM_SPEC] * n,
         compiler_params=PARAMS, name="split",
@@ -315,33 +315,45 @@
     ya = planes(a)
     swaps = [other_core(a), other_core(x)]
     states = [moved(parts[0], to(0))]
-    events = [*swaps, states[0]]
-    parts = after(parts, [b, ya, *events])
-    size = cut + hidden
-    yxa = planes(xa)
-    keep = size - 176
-    xb0 = across(b[:keep])
-    xb1 = along(xa[keep:])
-    states += [moved(p, to(k + 1)) for k, p in enumerate(parts[1:])]
-    xb = jnp.concatenate([xb0, xb1], 0)
-    rest = pack(shard, *which, cut + hidden, False)
-    mine = [own, a, b, x, xa, xb, ya, yxa]
-    swap_a, swap_x = swaps
-    bs, xas, yas = after([b, xa, ya], [states[-1]])
-    others = [swap_a, other_core(bs), swap_x, other_core(xas), other_core(xb), other_core(yas), other_core(yxa)]
-    arrays = mine + [rest] + others
-    places = [[(k, 0) for k in range(8)], [(k + 8, 0) for k in range(8)]]
+    first = after(shard[:3], [x])
+    rest = pack((*first[:3], first[2], *first[:2]), *which, cut + hidden, False)
+    b, xa, ya, rest, swaps[0], swaps[1], states[0], *parts = after(
+        [b, xa, ya, rest, *swaps, states[0], *parts[1:]], []
+    )
+    yxa0 = planes(xa[:cut])
+    xb0 = across(b[:cut])
+    states += [moved(p, to(k + 1)) for k, p in enumerate(parts)]
+    bl, xal, yal, xb0, yxa0, *states = after([b, xa, ya, xb0, yxa0, *states], [])
+    sxb0, syxa0 = other_core(xb0), other_core(yxa0)
+    (bs,) = after([bl], [sxb0])
+    xas, yas = after([xal, yal], [syxa0])
+    sb, sxa, sya = other_core(bs), other_core(xas), other_core(yas)
+    yxa1 = planes(xal[cut:])
+    xb1 = across(bl[cut:])
+    mine = [own, a, b, x, xa, ya]
+    others = [rest, swaps[0], sb, swaps[1], sxa, sya]
+    arrays = mine + [xb0, yxa0] + others + [sxb0, syxa0]
+    places = [
+        [(k, 0) for k in (0, 1, 2, 3, 4, 6, 5, 7)],
+        [(8, 0), (9, 0), (10, 0), (11, 0), (12, 0), (14, 0), (13, 0), (15, 0)],
+    ]
+    early = [[(k, 0) for k in range(6)], [(k + 6, 0) for k in range(6)]]
     head = head_norm[None]
-    state = conv(states, conv_norm, arrays, places, 0, hidden, taps)
-    (state,) = feed_forward(state, None, ff_norm, head, arrays, places, 0, 0, half, "state")
-    state = conv([state], conv_norm, arrays, places, 1, hidden + taps * chans // 2, taps)
-    (final,) = feed_forward(state, None, ff_norm, head, arrays, places, 1, cut, half, "head")
+    state = conv0 = conv(states, conv_norm, arrays, places, 0, hidden, taps)
+    (state,) = (ff0,) = feed_forward(state, None, ff_norm, head, arrays, places, 0, 0, half, "state")
+    state = conv1 = conv([state], conv_norm, arrays, places, 1, hidden + taps * chans // 2, taps)
+    state, mixed = feed_forward(state, None, ff_norm, head, mine + others, early, 1, cut, half, "")
+    late = jnp.concatenate(after([xb1, yxa1], [conv1]), 0)
+    places = [[(0, 0), (0, hidden)], [(1, 0), (1, hidden)]]
+    arrays = [late, other_core(late)]
+    (final,) = feed_forward(state, mixed, ff_norm, head, arrays, places, 1, 0, half, "head")
     opposite = other_core(final)
     results = pl.pallas_call(
         head_kernel, out_shape=[part] * n, in_specs=[VMEM_SPEC] * 5, out_specs=[VMEM_SPEC] * n,
         scratch_shapes=[pltpu.VMEM((rows, width), BF16)], compiler_params=PARAMS, name="head",
     )(final, opposite, value_weight, gate_weight, out_weight)
-    home = [moved(r, to(k)) for k, r in enumerate(results)]
+    home = {k: moved(results[k], to(k)) for k in (2, 3, 1, 0)}
+    home = [home[k] for k in range(n)]
     joined = pl.pallas_call(
         join_kernel, out_shape=jax.ShapeDtypeStruct((rows, width), BF16), in_specs=[VMEM_SPEC] * n,
         out_specs=VMEM_SPEC, compiler_params=PARAMS, name="join",

time: 90.1 us -> 88.9 us (0.987)
  waiting for transfers between devices: 49.6 us -> 41.9 us
  starting transfers between devices: 28.9 us -> 35 us
    ppermute x24 -> x26, waiting for transfers between devices: 49.6 us -> 41.9 us  [moved(): return lax.ppermute(value, AXES, pairs)]
    ppermute x24 -> x26, starting transfers between devices: 28.9 us -> 35 us  [moved(): return lax.ppermute(value, AXES, pairs)]
    pallas_call x2 -> x3, Pallas kernels: 4.14 us -> 4.52 us  [feed_forward(): pl.pallas_call(functools.partial(ff_kernel, block, mixed is None, ends, p...]
  transfers between devices with their start and end apart: 24 -> 26, of which waited for: 13 -> 14; matrix products, arithmetic and copies ran while one was open for 0% -> 0% of each run, Pallas kernels for 2% -> 8%
where the time goes in v5:
time: 88.9 us; the launch traced here: 88.7 us
  waiting for transfers between devices  41.9 us (47%)
  starting transfers between devices  35 us (39%)
  Pallas kernels  11.4 us (13%)
    ppermute x26, waiting for transfers between devices, moved(): return lax.ppermute(value, AXES, pairs)  41.9 us
    ppermute x26, starting transfers between devices, moved(): return lax.ppermute(value, AXES, pairs)  35 us
    pallas_call x3, Pallas kernels, feed_forward(): pl.pallas_call(functools.partial(ff_kernel, block, mixed is None, ends, p...  4.52 us
    pallas_call x2, Pallas kernels, pack(): pl.pallas_call(functools.partial(pack_kernel, (blocks, turned), mine), ou...  3.28 us
  transfers between devices with their start and end apart: 26, of which 14 were waited for; matrix products, arithmetic and copies ran while one was open for 0% of the time, Pallas kernels for 8%

profile of v5, /device:TPU:1, one launch (start us, length us, event | category | flops | bytes accessed | tf_op | source)
XLA Modules:
  0.0 88.7 jit_solution(13893091344694065788)
XLA Ops:
  0.0 1.7 %pack_own.1.refs_4_.refs_0_.refs_1_ = bf16[704,512]{1,0:T(8,128)(2,1)S(1)} custom-call(bf16[2,512,256]{2,1,0:T(8,128)(2,1)} %refs_4_.2, bf16[2,256,512]{2,1,0:T(8,128)(2,1)} %refs_5_.2, bf16[2,3,64,512]{3,2,1,0:T(8,128)(2,1)} %bitcast.8, bf16[2,3,64,512]{3,2,1,0:T(8,128)(2,1)} %bitcast.9, bf16[2,512,256]{2,1,0:T(8,128)(2,1)} %refs_4_.2, ...), custom_call_target="tpu_custom_call" | custom-call | tf_op jit(solution)/shard_map/pack_own/pallas_call | solution.py:152
  1.7 2.2 %collective-permute-start = (bf16[704,512]{1,0:T(8,128)(2,1)S(1)}, bf16[704,512]{1,0:T(8,128)(2,1)S(1)}, u32[]{:S(2)}, u32[]{:S(2)}) collective-permute-start(bf16[704,512]{1,0:T(8,128)(2,1)S(1)} %pack_own.1.refs_4_.refs_0_.refs_1_), channel_id=1, source_target_pairs={{0,4},{1,5},{2,6},{3,7},{4,8},{5,9},{6,10},{7,11},{8,12},{9,13},{1... | collective-permute-start | bytes 2162696 | tf_op jit(solution)/shard_map/ppermute | solution.py:80
  3.9 1.2 %collective-permute-start.4 = (bf16[704,512]{1,0:T(8,128)(2,1)S(1)}, bf16[704,512]{1,0:T(8,128)(2,1)S(1)}, u32[]{:S(2)}, u32[]{:S(2)}) collective-permute-start(bf16[704,512]{1,0:T(8,128)(2,1)S(1)} %pack_own.1.refs_4_.refs_0_.refs_1_), channel_id=1, source_target_pairs={{0,1},{1,0},{2,3},{3,2},{4,5},{5,4},{6,7},{7,6},{8,9},{9,8},{10,11... | collective-permute-start | bytes 2162696 | tf_op jit(solution)/shard_map/ppermute | solution.py:80
  5.1 2.2 %collective-permute-start.7 = (bf16[96,512]{1,0:T(8,128)(2,1)S(1)}, bf16[96,512]{1,0:T(8,128)(2,1)S(1)}, u32[]{:S(2)}, u32[]{:S(2)}) collective-permute-start(bf16[96,512]{1,0:T(8,128)(2,1)S(1)} %get-tuple-element.45), channel_id=1, source_target_pairs={{0,0},{1,1},{2,3},{3,2},{4,4},{5,5},{6,7},{7,6},{8,8},{9,9},{10,11... | collective-permute-start | bytes 294920 | tf_op jit(solution)/shard_map/ppermute | solution.py:80
  7.3 14.5 %collective-permute-done.refs_5_.refs_1_.refs_2_ = bf16[704,512]{1,0:T(8,128)(2,1)S(1)} collective-permute-done((bf16[704,512]{1,0:T(8,128)(2,1)S(1)}, bf16[704,512]{1,0:T(8,128)(2,1)S(1)}, u32[]{:S(2)}, u32[]{:S(2)}) %collective-permute-start) | collective-permute-done | bytes 720928 | tf_op jit(solution)/shard_map/ppermute | solution.py:80
  21.7 1.0 %collective-permute-start.2 = (bf16[704,512]{1,0:T(8,128)(2,1)S(1)}, bf16[704,512]{1,0:T(8,128)(2,1)S(1)}, u32[]{:S(2)}, u32[]{:S(2)}) collective-permute-start(bf16[704,512]{1,0:T(8,128)(2,1)S(1)} %collective-permute-done.refs_5_.refs_1_.refs_2_), channel_id=1, source_target_pairs={{0,1},{1,0},{2,3},{3,2},{4,5},{5,4},{6,7},{7,6},{8,9},{9,8},{10,11... | collective-permute-start | bytes 2162696 | tf_op jit(solution)/shard_map/ppermute | solution.py:80
  22.7 4.4 %collective-permute-start.3 = (bf16[704,512]{1,0:T(8,128)(2,1)S(1)}, bf16[704,512]{1,0:T(8,128)(2,1)S(1)}, u32[]{:S(2)}, u32[]{:S(2)}) collective-permute-start(bf16[704,512]{1,0:T(8,128)(2,1)S(1)} %collective-permute-done.refs_5_.refs_1_.refs_2_), channel_id=1, source_target_pairs={{0,16},{1,17},{2,18},{3,19},{4,20},{5,21},{6,22},{7,23},{8,24},{9,... | collective-permute-start | bytes 2162696 | tf_op jit(solution)/shard_map/ppermute | solution.py:80
  27.1 2.4 %collective-permute-start.5 = (bf16[704,512]{1,0:T(8,128)(2,1)S(1)}, bf16[704,512]{1,0:T(8,128)(2,1)S(1)}, u32[]{:S(2)}, u32[]{:S(2)}) collective-permute-start(bf16[704,512]{1,0:T(8,128)(2,1)S(1)} %collective-permute-done.refs_5_.refs_1_.refs_2_), channel_id=1, source_target_pairs={{0,2},{1,3},{2,0},{3,1},{4,6},{5,7},{6,4},{7,5},{8,10},{9,11},{10,... | collective-permute-start | bytes 2162696 | tf_op jit(solution)/shard_map/ppermute | solution.py:80
  29.5 0.1 collective-permute-start.6
  29.6 1.6 %pack_rest.1.refs_12_.refs_8_.refs_9_.refs_6_ = bf16[704,512]{1,0:T(8,128)(2,1)S(1)} custom-call(bf16[2,512,256]{2,1,0:T(8,128)(2,1)} %refs_4_.2, bf16[2,256,512]{2,1,0:T(8,128)(2,1)} %refs_5_.2, bf16[2,3,64,512]{3,2,1,0:T(8,128)(2,1)} %bitcast.10, bf16[2,3,64,512]{3,2,1,0:T(8,128)(2,1)} %bitcast.11, bf16[2,512,256]{2,1,0:T(8,128)(2,1)} %refs_4_.2, ...), custom_call_target="tpu_custom_call" | custom-call | tf_op jit(solution)/shard_map/pack_rest/pallas_call | solution.py:152
  31.2 8.7 %collective-permute-done.1.refs_6_.refs_2_.refs_3_ = bf16[704,512]{1,0:T(8,128)(2,1)S(1)} collective-permute-done((bf16[704,512]{1,0:T(8,128)(2,1)S(1)}, bf16[704,512]{1,0:T(8,128)(2,1)S(1)}, u32[]{:S(2)}, u32[]{:S(2)}) %collective-permute-start.1) | collective-permute-done | bytes 720928 | tf_op jit(solution)/shard_map/ppermute | solution.py:80
  39.9 1.5 %collective-permute-done.3.refs_9_.refs_5_.refs_6_ = bf16[704,512]{1,0:T(8,128)(2,1)S(1)} collective-permute-done((bf16[704,512]{1,0:T(8,128)(2,1)S(1)}, bf16[704,512]{1,0:T(8,128)(2,1)S(1)}, u32[]{:S(2)}, u32[]{:S(2)}) %collective-permute-start.3) | collective-permute-done | bytes 720928 | tf_op jit(solution)/shard_map/ppermute | solution.py:80
  41.5 0.3 collective-permute-start.8
  41.9 1.3 %collective-permute-start.9 = (bf16[448,512]{1,0:T(8,128)(2,1)S(1)}, bf16[448,512]{1,0:T(8,128)(2,1)S(1)}, u32[]{:S(2)}, u32[]{:S(2)}) collective-permute-start(bf16[448,512]{1,0:T(8,128)(2,1)S(1)} %slice.13), channel_id=1, source_target_pairs={{0,16},{1,17},{2,18},{3,19},{4,20},{5,21},{6,22},{7,23},{8,24},{9,... | collective-permute-start | bytes 1376264 | tf_op jit(solution)/shard_map/ppermute | solution.py:80
  43.2 3.3 %collective-permute-start.11 = (bf16[96,512]{1,0:T(8,128)(2,1)S(1)}, bf16[96,512]{1,0:T(8,128)(2,1)S(1)}, u32[]{:S(2)}, u32[]{:S(2)}) collective-permute-start(bf16[96,512]{1,0:T(8,128)(2,1)S(1)} %get-tuple-element.54), channel_id=1, source_target_pairs={{0,8},{1,9},{2,11},{3,10},{4,12},{5,13},{6,15},{7,14},{8,0},{9,1},... | collective-permute-start | bytes 294920 | tf_op jit(solution)/shard_map/ppermute | solution.py:80
  46.4 2.1 %collective-permute-start.12 = (bf16[96,512]{1,0:T(8,128)(2,1)S(1)}, bf16[96,512]{1,0:T(8,128)(2,1)S(1)}, u32[]{:S(2)}, u32[]{:S(2)}) collective-permute-start(bf16[96,512]{1,0:T(8,128)(2,1)S(1)} %get-tuple-element.55), channel_id=1, source_target_pairs={{0,12},{1,13},{2,15},{3,14},{4,8},{5,9},{6,11},{7,10},{8,4},{9,5},... | collective-permute-start | bytes 294920 | tf_op jit(solution)/shard_map/ppermute | solution.py:80
  48.5 0.2 collective-permute-done.10.refs_1_
  48.7 4.1 %collective-permute-done.12.refs_3_ = bf16[96,512]{1,0:T(8,128)(2,1)S(1)} collective-permute-done((bf16[96,512]{1,0:T(8,128)(2,1)S(1)}, bf16[96,512]{1,0:T(8,128)(2,1)S(1)}, u32[]{:S(2)}, u32[]{:S(2)}) %collective-permute-start.12) | collective-permute-done | bytes 98336 | tf_op jit(solution)/shard_map/ppermute | solution.py:80
  52.8 1.9 %collective-permute-done.8.refs_10_.refs_6_.refs_7_ = bf16[448,512]{1,0:T(8,128)(2,1)S(1)} collective-permute-done((bf16[448,512]{1,0:T(8,128)(2,1)S(1)}, bf16[448,512]{1,0:T(8,128)(2,1)S(1)}, u32[]{:S(2)}, u32[]{:S(2)}) %collective-permute-start.8) | collective-permute-done | bytes 458784 | tf_op jit(solution)/shard_map/ppermute | solution.py:80
  54.6 3.0 %collective-permute-start.15 = (bf16[448,512]{1,0:T(8,128)(2,1)S(1)}, bf16[448,512]{1,0:T(8,128)(2,1)S(1)}, u32[]{:S(2)}, u32[]{:S(2)}) collective-permute-start(bf16[448,512]{1,0:T(8,128)(2,1)S(1)} %collective-permute-done.9.refs_11_.refs_7_.refs_8_), channel_id=1, source_target_pairs={{0,2},{1,3},{2,0},{3,1},{4,6},{5,7},{6,4},{7,5},{8,10},{9,11},{10,... | collective-permute-start | bytes 1376264 | tf_op jit(solution)/shard_map/ppermute | solution.py:80
  57.7 1.4 %collective-permute-done.15.refs_19_.refs_15_.refs_16_ = bf16[448,512]{1,0:T(8,128)(2,1)S(1)} collective-permute-done((bf16[448,512]{1,0:T(8,128)(2,1)S(1)}, bf16[448,512]{1,0:T(8,128)(2,1)S(1)}, u32[]{:S(2)}, u32[]{:S(2)}) %collective-permute-start.15) | collective-permute-done | bytes 458784 | tf_op jit(solution)/shard_map/ppermute | solution.py:80
  59.1 0.4 collective-permute-start.16
  59.5 0.1 collective-permute-start.17
  59.6 0.1 collective-permute-done.13.refs_18_.refs_14_.refs_15_
  59.8 0.4 collective-permute-start.14
  60.2 0.0 copy-start.6
  60.2 0.3 collective-permute-start.18
  60.5 1.2 %collective-permute-start.19 = (bf16[256,512]{1,0:T(8,128)(2,1)S(1)}, bf16[256,512]{1,0:T(8,128)(2,1)S(1)}, u32[]{:S(2)}, u32[]{:S(2)}) collective-permute-start(bf16[256,512]{1,0:T(8,128)(2,1)S(1)} %slice.15), channel_id=1, source_target_pairs={{0,16},{1,17},{2,18},{3,19},{4,20},{5,21},{6,22},{7,23},{8,24},{9,... | collective-permute-start | bytes 786440 | tf_op jit(solution)/shard_map/ppermute | solution.py:80
  61.8 0.6 collective-permute-done.17.refs_17_.refs_13_.refs_14_.refs_11_
  62.4 1.0 %collective-permute-done.14.refs_14_.refs_10_.refs_11_.refs_8_ = bf16[704,512]{1,0:T(8,128)(2,1)S(1)} collective-permute-done((bf16[704,512]{1,0:T(8,128)(2,1)S(1)}, bf16[704,512]{1,0:T(8,128)(2,1)S(1)}, u32[]{:S(2)}, u32[]{:S(2)}) %collective-permute-start.14) | collective-permute-done | bytes 720928 | tf_op jit(solution)/shard_map/ppermute | solution.py:80
  63.4 0.9 %conv0.1.state_ref = f32[384,512]{1,0:T(8,128)S(1)} custom-call(f32[2,512]{1,0:T(2,128)S(1)} %copy-done.6, bf16[96,512]{1,0:T(8,128)(2,1)S(1)} %collective-permute-done.7.refs_0_, bf16[96,512]{1,0:T(8,128)(2,1)S(1)} %collective-permute-done.10.refs_1_, bf16[96,512]{1,0:T(8,128)(2,1)S(1)} %collective-permute-done.11.refs_2_, ...), custom_call_target="tpu_custom_call" | custom-call | tf_op jit(solution)/shard_map/conv0/pallas_call | solution.py:220
  64.3 2.0 %ff0.1.refs_0_ = f32[384,512]{1,0:T(8,128)S(1)} custom-call(f32[2,512]{1,0:T(2,128)S(1)} %copy-done.4, f32[1,512]{1,0:T(1,128)S(1)} %bitcast.5, f32[384,512]{1,0:T(8,128)S(1)} %conv0.1.state_ref, bf16[704,512]{1,0:T(8,128)(2,1)S(1)} %pack_own.1.refs_4_.refs_0_.refs_1_, bf16[704,512]{1,0:T(8,128)(2,1)S(1)} %collective-permute-done.refs_5_.refs_1_.refs_2_, ...), custom_call_target="tpu_custom_call" | custom-call | tf_op jit(solution)/shard_map/ff0/pallas_call | solution.py:259
  66.3 0.9 conv1.1.state_ref
  67.2 0.8 collective-permute-done.18
  68.1 1.3 %collective-permute-start.20 = (bf16[512,512]{1,0:T(8,128)(2,1)S(1)}, bf16[512,512]{1,0:T(8,128)(2,1)S(1)}, u32[]{:S(2)}, u32[]{:S(2)}) collective-permute-start(bf16[512,512]{1,0:T(8,128)(2,1)S(1)} %constant_dynamic-update-slice_fusion.refs_1_), channel_id=1, source_target_pairs={{0,2},{1,3},{2,0},{3,1},{4,6},{5,7},{6,4},{7,5},{8,10},{9,11},{10,... | collective-permute-start | bytes 1572872 | tf_op jit(solution)/shard_map/ppermute | solution.py:80
  69.4 1.6 %ff1.2 = (f32[384,512]{1,0:T(8,128)S(1)}, bf16[384,512]{1,0:T(8,128)(2,1)S(1)}) custom-call(f32[2,512]{1,0:T(2,128)S(1)} %copy-done.4, f32[1,512]{1,0:T(1,128)S(1)} %bitcast.6, f32[384,512]{1,0:T(8,128)S(1)} %conv1.1.state_ref, bf16[704,512]{1,0:T(8,128)(2,1)S(1)} %pack_own.1.refs_4_.refs_0_.refs_1_, ...), custom_call_target="tpu_custom_call" | custom-call | tf_op jit(solution)/shard_map/ff1/pallas_call | solution.py:259
  71.0 0.0 copy-start
  71.0 0.9 ff1.3.final_ref
  71.9 0.3 collective-permute-start.21
  72.2 1.5 %collective-permute-done.21.opposite_ref = bf16[384,512]{1,0:T(8,128)(2,1)S(1)} collective-permute-done((bf16[384,512]{1,0:T(8,128)(2,1)S(1)}, bf16[384,512]{1,0:T(8,128)(2,1)S(1)}, u32[]{:S(2)}, u32[]{:S(2)}) %collective-permute-start.21) | collective-permute-done | bytes 393248 | tf_op jit(solution)/shard_map/ppermute | solution.py:80
  73.7 1.0 %head.1 = (bf16[96,512]{1,0:T(8,128)(2,1)S(1)}, bf16[96,512]{1,0:T(8,128)(2,1)S(1)}, bf16[96,512]{1,0:T(8,128)(2,1)S(1)}, bf16[96,512]{1,0:T(8,128)(2,1)S(1)}) custom-call(bf16[384,512]{1,0:T(8,128)(2,1)S(1)} %ff1.3.final_ref, bf16[384,512]{1,0:T(8,128)(2,1)S(1)} %collective-permute-done.21.opposite_ref, bf16[512,512]{1,0:T(8,128)(2,1)S(1)} %copy-done, ...), custom_call_target="tpu_custom_call" | custom-call | tf_op jit(solution)/shard_map/head/pallas_call | solution.py:351
  74.8 3.1 %collective-permute-start.22 = (bf16[96,512]{1,0:T(8,128)(2,1)S(1)}, bf16[96,512]{1,0:T(8,128)(2,1)S(1)}, u32[]{:S(2)}, u32[]{:S(2)}) collective-permute-start(bf16[96,512]{1,0:T(8,128)(2,1)S(1)} %get-tuple-element.75), channel_id=1, source_target_pairs={{0,0},{1,1},{2,3},{3,2},{4,4},{5,5},{6,7},{7,6},{8,8},{9,9},{10,11... | collective-permute-start | bytes 294920 | tf_op jit(solution)/shard_map/ppermute | solution.py:80
  77.9 0.1 collective-permute-start.23
  78.0 2.0 %collective-permute-start.24 = (bf16[96,512]{1,0:T(8,128)(2,1)S(1)}, bf16[96,512]{1,0:T(8,128)(2,1)S(1)}, u32[]{:S(2)}, u32[]{:S(2)}) collective-permute-start(bf16[96,512]{1,0:T(8,128)(2,1)S(1)} %get-tuple-element.77), channel_id=1, source_target_pairs={{0,8},{1,9},{2,11},{3,10},{4,12},{5,13},{6,15},{7,14},{8,0},{9,1},... | collective-permute-start | bytes 294920 | tf_op jit(solution)/shard_map/ppermute | solution.py:80
  80.0 2.3 %collective-permute-start.25 = (bf16[96,512]{1,0:T(8,128)(2,1)S(1)}, bf16[96,512]{1,0:T(8,128)(2,1)S(1)}, u32[]{:S(2)}, u32[]{:S(2)}) collective-permute-start(bf16[96,512]{1,0:T(8,128)(2,1)S(1)} %get-tuple-element.78), channel_id=1, source_target_pairs={{0,12},{1,13},{2,15},{3,14},{4,8},{5,9},{6,11},{7,10},{8,4},{9,5},... | collective-permute-start | bytes 294920 | tf_op jit(solution)/shard_map/ppermute | solution.py:80
  82.4 0.3 collective-permute-done.23.refs_1_
  82.7 5.2 %collective-permute-done.24.refs_2_ = bf16[96,512]{1,0:T(8,128)(2,1)S(1)} collective-permute-done((bf16[96,512]{1,0:T(8,128)(2,1)S(1)}, bf16[96,512]{1,0:T(8,128)(2,1)S(1)}, u32[]{:S(2)}, u32[]{:S(2)}) %collective-permute-start.24) | collective-permute-done | bytes 98336 | tf_op jit(solution)/shard_map/ppermute | solution.py:80
  87.9 0.8 join.1
  (34 shorter events, 0.2 us)
Async XLA Ops:
  0.0 5.1 %copy-start.3 = (bf16[1,384,512]{2,1,0:T(8,128)(2,1)S(1)}, bf16[1,384,512]{2,1,0:T(8,128)(2,1)}, u32[]{:S(2)}) copy-start(bf16[1,384,512]{2,1,0:T(8,128)(2,1)} %param.10) | copy-start | bytes 1179652
  1.7 20.1 %collective-permute-start = (bf16[704,512]{1,0:T(8,128)(2,1)S(1)}, bf16[704,512]{1,0:T(8,128)(2,1)S(1)}, u32[]{:S(2)}, u32[]{:S(2)}) collective-permute-start(bf16[704,512]{1,0:T(8,128)(2,1)S(1)} %pack_own.1.refs_4_.refs_0_.refs_1_), channel_id=1, source_target_pairs={{0,4},{1,5},{2,6},{3,7},{4,8},{5,9},{6,10},{7,11},{8,12},{9,13},{1... | collective-permute-start | bytes 2162696 | tf_op jit(solution)/shard_map/ppermute | solution.py:80
  3.9 25.7 %collective-permute-start.4 = (bf16[704,512]{1,0:T(8,128)(2,1)S(1)}, bf16[704,512]{1,0:T(8,128)(2,1)S(1)}, u32[]{:S(2)}, u32[]{:S(2)}) collective-permute-start(bf16[704,512]{1,0:T(8,128)(2,1)S(1)} %pack_own.1.refs_4_.refs_0_.refs_1_), channel_id=1, source_target_pairs={{0,1},{1,0},{2,3},{3,2},{4,5},{5,4},{6,7},{7,6},{8,9},{9,8},{10,11... | collective-permute-start | bytes 2162696 | tf_op jit(solution)/shard_map/ppermute | solution.py:80
  5.1 22.0 %collective-permute-start.7 = (bf16[96,512]{1,0:T(8,128)(2,1)S(1)}, bf16[96,512]{1,0:T(8,128)(2,1)S(1)}, u32[]{:S(2)}, u32[]{:S(2)}) collective-permute-start(bf16[96,512]{1,0:T(8,128)(2,1)S(1)} %get-tuple-element.45), channel_id=1, source_target_pairs={{0,0},{1,1},{2,3},{3,2},{4,4},{5,5},{6,7},{7,6},{8,8},{9,9},{10,11... | collective-permute-start | bytes 294920 | tf_op jit(solution)/shard_map/ppermute | solution.py:80
  21.7 18.2 %collective-permute-start.1 = (bf16[704,512]{1,0:T(8,128)(2,1)S(1)}, bf16[704,512]{1,0:T(8,128)(2,1)S(1)}, u32[]{:S(2)}, u32[]{:S(2)}) collective-permute-start(bf16[704,512]{1,0:T(8,128)(2,1)S(1)} %collective-permute-done.refs_5_.refs_1_.refs_2_), channel_id=1, source_target_pairs={{0,4},{1,5},{2,6},{3,7},{4,8},{5,9},{6,10},{7,11},{8,12},{9,13},{1... | collective-permute-start | bytes 2162696 | tf_op jit(solution)/shard_map/ppermute | solution.py:80
  21.7 18.2 %collective-permute-start.2 = (bf16[704,512]{1,0:T(8,128)(2,1)S(1)}, bf16[704,512]{1,0:T(8,128)(2,1)S(1)}, u32[]{:S(2)}, u32[]{:S(2)}) collective-permute-start(bf16[704,512]{1,0:T(8,128)(2,1)S(1)} %collective-permute-done.refs_5_.refs_1_.refs_2_), channel_id=1, source_target_pairs={{0,1},{1,0},{2,3},{3,2},{4,5},{5,4},{6,7},{7,6},{8,9},{9,8},{10,11... | collective-permute-start | bytes 2162696 | tf_op jit(solution)/shard_map/ppermute | solution.py:80
  22.7 18.8 %collective-permute-start.3 = (bf16[704,512]{1,0:T(8,128)(2,1)S(1)}, bf16[704,512]{1,0:T(8,128)(2,1)S(1)}, u32[]{:S(2)}, u32[]{:S(2)}) collective-permute-start(bf16[704,512]{1,0:T(8,128)(2,1)S(1)} %collective-permute-done.refs_5_.refs_1_.refs_2_), channel_id=1, source_target_pairs={{0,16},{1,17},{2,18},{3,19},{4,20},{5,21},{6,22},{7,23},{8,24},{9,... | collective-permute-start | bytes 2162696 | tf_op jit(solution)/shard_map/ppermute | solution.py:80
  27.1 14.3 %collective-permute-start.5 = (bf16[704,512]{1,0:T(8,128)(2,1)S(1)}, bf16[704,512]{1,0:T(8,128)(2,1)S(1)}, u32[]{:S(2)}, u32[]{:S(2)}) collective-permute-start(bf16[704,512]{1,0:T(8,128)(2,1)S(1)} %collective-permute-done.refs_5_.refs_1_.refs_2_), channel_id=1, source_target_pairs={{0,2},{1,3},{2,0},{3,1},{4,6},{5,7},{6,4},{7,5},{8,10},{9,11},{10,... | collective-permute-start | bytes 2162696 | tf_op jit(solution)/shard_map/ppermute | solution.py:80
  29.5 12.0 %collective-permute-start.6 = (bf16[704,512]{1,0:T(8,128)(2,1)S(1)}, bf16[704,512]{1,0:T(8,128)(2,1)S(1)}, u32[]{:S(2)}, u32[]{:S(2)}) collective-permute-start(bf16[704,512]{1,0:T(8,128)(2,1)S(1)} %collective-permute-done.4.refs_7_.refs_3_.refs_4_), channel_id=1, source_target_pairs={{0,2},{1,3},{2,0},{3,1},{4,6},{5,7},{6,4},{7,5},{8,10},{9,11},{10,... | collective-permute-start | bytes 2162696 | tf_op jit(solution)/shard_map/ppermute | solution.py:80
  41.5 13.1 %collective-permute-start.8 = (bf16[448,512]{1,0:T(8,128)(2,1)S(1)}, bf16[448,512]{1,0:T(8,128)(2,1)S(1)}, u32[]{:S(2)}, u32[]{:S(2)}) collective-permute-start(bf16[448,512]{1,0:T(8,128)(2,1)S(1)} %slice.12), channel_id=1, source_target_pairs={{0,1},{1,0},{2,3},{3,2},{4,5},{5,4},{6,7},{7,6},{8,9},{9,8},{10,11... | collective-permute-start | bytes 1376264 | tf_op jit(solution)/shard_map/ppermute | solution.py:80
  41.9 12.8 %collective-permute-start.9 = (bf16[448,512]{1,0:T(8,128)(2,1)S(1)}, bf16[448,512]{1,0:T(8,128)(2,1)S(1)}, u32[]{:S(2)}, u32[]{:S(2)}) collective-permute-start(bf16[448,512]{1,0:T(8,128)(2,1)S(1)} %slice.13), channel_id=1, source_target_pairs={{0,16},{1,17},{2,18},{3,19},{4,20},{5,21},{6,22},{7,23},{8,24},{9,... | collective-permute-start | bytes 1376264 | tf_op jit(solution)/shard_map/ppermute | solution.py:80
  43.2 5.5 %collective-permute-start.10 = (bf16[96,512]{1,0:T(8,128)(2,1)S(1)}, bf16[96,512]{1,0:T(8,128)(2,1)S(1)}, u32[]{:S(2)}, u32[]{:S(2)}) collective-permute-start(bf16[96,512]{1,0:T(8,128)(2,1)S(1)} %get-tuple-element.53), channel_id=1, source_target_pairs={{0,4},{1,5},{2,7},{3,6},{4,0},{5,1},{6,3},{7,2},{8,12},{9,13},{10,... | collective-permute-start | bytes 294920 | tf_op jit(solution)/shard_map/ppermute | solution.py:80
  43.2 5.5 %collective-permute-start.11 = (bf16[96,512]{1,0:T(8,128)(2,1)S(1)}, bf16[96,512]{1,0:T(8,128)(2,1)S(1)}, u32[]{:S(2)}, u32[]{:S(2)}) collective-permute-start(bf16[96,512]{1,0:T(8,128)(2,1)S(1)} %get-tuple-element.54), channel_id=1, source_target_pairs={{0,8},{1,9},{2,11},{3,10},{4,12},{5,13},{6,15},{7,14},{8,0},{9,1},... | collective-permute-start | bytes 294920 | tf_op jit(solution)/shard_map/ppermute | solution.py:80
  46.4 6.4 %collective-permute-start.12 = (bf16[96,512]{1,0:T(8,128)(2,1)S(1)}, bf16[96,512]{1,0:T(8,128)(2,1)S(1)}, u32[]{:S(2)}, u32[]{:S(2)}) collective-permute-start(bf16[96,512]{1,0:T(8,128)(2,1)S(1)} %get-tuple-element.55), channel_id=1, source_target_pairs={{0,12},{1,13},{2,15},{3,14},{4,8},{5,9},{6,11},{7,10},{8,4},{9,5},... | collective-permute-start | bytes 294920 | tf_op jit(solution)/shard_map/ppermute | solution.py:80
  54.6 4.5 %collective-permute-start.15 = (bf16[448,512]{1,0:T(8,128)(2,1)S(1)}, bf16[448,512]{1,0:T(8,128)(2,1)S(1)}, u32[]{:S(2)}, u32[]{:S(2)}) collective-permute-start(bf16[448,512]{1,0:T(8,128)(2,1)S(1)} %collective-permute-done.9.refs_11_.refs_7_.refs_8_), channel_id=1, source_target_pairs={{0,2},{1,3},{2,0},{3,1},{4,6},{5,7},{6,4},{7,5},{8,10},{9,11},{10,... | collective-permute-start | bytes 1376264 | tf_op jit(solution)/shard_map/ppermute | solution.py:80
  57.7 2.1 %collective-permute-start.13 = (bf16[448,512]{1,0:T(8,128)(2,1)S(1)}, bf16[448,512]{1,0:T(8,128)(2,1)S(1)}, u32[]{:S(2)}, u32[]{:S(2)}) collective-permute-start(bf16[448,512]{1,0:T(8,128)(2,1)S(1)} %collective-permute-done.8.refs_10_.refs_6_.refs_7_), channel_id=1, source_target_pairs={{0,2},{1,3},{2,0},{3,1},{4,6},{5,7},{6,4},{7,5},{8,10},{9,11},{10,... | collective-permute-start | bytes 1376264 | tf_op jit(solution)/shard_map/ppermute | solution.py:80
  59.1 2.6 %collective-permute-start.16 = (bf16[704,512]{1,0:T(8,128)(2,1)S(1)}, bf16[704,512]{1,0:T(8,128)(2,1)S(1)}, u32[]{:S(2)}, u32[]{:S(2)}) collective-permute-start(bf16[704,512]{1,0:T(8,128)(2,1)S(1)} %collective-permute-done.2.refs_8_.refs_4_.refs_5_), channel_id=1, source_target_pairs={{0,2},{1,3},{2,0},{3,1},{4,6},{5,7},{6,4},{7,5},{8,10},{9,11},{10,... | collective-permute-start | bytes 2162696 | tf_op jit(solution)/shard_map/ppermute | solution.py:80
  59.5 2.8 %collective-permute-start.17 = (bf16[704,512]{1,0:T(8,128)(2,1)S(1)}, bf16[704,512]{1,0:T(8,128)(2,1)S(1)}, u32[]{:S(2)}, u32[]{:S(2)}) collective-permute-start(bf16[704,512]{1,0:T(8,128)(2,1)S(1)} %collective-permute-done.3.refs_9_.refs_5_.refs_6_), channel_id=1, source_target_pairs={{0,2},{1,3},{2,0},{3,1},{4,6},{5,7},{6,4},{7,5},{8,10},{9,11},{10,... | collective-permute-start | bytes 2162696 | tf_op jit(solution)/shard_map/ppermute | solution.py:80
  59.8 3.6 %collective-permute-start.14 = (bf16[704,512]{1,0:T(8,128)(2,1)S(1)}, bf16[704,512]{1,0:T(8,128)(2,1)S(1)}, u32[]{:S(2)}, u32[]{:S(2)}) collective-permute-start(bf16[704,512]{1,0:T(8,128)(2,1)S(1)} %collective-permute-done.1.refs_6_.refs_2_.refs_3_), channel_id=1, source_target_pairs={{0,2},{1,3},{2,0},{3,1},{4,6},{5,7},{6,4},{7,5},{8,10},{9,11},{10,... | collective-permute-start | bytes 2162696 | tf_op jit(solution)/shard_map/ppermute | solution.py:80
  60.2 3.2 %copy-start.6 = (f32[2,512]{1,0:T(2,128)S(1)}, f32[2,512]{1,0:T(2,128)}, u32[]{:S(2)}) copy-start(f32[2,512]{1,0:T(2,128)} %gain_ref.7) | copy-start | bytes 12292
  60.2 7.8 %collective-permute-start.18 = (bf16[256,512]{1,0:T(8,128)(2,1)S(1)}, bf16[256,512]{1,0:T(8,128)(2,1)S(1)}, u32[]{:S(2)}, u32[]{:S(2)}) collective-permute-start(bf16[256,512]{1,0:T(8,128)(2,1)S(1)} %slice.14), channel_id=1, source_target_pairs={{0,1},{1,0},{2,3},{3,2},{4,5},{5,4},{6,7},{7,6},{8,9},{9,8},{10,11... | collective-permute-start | bytes 786440 | tf_op jit(solution)/shard_map/ppermute | solution.py:80
  60.5 7.5 %collective-permute-start.19 = (bf16[256,512]{1,0:T(8,128)(2,1)S(1)}, bf16[256,512]{1,0:T(8,128)(2,1)S(1)}, u32[]{:S(2)}, u32[]{:S(2)}) collective-permute-start(bf16[256,512]{1,0:T(8,128)(2,1)S(1)} %slice.15), channel_id=1, source_target_pairs={{0,16},{1,17},{2,18},{3,19},{4,20},{5,21},{6,22},{7,23},{8,24},{9,... | collective-permute-start | bytes 786440 | tf_op jit(solution)/shard_map/ppermute | solution.py:80
  63.4 0.9 %copy-start.4 = (f32[2,512]{1,0:T(2,128)S(1)}, f32[2,512]{1,0:T(2,128)}, u32[]{:S(2)}) copy-start(f32[2,512]{1,0:T(2,128)} %gain_ref.9) | copy-start | bytes 12292
  63.4 0.9 %copy-start.5 = (f32[512]{0:T(512)S(1)}, f32[512]{0:T(512)}, u32[]{:S(2)}) copy-start(f32[512]{0:T(512)} %param.16) | copy-start | bytes 6148
  68.1 2.9 %collective-permute-start.20 = (bf16[512,512]{1,0:T(8,128)(2,1)S(1)}, bf16[512,512]{1,0:T(8,128)(2,1)S(1)}, u32[]{:S(2)}, u32[]{:S(2)}) collective-permute-start(bf16[512,512]{1,0:T(8,128)(2,1)S(1)} %constant_dynamic-update-slice_fusion.refs_1_), channel_id=1, source_target_pairs={{0,2},{1,3},{2,0},{3,1},{4,6},{5,7},{6,4},{7,5},{8,10},{9,11},{10,... | collective-permute-start | bytes 1572872 | tf_op jit(solution)/shard_map/ppermute | solution.py:80
  71.0 2.7 %copy-start = (bf16[512,512]{1,0:T(8,128)(2,1)S(1)}, bf16[512,512]{1,0:T(8,128)(2,1)}, u32[]{:S(2)}) copy-start(bf16[512,512]{1,0:T(8,128)(2,1)} %value_ref.1) | copy-start | bytes 1572868
  71.0 2.7 %copy-start.1 = (bf16[512,512]{1,0:T(8,128)(2,1)S(1)}, bf16[512,512]{1,0:T(8,128)(2,1)}, u32[]{:S(2)}) copy-start(bf16[512,512]{1,0:T(8,128)(2,1)} %gate_ref.1) | copy-start | bytes 1572868
  71.0 2.7 %copy-start.2 = (bf16[512,512]{1,0:T(8,128)(2,1)S(1)}, bf16[512,512]{1,0:T(8,128)(2,1)}, u32[]{:S(2)}) copy-start(bf16[512,512]{1,0:T(8,128)(2,1)} %out_ref.1) | copy-start | bytes 1572868
  71.9 1.8 %collective-permute-start.21 = (bf16[384,512]{1,0:T(8,128)(2,1)S(1)}, bf16[384,512]{1,0:T(8,128)(2,1)S(1)}, u32[]{:S(2)}, u32[]{:S(2)}) collective-permute-start(bf16[384,512]{1,0:T(8,128)(2,1)S(1)} %ff1.3.final_ref), channel_id=1, source_target_pairs={{0,2},{1,3},{2,0},{3,1},{4,6},{5,7},{6,4},{7,5},{8,10},{9,11},{10,... | collective-permute-start | bytes 1179656 | tf_op jit(solution)/shard_map/ppermute | solution.py:80
  74.8 7.6 %collective-permute-start.22 = (bf16[96,512]{1,0:T(8,128)(2,1)S(1)}, bf16[96,512]{1,0:T(8,128)(2,1)S(1)}, u32[]{:S(2)}, u32[]{:S(2)}) collective-permute-start(bf16[96,512]{1,0:T(8,128)(2,1)S(1)} %get-tuple-element.75), channel_id=1, source_target_pairs={{0,0},{1,1},{2,3},{3,2},{4,4},{5,5},{6,7},{7,6},{8,8},{9,9},{10,11... | collective-permute-start | bytes 294920 | tf_op jit(solution)/shard_map/ppermute | solution.py:80
  77.9 4.8 %collective-permute-start.23 = (bf16[96,512]{1,0:T(8,128)(2,1)S(1)}, bf16[96,512]{1,0:T(8,128)(2,1)S(1)}, u32[]{:S(2)}, u32[]{:S(2)}) collective-permute-start(bf16[96,512]{1,0:T(8,128)(2,1)S(1)} %get-tuple-element.76), channel_id=1, source_target_pairs={{0,4},{1,5},{2,7},{3,6},{4,0},{5,1},{6,3},{7,2},{8,12},{9,13},{10,... | collective-permute-start | bytes 294920 | tf_op jit(solution)/shard_map/ppermute | solution.py:80
  78.0 9.9 %collective-permute-start.24 = (bf16[96,512]{1,0:T(8,128)(2,1)S(1)}, bf16[96,512]{1,0:T(8,128)(2,1)S(1)}, u32[]{:S(2)}, u32[]{:S(2)}) collective-permute-start(bf16[96,512]{1,0:T(8,128)(2,1)S(1)} %get-tuple-element.77), channel_id=1, source_target_pairs={{0,8},{1,9},{2,11},{3,10},{4,12},{5,13},{6,15},{7,14},{8,0},{9,1},... | collective-permute-start | bytes 294920 | tf_op jit(solution)/shard_map/ppermute | solution.py:80
  80.0 7.9 %collective-permute-start.25 = (bf16[96,512]{1,0:T(8,128)(2,1)S(1)}, bf16[96,512]{1,0:T(8,128)(2,1)S(1)}, u32[]{:S(2)}, u32[]{:S(2)}) collective-permute-start(bf16[96,512]{1,0:T(8,128)(2,1)S(1)} %get-tuple-element.78), channel_id=1, source_target_pairs={{0,12},{1,13},{2,15},{3,14},{4,8},{5,9},{6,11},{7,10},{8,4},{9,5},... | collective-permute-start | bytes 294920 | tf_op jit(solution)/shard_map/ppermute | solution.py:80

commit v6 on v5

--- a/solution.py
+++ b/solution.py
@@ -324,25 +324,30 @@
     xb0 = across(b[:cut])
     states += [moved(p, to(k + 1)) for k, p in enumerate(parts)]
     bl, xal, yal, xb0, yxa0, *states = after([b, xa, ya, xb0, yxa0, *states], [])
-    sxb0, syxa0 = other_core(xb0), other_core(yxa0)
-    (bs,) = after([bl], [sxb0])
-    xas, yas = after([xal, yal], [syxa0])
-    sb, sxa, sya = other_core(bs), other_core(xas), other_core(yas)
+    stay = [bl, xal, yal]
+    swap0 = other_core(jnp.concatenate([*(v[:cut] for v in stay), xb0, yxa0], 0))
     yxa1 = planes(xal[cut:])
     xb1 = across(bl[cut:])
     mine = [own, a, b, x, xa, ya]
-    others = [rest, swaps[0], sb, swaps[1], sxa, sya]
-    arrays = mine + [xb0, yxa0] + others + [sxb0, syxa0]
+    others = [rest, *swaps]
+    arrays = mine + [xb0, yxa0] + others + [swap0]
     places = [
         [(k, 0) for k in (0, 1, 2, 3, 4, 6, 5, 7)],
-        [(8, 0), (9, 0), (10, 0), (11, 0), (12, 0), (14, 0), (13, 0), (15, 0)],
+        [(8, 0), (9, 0), (11, 0), (10, 0), (11, cut), (11, 3 * cut), (11, 2 * cut), (11, 4 * cut)],
     ]
-    early = [[(k, 0) for k in range(6)], [(k + 6, 0) for k in range(6)]]
+    early = [
+        [(k, cut) for k in range(6)],
+        [(6, cut), (7, cut), (9, 0), (8, cut), (9, hidden), (9, 2 * hidden)],
+    ]
     head = head_norm[None]
     state = conv0 = conv(states, conv_norm, arrays, places, 0, hidden, taps)
     (state,) = (ff0,) = feed_forward(state, None, ff_norm, head, arrays, places, 0, 0, half, "state")
     state = conv1 = conv([state], conv_norm, arrays, places, 1, hidden + taps * chans // 2, taps)
-    state, mixed = feed_forward(state, None, ff_norm, head, mine + others, early, 1, cut, half, "")
+    tail, _ = lax.optimization_barrier((jnp.concatenate([v[cut:] for v in stay], 0), conv0))
+    swap1 = other_core(tail)
+    state, mixed = feed_forward(
+        state, None, ff_norm, head, mine + others + [swap1], early, 1, 0, half, ""
+    )
     late = jnp.concatenate(after([xb1, yxa1], [conv1]), 0)
     places = [[(0, 0), (0, hidden)], [(1, 0), (1, hidden)]]
     arrays = [late, other_core(late)]

time: 88.9 us -> 86.7 us (0.975)
  waiting for transfers between devices: 41.9 us -> 40.3 us
  starting transfers between devices: 35 us -> 34.1 us
    ppermute x26 -> x23, waiting for transfers between devices: 41.9 us -> 40.3 us  [moved(): return lax.ppermute(value, AXES, pairs)]
    ppermute x26 -> x23, starting transfers between devices: 35 us -> 34.1 us  [moved(): return lax.ppermute(value, AXES, pairs)]
  transfers between devices with their start and end apart: 26 -> 23, of which waited for: 14 -> 10; matrix products, arithmetic and copies ran while one was open for 0% -> 0% of each run, Pallas kernels for 8% -> 8%
where the time goes in v6:
time: 86.7 us; the launch traced here: 86.5 us
  waiting for transfers between devices  40.3 us (46%)
  starting transfers between devices  34.1 us (39%)
  Pallas kernels  11.4 us (13%)
    ppermute x23, waiting for transfers between devices, moved(): return lax.ppermute(value, AXES, pairs)  40.3 us
    ppermute x23, starting transfers between devices, moved(): return lax.ppermute(value, AXES, pairs)  34.1 us
    pallas_call x3, Pallas kernels, feed_forward(): pl.pallas_call(functools.partial(ff_kernel, block, mixed is None, ends, p...  4.5 us
    pallas_call x2, Pallas kernels, pack(): pl.pallas_call(functools.partial(pack_kernel, (blocks, turned), mine), ou...  3.28 us
    pallas_call x2, Pallas kernels, conv(): pl.pallas_call(functools.partial(conv_kernel, block, len(states), places,...  1.76 us
  transfers between devices with their start and end apart: 23, of which 10 were waited for; matrix products, arithmetic and copies ran while one was open for 0% of the time, Pallas kernels for 8%

profile of v6, /device:TPU:1, one launch (start us, length us, event | category | flops | bytes accessed | tf_op | source)
XLA Modules:
  0.0 86.5 jit_solution(3341089140027906724)
XLA Ops:
  0.0 1.7 %pack_own.1.refs_4_.refs_0_.refs_1_ = bf16[704,512]{1,0:T(8,128)(2,1)S(1)} custom-call(bf16[2,512,256]{2,1,0:T(8,128)(2,1)} %refs_4_.2, bf16[2,256,512]{2,1,0:T(8,128)(2,1)} %refs_5_.2, bf16[2,3,64,512]{3,2,1,0:T(8,128)(2,1)} %bitcast.8, bf16[2,3,64,512]{3,2,1,0:T(8,128)(2,1)} %bitcast.9, bf16[2,512,256]{2,1,0:T(8,128)(2,1)} %refs_4_.2, ...), custom_call_target="tpu_custom_call" | custom-call | tf_op jit(solution)/shard_map/pack_own/pallas_call | solution.py:152
  1.7 2.2 %collective-permute-start = (bf16[704,512]{1,0:T(8,128)(2,1)S(1)}, bf16[704,512]{1,0:T(8,128)(2,1)S(1)}, u32[]{:S(2)}, u32[]{:S(2)}) collective-permute-start(bf16[704,512]{1,0:T(8,128)(2,1)S(1)} %pack_own.1.refs_4_.refs_0_.refs_1_), channel_id=1, source_target_pairs={{0,4},{1,5},{2,6},{3,7},{4,8},{5,9},{6,10},{7,11},{8,12},{9,13},{1... | collective-permute-start | bytes 2162696 | tf_op jit(solution)/shard_map/ppermute | solution.py:80
  3.9 1.2 %collective-permute-start.4 = (bf16[704,512]{1,0:T(8,128)(2,1)S(1)}, bf16[704,512]{1,0:T(8,128)(2,1)S(1)}, u32[]{:S(2)}, u32[]{:S(2)}) collective-permute-start(bf16[704,512]{1,0:T(8,128)(2,1)S(1)} %pack_own.1.refs_4_.refs_0_.refs_1_), channel_id=1, source_target_pairs={{0,1},{1,0},{2,3},{3,2},{4,5},{5,4},{6,7},{7,6},{8,9},{9,8},{10,11... | collective-permute-start | bytes 2162696 | tf_op jit(solution)/shard_map/ppermute | solution.py:80
  5.1 2.2 %collective-permute-start.7 = (bf16[96,512]{1,0:T(8,128)(2,1)S(1)}, bf16[96,512]{1,0:T(8,128)(2,1)S(1)}, u32[]{:S(2)}, u32[]{:S(2)}) collective-permute-start(bf16[96,512]{1,0:T(8,128)(2,1)S(1)} %get-tuple-element.43), channel_id=1, source_target_pairs={{0,0},{1,1},{2,3},{3,2},{4,4},{5,5},{6,7},{7,6},{8,8},{9,9},{10,11... | collective-permute-start | bytes 294920 | tf_op jit(solution)/shard_map/ppermute | solution.py:80
  7.3 14.5 %collective-permute-done.refs_5_.refs_1_.refs_2_ = bf16[704,512]{1,0:T(8,128)(2,1)S(1)} collective-permute-done((bf16[704,512]{1,0:T(8,128)(2,1)S(1)}, bf16[704,512]{1,0:T(8,128)(2,1)S(1)}, u32[]{:S(2)}, u32[]{:S(2)}) %collective-permute-start) | collective-permute-done | bytes 720928 | tf_op jit(solution)/shard_map/ppermute | solution.py:80
  21.7 0.0 collective-permute-start.1
  21.7 1.0 %collective-permute-start.2 = (bf16[704,512]{1,0:T(8,128)(2,1)S(1)}, bf16[704,512]{1,0:T(8,128)(2,1)S(1)}, u32[]{:S(2)}, u32[]{:S(2)}) collective-permute-start(bf16[704,512]{1,0:T(8,128)(2,1)S(1)} %collective-permute-done.refs_5_.refs_1_.refs_2_), channel_id=1, source_target_pairs={{0,1},{1,0},{2,3},{3,2},{4,5},{5,4},{6,7},{7,6},{8,9},{9,8},{10,11... | collective-permute-start | bytes 2162696 | tf_op jit(solution)/shard_map/ppermute | solution.py:80
  22.7 4.4 %collective-permute-start.3 = (bf16[704,512]{1,0:T(8,128)(2,1)S(1)}, bf16[704,512]{1,0:T(8,128)(2,1)S(1)}, u32[]{:S(2)}, u32[]{:S(2)}) collective-permute-start(bf16[704,512]{1,0:T(8,128)(2,1)S(1)} %collective-permute-done.refs_5_.refs_1_.refs_2_), channel_id=1, source_target_pairs={{0,16},{1,17},{2,18},{3,19},{4,20},{5,21},{6,22},{7,23},{8,24},{9,... | collective-permute-start | bytes 2162696 | tf_op jit(solution)/shard_map/ppermute | solution.py:80
  27.1 2.4 %collective-permute-start.5 = (bf16[704,512]{1,0:T(8,128)(2,1)S(1)}, bf16[704,512]{1,0:T(8,128)(2,1)S(1)}, u32[]{:S(2)}, u32[]{:S(2)}) collective-permute-start(bf16[704,512]{1,0:T(8,128)(2,1)S(1)} %collective-permute-done.refs_5_.refs_1_.refs_2_), channel_id=1, source_target_pairs={{0,2},{1,3},{2,0},{3,1},{4,6},{5,7},{6,4},{7,5},{8,10},{9,11},{10,... | collective-permute-start | bytes 2162696 | tf_op jit(solution)/shard_map/ppermute | solution.py:80
  29.5 0.1 collective-permute-start.6
  29.6 1.6 %pack_rest.1.refs_12_.refs_8_.refs_9_.refs_6_ = bf16[704,512]{1,0:T(8,128)(2,1)S(1)} custom-call(bf16[2,512,256]{2,1,0:T(8,128)(2,1)} %refs_4_.2, bf16[2,256,512]{2,1,0:T(8,128)(2,1)} %refs_5_.2, bf16[2,3,64,512]{3,2,1,0:T(8,128)(2,1)} %bitcast.10, bf16[2,3,64,512]{3,2,1,0:T(8,128)(2,1)} %bitcast.11, bf16[2,512,256]{2,1,0:T(8,128)(2,1)} %refs_4_.2, ...), custom_call_target="tpu_custom_call" | custom-call | tf_op jit(solution)/shard_map/pack_rest/pallas_call | solution.py:152
  31.2 8.7 %collective-permute-done.1.refs_6_.refs_2_.refs_3_ = bf16[704,512]{1,0:T(8,128)(2,1)S(1)} collective-permute-done((bf16[704,512]{1,0:T(8,128)(2,1)S(1)}, bf16[704,512]{1,0:T(8,128)(2,1)S(1)}, u32[]{:S(2)}, u32[]{:S(2)}) %collective-permute-start.1) | collective-permute-done | bytes 720928 | tf_op jit(solution)/shard_map/ppermute | solution.py:80
  39.9 1.5 %collective-permute-done.3.refs_9_.refs_5_.refs_6_ = bf16[704,512]{1,0:T(8,128)(2,1)S(1)} collective-permute-done((bf16[704,512]{1,0:T(8,128)(2,1)S(1)}, bf16[704,512]{1,0:T(8,128)(2,1)S(1)}, u32[]{:S(2)}, u32[]{:S(2)}) %collective-permute-start.3) | collective-permute-done | bytes 720928 | tf_op jit(solution)/shard_map/ppermute | solution.py:80
  41.5 0.3 collective-permute-start.8
  41.9 1.3 %collective-permute-start.9 = (bf16[448,512]{1,0:T(8,128)(2,1)S(1)}, bf16[448,512]{1,0:T(8,128)(2,1)S(1)}, u32[]{:S(2)}, u32[]{:S(2)}) collective-permute-start(bf16[448,512]{1,0:T(8,128)(2,1)S(1)} %slice.27), channel_id=1, source_target_pairs={{0,16},{1,17},{2,18},{3,19},{4,20},{5,21},{6,22},{7,23},{8,24},{9,... | collective-permute-start | bytes 1376264 | tf_op jit(solution)/shard_map/ppermute | solution.py:80
  43.2 3.3 %collective-permute-start.11 = (bf16[96,512]{1,0:T(8,128)(2,1)S(1)}, bf16[96,512]{1,0:T(8,128)(2,1)S(1)}, u32[]{:S(2)}, u32[]{:S(2)}) collective-permute-start(bf16[96,512]{1,0:T(8,128)(2,1)S(1)} %get-tuple-element.52), channel_id=1, source_target_pairs={{0,8},{1,9},{2,11},{3,10},{4,12},{5,13},{6,15},{7,14},{8,0},{9,1},... | collective-permute-start | bytes 294920 | tf_op jit(solution)/shard_map/ppermute | solution.py:80
  46.4 2.1 %collective-permute-start.12 = (bf16[96,512]{1,0:T(8,128)(2,1)S(1)}, bf16[96,512]{1,0:T(8,128)(2,1)S(1)}, u32[]{:S(2)}, u32[]{:S(2)}) collective-permute-start(bf16[96,512]{1,0:T(8,128)(2,1)S(1)} %get-tuple-element.53), channel_id=1, source_target_pairs={{0,12},{1,13},{2,15},{3,14},{4,8},{5,9},{6,11},{7,10},{8,4},{9,5},... | collective-permute-start | bytes 294920 | tf_op jit(solution)/shard_map/ppermute | solution.py:80
  48.5 0.2 collective-permute-done.10.refs_1_
  48.7 4.1 %collective-permute-done.12.refs_3_ = bf16[96,512]{1,0:T(8,128)(2,1)S(1)} collective-permute-done((bf16[96,512]{1,0:T(8,128)(2,1)S(1)}, bf16[96,512]{1,0:T(8,128)(2,1)S(1)}, u32[]{:S(2)}, u32[]{:S(2)}) %collective-permute-start.12) | collective-permute-done | bytes 98336 | tf_op jit(solution)/shard_map/ppermute | solution.py:80
  52.8 1.9 %collective-permute-done.8.refs_10_.refs_6_.refs_7_ = bf16[448,512]{1,0:T(8,128)(2,1)S(1)} collective-permute-done((bf16[448,512]{1,0:T(8,128)(2,1)S(1)}, bf16[448,512]{1,0:T(8,128)(2,1)S(1)}, u32[]{:S(2)}, u32[]{:S(2)}) %collective-permute-start.8) | collective-permute-done | bytes 458784 | tf_op jit(solution)/shard_map/ppermute | solution.py:80
  54.8 0.0 copy-start.6
  54.9 3.1 %collective-permute-start.13 = (bf16[2240,512]{1,0:T(8,128)(2,1)S(1)}, bf16[2240,512]{1,0:T(8,128)(2,1)S(1)}, u32[]{:S(2)}, u32[]{:S(2)}) collective-permute-start(bf16[2240,512]{1,0:T(8,128)(2,1)S(1)} %constant_dynamic-update-slice_fusion), channel_id=1, source_target_pairs={{0,2},{1,3},{2,0},{3,1},{4,6},{5,7},{6,4},{7,5},{8,10},{9,11},{10,... | collective-permute-start | bytes 6881288 | tf_op jit(solution)/shard_map/ppermute | solution.py:80
  58.0 0.3 collective-permute-start.15
  58.3 1.2 %collective-permute-start.16 = (bf16[256,512]{1,0:T(8,128)(2,1)S(1)}, bf16[256,512]{1,0:T(8,128)(2,1)S(1)}, u32[]{:S(2)}, u32[]{:S(2)}) collective-permute-start(bf16[256,512]{1,0:T(8,128)(2,1)S(1)} %slice.32), channel_id=1, source_target_pairs={{0,16},{1,17},{2,18},{3,19},{4,20},{5,21},{6,22},{7,23},{8,24},{9,... | collective-permute-start | bytes 786440 | tf_op jit(solution)/shard_map/ppermute | solution.py:80
  59.6 0.1 pad_maximum_fusion
  59.6 0.0 copy-start.4
  59.6 0.0 copy-start.5
  59.6 2.4 %collective-permute-done.13.refs_15_.refs_11_.refs_12_ = bf16[2240,512]{1,0:T(8,128)(2,1)S(1)} collective-permute-done((bf16[2240,512]{1,0:T(8,128)(2,1)S(1)}, bf16[2240,512]{1,0:T(8,128)(2,1)S(1)}, u32[]{:S(2)}, u32[]{:S(2)}) %collective-permute-start.13) | collective-permute-done | bytes 2293792 | tf_op jit(solution)/shard_map/ppermute | solution.py:80
  62.0 0.9 %conv0.1.state_ref = f32[384,512]{1,0:T(8,128)S(1)} custom-call(f32[2,512]{1,0:T(2,128)S(1)} %copy-done.6, bf16[96,512]{1,0:T(8,128)(2,1)S(1)} %collective-permute-done.7.refs_0_, bf16[96,512]{1,0:T(8,128)(2,1)S(1)} %collective-permute-done.10.refs_1_, bf16[96,512]{1,0:T(8,128)(2,1)S(1)} %collective-permute-done.11.refs_2_, ...), custom_call_target="tpu_custom_call" | custom-call | tf_op jit(solution)/shard_map/conv0/pallas_call | solution.py:220
  62.9 0.4 collective-permute-start.14
  63.4 2.0 %ff0.1.refs_0_ = f32[384,512]{1,0:T(8,128)S(1)} custom-call(f32[2,512]{1,0:T(2,128)S(1)} %copy-done.4, f32[1,512]{1,0:T(1,128)S(1)} %bitcast.5, f32[384,512]{1,0:T(8,128)S(1)} %conv0.1.state_ref, bf16[704,512]{1,0:T(8,128)(2,1)S(1)} %pack_own.1.refs_4_.refs_0_.refs_1_, bf16[704,512]{1,0:T(8,128)(2,1)S(1)} %collective-permute-done.refs_5_.refs_1_.refs_2_, ...), custom_call_target="tpu_custom_call" | custom-call | tf_op jit(solution)/shard_map/ff0/pallas_call | solution.py:259
  65.4 0.9 conv1.1.state_ref
  66.3 0.8 collective-permute-start.17
  67.2 1.6 %ff1.2 = (f32[384,512]{1,0:T(8,128)S(1)}, bf16[384,512]{1,0:T(8,128)(2,1)S(1)}) custom-call(f32[2,512]{1,0:T(2,128)S(1)} %copy-done.4, f32[1,512]{1,0:T(1,128)S(1)} %bitcast.6, f32[384,512]{1,0:T(8,128)S(1)} %conv1.1.state_ref, bf16[704,512]{1,0:T(8,128)(2,1)S(1)} %pack_own.1.refs_4_.refs_0_.refs_1_, ...), custom_call_target="tpu_custom_call" | custom-call | tf_op jit(solution)/shard_map/ff1/pallas_call | solution.py:259
  68.8 0.0 copy-start
  68.8 0.0 copy-start.1
  68.8 0.0 copy-start.2
  68.8 0.9 %ff1.3.final_ref = bf16[384,512]{1,0:T(8,128)(2,1)S(1)} custom-call(f32[2,512]{1,0:T(2,128)S(1)} %copy-done.4, f32[1,512]{1,0:T(1,128)S(1)} %bitcast.7, f32[384,512]{1,0:T(8,128)S(1)} %get-tuple-element.67.state_ref, bf16[384,512]{1,0:T(8,128)(2,1)S(1)} %get-tuple-element.68.refs_0_, bf16[512,512]{1,0:T(8,128)(2,1)S(1)} %constant_dynamic-update-slice_fusion.2.refs_1_, ...), custom_call_target="tpu_custom_call" | custom-call | tf_op jit(solution)/shard_map/ff1/pallas_call | solution.py:259
  69.7 0.3 collective-permute-start.18
  70.0 1.5 %collective-permute-done.18.opposite_ref = bf16[384,512]{1,0:T(8,128)(2,1)S(1)} collective-permute-done((bf16[384,512]{1,0:T(8,128)(2,1)S(1)}, bf16[384,512]{1,0:T(8,128)(2,1)S(1)}, u32[]{:S(2)}, u32[]{:S(2)}) %collective-permute-start.18) | collective-permute-done | bytes 393248 | tf_op jit(solution)/shard_map/ppermute | solution.py:80
  71.5 1.1 %head.1 = (bf16[96,512]{1,0:T(8,128)(2,1)S(1)}, bf16[96,512]{1,0:T(8,128)(2,1)S(1)}, bf16[96,512]{1,0:T(8,128)(2,1)S(1)}, bf16[96,512]{1,0:T(8,128)(2,1)S(1)}) custom-call(bf16[384,512]{1,0:T(8,128)(2,1)S(1)} %ff1.3.final_ref, bf16[384,512]{1,0:T(8,128)(2,1)S(1)} %collective-permute-done.18.opposite_ref, bf16[512,512]{1,0:T(8,128)(2,1)S(1)} %copy-done, ...), custom_call_target="tpu_custom_call" | custom-call | tf_op jit(solution)/shard_map/head/pallas_call | solution.py:356
  72.6 3.1 %collective-permute-start.19 = (bf16[96,512]{1,0:T(8,128)(2,1)S(1)}, bf16[96,512]{1,0:T(8,128)(2,1)S(1)}, u32[]{:S(2)}, u32[]{:S(2)}) collective-permute-start(bf16[96,512]{1,0:T(8,128)(2,1)S(1)} %get-tuple-element.71), channel_id=1, source_target_pairs={{0,0},{1,1},{2,3},{3,2},{4,4},{5,5},{6,7},{7,6},{8,8},{9,9},{10,11... | collective-permute-start | bytes 294920 | tf_op jit(solution)/shard_map/ppermute | solution.py:80
  75.7 0.1 collective-permute-start.20
  75.8 2.0 %collective-permute-start.21 = (bf16[96,512]{1,0:T(8,128)(2,1)S(1)}, bf16[96,512]{1,0:T(8,128)(2,1)S(1)}, u32[]{:S(2)}, u32[]{:S(2)}) collective-permute-start(bf16[96,512]{1,0:T(8,128)(2,1)S(1)} %get-tuple-element.73), channel_id=1, source_target_pairs={{0,8},{1,9},{2,11},{3,10},{4,12},{5,13},{6,15},{7,14},{8,0},{9,1},... | collective-permute-start | bytes 294920 | tf_op jit(solution)/shard_map/ppermute | solution.py:80
  77.9 2.3 %collective-permute-start.22 = (bf16[96,512]{1,0:T(8,128)(2,1)S(1)}, bf16[96,512]{1,0:T(8,128)(2,1)S(1)}, u32[]{:S(2)}, u32[]{:S(2)}) collective-permute-start(bf16[96,512]{1,0:T(8,128)(2,1)S(1)} %get-tuple-element.74), channel_id=1, source_target_pairs={{0,12},{1,13},{2,15},{3,14},{4,8},{5,9},{6,11},{7,10},{8,4},{9,5},... | collective-permute-start | bytes 294920 | tf_op jit(solution)/shard_map/ppermute | solution.py:80
  80.2 0.3 collective-permute-done.20.refs_1_
  80.5 5.2 %collective-permute-done.21.refs_2_ = bf16[96,512]{1,0:T(8,128)(2,1)S(1)} collective-permute-done((bf16[96,512]{1,0:T(8,128)(2,1)S(1)}, bf16[96,512]{1,0:T(8,128)(2,1)S(1)}, u32[]{:S(2)}, u32[]{:S(2)}) %collective-permute-start.21) | collective-permute-done | bytes 98336 | tf_op jit(solution)/shard_map/ppermute | solution.py:80
  85.7 0.8 join.1
  (35 shorter events, 0.4 us)
Async XLA Ops:
  0.0 5.1 %copy-start.3 = (bf16[1,384,512]{2,1,0:T(8,128)(2,1)S(1)}, bf16[1,384,512]{2,1,0:T(8,128)(2,1)}, u32[]{:S(2)}) copy-start(bf16[1,384,512]{2,1,0:T(8,128)(2,1)} %param.10) | copy-start | bytes 1179652
  1.7 20.1 %collective-permute-start = (bf16[704,512]{1,0:T(8,128)(2,1)S(1)}, bf16[704,512]{1,0:T(8,128)(2,1)S(1)}, u32[]{:S(2)}, u32[]{:S(2)}) collective-permute-start(bf16[704,512]{1,0:T(8,128)(2,1)S(1)} %pack_own.1.refs_4_.refs_0_.refs_1_), channel_id=1, source_target_pairs={{0,4},{1,5},{2,6},{3,7},{4,8},{5,9},{6,10},{7,11},{8,12},{9,13},{1... | collective-permute-start | bytes 2162696 | tf_op jit(solution)/shard_map/ppermute | solution.py:80
  3.9 25.7 %collective-permute-start.4 = (bf16[704,512]{1,0:T(8,128)(2,1)S(1)}, bf16[704,512]{1,0:T(8,128)(2,1)S(1)}, u32[]{:S(2)}, u32[]{:S(2)}) collective-permute-start(bf16[704,512]{1,0:T(8,128)(2,1)S(1)} %pack_own.1.refs_4_.refs_0_.refs_1_), channel_id=1, source_target_pairs={{0,1},{1,0},{2,3},{3,2},{4,5},{5,4},{6,7},{7,6},{8,9},{9,8},{10,11... | collective-permute-start | bytes 2162696 | tf_op jit(solution)/shard_map/ppermute | solution.py:80
  5.1 22.0 %collective-permute-start.7 = (bf16[96,512]{1,0:T(8,128)(2,1)S(1)}, bf16[96,512]{1,0:T(8,128)(2,1)S(1)}, u32[]{:S(2)}, u32[]{:S(2)}) collective-permute-start(bf16[96,512]{1,0:T(8,128)(2,1)S(1)} %get-tuple-element.43), channel_id=1, source_target_pairs={{0,0},{1,1},{2,3},{3,2},{4,4},{5,5},{6,7},{7,6},{8,8},{9,9},{10,11... | collective-permute-start | bytes 294920 | tf_op jit(solution)/shard_map/ppermute | solution.py:80
  21.7 18.2 %collective-permute-start.1 = (bf16[704,512]{1,0:T(8,128)(2,1)S(1)}, bf16[704,512]{1,0:T(8,128)(2,1)S(1)}, u32[]{:S(2)}, u32[]{:S(2)}) collective-permute-start(bf16[704,512]{1,0:T(8,128)(2,1)S(1)} %collective-permute-done.refs_5_.refs_1_.refs_2_), channel_id=1, source_target_pairs={{0,4},{1,5},{2,6},{3,7},{4,8},{5,9},{6,10},{7,11},{8,12},{9,13},{1... | collective-permute-start | bytes 2162696 | tf_op jit(solution)/shard_map/ppermute | solution.py:80
  21.7 18.2 %collective-permute-start.2 = (bf16[704,512]{1,0:T(8,128)(2,1)S(1)}, bf16[704,512]{1,0:T(8,128)(2,1)S(1)}, u32[]{:S(2)}, u32[]{:S(2)}) collective-permute-start(bf16[704,512]{1,0:T(8,128)(2,1)S(1)} %collective-permute-done.refs_5_.refs_1_.refs_2_), channel_id=1, source_target_pairs={{0,1},{1,0},{2,3},{3,2},{4,5},{5,4},{6,7},{7,6},{8,9},{9,8},{10,11... | collective-permute-start | bytes 2162696 | tf_op jit(solution)/shard_map/ppermute | solution.py:80
  22.7 18.8 %collective-permute-start.3 = (bf16[704,512]{1,0:T(8,128)(2,1)S(1)}, bf16[704,512]{1,0:T(8,128)(2,1)S(1)}, u32[]{:S(2)}, u32[]{:S(2)}) collective-permute-start(bf16[704,512]{1,0:T(8,128)(2,1)S(1)} %collective-permute-done.refs_5_.refs_1_.refs_2_), channel_id=1, source_target_pairs={{0,16},{1,17},{2,18},{3,19},{4,20},{5,21},{6,22},{7,23},{8,24},{9,... | collective-permute-start | bytes 2162696 | tf_op jit(solution)/shard_map/ppermute | solution.py:80
  27.1 14.3 %collective-permute-start.5 = (bf16[704,512]{1,0:T(8,128)(2,1)S(1)}, bf16[704,512]{1,0:T(8,128)(2,1)S(1)}, u32[]{:S(2)}, u32[]{:S(2)}) collective-permute-start(bf16[704,512]{1,0:T(8,128)(2,1)S(1)} %collective-permute-done.refs_5_.refs_1_.refs_2_), channel_id=1, source_target_pairs={{0,2},{1,3},{2,0},{3,1},{4,6},{5,7},{6,4},{7,5},{8,10},{9,11},{10,... | collective-permute-start | bytes 2162696 | tf_op jit(solution)/shard_map/ppermute | solution.py:80
  29.5 12.0 %collective-permute-start.6 = (bf16[704,512]{1,0:T(8,128)(2,1)S(1)}, bf16[704,512]{1,0:T(8,128)(2,1)S(1)}, u32[]{:S(2)}, u32[]{:S(2)}) collective-permute-start(bf16[704,512]{1,0:T(8,128)(2,1)S(1)} %collective-permute-done.4.refs_7_.refs_3_.refs_4_), channel_id=1, source_target_pairs={{0,2},{1,3},{2,0},{3,1},{4,6},{5,7},{6,4},{7,5},{8,10},{9,11},{10,... | collective-permute-start | bytes 2162696 | tf_op jit(solution)/shard_map/ppermute | solution.py:80
  41.5 13.1 %collective-permute-start.8 = (bf16[448,512]{1,0:T(8,128)(2,1)S(1)}, bf16[448,512]{1,0:T(8,128)(2,1)S(1)}, u32[]{:S(2)}, u32[]{:S(2)}) collective-permute-start(bf16[448,512]{1,0:T(8,128)(2,1)S(1)} %slice.26), channel_id=1, source_target_pairs={{0,1},{1,0},{2,3},{3,2},{4,5},{5,4},{6,7},{7,6},{8,9},{9,8},{10,11... | collective-permute-start | bytes 1376264 | tf_op jit(solution)/shard_map/ppermute | solution.py:80
  41.9 12.8 %collective-permute-start.9 = (bf16[448,512]{1,0:T(8,128)(2,1)S(1)}, bf16[448,512]{1,0:T(8,128)(2,1)S(1)}, u32[]{:S(2)}, u32[]{:S(2)}) collective-permute-start(bf16[448,512]{1,0:T(8,128)(2,1)S(1)} %slice.27), channel_id=1, source_target_pairs={{0,16},{1,17},{2,18},{3,19},{4,20},{5,21},{6,22},{7,23},{8,24},{9,... | collective-permute-start | bytes 1376264 | tf_op jit(solution)/shard_map/ppermute | solution.py:80
  43.2 5.5 %collective-permute-start.10 = (bf16[96,512]{1,0:T(8,128)(2,1)S(1)}, bf16[96,512]{1,0:T(8,128)(2,1)S(1)}, u32[]{:S(2)}, u32[]{:S(2)}) collective-permute-start(bf16[96,512]{1,0:T(8,128)(2,1)S(1)} %get-tuple-element.51), channel_id=1, source_target_pairs={{0,4},{1,5},{2,7},{3,6},{4,0},{5,1},{6,3},{7,2},{8,12},{9,13},{10,... | collective-permute-start | bytes 294920 | tf_op jit(solution)/shard_map/ppermute | solution.py:80
  43.2 5.5 %collective-permute-start.11 = (bf16[96,512]{1,0:T(8,128)(2,1)S(1)}, bf16[96,512]{1,0:T(8,128)(2,1)S(1)}, u32[]{:S(2)}, u32[]{:S(2)}) collective-permute-start(bf16[96,512]{1,0:T(8,128)(2,1)S(1)} %get-tuple-element.52), channel_id=1, source_target_pairs={{0,8},{1,9},{2,11},{3,10},{4,12},{5,13},{6,15},{7,14},{8,0},{9,1},... | collective-permute-start | bytes 294920 | tf_op jit(solution)/shard_map/ppermute | solution.py:80
  46.4 6.4 %collective-permute-start.12 = (bf16[96,512]{1,0:T(8,128)(2,1)S(1)}, bf16[96,512]{1,0:T(8,128)(2,1)S(1)}, u32[]{:S(2)}, u32[]{:S(2)}) collective-permute-start(bf16[96,512]{1,0:T(8,128)(2,1)S(1)} %get-tuple-element.53), channel_id=1, source_target_pairs={{0,12},{1,13},{2,15},{3,14},{4,8},{5,9},{6,11},{7,10},{8,4},{9,5},... | collective-permute-start | bytes 294920 | tf_op jit(solution)/shard_map/ppermute | solution.py:80
  54.8 7.3 %copy-start.6 = (f32[2,512]{1,0:T(2,128)S(1)}, f32[2,512]{1,0:T(2,128)}, u32[]{:S(2)}) copy-start(f32[2,512]{1,0:T(2,128)} %gain_ref.7) | copy-start | bytes 12292
  54.9 7.2 %collective-permute-start.13 = (bf16[2240,512]{1,0:T(8,128)(2,1)S(1)}, bf16[2240,512]{1,0:T(8,128)(2,1)S(1)}, u32[]{:S(2)}, u32[]{:S(2)}) collective-permute-start(bf16[2240,512]{1,0:T(8,128)(2,1)S(1)} %constant_dynamic-update-slice_fusion), channel_id=1, source_target_pairs={{0,2},{1,3},{2,0},{3,1},{4,6},{5,7},{6,4},{7,5},{8,10},{9,11},{10,... | collective-permute-start | bytes 6881288 | tf_op jit(solution)/shard_map/ppermute | solution.py:80
  58.0 8.3 %collective-permute-start.15 = (bf16[256,512]{1,0:T(8,128)(2,1)S(1)}, bf16[256,512]{1,0:T(8,128)(2,1)S(1)}, u32[]{:S(2)}, u32[]{:S(2)}) collective-permute-start(bf16[256,512]{1,0:T(8,128)(2,1)S(1)} %slice.31), channel_id=1, source_target_pairs={{0,1},{1,0},{2,3},{3,2},{4,5},{5,4},{6,7},{7,6},{8,9},{9,8},{10,11... | collective-permute-start | bytes 786440 | tf_op jit(solution)/shard_map/ppermute | solution.py:80
  58.3 7.9 %collective-permute-start.16 = (bf16[256,512]{1,0:T(8,128)(2,1)S(1)}, bf16[256,512]{1,0:T(8,128)(2,1)S(1)}, u32[]{:S(2)}, u32[]{:S(2)}) collective-permute-start(bf16[256,512]{1,0:T(8,128)(2,1)S(1)} %slice.32), channel_id=1, source_target_pairs={{0,16},{1,17},{2,18},{3,19},{4,20},{5,21},{6,22},{7,23},{8,24},{9,... | collective-permute-start | bytes 786440 | tf_op jit(solution)/shard_map/ppermute | solution.py:80
  59.6 3.8 %copy-start.4 = (f32[2,512]{1,0:T(2,128)S(1)}, f32[2,512]{1,0:T(2,128)}, u32[]{:S(2)}) copy-start(f32[2,512]{1,0:T(2,128)} %gain_ref.9) | copy-start | bytes 12292
  59.6 3.7 %copy-start.5 = (f32[512]{0:T(512)S(1)}, f32[512]{0:T(512)}, u32[]{:S(2)}) copy-start(f32[512]{0:T(512)} %param.16) | copy-start | bytes 6148
  62.9 4.2 %collective-permute-start.14 = (bf16[768,512]{1,0:T(8,128)(2,1)S(1)}, bf16[768,512]{1,0:T(8,128)(2,1)S(1)}, u32[]{:S(2)}, u32[]{:S(2)}) collective-permute-start(bf16[768,512]{1,0:T(8,128)(2,1)S(1)} %pad_maximum_fusion), channel_id=1, source_target_pairs={{0,2},{1,3},{2,0},{3,1},{4,6},{5,7},{6,4},{7,5},{8,10},{9,11},{10,... | collective-permute-start | bytes 2359304 | tf_op jit(solution)/shard_map/ppermute | solution.py:80
  66.3 2.5 %collective-permute-start.17 = (bf16[512,512]{1,0:T(8,128)(2,1)S(1)}, bf16[512,512]{1,0:T(8,128)(2,1)S(1)}, u32[]{:S(2)}, u32[]{:S(2)}) collective-permute-start(bf16[512,512]{1,0:T(8,128)(2,1)S(1)} %constant_dynamic-update-slice_fusion.2.refs_1_), channel_id=1, source_target_pairs={{0,2},{1,3},{2,0},{3,1},{4,6},{5,7},{6,4},{7,5},{8,10},{9,11},{10,... | collective-permute-start | bytes 1572872 | tf_op jit(solution)/shard_map/ppermute | solution.py:80
  68.8 2.7 %copy-start = (bf16[512,512]{1,0:T(8,128)(2,1)S(1)}, bf16[512,512]{1,0:T(8,128)(2,1)}, u32[]{:S(2)}) copy-start(bf16[512,512]{1,0:T(8,128)(2,1)} %value_ref.1) | copy-start | bytes 1572868
  68.8 2.7 %copy-start.1 = (bf16[512,512]{1,0:T(8,128)(2,1)S(1)}, bf16[512,512]{1,0:T(8,128)(2,1)}, u32[]{:S(2)}) copy-start(bf16[512,512]{1,0:T(8,128)(2,1)} %gate_ref.1) | copy-start | bytes 1572868
  68.8 2.7 %copy-start.2 = (bf16[512,512]{1,0:T(8,128)(2,1)S(1)}, bf16[512,512]{1,0:T(8,128)(2,1)}, u32[]{:S(2)}) copy-start(bf16[512,512]{1,0:T(8,128)(2,1)} %out_ref.1) | copy-start | bytes 1572868
  69.7 1.8 %collective-permute-start.18 = (bf16[384,512]{1,0:T(8,128)(2,1)S(1)}, bf16[384,512]{1,0:T(8,128)(2,1)S(1)}, u32[]{:S(2)}, u32[]{:S(2)}) collective-permute-start(bf16[384,512]{1,0:T(8,128)(2,1)S(1)} %ff1.3.final_ref), channel_id=1, source_target_pairs={{0,2},{1,3},{2,0},{3,1},{4,6},{5,7},{6,4},{7,5},{8,10},{9,11},{10,... | collective-permute-start | bytes 1179656 | tf_op jit(solution)/shard_map/ppermute | solution.py:80
  72.6 7.6 %collective-permute-start.19 = (bf16[96,512]{1,0:T(8,128)(2,1)S(1)}, bf16[96,512]{1,0:T(8,128)(2,1)S(1)}, u32[]{:S(2)}, u32[]{:S(2)}) collective-permute-start(bf16[96,512]{1,0:T(8,128)(2,1)S(1)} %get-tuple-element.71), channel_id=1, source_target_pairs={{0,0},{1,1},{2,3},{3,2},{4,4},{5,5},{6,7},{7,6},{8,8},{9,9},{10,11... | collective-permute-start | bytes 294920 | tf_op jit(solution)/shard_map/ppermute | solution.py:80
  75.7 4.8 %collective-permute-start.20 = (bf16[96,512]{1,0:T(8,128)(2,1)S(1)}, bf16[96,512]{1,0:T(8,128)(2,1)S(1)}, u32[]{:S(2)}, u32[]{:S(2)}) collective-permute-start(bf16[96,512]{1,0:T(8,128)(2,1)S(1)} %get-tuple-element.72), channel_id=1, source_target_pairs={{0,4},{1,5},{2,7},{3,6},{4,0},{5,1},{6,3},{7,2},{8,12},{9,13},{10,... | collective-permute-start | bytes 294920 | tf_op jit(solution)/shard_map/ppermute | solution.py:80
  75.8 9.9 %collective-permute-start.21 = (bf16[96,512]{1,0:T(8,128)(2,1)S(1)}, bf16[96,512]{1,0:T(8,128)(2,1)S(1)}, u32[]{:S(2)}, u32[]{:S(2)}) collective-permute-start(bf16[96,512]{1,0:T(8,128)(2,1)S(1)} %get-tuple-element.73), channel_id=1, source_target_pairs={{0,8},{1,9},{2,11},{3,10},{4,12},{5,13},{6,15},{7,14},{8,0},{9,1},... | collective-permute-start | bytes 294920 | tf_op jit(solution)/shard_map/ppermute | solution.py:80
  77.9 7.9 %collective-permute-start.22 = (bf16[96,512]{1,0:T(8,128)(2,1)S(1)}, bf16[96,512]{1,0:T(8,128)(2,1)S(1)}, u32[]{:S(2)}, u32[]{:S(2)}) collective-permute-start(bf16[96,512]{1,0:T(8,128)(2,1)S(1)} %get-tuple-element.74), channel_id=1, source_target_pairs={{0,12},{1,13},{2,15},{3,14},{4,8},{5,9},{6,11},{7,10},{8,4},{9,5},... | collective-permute-start | bytes 294920 | tf_op jit(solution)/shard_map/ppermute | solution.py:80

commit v7 on v6

--- a/solution.py
+++ b/solution.py
@@ -267,7 +267,7 @@
     )(gain, head, *given, *arrays)
 
 
-def head_kernel(final_ref, opposite_ref, value_ref, gate_ref, out_ref, *refs):
+def head_kernel(sends, final_ref, opposite_ref, value_ref, gate_ref, out_ref, *refs):
     *outs, result = refs
     n = len(outs)
     size = outs[0].shape[0]
@@ -282,7 +282,7 @@
     mirrored = matmul(jnp.concatenate(flipped, 0), gate_ref[...]).astype(BF16)
     gated = (value * jax.nn.sigmoid(mirrored.astype(F32))).astype(BF16)
     result[...] = matmul(gated, out_ref[...]).astype(BF16)
-    for k, out in enumerate(outs):
+    for k, out in zip(sends, outs):
         at = j ^ k
         out[...] = result[pl.ds(pl.multiple_of(at * size, size), size)]
 
@@ -353,12 +353,15 @@
     arrays = [late, other_core(late)]
     (final,) = feed_forward(state, mixed, ff_norm, head, arrays, places, 1, 0, half, "head")
     opposite = other_core(final)
+    sends = [2, 3, 1, 0]
     results = pl.pallas_call(
-        head_kernel, out_shape=[part] * n, in_specs=[VMEM_SPEC] * 5, out_specs=[VMEM_SPEC] * n,
+        functools.partial(head_kernel, sends), out_shape=[part] * n, in_specs=[VMEM_SPEC] * 5, out_specs=[VMEM_SPEC] * n,
         scratch_shapes=[pltpu.VMEM((rows, width), BF16)], compiler_params=PARAMS, name="head",
     )(final, opposite, value_weight, gate_weight, out_weight)
-    home = {k: moved(results[k], to(k)) for k in (2, 3, 1, 0)}
-    home = [home[k] for k in range(n)]
+    ready = dict(zip(sends, results))
+    home = {k: moved(ready[k], to(k)) for k in sends if k}
+    (near,) = after([ready[0]], [home[1]])
+    home = [moved(near, to(0))] + [home[k] for k in range(1, n)]
     joined = pl.pallas_call(
         join_kernel, out_shape=jax.ShapeDtypeStruct((rows, width), BF16), in_specs=[VMEM_SPEC] * n,
         out_specs=VMEM_SPEC, compiler_params=PARAMS, name="join",

time: 86.7 us -> 85.8 us (0.990)
  waiting for transfers between devices: 40.3 us -> 38.6 us
    ppermute x23, waiting for transfers between devices: 40.3 us -> 38.6 us  [moved(): return lax.ppermute(value, AXES, pairs)]
  transfers between devices with their start and end apart: 23 -> 23, of which waited for: 10 -> 11; matrix products, arithmetic and copies ran while one was open for 0% -> 0% of each run, Pallas kernels for 8% -> 8%
where the time goes in v7:
time: 85.8 us; the launch traced here: 85.6 us
  waiting for transfers between devices  38.6 us (45%)
  starting transfers between devices  34.9 us (41%)
  Pallas kernels  11.4 us (13%)
    ppermute x23, waiting for transfers between devices, moved(): return lax.ppermute(value, AXES, pairs)  38.6 us
    ppermute x23, starting transfers between devices, moved(): return lax.ppermute(value, AXES, pairs)  34.9 us
    pallas_call x3, Pallas kernels, feed_forward(): pl.pallas_call(functools.partial(ff_kernel, block, mixed is None, ends, p...  4.5 us
    pallas_call x2, Pallas kernels, pack(): pl.pallas_call(functools.partial(pack_kernel, (blocks, turned), mine), ou...  3.28 us
    pallas_call x2, Pallas kernels, conv(): pl.pallas_call(functools.partial(conv_kernel, block, len(states), places,...  1.76 us
  transfers between devices with their start and end apart: 23, of which 11 were waited for; matrix products, arithmetic and copies ran while one was open for 0% of the time, Pallas kernels for 8%

profile of v7, /device:TPU:1, one launch (start us, length us, event | category | flops | bytes accessed | tf_op | source)
XLA Modules:
  0.0 85.6 jit_solution(6663904402219317559)
XLA Ops:
  0.0 1.7 %pack_own.1.refs_4_.refs_0_.refs_1_ = bf16[704,512]{1,0:T(8,128)(2,1)S(1)} custom-call(bf16[2,512,256]{2,1,0:T(8,128)(2,1)} %refs_4_.2, bf16[2,256,512]{2,1,0:T(8,128)(2,1)} %refs_5_.2, bf16[2,3,64,512]{3,2,1,0:T(8,128)(2,1)} %bitcast.8, bf16[2,3,64,512]{3,2,1,0:T(8,128)(2,1)} %bitcast.9, bf16[2,512,256]{2,1,0:T(8,128)(2,1)} %refs_4_.2, ...), custom_call_target="tpu_custom_call" | custom-call | tf_op jit(solution)/shard_map/pack_own/pallas_call | solution.py:152
  1.7 2.2 %collective-permute-start = (bf16[704,512]{1,0:T(8,128)(2,1)S(1)}, bf16[704,512]{1,0:T(8,128)(2,1)S(1)}, u32[]{:S(2)}, u32[]{:S(2)}) collective-permute-start(bf16[704,512]{1,0:T(8,128)(2,1)S(1)} %pack_own.1.refs_4_.refs_0_.refs_1_), channel_id=1, source_target_pairs={{0,4},{1,5},{2,6},{3,7},{4,8},{5,9},{6,10},{7,11},{8,12},{9,13},{1... | collective-permute-start | bytes 2162696 | tf_op jit(solution)/shard_map/ppermute | solution.py:80
  3.9 1.2 %collective-permute-start.4 = (bf16[704,512]{1,0:T(8,128)(2,1)S(1)}, bf16[704,512]{1,0:T(8,128)(2,1)S(1)}, u32[]{:S(2)}, u32[]{:S(2)}) collective-permute-start(bf16[704,512]{1,0:T(8,128)(2,1)S(1)} %pack_own.1.refs_4_.refs_0_.refs_1_), channel_id=1, source_target_pairs={{0,1},{1,0},{2,3},{3,2},{4,5},{5,4},{6,7},{7,6},{8,9},{9,8},{10,11... | collective-permute-start | bytes 2162696 | tf_op jit(solution)/shard_map/ppermute | solution.py:80
  5.1 2.2 %collective-permute-start.7 = (bf16[96,512]{1,0:T(8,128)(2,1)S(1)}, bf16[96,512]{1,0:T(8,128)(2,1)S(1)}, u32[]{:S(2)}, u32[]{:S(2)}) collective-permute-start(bf16[96,512]{1,0:T(8,128)(2,1)S(1)} %get-tuple-element.44), channel_id=1, source_target_pairs={{0,0},{1,1},{2,3},{3,2},{4,4},{5,5},{6,7},{7,6},{8,8},{9,9},{10,11... | collective-permute-start | bytes 294920 | tf_op jit(solution)/shard_map/ppermute | solution.py:80
  7.3 14.5 %collective-permute-done.refs_5_.refs_1_.refs_2_ = bf16[704,512]{1,0:T(8,128)(2,1)S(1)} collective-permute-done((bf16[704,512]{1,0:T(8,128)(2,1)S(1)}, bf16[704,512]{1,0:T(8,128)(2,1)S(1)}, u32[]{:S(2)}, u32[]{:S(2)}) %collective-permute-start) | collective-permute-done | bytes 720928 | tf_op jit(solution)/shard_map/ppermute | solution.py:80
  21.7 1.0 %collective-permute-start.2 = (bf16[704,512]{1,0:T(8,128)(2,1)S(1)}, bf16[704,512]{1,0:T(8,128)(2,1)S(1)}, u32[]{:S(2)}, u32[]{:S(2)}) collective-permute-start(bf16[704,512]{1,0:T(8,128)(2,1)S(1)} %collective-permute-done.refs_5_.refs_1_.refs_2_), channel_id=1, source_target_pairs={{0,1},{1,0},{2,3},{3,2},{4,5},{5,4},{6,7},{7,6},{8,9},{9,8},{10,11... | collective-permute-start | bytes 2162696 | tf_op jit(solution)/shard_map/ppermute | solution.py:80
  22.7 4.4 %collective-permute-start.3 = (bf16[704,512]{1,0:T(8,128)(2,1)S(1)}, bf16[704,512]{1,0:T(8,128)(2,1)S(1)}, u32[]{:S(2)}, u32[]{:S(2)}) collective-permute-start(bf16[704,512]{1,0:T(8,128)(2,1)S(1)} %collective-permute-done.refs_5_.refs_1_.refs_2_), channel_id=1, source_target_pairs={{0,16},{1,17},{2,18},{3,19},{4,20},{5,21},{6,22},{7,23},{8,24},{9,... | collective-permute-start | bytes 2162696 | tf_op jit(solution)/shard_map/ppermute | solution.py:80
  27.1 2.4 %collective-permute-start.5 = (bf16[704,512]{1,0:T(8,128)(2,1)S(1)}, bf16[704,512]{1,0:T(8,128)(2,1)S(1)}, u32[]{:S(2)}, u32[]{:S(2)}) collective-permute-start(bf16[704,512]{1,0:T(8,128)(2,1)S(1)} %collective-permute-done.refs_5_.refs_1_.refs_2_), channel_id=1, source_target_pairs={{0,2},{1,3},{2,0},{3,1},{4,6},{5,7},{6,4},{7,5},{8,10},{9,11},{10,... | collective-permute-start | bytes 2162696 | tf_op jit(solution)/shard_map/ppermute | solution.py:80
  29.5 0.1 collective-permute-start.6
  29.6 1.6 %pack_rest.1.refs_12_.refs_8_.refs_9_.refs_6_ = bf16[704,512]{1,0:T(8,128)(2,1)S(1)} custom-call(bf16[2,512,256]{2,1,0:T(8,128)(2,1)} %refs_4_.2, bf16[2,256,512]{2,1,0:T(8,128)(2,1)} %refs_5_.2, bf16[2,3,64,512]{3,2,1,0:T(8,128)(2,1)} %bitcast.10, bf16[2,3,64,512]{3,2,1,0:T(8,128)(2,1)} %bitcast.11, bf16[2,512,256]{2,1,0:T(8,128)(2,1)} %refs_4_.2, ...), custom_call_target="tpu_custom_call" | custom-call | tf_op jit(solution)/shard_map/pack_rest/pallas_call | solution.py:152
  31.2 8.7 %collective-permute-done.1.refs_6_.refs_2_.refs_3_ = bf16[704,512]{1,0:T(8,128)(2,1)S(1)} collective-permute-done((bf16[704,512]{1,0:T(8,128)(2,1)S(1)}, bf16[704,512]{1,0:T(8,128)(2,1)S(1)}, u32[]{:S(2)}, u32[]{:S(2)}) %collective-permute-start.1) | collective-permute-done | bytes 720928 | tf_op jit(solution)/shard_map/ppermute | solution.py:80
  39.9 1.5 %collective-permute-done.3.refs_9_.refs_5_.refs_6_ = bf16[704,512]{1,0:T(8,128)(2,1)S(1)} collective-permute-done((bf16[704,512]{1,0:T(8,128)(2,1)S(1)}, bf16[704,512]{1,0:T(8,128)(2,1)S(1)}, u32[]{:S(2)}, u32[]{:S(2)}) %collective-permute-start.3) | collective-permute-done | bytes 720928 | tf_op jit(solution)/shard_map/ppermute | solution.py:80
  41.5 0.3 collective-permute-start.8
  41.9 1.3 %collective-permute-start.9 = (bf16[448,512]{1,0:T(8,128)(2,1)S(1)}, bf16[448,512]{1,0:T(8,128)(2,1)S(1)}, u32[]{:S(2)}, u32[]{:S(2)}) collective-permute-start(bf16[448,512]{1,0:T(8,128)(2,1)S(1)} %slice.27), channel_id=1, source_target_pairs={{0,16},{1,17},{2,18},{3,19},{4,20},{5,21},{6,22},{7,23},{8,24},{9,... | collective-permute-start | bytes 1376264 | tf_op jit(solution)/shard_map/ppermute | solution.py:80
  43.2 3.3 %collective-permute-start.11 = (bf16[96,512]{1,0:T(8,128)(2,1)S(1)}, bf16[96,512]{1,0:T(8,128)(2,1)S(1)}, u32[]{:S(2)}, u32[]{:S(2)}) collective-permute-start(bf16[96,512]{1,0:T(8,128)(2,1)S(1)} %get-tuple-element.53), channel_id=1, source_target_pairs={{0,8},{1,9},{2,11},{3,10},{4,12},{5,13},{6,15},{7,14},{8,0},{9,1},... | collective-permute-start | bytes 294920 | tf_op jit(solution)/shard_map/ppermute | solution.py:80
  46.4 2.1 %collective-permute-start.12 = (bf16[96,512]{1,0:T(8,128)(2,1)S(1)}, bf16[96,512]{1,0:T(8,128)(2,1)S(1)}, u32[]{:S(2)}, u32[]{:S(2)}) collective-permute-start(bf16[96,512]{1,0:T(8,128)(2,1)S(1)} %get-tuple-element.54), channel_id=1, source_target_pairs={{0,12},{1,13},{2,15},{3,14},{4,8},{5,9},{6,11},{7,10},{8,4},{9,5},... | collective-permute-start | bytes 294920 | tf_op jit(solution)/shard_map/ppermute | solution.py:80
  48.5 0.2 collective-permute-done.10.refs_1_
  48.7 4.1 %collective-permute-done.12.refs_3_ = bf16[96,512]{1,0:T(8,128)(2,1)S(1)} collective-permute-done((bf16[96,512]{1,0:T(8,128)(2,1)S(1)}, bf16[96,512]{1,0:T(8,128)(2,1)S(1)}, u32[]{:S(2)}, u32[]{:S(2)}) %collective-permute-start.12) | collective-permute-done | bytes 98336 | tf_op jit(solution)/shard_map/ppermute | solution.py:80
  52.8 1.9 %collective-permute-done.8.refs_10_.refs_6_.refs_7_ = bf16[448,512]{1,0:T(8,128)(2,1)S(1)} collective-permute-done((bf16[448,512]{1,0:T(8,128)(2,1)S(1)}, bf16[448,512]{1,0:T(8,128)(2,1)S(1)}, u32[]{:S(2)}, u32[]{:S(2)}) %collective-permute-start.8) | collective-permute-done | bytes 458784 | tf_op jit(solution)/shard_map/ppermute | solution.py:80
  54.8 0.0 copy-start.6
  54.9 3.1 %collective-permute-start.13 = (bf16[2240,512]{1,0:T(8,128)(2,1)S(1)}, bf16[2240,512]{1,0:T(8,128)(2,1)S(1)}, u32[]{:S(2)}, u32[]{:S(2)}) collective-permute-start(bf16[2240,512]{1,0:T(8,128)(2,1)S(1)} %constant_dynamic-update-slice_fusion), channel_id=1, source_target_pairs={{0,2},{1,3},{2,0},{3,1},{4,6},{5,7},{6,4},{7,5},{8,10},{9,11},{10,... | collective-permute-start | bytes 6881288 | tf_op jit(solution)/shard_map/ppermute | solution.py:80
  58.0 0.3 collective-permute-start.15
  58.3 1.2 %collective-permute-start.16 = (bf16[256,512]{1,0:T(8,128)(2,1)S(1)}, bf16[256,512]{1,0:T(8,128)(2,1)S(1)}, u32[]{:S(2)}, u32[]{:S(2)}) collective-permute-start(bf16[256,512]{1,0:T(8,128)(2,1)S(1)} %slice.32), channel_id=1, source_target_pairs={{0,16},{1,17},{2,18},{3,19},{4,20},{5,21},{6,22},{7,23},{8,24},{9,... | collective-permute-start | bytes 786440 | tf_op jit(solution)/shard_map/ppermute | solution.py:80
  59.6 0.1 pad_maximum_fusion
  59.6 0.0 copy-start.4
  59.6 0.0 copy-start.5
  59.6 2.4 %collective-permute-done.13.refs_15_.refs_11_.refs_12_ = bf16[2240,512]{1,0:T(8,128)(2,1)S(1)} collective-permute-done((bf16[2240,512]{1,0:T(8,128)(2,1)S(1)}, bf16[2240,512]{1,0:T(8,128)(2,1)S(1)}, u32[]{:S(2)}, u32[]{:S(2)}) %collective-permute-start.13) | collective-permute-done | bytes 2293792 | tf_op jit(solution)/shard_map/ppermute | solution.py:80
  62.0 0.9 %conv0.1.state_ref = f32[384,512]{1,0:T(8,128)S(1)} custom-call(f32[2,512]{1,0:T(2,128)S(1)} %copy-done.6, bf16[96,512]{1,0:T(8,128)(2,1)S(1)} %collective-permute-done.7.refs_0_, bf16[96,512]{1,0:T(8,128)(2,1)S(1)} %collective-permute-done.10.refs_1_, bf16[96,512]{1,0:T(8,128)(2,1)S(1)} %collective-permute-done.11.refs_2_, ...), custom_call_target="tpu_custom_call" | custom-call | tf_op jit(solution)/shard_map/conv0/pallas_call | solution.py:220
  62.9 0.4 collective-permute-start.14
  63.4 2.0 %ff0.1.refs_0_ = f32[384,512]{1,0:T(8,128)S(1)} custom-call(f32[2,512]{1,0:T(2,128)S(1)} %copy-done.4, f32[1,512]{1,0:T(1,128)S(1)} %bitcast.5, f32[384,512]{1,0:T(8,128)S(1)} %conv0.1.state_ref, bf16[704,512]{1,0:T(8,128)(2,1)S(1)} %pack_own.1.refs_4_.refs_0_.refs_1_, bf16[704,512]{1,0:T(8,128)(2,1)S(1)} %collective-permute-done.refs_5_.refs_1_.refs_2_, ...), custom_call_target="tpu_custom_call" | custom-call | tf_op jit(solution)/shard_map/ff0/pallas_call | solution.py:259
  65.4 0.9 conv1.1.state_ref
  66.3 0.8 collective-permute-start.17
  67.2 1.6 %ff1.2 = (f32[384,512]{1,0:T(8,128)S(1)}, bf16[384,512]{1,0:T(8,128)(2,1)S(1)}) custom-call(f32[2,512]{1,0:T(2,128)S(1)} %copy-done.4, f32[1,512]{1,0:T(1,128)S(1)} %bitcast.6, f32[384,512]{1,0:T(8,128)S(1)} %conv1.1.state_ref, bf16[704,512]{1,0:T(8,128)(2,1)S(1)} %pack_own.1.refs_4_.refs_0_.refs_1_, ...), custom_call_target="tpu_custom_call" | custom-call | tf_op jit(solution)/shard_map/ff1/pallas_call | solution.py:259
  68.8 0.0 copy-start
  68.8 0.0 copy-start.1
  68.8 0.0 copy-start.2
  68.8 0.9 %ff1.3.final_ref = bf16[384,512]{1,0:T(8,128)(2,1)S(1)} custom-call(f32[2,512]{1,0:T(2,128)S(1)} %copy-done.4, f32[1,512]{1,0:T(1,128)S(1)} %bitcast.7, f32[384,512]{1,0:T(8,128)S(1)} %get-tuple-element.68.state_ref, bf16[384,512]{1,0:T(8,128)(2,1)S(1)} %get-tuple-element.69.refs_0_, bf16[512,512]{1,0:T(8,128)(2,1)S(1)} %constant_dynamic-update-slice_fusion.2.refs_1_, ...), custom_call_target="tpu_custom_call" | custom-call | tf_op jit(solution)/shard_map/ff1/pallas_call | solution.py:259
  69.7 0.3 collective-permute-start.18
  70.0 1.5 %collective-permute-done.18.opposite_ref = bf16[384,512]{1,0:T(8,128)(2,1)S(1)} collective-permute-done((bf16[384,512]{1,0:T(8,128)(2,1)S(1)}, bf16[384,512]{1,0:T(8,128)(2,1)S(1)}, u32[]{:S(2)}, u32[]{:S(2)}) %collective-permute-start.18) | collective-permute-done | bytes 393248 | tf_op jit(solution)/shard_map/ppermute | solution.py:80
  71.5 1.1 %head.1 = (bf16[96,512]{1,0:T(8,128)(2,1)S(1)}, bf16[96,512]{1,0:T(8,128)(2,1)S(1)}, bf16[96,512]{1,0:T(8,128)(2,1)S(1)}, bf16[96,512]{1,0:T(8,128)(2,1)S(1)}) custom-call(bf16[384,512]{1,0:T(8,128)(2,1)S(1)} %ff1.3.final_ref, bf16[384,512]{1,0:T(8,128)(2,1)S(1)} %collective-permute-done.18.opposite_ref, bf16[512,512]{1,0:T(8,128)(2,1)S(1)} %copy-done, ...), custom_call_target="tpu_custom_call" | custom-call | tf_op jit(solution)/shard_map/head/pallas_call | solution.py:357
  72.6 0.3 collective-permute-start.19
  72.8 2.8 %collective-permute-start.21 = (bf16[96,512]{1,0:T(8,128)(2,1)S(1)}, bf16[96,512]{1,0:T(8,128)(2,1)S(1)}, u32[]{:S(2)}, u32[]{:S(2)}) collective-permute-start(bf16[96,512]{1,0:T(8,128)(2,1)S(1)} %get-tuple-element.75), channel_id=1, source_target_pairs={{0,8},{1,9},{2,11},{3,10},{4,12},{5,13},{6,15},{7,14},{8,0},{9,1},... | collective-permute-start | bytes 294920 | tf_op jit(solution)/shard_map/ppermute | solution.py:80
  75.7 2.3 %collective-permute-start.22 = (bf16[96,512]{1,0:T(8,128)(2,1)S(1)}, bf16[96,512]{1,0:T(8,128)(2,1)S(1)}, u32[]{:S(2)}, u32[]{:S(2)}) collective-permute-start(bf16[96,512]{1,0:T(8,128)(2,1)S(1)} %get-tuple-element.76), channel_id=1, source_target_pairs={{0,12},{1,13},{2,15},{3,14},{4,8},{5,9},{6,11},{7,10},{8,4},{9,5},... | collective-permute-start | bytes 294920 | tf_op jit(solution)/shard_map/ppermute | solution.py:80
  78.0 1.5 %collective-permute-done.19.refs_1_ = bf16[96,512]{1,0:T(8,128)(2,1)S(1)} collective-permute-done((bf16[96,512]{1,0:T(8,128)(2,1)S(1)}, bf16[96,512]{1,0:T(8,128)(2,1)S(1)}, u32[]{:S(2)}, u32[]{:S(2)}) %collective-permute-start.19) | collective-permute-done | bytes 98336 | tf_op jit(solution)/shard_map/ppermute | solution.py:80
  79.4 2.9 %collective-permute-start.20 = (bf16[96,512]{1,0:T(8,128)(2,1)S(1)}, bf16[96,512]{1,0:T(8,128)(2,1)S(1)}, u32[]{:S(2)}, u32[]{:S(2)}) collective-permute-start(bf16[96,512]{1,0:T(8,128)(2,1)S(1)} %get-tuple-element.74), channel_id=1, source_target_pairs={{0,0},{1,1},{2,3},{3,2},{4,4},{5,5},{6,7},{7,6},{8,8},{9,9},{10,11... | collective-permute-start | bytes 294920 | tf_op jit(solution)/shard_map/ppermute | solution.py:80
  82.4 0.7 collective-permute-done.22.refs_3_
  83.2 1.6 %collective-permute-done.20.refs_0_ = bf16[96,512]{1,0:T(8,128)(2,1)S(1)} collective-permute-done((bf16[96,512]{1,0:T(8,128)(2,1)S(1)}, bf16[96,512]{1,0:T(8,128)(2,1)S(1)}, u32[]{:S(2)}, u32[]{:S(2)}) %collective-permute-start.20) | collective-permute-done | bytes 98336 | tf_op jit(solution)/shard_map/ppermute | solution.py:80
  84.8 0.8 join.1
  (35 shorter events, 0.4 us)
Async XLA Ops:
  0.0 5.1 %copy-start.3 = (bf16[1,384,512]{2,1,0:T(8,128)(2,1)S(1)}, bf16[1,384,512]{2,1,0:T(8,128)(2,1)}, u32[]{:S(2)}) copy-start(bf16[1,384,512]{2,1,0:T(8,128)(2,1)} %param.10) | copy-start | bytes 1179652
  1.7 20.1 %collective-permute-start = (bf16[704,512]{1,0:T(8,128)(2,1)S(1)}, bf16[704,512]{1,0:T(8,128)(2,1)S(1)}, u32[]{:S(2)}, u32[]{:S(2)}) collective-permute-start(bf16[704,512]{1,0:T(8,128)(2,1)S(1)} %pack_own.1.refs_4_.refs_0_.refs_1_), channel_id=1, source_target_pairs={{0,4},{1,5},{2,6},{3,7},{4,8},{5,9},{6,10},{7,11},{8,12},{9,13},{1... | collective-permute-start | bytes 2162696 | tf_op jit(solution)/shard_map/ppermute | solution.py:80
  3.9 25.7 %collective-permute-start.4 = (bf16[704,512]{1,0:T(8,128)(2,1)S(1)}, bf16[704,512]{1,0:T(8,128)(2,1)S(1)}, u32[]{:S(2)}, u32[]{:S(2)}) collective-permute-start(bf16[704,512]{1,0:T(8,128)(2,1)S(1)} %pack_own.1.refs_4_.refs_0_.refs_1_), channel_id=1, source_target_pairs={{0,1},{1,0},{2,3},{3,2},{4,5},{5,4},{6,7},{7,6},{8,9},{9,8},{10,11... | collective-permute-start | bytes 2162696 | tf_op jit(solution)/shard_map/ppermute | solution.py:80
  5.1 22.0 %collective-permute-start.7 = (bf16[96,512]{1,0:T(8,128)(2,1)S(1)}, bf16[96,512]{1,0:T(8,128)(2,1)S(1)}, u32[]{:S(2)}, u32[]{:S(2)}) collective-permute-start(bf16[96,512]{1,0:T(8,128)(2,1)S(1)} %get-tuple-element.44), channel_id=1, source_target_pairs={{0,0},{1,1},{2,3},{3,2},{4,4},{5,5},{6,7},{7,6},{8,8},{9,9},{10,11... | collective-permute-start | bytes 294920 | tf_op jit(solution)/shard_map/ppermute | solution.py:80
  21.7 18.2 %collective-permute-start.1 = (bf16[704,512]{1,0:T(8,128)(2,1)S(1)}, bf16[704,512]{1,0:T(8,128)(2,1)S(1)}, u32[]{:S(2)}, u32[]{:S(2)}) collective-permute-start(bf16[704,512]{1,0:T(8,128)(2,1)S(1)} %collective-permute-done.refs_5_.refs_1_.refs_2_), channel_id=1, source_target_pairs={{0,4},{1,5},{2,6},{3,7},{4,8},{5,9},{6,10},{7,11},{8,12},{9,13},{1... | collective-permute-start | bytes 2162696 | tf_op jit(solution)/shard_map/ppermute | solution.py:80
  21.7 18.2 %collective-permute-start.2 = (bf16[704,512]{1,0:T(8,128)(2,1)S(1)}, bf16[704,512]{1,0:T(8,128)(2,1)S(1)}, u32[]{:S(2)}, u32[]{:S(2)}) collective-permute-start(bf16[704,512]{1,0:T(8,128)(2,1)S(1)} %collective-permute-done.refs_5_.refs_1_.refs_2_), channel_id=1, source_target_pairs={{0,1},{1,0},{2,3},{3,2},{4,5},{5,4},{6,7},{7,6},{8,9},{9,8},{10,11... | collective-permute-start | bytes 2162696 | tf_op jit(solution)/shard_map/ppermute | solution.py:80
  22.7 18.8 %collective-permute-start.3 = (bf16[704,512]{1,0:T(8,128)(2,1)S(1)}, bf16[704,512]{1,0:T(8,128)(2,1)S(1)}, u32[]{:S(2)}, u32[]{:S(2)}) collective-permute-start(bf16[704,512]{1,0:T(8,128)(2,1)S(1)} %collective-permute-done.refs_5_.refs_1_.refs_2_), channel_id=1, source_target_pairs={{0,16},{1,17},{2,18},{3,19},{4,20},{5,21},{6,22},{7,23},{8,24},{9,... | collective-permute-start | bytes 2162696 | tf_op jit(solution)/shard_map/ppermute | solution.py:80
  27.1 14.3 %collective-permute-start.5 = (bf16[704,512]{1,0:T(8,128)(2,1)S(1)}, bf16[704,512]{1,0:T(8,128)(2,1)S(1)}, u32[]{:S(2)}, u32[]{:S(2)}) collective-permute-start(bf16[704,512]{1,0:T(8,128)(2,1)S(1)} %collective-permute-done.refs_5_.refs_1_.refs_2_), channel_id=1, source_target_pairs={{0,2},{1,3},{2,0},{3,1},{4,6},{5,7},{6,4},{7,5},{8,10},{9,11},{10,... | collective-permute-start | bytes 2162696 | tf_op jit(solution)/shard_map/ppermute | solution.py:80
  29.5 12.0 %collective-permute-start.6 = (bf16[704,512]{1,0:T(8,128)(2,1)S(1)}, bf16[704,512]{1,0:T(8,128)(2,1)S(1)}, u32[]{:S(2)}, u32[]{:S(2)}) collective-permute-start(bf16[704,512]{1,0:T(8,128)(2,1)S(1)} %collective-permute-done.4.refs_7_.refs_3_.refs_4_), channel_id=1, source_target_pairs={{0,2},{1,3},{2,0},{3,1},{4,6},{5,7},{6,4},{7,5},{8,10},{9,11},{10,... | collective-permute-start | bytes 2162696 | tf_op jit(solution)/shard_map/ppermute | solution.py:80
  41.5 13.1 %collective-permute-start.8 = (bf16[448,512]{1,0:T(8,128)(2,1)S(1)}, bf16[448,512]{1,0:T(8,128)(2,1)S(1)}, u32[]{:S(2)}, u32[]{:S(2)}) collective-permute-start(bf16[448,512]{1,0:T(8,128)(2,1)S(1)} %slice.26), channel_id=1, source_target_pairs={{0,1},{1,0},{2,3},{3,2},{4,5},{5,4},{6,7},{7,6},{8,9},{9,8},{10,11... | collective-permute-start | bytes 1376264 | tf_op jit(solution)/shard_map/ppermute | solution.py:80
  41.9 12.8 %collective-permute-start.9 = (bf16[448,512]{1,0:T(8,128)(2,1)S(1)}, bf16[448,512]{1,0:T(8,128)(2,1)S(1)}, u32[]{:S(2)}, u32[]{:S(2)}) collective-permute-start(bf16[448,512]{1,0:T(8,128)(2,1)S(1)} %slice.27), channel_id=1, source_target_pairs={{0,16},{1,17},{2,18},{3,19},{4,20},{5,21},{6,22},{7,23},{8,24},{9,... | collective-permute-start | bytes 1376264 | tf_op jit(solution)/shard_map/ppermute | solution.py:80
  43.2 5.5 %collective-permute-start.10 = (bf16[96,512]{1,0:T(8,128)(2,1)S(1)}, bf16[96,512]{1,0:T(8,128)(2,1)S(1)}, u32[]{:S(2)}, u32[]{:S(2)}) collective-permute-start(bf16[96,512]{1,0:T(8,128)(2,1)S(1)} %get-tuple-element.52), channel_id=1, source_target_pairs={{0,4},{1,5},{2,7},{3,6},{4,0},{5,1},{6,3},{7,2},{8,12},{9,13},{10,... | collective-permute-start | bytes 294920 | tf_op jit(solution)/shard_map/ppermute | solution.py:80
  43.2 5.5 %collective-permute-start.11 = (bf16[96,512]{1,0:T(8,128)(2,1)S(1)}, bf16[96,512]{1,0:T(8,128)(2,1)S(1)}, u32[]{:S(2)}, u32[]{:S(2)}) collective-permute-start(bf16[96,512]{1,0:T(8,128)(2,1)S(1)} %get-tuple-element.53), channel_id=1, source_target_pairs={{0,8},{1,9},{2,11},{3,10},{4,12},{5,13},{6,15},{7,14},{8,0},{9,1},... | collective-permute-start | bytes 294920 | tf_op jit(solution)/shard_map/ppermute | solution.py:80
  46.4 6.4 %collective-permute-start.12 = (bf16[96,512]{1,0:T(8,128)(2,1)S(1)}, bf16[96,512]{1,0:T(8,128)(2,1)S(1)}, u32[]{:S(2)}, u32[]{:S(2)}) collective-permute-start(bf16[96,512]{1,0:T(8,128)(2,1)S(1)} %get-tuple-element.54), channel_id=1, source_target_pairs={{0,12},{1,13},{2,15},{3,14},{4,8},{5,9},{6,11},{7,10},{8,4},{9,5},... | collective-permute-start | bytes 294920 | tf_op jit(solution)/shard_map/ppermute | solution.py:80
  54.8 7.3 %copy-start.6 = (f32[2,512]{1,0:T(2,128)S(1)}, f32[2,512]{1,0:T(2,128)}, u32[]{:S(2)}) copy-start(f32[2,512]{1,0:T(2,128)} %gain_ref.7) | copy-start | bytes 12292
  54.9 7.2 %collective-permute-start.13 = (bf16[2240,512]{1,0:T(8,128)(2,1)S(1)}, bf16[2240,512]{1,0:T(8,128)(2,1)S(1)}, u32[]{:S(2)}, u32[]{:S(2)}) collective-permute-start(bf16[2240,512]{1,0:T(8,128)(2,1)S(1)} %constant_dynamic-update-slice_fusion), channel_id=1, source_target_pairs={{0,2},{1,3},{2,0},{3,1},{4,6},{5,7},{6,4},{7,5},{8,10},{9,11},{10,... | collective-permute-start | bytes 6881288 | tf_op jit(solution)/shard_map/ppermute | solution.py:80
  58.0 8.3 %collective-permute-start.15 = (bf16[256,512]{1,0:T(8,128)(2,1)S(1)}, bf16[256,512]{1,0:T(8,128)(2,1)S(1)}, u32[]{:S(2)}, u32[]{:S(2)}) collective-permute-start(bf16[256,512]{1,0:T(8,128)(2,1)S(1)} %slice.31), channel_id=1, source_target_pairs={{0,1},{1,0},{2,3},{3,2},{4,5},{5,4},{6,7},{7,6},{8,9},{9,8},{10,11... | collective-permute-start | bytes 786440 | tf_op jit(solution)/shard_map/ppermute | solution.py:80
  58.3 7.9 %collective-permute-start.16 = (bf16[256,512]{1,0:T(8,128)(2,1)S(1)}, bf16[256,512]{1,0:T(8,128)(2,1)S(1)}, u32[]{:S(2)}, u32[]{:S(2)}) collective-permute-start(bf16[256,512]{1,0:T(8,128)(2,1)S(1)} %slice.32), channel_id=1, source_target_pairs={{0,16},{1,17},{2,18},{3,19},{4,20},{5,21},{6,22},{7,23},{8,24},{9,... | collective-permute-start | bytes 786440 | tf_op jit(solution)/shard_map/ppermute | solution.py:80
  59.6 3.8 %copy-start.4 = (f32[2,512]{1,0:T(2,128)S(1)}, f32[2,512]{1,0:T(2,128)}, u32[]{:S(2)}) copy-start(f32[2,512]{1,0:T(2,128)} %gain_ref.9) | copy-start | bytes 12292
  59.6 3.7 %copy-start.5 = (f32[512]{0:T(512)S(1)}, f32[512]{0:T(512)}, u32[]{:S(2)}) copy-start(f32[512]{0:T(512)} %param.16) | copy-start | bytes 6148
  62.9 4.2 %collective-permute-start.14 = (bf16[768,512]{1,0:T(8,128)(2,1)S(1)}, bf16[768,512]{1,0:T(8,128)(2,1)S(1)}, u32[]{:S(2)}, u32[]{:S(2)}) collective-permute-start(bf16[768,512]{1,0:T(8,128)(2,1)S(1)} %pad_maximum_fusion), channel_id=1, source_target_pairs={{0,2},{1,3},{2,0},{3,1},{4,6},{5,7},{6,4},{7,5},{8,10},{9,11},{10,... | collective-permute-start | bytes 2359304 | tf_op jit(solution)/shard_map/ppermute | solution.py:80
  66.3 2.5 %collective-permute-start.17 = (bf16[512,512]{1,0:T(8,128)(2,1)S(1)}, bf16[512,512]{1,0:T(8,128)(2,1)S(1)}, u32[]{:S(2)}, u32[]{:S(2)}) collective-permute-start(bf16[512,512]{1,0:T(8,128)(2,1)S(1)} %constant_dynamic-update-slice_fusion.2.refs_1_), channel_id=1, source_target_pairs={{0,2},{1,3},{2,0},{3,1},{4,6},{5,7},{6,4},{7,5},{8,10},{9,11},{10,... | collective-permute-start | bytes 1572872 | tf_op jit(solution)/shard_map/ppermute | solution.py:80
  68.8 2.7 %copy-start = (bf16[512,512]{1,0:T(8,128)(2,1)S(1)}, bf16[512,512]{1,0:T(8,128)(2,1)}, u32[]{:S(2)}) copy-start(bf16[512,512]{1,0:T(8,128)(2,1)} %value_ref.1) | copy-start | bytes 1572868
  68.8 2.7 %copy-start.1 = (bf16[512,512]{1,0:T(8,128)(2,1)S(1)}, bf16[512,512]{1,0:T(8,128)(2,1)}, u32[]{:S(2)}) copy-start(bf16[512,512]{1,0:T(8,128)(2,1)} %gate_ref.1) | copy-start | bytes 1572868
  68.8 2.7 %copy-start.2 = (bf16[512,512]{1,0:T(8,128)(2,1)S(1)}, bf16[512,512]{1,0:T(8,128)(2,1)}, u32[]{:S(2)}) copy-start(bf16[512,512]{1,0:T(8,128)(2,1)} %out_ref.1) | copy-start | bytes 1572868
  69.7 1.8 %collective-permute-start.18 = (bf16[384,512]{1,0:T(8,128)(2,1)S(1)}, bf16[384,512]{1,0:T(8,128)(2,1)S(1)}, u32[]{:S(2)}, u32[]{:S(2)}) collective-permute-start(bf16[384,512]{1,0:T(8,128)(2,1)S(1)} %ff1.3.final_ref), channel_id=1, source_target_pairs={{0,2},{1,3},{2,0},{3,1},{4,6},{5,7},{6,4},{7,5},{8,10},{9,11},{10,... | collective-permute-start | bytes 1179656 | tf_op jit(solution)/shard_map/ppermute | solution.py:80
  72.6 6.9 %collective-permute-start.19 = (bf16[96,512]{1,0:T(8,128)(2,1)S(1)}, bf16[96,512]{1,0:T(8,128)(2,1)S(1)}, u32[]{:S(2)}, u32[]{:S(2)}) collective-permute-start(bf16[96,512]{1,0:T(8,128)(2,1)S(1)} %get-tuple-element.73), channel_id=1, source_target_pairs={{0,4},{1,5},{2,7},{3,6},{4,0},{5,1},{6,3},{7,2},{8,12},{9,13},{10,... | collective-permute-start | bytes 294920 | tf_op jit(solution)/shard_map/ppermute | solution.py:80
  72.8 9.6 %collective-permute-start.21 = (bf16[96,512]{1,0:T(8,128)(2,1)S(1)}, bf16[96,512]{1,0:T(8,128)(2,1)S(1)}, u32[]{:S(2)}, u32[]{:S(2)}) collective-permute-start(bf16[96,512]{1,0:T(8,128)(2,1)S(1)} %get-tuple-element.75), channel_id=1, source_target_pairs={{0,8},{1,9},{2,11},{3,10},{4,12},{5,13},{6,15},{7,14},{8,0},{9,1},... | collective-permute-start | bytes 294920 | tf_op jit(solution)/shard_map/ppermute | solution.py:80
  75.7 7.5 %collective-permute-start.22 = (bf16[96,512]{1,0:T(8,128)(2,1)S(1)}, bf16[96,512]{1,0:T(8,128)(2,1)S(1)}, u32[]{:S(2)}, u32[]{:S(2)}) collective-permute-start(bf16[96,512]{1,0:T(8,128)(2,1)S(1)} %get-tuple-element.76), channel_id=1, source_target_pairs={{0,12},{1,13},{2,15},{3,14},{4,8},{5,9},{6,11},{7,10},{8,4},{9,5},... | collective-permute-start | bytes 294920 | tf_op jit(solution)/shard_map/ppermute | solution.py:80
  79.4 5.3 %collective-permute-start.20 = (bf16[96,512]{1,0:T(8,128)(2,1)S(1)}, bf16[96,512]{1,0:T(8,128)(2,1)S(1)}, u32[]{:S(2)}, u32[]{:S(2)}) collective-permute-start(bf16[96,512]{1,0:T(8,128)(2,1)S(1)} %get-tuple-element.74), channel_id=1, source_target_pairs={{0,0},{1,1},{2,3},{3,2},{4,4},{5,5},{6,7},{7,6},{8,8},{9,9},{10,11... | collective-permute-start | bytes 294920 | tf_op jit(solution)/shard_map/ppermute | solution.py:80

commit v8 on v7

--- a/solution.py
+++ b/solution.py
@@ -173,15 +173,35 @@
         out[...] = rows_ref[pl.ds(pl.multiple_of(sub * size, size), size)]
 
 
-def join_kernel(*refs):
-    *parts, out = refs
+def join_kernel(order, *refs):
+    parts, out, sems = refs[: len(order)], refs[-2], refs[-1]
     n = lax.axis_size("seq")
     i, s = lax.axis_index("seq"), lax.axis_index("strand")
     size = parts[0].shape[0]
-    for k, part in enumerate(parts):
+    copies = []
+    for k, part in zip(order, parts):
         j = i ^ k
         sub = jnp.where(s == 0, j, n - 1 - j)
-        out[pl.ds(pl.multiple_of(sub * size, size), size)] = part[...]
+        rows = pl.ds(pl.multiple_of(sub * size, size), size)
+        copies.append(pltpu.make_async_copy(part, out.at[rows], sems.at[len(copies)]))
+        copies[-1].start()
+    for copy in copies:
+        copy.wait()
+
+
+def join(parts, order, begun, shape):
+    hbm = pl.BlockSpec(memory_space=pltpu.HBM)
+    extra = [] if begun is None else [begun]
+    return pl.pallas_call(
+        functools.partial(join_kernel, order),
+        out_shape=shape,
+        in_specs=[VMEM_SPEC] * len(parts) + [hbm] * len(extra),
+        out_specs=hbm,
+        scratch_shapes=[pltpu.SemaphoreType.DMA((len(parts),))],
+        input_output_aliases={len(parts): 0} if extra else {},
+        compiler_params=PARAMS,
+        name="join_rest" if extra else "join_first",
+    )(*parts, *extra)
 
 
 def conv_kernel(block, parts, places, start, gain_ref, *refs):
@@ -267,12 +287,16 @@
     )(gain, head, *given, *arrays)
 
 
-def head_kernel(sends, final_ref, opposite_ref, value_ref, gate_ref, out_ref, *refs):
+def value_kernel(final_ref, weight_ref, value_ref):
+    value_ref[...] = matmul(final_ref[...], weight_ref[...])
+
+
+def head_kernel(sends, value_ref, opposite_ref, gate_ref, out_ref, *refs):
     *outs, result = refs
     n = len(outs)
     size = outs[0].shape[0]
     j = lax.axis_index("seq")
-    value = matmul(final_ref[...], value_ref[...])
+    value = value_ref[...]
     row = lax.broadcasted_iota(jnp.int32, (size, size), 0)
     col = lax.broadcasted_iota(jnp.int32, (size, size), 1)
     reverse = jnp.where(row + col == size - 1, 1.0, 0.0).astype(BF16)
@@ -310,6 +334,7 @@
 
     a = along(own)
     x = across(own)
+    a, x = after([a, x], [])
     b = along(a)
     xa = across(a)
     ya = planes(a)
@@ -353,19 +378,23 @@
     arrays = [late, other_core(late)]
     (final,) = feed_forward(state, mixed, ff_norm, head, arrays, places, 1, 0, half, "head")
     opposite = other_core(final)
+    value = pl.pallas_call(
+        value_kernel, out_shape=jax.ShapeDtypeStruct((rows, width), F32), in_specs=[VMEM_SPEC] * 2,
+        out_specs=VMEM_SPEC, compiler_params=PARAMS, name="value",
+    )(final, value_weight)
     sends = [2, 3, 1, 0]
     results = pl.pallas_call(
-        functools.partial(head_kernel, sends), out_shape=[part] * n, in_specs=[VMEM_SPEC] * 5, out_specs=[VMEM_SPEC] * n,
+        functools.partial(head_kernel, sends), out_shape=[part] * n, in_specs=[VMEM_SPEC] * 4, out_specs=[VMEM_SPEC] * n,
         scratch_shapes=[pltpu.VMEM((rows, width), BF16)], compiler_params=PARAMS, name="head",
-    )(final, opposite, value_weight, gate_weight, out_weight)
+    )(value, opposite, gate_weight, out_weight)
     ready = dict(zip(sends, results))
     home = {k: moved(ready[k], to(k)) for k in sends if k}
     (near,) = after([ready[0]], [home[1]])
     home = [moved(near, to(0))] + [home[k] for k in range(1, n)]
-    joined = pl.pallas_call(
-        join_kernel, out_shape=jax.ShapeDtypeStruct((rows, width), BF16), in_specs=[VMEM_SPEC] * n,
-        out_specs=VMEM_SPEC, compiler_params=PARAMS, name="join",
-    )(*home)
+    whole = jax.ShapeDtypeStruct((rows, width), BF16)
+    joined = None
+    for order in ((1,), (0, 2, 3)):
+        joined = join([home[k] for k in order], order, joined, whole)
     return joined[None]
 
 

time: 85.8 us -> 85.4 us (level)
  waiting for transfers between devices: 38.6 us -> 37.6 us
    pallas_call x1 -> x3, Pallas kernels: 0.78 us -> 1.75 us  [the longest x2 1.39 us: join(): pl.pallas_call(functools.partial(join_kernel, order), out_shape=shape, in...]
    ppermute x23, waiting for transfers between devices: 38.6 us -> 37.6 us  [moved(): return lax.ppermute(value, AXES, pairs)]
  transfers between devices with their start and end apart: 23 -> 23, of which waited for: 11 -> 11; matrix products, arithmetic and copies ran while one was open for 0% -> 0% of each run, Pallas kernels for 8% -> 9%
where the time goes in v8:
time: 85.4 us; the launch traced here: 85.2 us
  waiting for transfers between devices  37.6 us (44%)
  starting transfers between devices  34.8 us (41%)
  Pallas kernels  12.1 us (14%)
    ppermute x23, waiting for transfers between devices, moved(): return lax.ppermute(value, AXES, pairs)  37.6 us
    ppermute x23, starting transfers between devices, moved(): return lax.ppermute(value, AXES, pairs)  34.8 us
    pallas_call x3, Pallas kernels, feed_forward(): pl.pallas_call(functools.partial(ff_kernel, block, mixed is None, ends, p...  4.5 us
    pallas_call x2, Pallas kernels, pack(): pl.pallas_call(functools.partial(pack_kernel, (blocks, turned), mine), ou...  3.28 us
    pallas_call x2, Pallas kernels, conv(): pl.pallas_call(functools.partial(conv_kernel, block, len(states), places,...  1.76 us
  transfers between devices with their start and end apart: 23, of which 11 were waited for; matrix products, arithmetic and copies ran while one was open for 0% of the time, Pallas kernels for 9%

profile of v8, /device:TPU:1, one launch (start us, length us, event | category | flops | bytes accessed | tf_op | source)
XLA Modules:
  0.0 85.2 jit_solution(837004139724630977)
XLA Ops:
  0.0 1.7 %pack_own.1.refs_4_.refs_0_.refs_1_ = bf16[704,512]{1,0:T(8,128)(2,1)S(1)} custom-call(bf16[2,512,256]{2,1,0:T(8,128)(2,1)} %refs_4_.2, bf16[2,256,512]{2,1,0:T(8,128)(2,1)} %refs_5_.2, bf16[2,3,64,512]{3,2,1,0:T(8,128)(2,1)} %bitcast.8, bf16[2,3,64,512]{3,2,1,0:T(8,128)(2,1)} %bitcast.9, bf16[2,512,256]{2,1,0:T(8,128)(2,1)} %refs_4_.2, ...), custom_call_target="tpu_custom_call" | custom-call | tf_op jit(solution)/shard_map/pack_own/pallas_call | solution.py:152
  1.7 2.2 %collective-permute-start = (bf16[704,512]{1,0:T(8,128)(2,1)S(1)}, bf16[704,512]{1,0:T(8,128)(2,1)S(1)}, u32[]{:S(2)}, u32[]{:S(2)}) collective-permute-start(bf16[704,512]{1,0:T(8,128)(2,1)S(1)} %pack_own.1.refs_4_.refs_0_.refs_1_), channel_id=1, source_target_pairs={{0,4},{1,5},{2,6},{3,7},{4,8},{5,9},{6,10},{7,11},{8,12},{9,13},{1... | collective-permute-start | bytes 2162696 | tf_op jit(solution)/shard_map/ppermute | solution.py:80
  3.9 1.2 %collective-permute-start.1 = (bf16[704,512]{1,0:T(8,128)(2,1)S(1)}, bf16[704,512]{1,0:T(8,128)(2,1)S(1)}, u32[]{:S(2)}, u32[]{:S(2)}) collective-permute-start(bf16[704,512]{1,0:T(8,128)(2,1)S(1)} %pack_own.1.refs_4_.refs_0_.refs_1_), channel_id=1, source_target_pairs={{0,1},{1,0},{2,3},{3,2},{4,5},{5,4},{6,7},{7,6},{8,9},{9,8},{10,11... | collective-permute-start | bytes 2162696 | tf_op jit(solution)/shard_map/ppermute | solution.py:80
  5.1 2.2 %collective-permute-start.7 = (bf16[96,512]{1,0:T(8,128)(2,1)S(1)}, bf16[96,512]{1,0:T(8,128)(2,1)S(1)}, u32[]{:S(2)}, u32[]{:S(2)}) collective-permute-start(bf16[96,512]{1,0:T(8,128)(2,1)S(1)} %get-tuple-element.48), channel_id=1, source_target_pairs={{0,0},{1,1},{2,3},{3,2},{4,4},{5,5},{6,7},{7,6},{8,8},{9,9},{10,11... | collective-permute-start | bytes 294920 | tf_op jit(solution)/shard_map/ppermute | solution.py:80
  7.3 14.5 %collective-permute-done.refs_5_.refs_1_.refs_2_ = bf16[704,512]{1,0:T(8,128)(2,1)S(1)} collective-permute-done((bf16[704,512]{1,0:T(8,128)(2,1)S(1)}, bf16[704,512]{1,0:T(8,128)(2,1)S(1)}, u32[]{:S(2)}, u32[]{:S(2)}) %collective-permute-start) | collective-permute-done | bytes 720928 | tf_op jit(solution)/shard_map/ppermute | solution.py:80
  21.7 0.1 collective-permute-start.2
  21.8 1.2 %collective-permute-start.3 = (bf16[704,512]{1,0:T(8,128)(2,1)S(1)}, bf16[704,512]{1,0:T(8,128)(2,1)S(1)}, u32[]{:S(2)}, u32[]{:S(2)}) collective-permute-start(bf16[704,512]{1,0:T(8,128)(2,1)S(1)} %collective-permute-done.refs_5_.refs_1_.refs_2_), channel_id=1, source_target_pairs={{0,1},{1,0},{2,3},{3,2},{4,5},{5,4},{6,7},{7,6},{8,9},{9,8},{10,11... | collective-permute-start | bytes 2162696 | tf_op jit(solution)/shard_map/ppermute | solution.py:80
  23.1 4.1 %collective-permute-start.4 = (bf16[704,512]{1,0:T(8,128)(2,1)S(1)}, bf16[704,512]{1,0:T(8,128)(2,1)S(1)}, u32[]{:S(2)}, u32[]{:S(2)}) collective-permute-start(bf16[704,512]{1,0:T(8,128)(2,1)S(1)} %collective-permute-done.refs_5_.refs_1_.refs_2_), channel_id=1, source_target_pairs={{0,16},{1,17},{2,18},{3,19},{4,20},{5,21},{6,22},{7,23},{8,24},{9,... | collective-permute-start | bytes 2162696 | tf_op jit(solution)/shard_map/ppermute | solution.py:80
  27.1 2.4 %collective-permute-start.5 = (bf16[704,512]{1,0:T(8,128)(2,1)S(1)}, bf16[704,512]{1,0:T(8,128)(2,1)S(1)}, u32[]{:S(2)}, u32[]{:S(2)}) collective-permute-start(bf16[704,512]{1,0:T(8,128)(2,1)S(1)} %collective-permute-done.refs_5_.refs_1_.refs_2_), channel_id=1, source_target_pairs={{0,2},{1,3},{2,0},{3,1},{4,6},{5,7},{6,4},{7,5},{8,10},{9,11},{10,... | collective-permute-start | bytes 2162696 | tf_op jit(solution)/shard_map/ppermute | solution.py:80
  29.5 1.6 %pack_rest.1.refs_12_.refs_8_.refs_9_.refs_6_ = bf16[704,512]{1,0:T(8,128)(2,1)S(1)} custom-call(bf16[2,512,256]{2,1,0:T(8,128)(2,1)} %refs_4_.2, bf16[2,256,512]{2,1,0:T(8,128)(2,1)} %refs_5_.2, bf16[2,3,64,512]{3,2,1,0:T(8,128)(2,1)} %bitcast.10, bf16[2,3,64,512]{3,2,1,0:T(8,128)(2,1)} %bitcast.11, bf16[2,512,256]{2,1,0:T(8,128)(2,1)} %refs_4_.2, ...), custom_call_target="tpu_custom_call" | custom-call | tf_op jit(solution)/shard_map/pack_rest/pallas_call | solution.py:152
  31.2 8.3 %collective-permute-done.2.refs_6_.refs_2_.refs_3_ = bf16[704,512]{1,0:T(8,128)(2,1)S(1)} collective-permute-done((bf16[704,512]{1,0:T(8,128)(2,1)S(1)}, bf16[704,512]{1,0:T(8,128)(2,1)S(1)}, u32[]{:S(2)}, u32[]{:S(2)}) %collective-permute-start.2) | collective-permute-done | bytes 720928 | tf_op jit(solution)/shard_map/ppermute | solution.py:80
  39.5 2.0 %collective-permute-done.4.refs_9_.refs_5_.refs_6_ = bf16[704,512]{1,0:T(8,128)(2,1)S(1)} collective-permute-done((bf16[704,512]{1,0:T(8,128)(2,1)S(1)}, bf16[704,512]{1,0:T(8,128)(2,1)S(1)}, u32[]{:S(2)}, u32[]{:S(2)}) %collective-permute-start.4) | collective-permute-done | bytes 720928 | tf_op jit(solution)/shard_map/ppermute | solution.py:80
  41.5 0.3 collective-permute-start.8
  41.9 1.3 %collective-permute-start.9 = (bf16[448,512]{1,0:T(8,128)(2,1)S(1)}, bf16[448,512]{1,0:T(8,128)(2,1)S(1)}, u32[]{:S(2)}, u32[]{:S(2)}) collective-permute-start(bf16[448,512]{1,0:T(8,128)(2,1)S(1)} %slice.27), channel_id=1, source_target_pairs={{0,16},{1,17},{2,18},{3,19},{4,20},{5,21},{6,22},{7,23},{8,24},{9,... | collective-permute-start | bytes 1376264 | tf_op jit(solution)/shard_map/ppermute | solution.py:80
  43.2 3.3 %collective-permute-start.11 = (bf16[96,512]{1,0:T(8,128)(2,1)S(1)}, bf16[96,512]{1,0:T(8,128)(2,1)S(1)}, u32[]{:S(2)}, u32[]{:S(2)}) collective-permute-start(bf16[96,512]{1,0:T(8,128)(2,1)S(1)} %get-tuple-element.57), channel_id=1, source_target_pairs={{0,8},{1,9},{2,11},{3,10},{4,12},{5,13},{6,15},{7,14},{8,0},{9,1},... | collective-permute-start | bytes 294920 | tf_op jit(solution)/shard_map/ppermute | solution.py:80
  46.4 2.1 %collective-permute-start.12 = (bf16[96,512]{1,0:T(8,128)(2,1)S(1)}, bf16[96,512]{1,0:T(8,128)(2,1)S(1)}, u32[]{:S(2)}, u32[]{:S(2)}) collective-permute-start(bf16[96,512]{1,0:T(8,128)(2,1)S(1)} %get-tuple-element.58), channel_id=1, source_target_pairs={{0,12},{1,13},{2,15},{3,14},{4,8},{5,9},{6,11},{7,10},{8,4},{9,5},... | collective-permute-start | bytes 294920 | tf_op jit(solution)/shard_map/ppermute | solution.py:80
  48.5 0.2 collective-permute-done.10.refs_1_
  48.7 4.0 %collective-permute-done.12.refs_3_ = bf16[96,512]{1,0:T(8,128)(2,1)S(1)} collective-permute-done((bf16[96,512]{1,0:T(8,128)(2,1)S(1)}, bf16[96,512]{1,0:T(8,128)(2,1)S(1)}, u32[]{:S(2)}, u32[]{:S(2)}) %collective-permute-start.12) | collective-permute-done | bytes 98336 | tf_op jit(solution)/shard_map/ppermute | solution.py:80
  52.7 1.9 %collective-permute-done.8.refs_10_.refs_6_.refs_7_ = bf16[448,512]{1,0:T(8,128)(2,1)S(1)} collective-permute-done((bf16[448,512]{1,0:T(8,128)(2,1)S(1)}, bf16[448,512]{1,0:T(8,128)(2,1)S(1)}, u32[]{:S(2)}, u32[]{:S(2)}) %collective-permute-start.8) | collective-permute-done | bytes 458784 | tf_op jit(solution)/shard_map/ppermute | solution.py:80
  54.8 0.0 copy-start.6
  54.9 3.1 %collective-permute-start.13 = (bf16[2240,512]{1,0:T(8,128)(2,1)S(1)}, bf16[2240,512]{1,0:T(8,128)(2,1)S(1)}, u32[]{:S(2)}, u32[]{:S(2)}) collective-permute-start(bf16[2240,512]{1,0:T(8,128)(2,1)S(1)} %constant_dynamic-update-slice_fusion), channel_id=1, source_target_pairs={{0,2},{1,3},{2,0},{3,1},{4,6},{5,7},{6,4},{7,5},{8,10},{9,11},{10,... | collective-permute-start | bytes 6881288 | tf_op jit(solution)/shard_map/ppermute | solution.py:80
  58.0 0.3 collective-permute-start.15
  58.3 1.2 %collective-permute-start.16 = (bf16[256,512]{1,0:T(8,128)(2,1)S(1)}, bf16[256,512]{1,0:T(8,128)(2,1)S(1)}, u32[]{:S(2)}, u32[]{:S(2)}) collective-permute-start(bf16[256,512]{1,0:T(8,128)(2,1)S(1)} %slice.32), channel_id=1, source_target_pairs={{0,16},{1,17},{2,18},{3,19},{4,20},{5,21},{6,22},{7,23},{8,24},{9,... | collective-permute-start | bytes 786440 | tf_op jit(solution)/shard_map/ppermute | solution.py:80
  59.6 0.1 pad_maximum_fusion
  59.6 0.0 copy-start.4
  59.6 0.0 copy-start.5
  59.7 2.4 %collective-permute-done.13.refs_15_.refs_11_.refs_12_ = bf16[2240,512]{1,0:T(8,128)(2,1)S(1)} collective-permute-done((bf16[2240,512]{1,0:T(8,128)(2,1)S(1)}, bf16[2240,512]{1,0:T(8,128)(2,1)S(1)}, u32[]{:S(2)}, u32[]{:S(2)}) %collective-permute-start.13) | collective-permute-done | bytes 2293792 | tf_op jit(solution)/shard_map/ppermute | solution.py:80
  62.0 0.9 %conv0.1.state_ref = f32[384,512]{1,0:T(8,128)S(1)} custom-call(f32[2,512]{1,0:T(2,128)S(1)} %copy-done.6, bf16[96,512]{1,0:T(8,128)(2,1)S(1)} %collective-permute-done.7.refs_0_, bf16[96,512]{1,0:T(8,128)(2,1)S(1)} %collective-permute-done.10.refs_1_, bf16[96,512]{1,0:T(8,128)(2,1)S(1)} %collective-permute-done.11.refs_2_, ...), custom_call_target="tpu_custom_call" | custom-call | tf_op jit(solution)/shard_map/conv0/pallas_call | solution.py:240
  62.9 0.4 collective-permute-start.14
  63.4 2.0 %ff0.1.refs_0_ = f32[384,512]{1,0:T(8,128)S(1)} custom-call(f32[2,512]{1,0:T(2,128)S(1)} %copy-done.4, f32[1,512]{1,0:T(1,128)S(1)} %bitcast.5, f32[384,512]{1,0:T(8,128)S(1)} %conv0.1.state_ref, bf16[704,512]{1,0:T(8,128)(2,1)S(1)} %pack_own.1.refs_4_.refs_0_.refs_1_, bf16[704,512]{1,0:T(8,128)(2,1)S(1)} %collective-permute-done.refs_5_.refs_1_.refs_2_, ...), custom_call_target="tpu_custom_call" | custom-call | tf_op jit(solution)/shard_map/ff0/pallas_call | solution.py:279
  65.4 0.9 conv1.1.state_ref
  66.3 0.8 collective-permute-start.17
  67.2 1.6 %ff1.2 = (f32[384,512]{1,0:T(8,128)S(1)}, bf16[384,512]{1,0:T(8,128)(2,1)S(1)}) custom-call(f32[2,512]{1,0:T(2,128)S(1)} %copy-done.4, f32[1,512]{1,0:T(1,128)S(1)} %bitcast.6, f32[384,512]{1,0:T(8,128)S(1)} %conv1.1.state_ref, bf16[704,512]{1,0:T(8,128)(2,1)S(1)} %pack_own.1.refs_4_.refs_0_.refs_1_, ...), custom_call_target="tpu_custom_call" | custom-call | tf_op jit(solution)/shard_map/ff1/pallas_call | solution.py:279
  68.8 0.0 copy-start.1
  68.8 0.9 %ff1.3.final_ref = bf16[384,512]{1,0:T(8,128)(2,1)S(1)} custom-call(f32[2,512]{1,0:T(2,128)S(1)} %copy-done.4, f32[1,512]{1,0:T(1,128)S(1)} %bitcast.7, f32[384,512]{1,0:T(8,128)S(1)} %get-tuple-element.72.state_ref, bf16[384,512]{1,0:T(8,128)(2,1)S(1)} %get-tuple-element.73.refs_0_, bf16[512,512]{1,0:T(8,128)(2,1)S(1)} %constant_dynamic-update-slice_fusion.2.refs_1_, ...), custom_call_target="tpu_custom_call" | custom-call | tf_op jit(solution)/shard_map/ff1/pallas_call | solution.py:279
  69.7 0.3 collective-permute-start.18
  70.0 0.4 value.1.value_ref
  70.4 1.1 %collective-permute-done.18.opposite_ref = bf16[384,512]{1,0:T(8,128)(2,1)S(1)} collective-permute-done((bf16[384,512]{1,0:T(8,128)(2,1)S(1)}, bf16[384,512]{1,0:T(8,128)(2,1)S(1)}, u32[]{:S(2)}, u32[]{:S(2)}) %collective-permute-start.18) | collective-permute-done | bytes 393248 | tf_op jit(solution)/shard_map/ppermute | solution.py:80
  71.5 0.8 head.1
  72.3 0.3 collective-permute-start.19
  72.6 2.8 %collective-permute-start.21 = (bf16[96,512]{1,0:T(8,128)(2,1)S(1)}, bf16[96,512]{1,0:T(8,128)(2,1)S(1)}, u32[]{:S(2)}, u32[]{:S(2)}) collective-permute-start(bf16[96,512]{1,0:T(8,128)(2,1)S(1)} %get-tuple-element.79), channel_id=1, source_target_pairs={{0,8},{1,9},{2,11},{3,10},{4,12},{5,13},{6,15},{7,14},{8,0},{9,1},... | collective-permute-start | bytes 294920 | tf_op jit(solution)/shard_map/ppermute | solution.py:80
  75.4 2.3 %collective-permute-start.22 = (bf16[96,512]{1,0:T(8,128)(2,1)S(1)}, bf16[96,512]{1,0:T(8,128)(2,1)S(1)}, u32[]{:S(2)}, u32[]{:S(2)}) collective-permute-start(bf16[96,512]{1,0:T(8,128)(2,1)S(1)} %get-tuple-element.80), channel_id=1, source_target_pairs={{0,12},{1,13},{2,15},{3,14},{4,8},{5,9},{6,11},{7,10},{8,4},{9,5},... | collective-permute-start | bytes 294920 | tf_op jit(solution)/shard_map/ppermute | solution.py:80
  77.7 1.4 %collective-permute-done.19.refs_0_ = bf16[96,512]{1,0:T(8,128)(2,1)S(1)} collective-permute-done((bf16[96,512]{1,0:T(8,128)(2,1)S(1)}, bf16[96,512]{1,0:T(8,128)(2,1)S(1)}, u32[]{:S(2)}, u32[]{:S(2)}) %collective-permute-start.19) | collective-permute-done | bytes 98336 | tf_op jit(solution)/shard_map/ppermute | solution.py:80
  79.2 2.9 %collective-permute-start.20 = (bf16[96,512]{1,0:T(8,128)(2,1)S(1)}, bf16[96,512]{1,0:T(8,128)(2,1)S(1)}, u32[]{:S(2)}, u32[]{:S(2)}) collective-permute-start(bf16[96,512]{1,0:T(8,128)(2,1)S(1)} %get-tuple-element.78), channel_id=1, source_target_pairs={{0,0},{1,1},{2,3},{3,2},{4,4},{5,5},{6,7},{7,6},{8,8},{9,9},{10,11... | collective-permute-start | bytes 294920 | tf_op jit(solution)/shard_map/ppermute | solution.py:80
  82.1 0.7 join_first.1.refs_3_
  82.8 0.1 collective-permute-done.22.refs_2_
  82.9 1.6 %collective-permute-done.20.refs_0_ = bf16[96,512]{1,0:T(8,128)(2,1)S(1)} collective-permute-done((bf16[96,512]{1,0:T(8,128)(2,1)S(1)}, bf16[96,512]{1,0:T(8,128)(2,1)S(1)}, u32[]{:S(2)}, u32[]{:S(2)}) %collective-permute-start.20) | collective-permute-done | bytes 98336 | tf_op jit(solution)/shard_map/ppermute | solution.py:80
  84.5 0.7 join_rest.1
  (37 shorter events, 0.4 us)
Async XLA Ops:
  0.0 5.1 %copy-start.3 = (bf16[1,384,512]{2,1,0:T(8,128)(2,1)S(1)}, bf16[1,384,512]{2,1,0:T(8,128)(2,1)}, u32[]{:S(2)}) copy-start(bf16[1,384,512]{2,1,0:T(8,128)(2,1)} %param.10) | copy-start | bytes 1179652
  1.7 20.1 %collective-permute-start = (bf16[704,512]{1,0:T(8,128)(2,1)S(1)}, bf16[704,512]{1,0:T(8,128)(2,1)S(1)}, u32[]{:S(2)}, u32[]{:S(2)}) collective-permute-start(bf16[704,512]{1,0:T(8,128)(2,1)S(1)} %pack_own.1.refs_4_.refs_0_.refs_1_), channel_id=1, source_target_pairs={{0,4},{1,5},{2,6},{3,7},{4,8},{5,9},{6,10},{7,11},{8,12},{9,13},{1... | collective-permute-start | bytes 2162696 | tf_op jit(solution)/shard_map/ppermute | solution.py:80
  3.9 17.9 %collective-permute-start.1 = (bf16[704,512]{1,0:T(8,128)(2,1)S(1)}, bf16[704,512]{1,0:T(8,128)(2,1)S(1)}, u32[]{:S(2)}, u32[]{:S(2)}) collective-permute-start(bf16[704,512]{1,0:T(8,128)(2,1)S(1)} %pack_own.1.refs_4_.refs_0_.refs_1_), channel_id=1, source_target_pairs={{0,1},{1,0},{2,3},{3,2},{4,5},{5,4},{6,7},{7,6},{8,9},{9,8},{10,11... | collective-permute-start | bytes 2162696 | tf_op jit(solution)/shard_map/ppermute | solution.py:80
  5.1 24.4 %collective-permute-start.7 = (bf16[96,512]{1,0:T(8,128)(2,1)S(1)}, bf16[96,512]{1,0:T(8,128)(2,1)S(1)}, u32[]{:S(2)}, u32[]{:S(2)}) collective-permute-start(bf16[96,512]{1,0:T(8,128)(2,1)S(1)} %get-tuple-element.48), channel_id=1, source_target_pairs={{0,0},{1,1},{2,3},{3,2},{4,4},{5,5},{6,7},{7,6},{8,8},{9,9},{10,11... | collective-permute-start | bytes 294920 | tf_op jit(solution)/shard_map/ppermute | solution.py:80
  21.7 17.7 %collective-permute-start.2 = (bf16[704,512]{1,0:T(8,128)(2,1)S(1)}, bf16[704,512]{1,0:T(8,128)(2,1)S(1)}, u32[]{:S(2)}, u32[]{:S(2)}) collective-permute-start(bf16[704,512]{1,0:T(8,128)(2,1)S(1)} %collective-permute-done.refs_5_.refs_1_.refs_2_), channel_id=1, source_target_pairs={{0,4},{1,5},{2,6},{3,7},{4,8},{5,9},{6,10},{7,11},{8,12},{9,13},{1... | collective-permute-start | bytes 2162696 | tf_op jit(solution)/shard_map/ppermute | solution.py:80
  21.8 17.6 %collective-permute-start.3 = (bf16[704,512]{1,0:T(8,128)(2,1)S(1)}, bf16[704,512]{1,0:T(8,128)(2,1)S(1)}, u32[]{:S(2)}, u32[]{:S(2)}) collective-permute-start(bf16[704,512]{1,0:T(8,128)(2,1)S(1)} %collective-permute-done.refs_5_.refs_1_.refs_2_), channel_id=1, source_target_pairs={{0,1},{1,0},{2,3},{3,2},{4,5},{5,4},{6,7},{7,6},{8,9},{9,8},{10,11... | collective-permute-start | bytes 2162696 | tf_op jit(solution)/shard_map/ppermute | solution.py:80
  23.1 18.4 %collective-permute-start.4 = (bf16[704,512]{1,0:T(8,128)(2,1)S(1)}, bf16[704,512]{1,0:T(8,128)(2,1)S(1)}, u32[]{:S(2)}, u32[]{:S(2)}) collective-permute-start(bf16[704,512]{1,0:T(8,128)(2,1)S(1)} %collective-permute-done.refs_5_.refs_1_.refs_2_), channel_id=1, source_target_pairs={{0,16},{1,17},{2,18},{3,19},{4,20},{5,21},{6,22},{7,23},{8,24},{9,... | collective-permute-start | bytes 2162696 | tf_op jit(solution)/shard_map/ppermute | solution.py:80
  27.1 14.3 %collective-permute-start.5 = (bf16[704,512]{1,0:T(8,128)(2,1)S(1)}, bf16[704,512]{1,0:T(8,128)(2,1)S(1)}, u32[]{:S(2)}, u32[]{:S(2)}) collective-permute-start(bf16[704,512]{1,0:T(8,128)(2,1)S(1)} %collective-permute-done.refs_5_.refs_1_.refs_2_), channel_id=1, source_target_pairs={{0,2},{1,3},{2,0},{3,1},{4,6},{5,7},{6,4},{7,5},{8,10},{9,11},{10,... | collective-permute-start | bytes 2162696 | tf_op jit(solution)/shard_map/ppermute | solution.py:80
  29.5 12.0 %collective-permute-start.6 = (bf16[704,512]{1,0:T(8,128)(2,1)S(1)}, bf16[704,512]{1,0:T(8,128)(2,1)S(1)}, u32[]{:S(2)}, u32[]{:S(2)}) collective-permute-start(bf16[704,512]{1,0:T(8,128)(2,1)S(1)} %collective-permute-done.1.refs_7_.refs_3_.refs_4_), channel_id=1, source_target_pairs={{0,2},{1,3},{2,0},{3,1},{4,6},{5,7},{6,4},{7,5},{8,10},{9,11},{10,... | collective-permute-start | bytes 2162696 | tf_op jit(solution)/shard_map/ppermute | solution.py:80
  41.5 13.1 %collective-permute-start.8 = (bf16[448,512]{1,0:T(8,128)(2,1)S(1)}, bf16[448,512]{1,0:T(8,128)(2,1)S(1)}, u32[]{:S(2)}, u32[]{:S(2)}) collective-permute-start(bf16[448,512]{1,0:T(8,128)(2,1)S(1)} %slice.26), channel_id=1, source_target_pairs={{0,1},{1,0},{2,3},{3,2},{4,5},{5,4},{6,7},{7,6},{8,9},{9,8},{10,11... | collective-permute-start | bytes 1376264 | tf_op jit(solution)/shard_map/ppermute | solution.py:80
  41.9 12.8 %collective-permute-start.9 = (bf16[448,512]{1,0:T(8,128)(2,1)S(1)}, bf16[448,512]{1,0:T(8,128)(2,1)S(1)}, u32[]{:S(2)}, u32[]{:S(2)}) collective-permute-start(bf16[448,512]{1,0:T(8,128)(2,1)S(1)} %slice.27), channel_id=1, source_target_pairs={{0,16},{1,17},{2,18},{3,19},{4,20},{5,21},{6,22},{7,23},{8,24},{9,... | collective-permute-start | bytes 1376264 | tf_op jit(solution)/shard_map/ppermute | solution.py:80
  43.2 5.5 %collective-permute-start.10 = (bf16[96,512]{1,0:T(8,128)(2,1)S(1)}, bf16[96,512]{1,0:T(8,128)(2,1)S(1)}, u32[]{:S(2)}, u32[]{:S(2)}) collective-permute-start(bf16[96,512]{1,0:T(8,128)(2,1)S(1)} %get-tuple-element.56), channel_id=1, source_target_pairs={{0,4},{1,5},{2,7},{3,6},{4,0},{5,1},{6,3},{7,2},{8,12},{9,13},{10,... | collective-permute-start | bytes 294920 | tf_op jit(solution)/shard_map/ppermute | solution.py:80
  43.2 5.5 %collective-permute-start.11 = (bf16[96,512]{1,0:T(8,128)(2,1)S(1)}, bf16[96,512]{1,0:T(8,128)(2,1)S(1)}, u32[]{:S(2)}, u32[]{:S(2)}) collective-permute-start(bf16[96,512]{1,0:T(8,128)(2,1)S(1)} %get-tuple-element.57), channel_id=1, source_target_pairs={{0,8},{1,9},{2,11},{3,10},{4,12},{5,13},{6,15},{7,14},{8,0},{9,1},... | collective-permute-start | bytes 294920 | tf_op jit(solution)/shard_map/ppermute | solution.py:80
  46.4 6.3 %collective-permute-start.12 = (bf16[96,512]{1,0:T(8,128)(2,1)S(1)}, bf16[96,512]{1,0:T(8,128)(2,1)S(1)}, u32[]{:S(2)}, u32[]{:S(2)}) collective-permute-start(bf16[96,512]{1,0:T(8,128)(2,1)S(1)} %get-tuple-element.58), channel_id=1, source_target_pairs={{0,12},{1,13},{2,15},{3,14},{4,8},{5,9},{6,11},{7,10},{8,4},{9,5},... | collective-permute-start | bytes 294920 | tf_op jit(solution)/shard_map/ppermute | solution.py:80
  54.8 7.3 %copy-start.6 = (f32[2,512]{1,0:T(2,128)S(1)}, f32[2,512]{1,0:T(2,128)}, u32[]{:S(2)}) copy-start(f32[2,512]{1,0:T(2,128)} %gain_ref.7) | copy-start | bytes 12292
  54.9 7.2 %collective-permute-start.13 = (bf16[2240,512]{1,0:T(8,128)(2,1)S(1)}, bf16[2240,512]{1,0:T(8,128)(2,1)S(1)}, u32[]{:S(2)}, u32[]{:S(2)}) collective-permute-start(bf16[2240,512]{1,0:T(8,128)(2,1)S(1)} %constant_dynamic-update-slice_fusion), channel_id=1, source_target_pairs={{0,2},{1,3},{2,0},{3,1},{4,6},{5,7},{6,4},{7,5},{8,10},{9,11},{10,... | collective-permute-start | bytes 6881288 | tf_op jit(solution)/shard_map/ppermute | solution.py:80
  58.0 8.3 %collective-permute-start.15 = (bf16[256,512]{1,0:T(8,128)(2,1)S(1)}, bf16[256,512]{1,0:T(8,128)(2,1)S(1)}, u32[]{:S(2)}, u32[]{:S(2)}) collective-permute-start(bf16[256,512]{1,0:T(8,128)(2,1)S(1)} %slice.31), channel_id=1, source_target_pairs={{0,1},{1,0},{2,3},{3,2},{4,5},{5,4},{6,7},{7,6},{8,9},{9,8},{10,11... | collective-permute-start | bytes 786440 | tf_op jit(solution)/shard_map/ppermute | solution.py:80
  58.3 7.9 %collective-permute-start.16 = (bf16[256,512]{1,0:T(8,128)(2,1)S(1)}, bf16[256,512]{1,0:T(8,128)(2,1)S(1)}, u32[]{:S(2)}, u32[]{:S(2)}) collective-permute-start(bf16[256,512]{1,0:T(8,128)(2,1)S(1)} %slice.32), channel_id=1, source_target_pairs={{0,16},{1,17},{2,18},{3,19},{4,20},{5,21},{6,22},{7,23},{8,24},{9,... | collective-permute-start | bytes 786440 | tf_op jit(solution)/shard_map/ppermute | solution.py:80
  59.6 3.8 %copy-start.4 = (f32[2,512]{1,0:T(2,128)S(1)}, f32[2,512]{1,0:T(2,128)}, u32[]{:S(2)}) copy-start(f32[2,512]{1,0:T(2,128)} %gain_ref.9) | copy-start | bytes 12292
  59.6 3.7 %copy-start.5 = (f32[512]{0:T(512)S(1)}, f32[512]{0:T(512)}, u32[]{:S(2)}) copy-start(f32[512]{0:T(512)} %param.16) | copy-start | bytes 6148
  62.9 4.2 %collective-permute-start.14 = (bf16[768,512]{1,0:T(8,128)(2,1)S(1)}, bf16[768,512]{1,0:T(8,128)(2,1)S(1)}, u32[]{:S(2)}, u32[]{:S(2)}) collective-permute-start(bf16[768,512]{1,0:T(8,128)(2,1)S(1)} %pad_maximum_fusion), channel_id=1, source_target_pairs={{0,2},{1,3},{2,0},{3,1},{4,6},{5,7},{6,4},{7,5},{8,10},{9,11},{10,... | collective-permute-start | bytes 2359304 | tf_op jit(solution)/shard_map/ppermute | solution.py:80
  66.3 2.5 %collective-permute-start.17 = (bf16[512,512]{1,0:T(8,128)(2,1)S(1)}, bf16[512,512]{1,0:T(8,128)(2,1)S(1)}, u32[]{:S(2)}, u32[]{:S(2)}) collective-permute-start(bf16[512,512]{1,0:T(8,128)(2,1)S(1)} %constant_dynamic-update-slice_fusion.2.refs_1_), channel_id=1, source_target_pairs={{0,2},{1,3},{2,0},{3,1},{4,6},{5,7},{6,4},{7,5},{8,10},{9,11},{10,... | collective-permute-start | bytes 1572872 | tf_op jit(solution)/shard_map/ppermute | solution.py:80
  68.8 1.2 %copy-start.2 = (bf16[512,512]{1,0:T(8,128)(2,1)S(1)}, bf16[512,512]{1,0:T(8,128)(2,1)}, u32[]{:S(2)}) copy-start(bf16[512,512]{1,0:T(8,128)(2,1)} %weight_ref.1) | copy-start | bytes 1572868
  68.8 2.7 %copy-start = (bf16[512,512]{1,0:T(8,128)(2,1)S(1)}, bf16[512,512]{1,0:T(8,128)(2,1)}, u32[]{:S(2)}) copy-start(bf16[512,512]{1,0:T(8,128)(2,1)} %gate_ref.1) | copy-start | bytes 1572868
  68.8 2.7 %copy-start.1 = (bf16[512,512]{1,0:T(8,128)(2,1)S(1)}, bf16[512,512]{1,0:T(8,128)(2,1)}, u32[]{:S(2)}) copy-start(bf16[512,512]{1,0:T(8,128)(2,1)} %out_ref.1) | copy-start | bytes 1572868
  69.7 1.8 %collective-permute-start.18 = (bf16[384,512]{1,0:T(8,128)(2,1)S(1)}, bf16[384,512]{1,0:T(8,128)(2,1)S(1)}, u32[]{:S(2)}, u32[]{:S(2)}) collective-permute-start(bf16[384,512]{1,0:T(8,128)(2,1)S(1)} %ff1.3.final_ref), channel_id=1, source_target_pairs={{0,2},{1,3},{2,0},{3,1},{4,6},{5,7},{6,4},{7,5},{8,10},{9,11},{10,... | collective-permute-start | bytes 1179656 | tf_op jit(solution)/shard_map/ppermute | solution.py:80
  72.3 6.9 %collective-permute-start.19 = (bf16[96,512]{1,0:T(8,128)(2,1)S(1)}, bf16[96,512]{1,0:T(8,128)(2,1)S(1)}, u32[]{:S(2)}, u32[]{:S(2)}) collective-permute-start(bf16[96,512]{1,0:T(8,128)(2,1)S(1)} %get-tuple-element.77), channel_id=1, source_target_pairs={{0,4},{1,5},{2,7},{3,6},{4,0},{5,1},{6,3},{7,2},{8,12},{9,13},{10,... | collective-permute-start | bytes 294920 | tf_op jit(solution)/shard_map/ppermute | solution.py:80
  72.6 10.2 %collective-permute-start.21 = (bf16[96,512]{1,0:T(8,128)(2,1)S(1)}, bf16[96,512]{1,0:T(8,128)(2,1)S(1)}, u32[]{:S(2)}, u32[]{:S(2)}) collective-permute-start(bf16[96,512]{1,0:T(8,128)(2,1)S(1)} %get-tuple-element.79), channel_id=1, source_target_pairs={{0,8},{1,9},{2,11},{3,10},{4,12},{5,13},{6,15},{7,14},{8,0},{9,1},... | collective-permute-start | bytes 294920 | tf_op jit(solution)/shard_map/ppermute | solution.py:80
  75.4 7.5 %collective-permute-start.22 = (bf16[96,512]{1,0:T(8,128)(2,1)S(1)}, bf16[96,512]{1,0:T(8,128)(2,1)S(1)}, u32[]{:S(2)}, u32[]{:S(2)}) collective-permute-start(bf16[96,512]{1,0:T(8,128)(2,1)S(1)} %get-tuple-element.80), channel_id=1, source_target_pairs={{0,12},{1,13},{2,15},{3,14},{4,8},{5,9},{6,11},{7,10},{8,4},{9,5},... | collective-permute-start | bytes 294920 | tf_op jit(solution)/shard_map/ppermute | solution.py:80
  79.2 5.3 %collective-permute-start.20 = (bf16[96,512]{1,0:T(8,128)(2,1)S(1)}, bf16[96,512]{1,0:T(8,128)(2,1)S(1)}, u32[]{:S(2)}, u32[]{:S(2)}) collective-permute-start(bf16[96,512]{1,0:T(8,128)(2,1)S(1)} %get-tuple-element.78), channel_id=1, source_target_pairs={{0,0},{1,1},{2,3},{3,2},{4,4},{5,5},{6,7},{7,6},{8,8},{9,9},{10,11... | collective-permute-start | bytes 294920 | tf_op jit(solution)/shard_map/ppermute | solution.py:80
